TPU v7x, 32 devices: a whole 2x2x4 slice. The times are simulated.
32 devices in a mesh: lat: 4 (over y, core), lon: 8 (over z, x).
Axes of the slice: x: 2, y: 2, z: 4, core: 2. Of those that a mesh axis runs over, the one named last changes fastest.
Arguments:
- tracers: float32 [128, 768, 128], P('lat', 'lon'), may hold values from -6 to 6
- owners: int32 [4, 8, 3072, 1], P('lat', 'lon'), may hold values from 0 to 7; in each aligned block of 3072 rows (0 to 3071, 3072 to 6143, ..., all dimensions but the last counted through in order) at most 1152 rows name the same one
- columns: int32 [128, 768], P('lat', 'lon'), may hold values from 0 to 95
- lat_shift: int32 [128, 768], P('lat', 'lon'), may hold values from 0 to 2
- fractions: float32 [2, 128, 768], P(None, 'lat', 'lon'), may hold values from 0 to 1
Outputs:
- advected: float32 [128, 768, 128], P('lat', 'lon')
Inputs may be any that keep to these rules, and one draw needn't show every extreme that they name: `owners`: among the 3072 cells of one device no sector is named more than 1152 times, a bound that some block reaches.
All inputs are finite; a program needn't handle non-finite values.
Results may differ from a plain program's by a relative error of at most 0.0003.
Values sent between devices are 32-bit elements; how exact they have to be, the bound alone decides.
No kernel may reach another device: no remote copies, remote signals or barrier semaphores. Data moves between devices by JAX's collectives and lax.ppermute only.
A program may use at most 192 MiB of HBM per device.

v0:
```python
import math

import jax
import jax.numpy as jnp
from jax import lax
from jax.sharding import PartitionSpec as P

RIM = 16


def extended_2(cells, sides, width, closed):
    for axis, dim in sides:
        count = lax.axis_size(axis)
        ends = count if closed else count - 1
        head = lax.slice_in_dim(cells, 0, width, axis=dim)
        tail = lax.slice_in_dim(cells, cells.shape[dim] - width, cells.shape[dim], axis=dim)
        cells = jnp.concatenate(
            [
                lax.ppermute(tail, axis, [(i, (i + 1) % count) for i in range(ends)]),
                cells,
                lax.ppermute(head, axis, [((i + 1) % count, i) for i in range(ends)]),
            ],
            axis=dim,
        )
    return cells


def spline_weights(shift):
    rest = 1.0 - shift
    cube = shift * shift * shift
    return [
        rest * rest * rest / 6.0,
        (3.0 * cube - 6.0 * shift * shift + 4.0) / 6.0,
        (-3.0 * cube + 3.0 * shift * shift + 3.0 * shift + 1.0) / 6.0,
        cube / 6.0,
    ]


def parity_of(distance):
    return (1 - 2 * (distance % 2)).astype(jnp.float32)


def periodic_green(length):
    ratio_abs = 2.0 - math.sqrt(3.0)
    places = jnp.arange(length, dtype=jnp.int32)
    distance = (places[:, None] - places[None, :]) % length
    far_side = length - distance
    near_term = parity_of(distance) * jnp.power(
        jnp.float32(ratio_abs), distance.astype(jnp.float32)
    )
    far_term = parity_of(far_side) * jnp.power(jnp.float32(ratio_abs), far_side.astype(jnp.float32))
    closing = 1.0 - (1.0 - 2.0 * (length % 2)) * ratio_abs**length
    return (math.sqrt(3.0) * (near_term + far_term) / closing).astype(jnp.float32)


def body(tracers, owners, columns, lat_shift, fractions):
    band_rows, sector_cols, channels = tracers.shape
    bands = lax.axis_size("lat")
    sectors = lax.axis_size("lon")
    band_index = lax.axis_index("lat")
    lat_total = band_rows * bands
    lon_total = sector_cols * sectors
    cells = band_rows * sector_cols
    extended = extended_2(tracers, (("lat", 0),), RIM, False)
    span_rows = band_rows + 2 * RIM
    global_row = band_index * band_rows - RIM + jnp.arange(span_rows, dtype=jnp.int32)
    fixed_row = (global_row <= 0) | (global_row >= lat_total - 1)
    diagonal = jnp.where(fixed_row, 1.0, 4.0 / 6.0).astype(jnp.float32)
    off_diag = jnp.where(fixed_row, 0.0, 1.0 / 6.0).astype(jnp.float32)
    lower = off_diag.at[0].set(0.0)
    upper = off_diag.at[span_rows - 1].set(0.0)
    solved = lax.linalg.tridiagonal_solve(
        lower, diagonal, upper, extended.reshape(span_rows, sector_cols * channels)
    )
    solved = solved[RIM : RIM + band_rows].reshape(band_rows, sector_cols, channels)
    full_lines = lax.all_to_all(solved, "lon", split_axis=0, concat_axis=1, tiled=True)
    filtered = jnp.einsum(
        "jk,rkc->rjc",
        periodic_green(lon_total),
        full_lines,
        precision=lax.Precision.HIGHEST,
        preferred_element_type=jnp.float32,
    )
    coeffs = lax.all_to_all(filtered, "lon", split_axis=1, concat_axis=0, tiled=True)
    bordered = extended_2(coeffs, (("lat", 0), ("lon", 1)), 3, True)
    stride = sector_cols + 6
    flat_coeffs = bordered.reshape(-1, channels)
    capacity = 3 * cells // sectors
    owner_ids = owners.reshape(cells)
    onehot = (owner_ids[:, None] == jnp.arange(sectors, dtype=jnp.int32)[None, :]).astype(jnp.int32)
    running = jnp.cumsum(onehot, axis=0) - 1
    slot_of = jnp.sum(running * onehot, axis=1)
    target = owner_ids * capacity + slot_of
    cell_row = jnp.arange(cells, dtype=jnp.int32) // sector_cols
    lat_dep = jnp.clip(
        band_index * band_rows + cell_row - 1 + lat_shift.reshape(cells), 1, lat_total - 3
    )
    local_row = (lat_dep - band_index * band_rows + 3).astype(jnp.float32)
    local_col = (columns.reshape(cells) + 3).astype(jnp.float32)
    lat_frac = fractions[0].reshape(cells)
    lon_frac = fractions[1].reshape(cells)
    payload = jnp.stack([local_row, local_col, lat_frac, lon_frac], axis=0)
    buffer = jnp.zeros((4, sectors * capacity), jnp.float32).at[0:2].set(3.0)
    buffer = buffer.at[:, target].set(payload).reshape(4, sectors, capacity)
    request = lax.all_to_all(buffer, "lon", split_axis=1, concat_axis=1, tiled=True)
    request_rows = request[0].astype(jnp.int32)
    request_cols = request[1].astype(jnp.int32)
    lat_w = spline_weights(request[2])
    lon_w = spline_weights(request[3])
    total = jnp.zeros(request_rows.shape + (channels,), jnp.float32)
    for lat_tap in range(4):
        for lon_tap in range(4):
            flat_index = (request_rows - 1 + lat_tap) * stride + request_cols - 1 + lon_tap
            total = total + (lat_w[lat_tap] * lon_w[lon_tap])[..., None] * flat_coeffs[flat_index]
    gotten = lax.all_to_all(total, "lon", split_axis=0, concat_axis=0, tiled=True)
    advected = gotten.reshape(-1, channels)[target]
    return advected.reshape(band_rows, sector_cols, channels)


def solution(mesh):
    in_specs = (
        P("lat", "lon", None),
        P("lat", "lon", None, None),
        P("lat", "lon"),
        P("lat", "lon"),
        P(None, "lat", "lon"),
    )
    out_specs = P("lat", "lon", None)
    return jax.shard_map(body, mesh=mesh, in_specs=in_specs, out_specs=out_specs, check_vma=False)
```

profile of v0, /device:TPU:0, one launch (start us, length us, event | category | flops | bytes accessed | tf_op | source)
XLA Modules:
  0.0 1027.8 jit_solution(13548067010759329038)
XLA Ops:
  0.0 2.7 fusion.207
  2.7 1.3 collective-permute-start.1
  4.0 3.1 collective-permute-start
  7.5 2.3 reduce-window.6
  11.1 4.0 copy.205
  15.1 12.6 %scatter_fusion = f32[4,9216]{0,1:T(8,128)} fusion(f32[4,9216]{0,1:T(8,128)} %copy.205, s32[3072]{0:T(1024)S(1)} %bitcast.891, f32[3072,4]{1,0:T(8,128)S(1)} %copy.34), kind=kCustom, calls=%fused_computation.17 | custom fusion | bytes 159744 | tf_op jit(solution)/shard_map/scatter | solution.py:104
  27.7 3.8 copy.35
  31.5 7.3 all-to-all-start
  40.9 0.7 fusion.215
  41.6 0.7 fusion.213
  163.4 0.7 fusion.208
  164.9 27.9 %fusion.157 = (f32[12288]{0:T(1024)S(1)}, f32[1,96,128]{2,1,0:T(8,128)S(1)}) fusion(f32[16,96,128]{2,1,0:T(8,128)S(1)} %collective-permute-done, f32[32,96,128]{2,1,0:T(8,128)S(1)} %copy-done, f32[]{:T(128)S(6)} %sub.9216, f32[]{:T(128)S(6)} %sub.9214, f32[]{:T(128)S(6)} %sub.9212, f32[]{:T(128)S(6)} %sub.9210, f32[]{:T(128)S(6)} %sub.9208, f32[]{:T(128)S(6)} %sub.9206, ...), kind=kLoop, calls=%fused_computation.289 | loop fusion | flops 1597440 | bytes 2261340 | tf_op jit(solution)/shard_map/eval_jaxpr/div | solution.py:72
  192.8 37.5 %constant_dynamic-update-slice_fusion.31 = (f32[32,96,128]{2,1,0:T(8,128)}, f32[1,96,128]{2,1,0:T(8,128)S(1)}, f32[1,96,128]{2,1,0:T(8,128)S(1)}, f32[1,96,128]{...) fusion(f32[]{:T(128)S(6)} %div.7454, ...), kind=kLoop, calls=%fused_computation.122 | loop fusion | flops 3293183 | bytes 4227724
  246.5 13.3 %constant_dynamic-update-slice_fusion.4 = (f32[32,96,128]{2,1,0:T(8,128)}, f32[12288]{0:T(1024)S(1)}, f32[12288]{0:T(1024)S(1)}, f32[12288]{0:T(1024)S(1)}, f32[12288]{0:T(1024)S(1)}) fusion(f32[32,96,128]{2,1,0:T(8,128)} %constant_dynamic-update-slice_fusion.5, f32[12288]{0:T(1024)S(1)} %get-tuple-element.96, f32[]{:T(128)S(6)} %div.7535, f32[]{:T(128)S(6)} %div.7538, ...), kind=kLoop, calls=%fused_computation.95 | loop fusion | flops 1228800 | bytes 1288352
  262.3 6.0 all-to-all-start.1
  268.6 37.5 %all-to-all-done.1 = f32[32,96,128]{2,1,0:T(8,128)S(1)} async-done(((f32[32,96,128]{2,1,0:T(8,128)}), f32[32,96,128]{2,1,0:T(8,128)S(1)}, u32[]{:S(2)}, u32[]{:S(2)}) %all-to-all-start.1) | async-done | bytes 1572896 | tf_op jit(solution)/shard_map/all_to_all | solution.py:76
  306.1 12.3 %fusion.32 = f32[4,768,128]{1,2,0:T(8,128)S(1)} fusion(f32[4,768,128]{2,1,0:T(8,128)S(1)} %bitcast.888), kind=kOutput, calls=%fused_computation.56 | convolution fusion | flops 3648651264 | bytes 3145728 | tf_op jit(solution)/shard_map/jk,rkc->rjc/dot_general | solution.py:77
  318.4 1.6 copy.40
  320.0 3.8 all-to-all-start.2
  325.2 0.9 fusion.190
  326.1 34.9 %all-to-all-done.2 = f32[4,768,128]{2,0,1:T(4,128)S(1)} async-done(((f32[4,768,128]{2,0,1:T(4,128)}), f32[4,768,128]{2,0,1:T(4,128)S(1)}, u32[]{:S(2)}, u32[]{:S(2)}) %all-to-all-start.2) | async-done | bytes 1572896 | tf_op jit(solution)/shard_map/all_to_all | solution.py:84
  361.3 1.7 collective-permute-start.3
  363.1 4.3 collective-permute-done.2
  367.4 1.5 collective-permute-start.4
  369.0 3.3 collective-permute-start.5
  372.2 2.4 collective-permute-done.4
  375.0 1.5 pad_maximum_fusion
  376.6 1.6 reshape.5413
  378.2 31.0 %gather_fusion.9 = f32[9216,128]{1,0:T(8,128)} fusion(f32[3876,128]{1,0:T(8,128)S(1)} %reshape.5413, s32[9216]{0:T(1024)S(1)} %broadcast_clamp_fusion.6), kind=kCustom, calls=%fused_computation.9 | custom fusion | bytes 9474048 | tf_op jit(solution)/shard_map/gather | solution.py:114
  409.2 31.0 %gather_fusion.10 = f32[9216,128]{1,0:T(8,128)} fusion(f32[3876,128]{1,0:T(8,128)S(1)} %reshape.5413, s32[9216]{0:T(1024)S(1)} %broadcast_clamp_fusion.5), kind=kCustom, calls=%fused_computation.10 | custom fusion | bytes 9474048 | tf_op jit(solution)/shard_map/gather | solution.py:114
  440.2 31.0 %gather_fusion.11 = f32[9216,128]{1,0:T(8,128)} fusion(f32[3876,128]{1,0:T(8,128)S(1)} %reshape.5413, s32[9216]{0:T(1024)S(1)} %broadcast_clamp_fusion.4), kind=kCustom, calls=%fused_computation.11 | custom fusion | bytes 9474048 | tf_op jit(solution)/shard_map/gather | solution.py:114
  471.2 31.0 %gather_fusion.15 = f32[9216,128]{1,0:T(8,128)} fusion(f32[3876,128]{1,0:T(8,128)S(1)} %reshape.5413, s32[9216]{0:T(1024)S(1)} %broadcast_clamp_fusion), kind=kCustom, calls=%fused_computation.15 | custom fusion | bytes 9474048 | tf_op jit(solution)/shard_map/gather | solution.py:114
  502.2 31.0 %gather_fusion.14 = f32[9216,128]{1,0:T(8,128)} fusion(f32[3876,128]{1,0:T(8,128)S(1)} %reshape.5413, s32[9216]{0:T(1024)S(1)} %broadcast_clamp_fusion.1), kind=kCustom, calls=%fused_computation.14 | custom fusion | bytes 9474048 | tf_op jit(solution)/shard_map/gather | solution.py:114
  533.3 31.0 %gather_fusion.13 = f32[9216,128]{1,0:T(8,128)} fusion(f32[3876,128]{1,0:T(8,128)S(1)} %reshape.5413, s32[9216]{0:T(1024)S(1)} %broadcast_clamp_fusion.2), kind=kCustom, calls=%fused_computation.13 | custom fusion | bytes 9474048 | tf_op jit(solution)/shard_map/gather | solution.py:114
  564.3 31.0 %gather_fusion.1 = f32[9216,128]{1,0:T(8,128)} fusion(f32[3876,128]{1,0:T(8,128)S(1)} %reshape.5413, s32[9216]{0:T(1024)S(1)} %broadcast_clamp_fusion.14), kind=kCustom, calls=%fused_computation.1 | custom fusion | bytes 9474048 | tf_op jit(solution)/shard_map/gather | solution.py:114
  595.3 31.0 %gather_fusion.2 = f32[9216,128]{1,0:T(8,128)} fusion(f32[3876,128]{1,0:T(8,128)S(1)} %reshape.5413, s32[9216]{0:T(1024)S(1)} %broadcast_clamp_fusion.13), kind=kCustom, calls=%fused_computation.2 | custom fusion | bytes 9474048 | tf_op jit(solution)/shard_map/gather | solution.py:114
  626.3 31.0 %gather_fusion.3 = f32[9216,128]{1,0:T(8,128)} fusion(f32[3876,128]{1,0:T(8,128)S(1)} %reshape.5413, s32[9216]{0:T(1024)S(1)} %broadcast_clamp_fusion.12), kind=kCustom, calls=%fused_computation.3 | custom fusion | bytes 9474048 | tf_op jit(solution)/shard_map/gather | solution.py:114
  657.3 31.1 %gather_fusion.7 = f32[9216,128]{1,0:T(8,128)} fusion(f32[3876,128]{1,0:T(8,128)S(1)} %reshape.5413, s32[9216]{0:T(1024)S(1)} %broadcast_clamp_fusion.8), kind=kCustom, calls=%fused_computation.7 | custom fusion | bytes 9474048 | tf_op jit(solution)/shard_map/gather | solution.py:114
  688.4 31.0 %gather_fusion.6 = f32[9216,128]{1,0:T(8,128)} fusion(f32[3876,128]{1,0:T(8,128)S(1)} %reshape.5413, s32[9216]{0:T(1024)S(1)} %broadcast_clamp_fusion.9), kind=kCustom, calls=%fused_computation.6 | custom fusion | bytes 9474048 | tf_op jit(solution)/shard_map/gather | solution.py:114
  719.4 31.0 %gather_fusion.5 = f32[9216,128]{1,0:T(8,128)} fusion(f32[3876,128]{1,0:T(8,128)S(1)} %reshape.5413, s32[9216]{0:T(1024)S(1)} %broadcast_clamp_fusion.10), kind=kCustom, calls=%fused_computation.5 | custom fusion | bytes 9474048 | tf_op jit(solution)/shard_map/gather | solution.py:114
  750.4 31.0 %gather_fusion.12 = f32[9216,128]{1,0:T(8,128)} fusion(f32[3876,128]{1,0:T(8,128)S(1)} %reshape.5413, s32[9216]{0:T(1024)S(1)} %get-tuple-element.307), kind=kCustom, calls=%fused_computation.12 | custom fusion | bytes 9474048 | tf_op jit(solution)/shard_map/gather | solution.py:114
  781.5 31.0 %gather_fusion.4 = f32[9216,128]{1,0:T(8,128)} fusion(f32[3876,128]{1,0:T(8,128)S(1)} %reshape.5413, s32[9216]{0:T(1024)S(1)} %copy-done.2), kind=kCustom, calls=%fused_computation.4 | custom fusion | bytes 9474048 | tf_op jit(solution)/shard_map/gather | solution.py:114
  812.5 31.0 %gather_fusion.8 = f32[9216,128]{1,0:T(8,128)} fusion(f32[3876,128]{1,0:T(8,128)S(1)} %reshape.5413, s32[9216]{0:T(1024)S(1)} %copy-done.3), kind=kCustom, calls=%fused_computation.8 | custom fusion | bytes 9474048 | tf_op jit(solution)/shard_map/gather | solution.py:114
  843.7 31.0 %gather_fusion = f32[9216,128]{1,0:T(8,128)} fusion(f32[3876,128]{1,0:T(8,128)S(1)} %reshape.5413, s32[9216]{0:T(1024)S(1)} %copy-done.1), kind=kCustom, calls=%fused_computation | custom fusion | bytes 9474048 | tf_op jit(solution)/shard_map/gather | solution.py:114
  874.8 30.8 %multiply_add_fusion = f32[8,1152,128]{2,1,0:T(8,128)} fusion(f32[8,1152,128]{2,1,0:T(8,128)} %bitcast.870, f32[8,1152,128]{2,1,0:T(8,128)} %bitcast.871, f32[8,1152,128]{2,1,0:T(8,128)} %bitcast.872, f32[8,1152,128]{2,1,0:T(8,128)} %bitcast.879, f32[8,1152,128]{2,1,0:T(8,128)} %bitcast.869, f32[8,1152,128]{2,1,0:T(8,128)} %bitcast.868, ...), kind=kLoop, calls=%fused_computation.18 | loop fusion | flops 36569088 | bytes 80805888 | tf_op jit(solution)/shard_map/add | solution.py:114
  905.7 5.6 all-to-all-start.3
  911.3 103.3 %all-to-all-done.3 = f32[8,1152,128]{2,1,0:T(8,128)} async-done(((f32[8,1152,128]{2,1,0:T(8,128)}), f32[8,1152,128]{2,1,0:T(8,128)}, u32[]{:S(2)}, u32[]{:S(2)}) %all-to-all-start.3) | async-done | bytes 4718624 | tf_op jit(solution)/shard_map/all_to_all | solution.py:115
  1014.6 13.2 %gather_fusion.16 = f32[3072,128]{1,0:T(8,128)} fusion(f32[9216,128]{1,0:T(8,128)} %bitcast.230, s32[3072]{0:T(1024)S(1)} %broadcast_clamp_fusion.16), kind=kCustom, calls=%fused_computation.16 | custom fusion | bytes 3158016 | tf_op jit(solution)/shard_map/gather | solution.py:116
  (157 shorter events, 27.7 us)
Async XLA Ops:
  0.0 7.1 copy-start.28
  0.0 7.2 copy-start.29
  0.0 7.3 copy-start.27
  0.0 7.5 copy-start.24
  2.7 190.1 %collective-permute-start.1 = (f32[16,96,128]{2,1,0:T(8,128)}, f32[16,96,128]{2,1,0:T(8,128)S(1)}, u32[]{:S(2)}, u32[]{:S(2)}) collective-permute-start(f32[16,96,128]{2,1,0:T(8,128)} %get-tuple-element.129), channel_id=1, source_target_pairs={{8,0},{16,8},{24,16},{9,1},{17,9},{25,17},{10,2},{18,10},{26,18},{... | collective-permute-start | bytes 2359304 | tf_op jit(solution)/shard_map/ppermute | solution.py:21
  4.0 160.9 %collective-permute-start = (f32[16,96,128]{2,1,0:T(8,128)}, f32[16,96,128]{2,1,0:T(8,128)S(1)}, u32[]{:S(2)}, u32[]{:S(2)}) collective-permute-start(f32[16,96,128]{2,1,0:T(8,128)} %get-tuple-element.130), channel_id=1, source_target_pairs={{0,8},{8,16},{16,24},{1,9},{9,17},{17,25},{2,10},{10,18},{18,26},{... | collective-permute-start | bytes 2359304 | tf_op jit(solution)/shard_map/ppermute | solution.py:19
  10.5 4.6 copy-start.25
  27.7 137.2 %copy-start = (f32[32,96,128]{2,1,0:T(8,128)S(1)}, f32[32,96,128]{2,1,0:T(8,128)}, u32[]{:S(2)}) copy-start(f32[32,96,128]{2,1,0:T(8,128)} %param.11) | copy-start | bytes 4718596
  31.5 131.9 %all-to-all-start = ((f32[4,8,1152]{2,0,1:T(4,128)}), f32[4,8,1152]{2,0,1:T(4,128)S(1)}, u32[]{:S(2)}, u32[]{:S(2)}) async-start(f32[4,8,1152]{2,0,1:T(4,128)} %copy.35), calls=%async_computation | async-start | bytes 294912 | tf_op jit(solution)/shard_map/all_to_all | solution.py:105
  246.5 21.9 %copy-start.21 = (s32[8,1152,1]{1,0,2:T(8,128)S(1)}, s32[8,1152,1]{1,0,2:T(8,128)}, u32[]{:S(2)}) copy-start(s32[8,1152,1]{1,0,2:T(8,128)} %get-tuple-element.160) | copy-start | bytes 110596
  246.5 21.9 %copy-start.20 = (s32[8,1152,1]{1,0,2:T(8,128)S(1)}, s32[8,1152,1]{1,0,2:T(8,128)}, u32[]{:S(2)}) copy-start(s32[8,1152,1]{1,0,2:T(8,128)} %get-tuple-element.161) | copy-start | bytes 110596
  262.3 43.7 %all-to-all-start.1 = ((f32[32,96,128]{2,1,0:T(8,128)}), f32[32,96,128]{2,1,0:T(8,128)S(1)}, u32[]{:S(2)}, u32[]{:S(2)}) async-start(f32[32,96,128]{2,1,0:T(8,128)} %constant_dynamic-update-slice_fusion), calls=%async_computation.1 | async-start | bytes 3145728 | tf_op jit(solution)/shard_map/all_to_all | solution.py:76
  320.0 5.2 copy-start.22
  320.0 5.2 copy-start.23
  320.0 41.0 %all-to-all-start.2 = ((f32[4,768,128]{2,0,1:T(4,128)}), f32[4,768,128]{2,0,1:T(4,128)S(1)}, u32[]{:S(2)}, u32[]{:S(2)}) async-start(f32[4,768,128]{2,0,1:T(4,128)} %copy.40), calls=%async_computation.2 | async-start | bytes 3145728 | tf_op jit(solution)/shard_map/all_to_all | solution.py:84
  361.2 6.2 collective-permute-start.2
  361.3 6.1 collective-permute-start.3
  367.4 7.2 collective-permute-start.4
  369.0 6.1 collective-permute-start.5
  750.4 31.0 %copy-start.2 = (s32[9216]{0:T(1024)S(1)}, s32[9216]{0:T(1024)}, u32[]{:S(2)}) copy-start(s32[9216]{0:T(1024)} %get-tuple-element.309) | copy-start | bytes 110596
  781.5 31.0 %copy-start.3 = (s32[9216]{0:T(1024)S(1)}, s32[9216]{0:T(1024)}, u32[]{:S(2)}) copy-start(s32[9216]{0:T(1024)} %get-tuple-element.308) | copy-start | bytes 110596
  812.5 31.0 %copy-start.1 = (s32[9216]{0:T(1024)S(1)}, s32[9216]{0:T(1024)}, u32[]{:S(2)}) copy-start(s32[9216]{0:T(1024)} %get-tuple-element.310) | copy-start | bytes 110596
  843.5 31.2 %copy-start.4 = (f32[8,1152]{1,0:T(8,128)S(1)}, f32[8,1152]{1,0:T(8,128)}, u32[]{:S(2)}) copy-start(f32[8,1152]{1,0:T(8,128)} %get-tuple-element.135) | copy-start | bytes 110596
  843.5 31.2 %copy-start.5 = (f32[8,1152]{1,0:T(8,128)S(1)}, f32[8,1152]{1,0:T(8,128)}, u32[]{:S(2)}) copy-start(f32[8,1152]{1,0:T(8,128)} %get-tuple-element.136) | copy-start | bytes 110596
  843.5 31.2 %copy-start.6 = (f32[8,1152]{1,0:T(8,128)S(1)}, f32[8,1152]{1,0:T(8,128)}, u32[]{:S(2)}) copy-start(f32[8,1152]{1,0:T(8,128)} %get-tuple-element.137) | copy-start | bytes 110596
  843.5 31.2 %copy-start.7 = (f32[8,1152]{1,0:T(8,128)S(1)}, f32[8,1152]{1,0:T(8,128)}, u32[]{:S(2)}) copy-start(f32[8,1152]{1,0:T(8,128)} %get-tuple-element.138) | copy-start | bytes 110596
  843.6 31.2 %copy-start.8 = (f32[8,1152]{1,0:T(8,128)S(1)}, f32[8,1152]{1,0:T(8,128)}, u32[]{:S(2)}) copy-start(f32[8,1152]{1,0:T(8,128)} %get-tuple-element.139) | copy-start | bytes 110596
  843.6 31.2 %copy-start.9 = (f32[8,1152]{1,0:T(8,128)S(1)}, f32[8,1152]{1,0:T(8,128)}, u32[]{:S(2)}) copy-start(f32[8,1152]{1,0:T(8,128)} %get-tuple-element.140) | copy-start | bytes 110596
  843.6 31.2 %copy-start.10 = (f32[8,1152]{1,0:T(8,128)S(1)}, f32[8,1152]{1,0:T(8,128)}, u32[]{:S(2)}) copy-start(f32[8,1152]{1,0:T(8,128)} %get-tuple-element.141) | copy-start | bytes 110596
  843.6 31.2 %copy-start.11 = (f32[8,1152]{1,0:T(8,128)S(1)}, f32[8,1152]{1,0:T(8,128)}, u32[]{:S(2)}) copy-start(f32[8,1152]{1,0:T(8,128)} %get-tuple-element.142) | copy-start | bytes 110596
  843.6 31.2 %copy-start.12 = (f32[8,1152]{1,0:T(8,128)S(1)}, f32[8,1152]{1,0:T(8,128)}, u32[]{:S(2)}) copy-start(f32[8,1152]{1,0:T(8,128)} %get-tuple-element.143) | copy-start | bytes 110596
  843.6 31.2 %copy-start.13 = (f32[8,1152]{1,0:T(8,128)S(1)}, f32[8,1152]{1,0:T(8,128)}, u32[]{:S(2)}) copy-start(f32[8,1152]{1,0:T(8,128)} %get-tuple-element.144) | copy-start | bytes 110596
  843.6 31.2 %copy-start.14 = (f32[8,1152]{1,0:T(8,128)S(1)}, f32[8,1152]{1,0:T(8,128)}, u32[]{:S(2)}) copy-start(f32[8,1152]{1,0:T(8,128)} %get-tuple-element.145) | copy-start | bytes 110596
  843.6 31.2 %copy-start.15 = (f32[8,1152]{1,0:T(8,128)S(1)}, f32[8,1152]{1,0:T(8,128)}, u32[]{:S(2)}) copy-start(f32[8,1152]{1,0:T(8,128)} %get-tuple-element.146) | copy-start | bytes 110596
  843.6 31.2 %copy-start.16 = (f32[8,1152]{1,0:T(8,128)S(1)}, f32[8,1152]{1,0:T(8,128)}, u32[]{:S(2)}) copy-start(f32[8,1152]{1,0:T(8,128)} %get-tuple-element.147) | copy-start | bytes 110596
  843.6 31.2 %copy-start.17 = (f32[8,1152]{1,0:T(8,128)S(1)}, f32[8,1152]{1,0:T(8,128)}, u32[]{:S(2)}) copy-start(f32[8,1152]{1,0:T(8,128)} %get-tuple-element.148) | copy-start | bytes 110596
  843.7 31.2 %copy-start.18 = (f32[8,1152]{1,0:T(8,128)S(1)}, f32[8,1152]{1,0:T(8,128)}, u32[]{:S(2)}) copy-start(f32[8,1152]{1,0:T(8,128)} %get-tuple-element.149) | copy-start | bytes 110596
  843.7 31.2 %copy-start.19 = (f32[8,1152]{1,0:T(8,128)S(1)}, f32[8,1152]{1,0:T(8,128)}, u32[]{:S(2)}) copy-start(f32[8,1152]{1,0:T(8,128)} %get-tuple-element.150) | copy-start | bytes 110596
  905.7 5.6 copy-start.26
  905.7 108.9 %all-to-all-start.3 = ((f32[8,1152,128]{2,1,0:T(8,128)}), f32[8,1152,128]{2,1,0:T(8,128)}, u32[]{:S(2)}, u32[]{:S(2)}) async-start(f32[8,1152,128]{2,1,0:T(8,128)} %multiply_add_fusion), calls=%async_computation.3 | async-start | bytes 9437184 | tf_op jit(solution)/shard_map/all_to_all | solution.py:115
where the time goes:
time: 1030 us
  local copies, waits for them, and re-layouts  553 us (54%)
  waiting for transfers between devices  183 us (18%)
  other arithmetic  126 us (12%)
  between operations  120 us (12%)
  starting transfers between devices  33.6 us (3%)
  matrix products  12.3 us (1%)
    gather x16, local copies, waits for them, and re-layouts, body(): flat_coeffs[flat_index]  496 us
    all_to_all x1, waiting for transfers between devices, body(): lax.all_to_all(total, 'lon', split_axis=0, concat_axis=0, tiled=True)  103 us
    unnamed x18, other arithmetic  60.3 us
    all_to_all x1, waiting for transfers between devices, body(): lax.all_to_all(solved, 'lon', split_axis=0, concat_axis=1, tiled=True)  37.5 us
    all_to_all x1, waiting for transfers between devices, body(): lax.all_to_all(filtered, 'lon', split_axis=1, concat_axis=0, tiled=True)  34.9 us
    add x1, other arithmetic, body(): total + (lat_w[lat_tap] * lon_w[lon_tap])[..., None] * flat_coeffs[flat_i...  30.8 us
    div x1, other arithmetic, body(): lax.linalg.tridiagonal_solve(lower, diagonal, upper, extended.reshape(spa...  27.9 us
  transfers between devices with their start and end apart: 10, of which 6 were waited for; matrix products, arithmetic and copies ran while one was open for 6% of the time, Pallas kernels for 0%

commit v1 on v0

v1 whole, which is shorter than its diff:
```python
import functools
import math

import jax
import jax.numpy as jnp
import numpy as np
from jax import lax
from jax.experimental import pallas as pl
from jax.experimental.pallas import tpu as pltpu
from jax.sharding import PartitionSpec as P

POLE = math.sqrt(3.0) - 2.0
GAIN = math.sqrt(3.0)
LANES = 128
TAPS = 6
UP, DOWN = 2, 3
LEFT, RIGHT = 1, 2
BF = jnp.bfloat16
F32 = jnp.float32
VMEM_LIMIT = 60 * 1024 * 1024


def split(x):
    high = x.astype(BF)
    return high, (x - high.astype(F32)).astype(BF)


def dot(a, b):
    return lax.dot_general(a, b, (((1,), (0,)), ((), ())), preferred_element_type=F32)


def spline_weights(shift):
    rest = 1.0 - shift
    cube = shift * shift * shift
    return [
        rest * rest * rest / 6.0,
        (3.0 * cube - 6.0 * shift * shift + 4.0) / 6.0,
        (-3.0 * cube + 3.0 * shift * shift + 3.0 * shift + 1.0) / 6.0,
        cube / 6.0,
    ]


def edge_kernel(s_ref, down_ref, up_ref, top_ref, bottom_ref):
    rows = s_ref.shape[0]
    first, last = s_ref[0], s_ref[rows - 1]
    far = 1.0 / (1.0 - POLE)

    acc = s_ref[0]
    for r in range(1, rows - UP):
        acc = s_ref[r] + POLE * acc
        if r == rows - 2 - DOWN:
            bottom_ref[DOWN] = 2.0 * far * last - acc
    down_ref[0] = acc
    for k in range(UP):
        down_ref[1 + k] = s_ref[rows - UP + k]
    for k in range(DOWN):
        bottom_ref[k] = 2.0 * last - s_ref[rows - 2 - k]

    acc = s_ref[rows - 1]
    for r in range(rows - 2, DOWN - 1, -1):
        acc = s_ref[r] + POLE * acc
    up_ref[DOWN] = acc
    for k in range(DOWN):
        up_ref[k] = s_ref[k]
    low = s_ref[rows - 1]
    for r in range(rows - 2, UP, -1):
        low = s_ref[r] + POLE * low
    top_ref[0] = 2.0 * far * first - low
    for k in range(UP):
        top_ref[1 + k] = 2.0 * first - s_ref[UP - k]


def edges(s):
    rows, cols, ch = s.shape
    shape = lambda n: jax.ShapeDtypeStruct((n, cols, ch), F32)
    return pl.pallas_call(
        edge_kernel,
        out_shape=(shape(UP + 1), shape(DOWN + 1), shape(UP + 1), shape(DOWN + 1)),
        cost_estimate=pl.CostEstimate(flops=6 * s.size, bytes_accessed=6 * s.size, transcendentals=0),
        compiler_params=pltpu.CompilerParams(vmem_limit_bytes=VMEM_LIMIT),
        name="edges",
    )(s)


def lat_kernel(s_ref, above_ref, below_ref, top_ref, bottom_ref, wr_ref, wl_ref, out_ref, right_ref, left_ref):
    rows, cols, _ = s_ref.shape
    band = lax.axis_index("lat")
    at_top = band == 0
    at_bottom = band == lax.axis_size("lat") - 1
    total = rows + UP + DOWN

    def row(e):
        if e < UP:
            return jnp.where(at_top, top_ref[1 + e], above_ref[1 + e])
        if e >= UP + rows:
            return jnp.where(at_bottom, bottom_ref[e - UP - rows], below_ref[e - UP - rows])
        return s_ref[e - UP]

    acc = jnp.where(at_bottom, bottom_ref[DOWN], below_ref[DOWN])
    for e in range(total - 1, -1, -1):
        acc = POLE * acc
        out_ref[e] = acc
        acc = acc + row(e)
    acc = jnp.where(at_top, top_ref[0], above_ref[0])
    for e in range(total):
        acc = row(e) + POLE * acc
        value = GAIN * (out_ref[e] + acc)
        out_ref[e] = value
        right_ref[0, pl.ds(e, 1)] = jnp.sum(value * wr_ref[...], axis=0, keepdims=True)
        for k in range(LEFT):
            right_ref[1 + k, pl.ds(e, 1)] = value[cols - LEFT + k : cols - LEFT + k + 1]
        for k in range(RIGHT):
            left_ref[k, pl.ds(e, 1)] = value[k : k + 1]
        left_ref[RIGHT, pl.ds(e, 1)] = jnp.sum(value * wl_ref[...], axis=0, keepdims=True)


def lat_solve(s, above, below, top, bottom):
    rows, cols, ch = s.shape
    total = rows + UP + DOWN
    place = np.arange(cols)
    wr = np.where(place < cols - LEFT, POLE ** np.maximum(cols - LEFT - 1 - place, 0), 0.0)
    wl = np.where(place >= RIGHT, POLE ** np.maximum(place - RIGHT, 0), 0.0)
    wide = lambda w: jnp.asarray(np.broadcast_to(w[:, None], (cols, ch)).astype(np.float32))
    return pl.pallas_call(
        lat_kernel,
        out_shape=(
            jax.ShapeDtypeStruct((total, cols, ch), F32),
            jax.ShapeDtypeStruct((LEFT + 1, total, ch), F32),
            jax.ShapeDtypeStruct((RIGHT + 1, total, ch), F32),
        ),
        cost_estimate=pl.CostEstimate(flops=10 * s.size, bytes_accessed=10 * s.size, transcendentals=0),
        compiler_params=pltpu.CompilerParams(vmem_limit_bytes=VMEM_LIMIT),
        name="lat_solve",
    )(s, above, below, top, bottom, wide(wr), wide(wl))


def lon_kernel(x_ref, west_ref, east_ref, gh_ref, gl_ref, out_ref):
    total, cols, ch = x_ref.shape
    pad = LANES - cols - (LEFT + RIGHT + 2)
    for e in range(total):
        parts = [x_ref[e]]
        parts += [west_ref[k, pl.ds(e, 1)] for k in range(LEFT + 1)]
        parts += [east_ref[k, pl.ds(e, 1)] for k in range(RIGHT + 1)]
        parts += [jnp.zeros((pad, ch), F32)]
        turned = jnp.concatenate(parts, axis=0).T
        high, low = split(turned)
        both = jnp.concatenate([high, low], axis=0)
        main = dot(both, gh_ref[...])
        value = main[:ch] + main[ch:] + dot(high, gl_ref[...])
        high, low = split(value)
        out_ref[:ch, e * LANES : (e + 1) * LANES] = high
        out_ref[ch:, e * LANES : (e + 1) * LANES] = low


def lon_solve(x, west, east):
    total, cols, ch = x.shape
    width = cols + LEFT + RIGHT
    j = np.arange(width) - LEFT
    green = np.zeros((LANES, LANES))
    green[:cols, :width] = POLE ** np.abs(np.arange(cols)[:, None] - j[None, :])
    green[cols, :width] = POLE ** (j + LEFT + 1)
    for k in range(LEFT):
        green[cols + 1 + k, :width] = POLE ** np.abs(j - (k - LEFT))
    for k in range(RIGHT):
        green[cols + LEFT + 1 + k, :width] = POLE ** np.abs(j - (cols + k))
    green[cols + LEFT + 1 + RIGHT, :width] = POLE ** (cols + RIGHT - j)
    green = jnp.asarray((GAIN * green).astype(np.float32))
    high, low = split(green)
    return pl.pallas_call(
        lon_kernel,
        out_shape=jax.ShapeDtypeStruct((2 * ch, total * LANES), BF),
        cost_estimate=pl.CostEstimate(
            flops=6 * total * LANES * LANES * ch, bytes_accessed=8 * x.size, transcendentals=0
        ),
        compiler_params=pltpu.CompilerParams(vmem_limit_bytes=VMEM_LIMIT),
        name="lon_solve",
    )(x, west, east, high, low)


def tap_kernel(dest_ref, base_ref, ct_ref, cells_ref, tri_ref, out_ref, rank, wh, wl, packed, sem, *, cap, span):
    rows = cells_ref.shape[2]
    ch = ct_ref.shape[0] // 2
    me = lax.axis_index("lon").astype(F32)
    band = lax.axis_index("lat")
    lat_total = rows * lax.axis_size("lat")
    wh[...] = jnp.zeros_like(wh)
    wl[...] = jnp.zeros_like(wl)
    mine = cells_ref[0, 0] == me
    before = dot(jnp.where(mine, 1.0, 0.0).astype(BF), tri_ref[...])
    rank[...] = jnp.where(mine, before, -1000.0)
    column = lax.broadcasted_iota(jnp.int32, (span, LANES), 0).astype(F32)
    step = lax.broadcasted_iota(jnp.int32, (8, LANES), 0)
    first = dest_ref[0] * rows

    @pl.loop(0, rows)
    def _(i):
        here = pl.ds(i, 1)
        one = jnp.where(cells_ref[0, 0, here] == me, 1.0, 0.0)
        a = spline_weights(cells_ref[0, 3, here])
        b = [w * one for w in spline_weights(cells_ref[0, 4, here])]
        glob = band * rows + i
        start = i - jnp.where(glob == lat_total - 1, 1, 0)
        dep = jnp.clip(glob.astype(F32) - 1.0 + cells_ref[0, 2, here], 1.0, lat_total - 3.0)
        turn = dep - (glob - i + start - 1).astype(F32)
        far = column - cells_ref[0, 1, here]
        basis = jnp.where(
            far == 0.0, b[0], jnp.where(far == 1.0, b[1], jnp.where(far == 2.0, b[2], jnp.where(far == 3.0, b[3], 0.0)))
        )
        zero = jnp.zeros_like(one)
        for e in range(TAPS):
            lat_w = zero
            for t in range(3):
                if 0 <= e - t < 4:
                    lat_w = jnp.where(turn == float(t), a[e - t], lat_w)
            high, low = split(basis * lat_w)
            wh[e * LANES : e * LANES + span] = high
            wl[e * LANES : e * LANES + span] = low
        window = pl.ds(pl.multiple_of(start * LANES, LANES), TAPS * LANES)
        main = dot(ct_ref[:, window], wh[...])
        value = main[:ch] + main[ch:] + dot(ct_ref[:ch, window], wl[...])
        high, low = split(value)
        base = base_ref[first + i]
        odd = lax.rem(base, 8)
        spot = rank[here] + odd.astype(F32)
        pick = jnp.where(column == spot, 1.0, 0.0).astype(BF)
        got = lax.dot_general(
            jnp.concatenate([pick, pick], axis=1),
            jnp.concatenate([high, low], axis=1),
            (((1,), (1,)), ((), ())),
            preferred_element_type=F32,
        )
        at = pl.multiple_of(base - odd, 8)
        packed[pl.ds(at, 8)] = jnp.where(step < odd, packed[pl.ds(at, 8)], got[:8])
        packed[pl.ds(pl.multiple_of(at + 8, 8), span - 8)] = got[8:]

    copy = pltpu.make_async_copy(packed.at[pl.ds(0, cap)], out_ref, sem)
    copy.start()
    copy.wait()


def taps(dest, base, ct, cells, cap):
    count, words, rows, lanes = cells.shape
    ch = ct.shape[0] // 2
    span = 104
    tri = jnp.asarray(np.triu(np.ones((lanes, lanes)), 1), BF)
    return pl.pallas_call(
        functools.partial(tap_kernel, cap=cap, span=span),
        out_shape=jax.ShapeDtypeStruct((cap, ch), F32),
        grid_spec=pltpu.PrefetchScalarGridSpec(
            num_scalar_prefetch=2,
            grid=(1,),
            in_specs=[
                pl.BlockSpec(ct.shape, lambda g, d, b: (0, 0)),
                pl.BlockSpec((1, words, rows, lanes), lambda g, d, b: (d[0], 0, 0, 0)),
                pl.BlockSpec(tri.shape, lambda g, d, b: (0, 0)),
            ],
            out_specs=pl.BlockSpec(memory_space=pl.ANY),
            scratch_shapes=[
                pltpu.VMEM((rows, lanes), F32),
                pltpu.VMEM((TAPS * LANES, lanes), BF),
                pltpu.VMEM((TAPS * LANES, lanes), BF),
                pltpu.VMEM((cap + span + 8, ch), F32),
                pltpu.SemaphoreType.DMA,
            ],
        ),
        cost_estimate=pl.CostEstimate(
            flops=6 * rows * TAPS * LANES * ch * LANES, bytes_accessed=2 * ct.size, transcendentals=0
        ),
        compiler_params=pltpu.CompilerParams(vmem_limit_bytes=VMEM_LIMIT),
        name="taps",
    )(dest, base, ct, cells, tri)


def place_kernel(target_ref, *refs, cap):
    *parts, out_ref, gathered, sems = refs
    copies = [
        pltpu.make_async_copy(part, gathered.at[pl.ds(k * cap, cap)], sems.at[k]) for k, part in enumerate(parts)
    ]
    for copy in copies:
        copy.start()
    for copy in copies:
        copy.wait()

    @pl.loop(0, out_ref.shape[0] // 8)
    def _(group):
        at = pl.multiple_of(group * 8, 8)
        lines = [gathered[pl.ds(target_ref[at + k], 1)] for k in range(8)]
        out_ref[pl.ds(at, 8)] = jnp.concatenate(lines, axis=0)


def place(target, parts):
    cap, ch = parts[0].shape
    cells = target.shape[0]
    count = len(parts)
    return pl.pallas_call(
        functools.partial(place_kernel, cap=cap),
        out_shape=jax.ShapeDtypeStruct((cells, ch), F32),
        grid_spec=pltpu.PrefetchScalarGridSpec(
            num_scalar_prefetch=1,
            grid=(1,),
            in_specs=[pl.BlockSpec(memory_space=pl.ANY)] * count,
            out_specs=pl.BlockSpec((cells, ch), lambda g, t: (0, 0)),
            scratch_shapes=[pltpu.VMEM((count * cap, ch), F32), pltpu.SemaphoreType.DMA((count,))],
        ),
        cost_estimate=pl.CostEstimate(flops=0, bytes_accessed=8 * count * cap * ch, transcendentals=0),
        compiler_params=pltpu.CompilerParams(vmem_limit_bytes=VMEM_LIMIT),
        name="place",
    )(target, *parts)


def earlier(mask):
    rows, cols = mask.shape[1:]
    ones = mask.astype(F32)
    before = lax.dot_general(
        mask.astype(BF),
        jnp.asarray(np.triu(np.ones((cols, cols)), 1), BF),
        (((2,), (0,)), ((), ())),
        preferred_element_type=F32,
    )
    return before, bases(ones)


def bases(ones):
    rows = ones.shape[1]
    totals = jnp.sum(ones, axis=2)
    return jnp.dot(totals, jnp.asarray(np.triu(np.ones((rows, rows)), 1), F32), precision=lax.Precision.HIGHEST)


def body(tracers, owners, columns, lat_shift, fractions):
    rows, cols, ch = tracers.shape
    bands = lax.axis_size("lat")
    sectors = lax.axis_size("lon")
    me = lax.axis_index("lon")
    cells = rows * cols
    cap = 3 * cells // sectors

    down, up, top, bottom = edges(tracers)
    above = lax.ppermute(down, "lat", [(i, i + 1) for i in range(bands - 1)])
    below = lax.ppermute(up, "lat", [(i + 1, i) for i in range(bands - 1)])

    owner = owners.reshape(rows, cols)
    words = jnp.stack(
        [owner.astype(F32), columns.astype(F32), lat_shift.astype(F32), fractions[0], fractions[1]], axis=0
    )
    words = jnp.pad(words, ((0, 0), (0, 0), (0, LANES - cols)), constant_values=-1.0)
    asked = lax.all_to_all(
        jnp.broadcast_to(words[None], (sectors,) + words.shape), "lon", split_axis=0, concat_axis=0, tiled=True
    )

    x, right, left = lat_solve(tracers, above, below, top, bottom)
    west = lax.ppermute(right, "lon", [(i, (i + 1) % sectors) for i in range(sectors)])
    east = lax.ppermute(left, "lon", [((i + 1) % sectors, i) for i in range(sectors)])

    base = bases((asked[:, 0] == me.astype(F32)).astype(F32)).astype(jnp.int32).reshape(-1)
    every = jnp.arange(sectors, dtype=jnp.int32)
    mask = owner[None] == every[:, None, None]
    before, own_base = earlier(mask)
    slot = jnp.sum(jnp.where(mask, before + own_base[:, :, None], 0.0), axis=0).astype(jnp.int32)
    target = ((me - owner) % sectors * cap + slot).reshape(cells)

    ct = lon_solve(x, west, east)
    parts = [None] * sectors
    for k in sorted(range(sectors), key=lambda k: (k == 0, abs(2 * k - sectors))):
        dest = ((me + k) % sectors).reshape(1)
        value = taps(dest, base, ct, asked, cap)
        if k:
            value = lax.ppermute(value, "lon", [(i, (i + k) % sectors) for i in range(sectors)])
        parts[k] = value
    return place(target, parts).reshape(rows, cols, ch)


def solution(mesh):
    in_specs = (
        P("lat", "lon", None),
        P("lat", "lon", None, None),
        P("lat", "lon"),
        P("lat", "lon"),
        P(None, "lat", "lon"),
    )
    out_specs = P("lat", "lon", None)
    return jax.shard_map(body, mesh=mesh, in_specs=in_specs, out_specs=out_specs, check_vma=False)
```

time: 1030 us -> 230 us (0.22)
  local copies, waits for them, and re-layouts: 553 us -> 4.39 us
  Pallas kernels: 0 us -> 183 us
  waiting for transfers between devices: 183 us -> 8.29 us
  other arithmetic: 126 us -> 5.68 us
  between operations: 120 us -> 0.31 us
  matrix products: 12.3 us -> 1.75 us
    gather x17 -> x0, local copies, waits for them, and re-layouts: 510 us -> none  [the longest x16 496 us: body(): flat_coeffs[flat_index]]
    pallas_call x0 -> x12, Pallas kernels: none -> 183 us  [the longest x8 164 us: taps(): pl.pallas_call(functools.partial(tap_kernel, cap=cap, span=span), out_sha...]
    all_to_all x4 -> x1, waiting for transfers between devices: 176 us -> 0.01 us  [body(): lax.all_to_all(jnp.broadcast_to(words[None], (sectors,) + words.shape), '...]
    unnamed x18 -> x0, other arithmetic: 60.3 us -> none
    add x1, other arithmetic: 30.8 us -> 1.33 us  [body(): target = ((me - owner) % sectors * cap + slot).reshape(cells)]
    div x1 -> x0, other arithmetic: 27.9 us -> none  [body(): lax.linalg.tridiagonal_solve(lower, diagonal, upper, extended.reshape(spa...]
    all_to_all x4 -> x1, starting transfers between devices: 22.6 us -> 7.28 us  [body(): lax.all_to_all(jnp.broadcast_to(words[None], (sectors,) + words.shape), '...]
    scatter x1 -> x0, local copies, waits for them, and re-layouts: 12.6 us -> none  [body(): buffer = buffer.at[:, target].set(payload).reshape(4, sectors, capacity)]
  transfers between devices with their start and end apart: 10 -> 12, of which waited for: 6 -> 2; matrix products, arithmetic and copies ran while one was open for 6% -> 3% of each run, Pallas kernels for 0% -> 67%
where the time goes in v1:
time: 230 us; the launch traced here: 229 us
  Pallas kernels  183 us (80%)
  starting transfers between devices  25.4 us (11%)
  waiting for transfers between devices  8.29 us (4%)
  other arithmetic  5.68 us (2%)
  local copies, waits for them, and re-layouts  4.39 us (2%)
    pallas_call x8, Pallas kernels, taps(): pl.pallas_call(functools.partial(tap_kernel, cap=cap, span=span), out_sha...  164 us
    ppermute x7, starting transfers between devices, body(): lax.ppermute(value, 'lon', [(i, (i + k) % sectors) for i in range(sectors)])  9.06 us
    pallas_call x1, Pallas kernels, place(): pl.pallas_call(functools.partial(place_kernel, cap=cap), out_shape=jax.Sh...  8.81 us
    all_to_all x1, starting transfers between devices, body(): lax.all_to_all(jnp.broadcast_to(words[None], (sectors,) + words.shape), '...  7.28 us
    ppermute x1, waiting for transfers between devices, body(): lax.ppermute(right, 'lon', [(i, (i + 1) % sectors) for i in range(sectors)])  6.31 us
    ppermute x1, starting transfers between devices, body(): lax.ppermute(left, 'lon', [((i + 1) % sectors, i) for i in range(sectors)])  4.72 us
  transfers between devices with their start and end apart: 12, of which 2 were waited for; matrix products, arithmetic and copies ran while one was open for 3% of the time, Pallas kernels for 67%

profile of v1, /device:TPU:0, one launch (start us, length us, event | category | flops | bytes accessed | tf_op | source)
XLA Modules:
  0.0 228.7 jit_solution(11138247648567537407)
XLA Ops:
  0.0 0.7 convert_reduce_fusion.2
  0.7 0.1 convert_element_type.53
  0.8 0.7 convert_bitcast_fusion
  1.6 0.8 select_maximum_fusion
  2.3 0.0 copy-start.12
  2.3 0.9 broadcast_in_dim.6
  3.3 7.3 %all-to-all-start = ((f32[8,5,32,128]{3,2,1,0:T(8,128)}), f32[8,5,32,128]{3,2,1,0:T(8,128)S(1)}, u32[]{:S(2)}, u32[]{:S(2)}) async-start(f32[8,5,32,128]{3,2,1,0:T(8,128)} %broadcast_in_dim.6), calls=%async_computation | async-start | bytes 1310720 | tf_op jit(solution)/shard_map/all_to_all | solution.py:346
  10.5 2.5 %edges.1 = (f32[3,96,128]{2,1,0:T(8,128)}, f32[4,96,128]{2,1,0:T(8,128)}, f32[3,96,128]{2,1,0:T(8,128)}, f32[4,96,128]{2,1,0:T(8,128)}) custom-call(f32[32,96,128]{2,1,0:T(8,128)} %s_ref.3), custom_call_target="tpu_custom_call" | custom-call | flops 2359296 | bytes 2359296 | tf_op jit(solution)/shard_map/edges/pallas_call | solution.py:76
  13.0 1.3 collective-permute-start.1
  14.3 3.0 %collective-permute-start = (f32[3,96,128]{2,1,0:T(8,128)}, f32[3,96,128]{2,1,0:T(8,128)S(1)}, u32[]{:S(2)}, u32[]{:S(2)}) collective-permute-start(f32[3,96,128]{2,1,0:T(8,128)} %get-tuple-element.12), channel_id=1, source_target_pairs={{0,8},{8,16},{16,24},{1,9},{9,17},{17,25},{2,10},{10,18},{18,26},{... | collective-permute-start | bytes 442376 | tf_op jit(solution)/shard_map/ppermute | solution.py:338
  17.4 0.6 broadcast.46
  17.9 1.3 broadcast_subtract_fusion
  19.2 0.1 eq.33
  19.3 0.0 collective-permute-done.above_ref
  19.3 0.6 copy-done.8
  20.0 0.1 copy-done.7
  20.1 3.5 %lat_solve.1 = (f32[37,96,128]{2,1,0:T(8,128)}, f32[2,37,128]{2,1,0:T(8,128)}, f32[3,37,128]{2,1,0:T(8,128)}) custom-call(f32[32,96,128]{2,1,0:T(8,128)} %s_ref.3, f32[3,96,128]{2,1,0:T(8,128)} %copy-done.8, f32[4,96,128]{2,1,0:T(8,128)} %copy-done.7, f32[3,96,128]{2,1,0:T(8,128)} %get-tuple-element.14.top_ref, f32[4,96,128]{2,1,0:T(8,128)} %get-tuple-element.15.bottom_ref, ...), custom_call_target="tpu_custom_call" | custom-call | flops 3932160 | bytes 3932160 | tf_op jit(solution)/shard_map/lat_solve/pallas_call | solution.py:124
  23.5 4.7 %collective-permute-start.3 = (f32[3,37,128]{2,1,0:T(8,128)}, f32[3,37,128]{2,1,0:T(8,128)S(1)}, u32[]{:S(2)}, u32[]{:S(2)}) collective-permute-start(f32[3,37,128]{2,1,0:T(8,128)} %get-tuple-element.18), channel_id=1, source_target_pairs={{1,0},{2,1},{3,2},{4,3},{5,4},{6,5},{7,6},{0,7},{9,8},{10,9},{11,1... | collective-permute-start | bytes 170504 | tf_op jit(solution)/shard_map/ppermute | solution.py:352
  28.3 0.7 convert_reduce_fusion.1
  29.0 6.3 %collective-permute-done.2.west_ref = f32[2,37,128]{2,1,0:T(8,128)S(1)} collective-permute-done((f32[2,37,128]{2,1,0:T(8,128)}, f32[2,37,128]{2,1,0:T(8,128)S(1)}, u32[]{:S(2)}, u32[]{:S(2)}) %collective-permute-start.2) | collective-permute-done | bytes 37920 | tf_op jit(solution)/shard_map/ppermute | solution.py:351
  35.3 0.6 copy-done.13
  35.9 0.0 copy-done.11
  35.9 4.2 %lon_solve.1.ct_ref = bf16[256,4736]{1,0:T(8,128)(2,1)} custom-call(f32[37,96,128]{2,1,0:T(8,128)} %get-tuple-element.16.x_ref, f32[2,37,128]{2,1,0:T(8,128)} %copy-done.13, f32[3,37,128]{2,1,0:T(8,128)} %copy-done.11, bf16[128,128]{1,0:T(8,128)(2,1)} %constant.93.gh_ref, bf16[128,128]{1,0:T(8,128)(2,1)} %constant.96.gl_ref), custom_call_target="tpu_custom_call" | custom-call | flops 465567744 | bytes 3637248 | tf_op jit(solution)/shard_map/lon_solve/pallas_call | solution.py:169
  40.2 0.1 convert_reduce_fusion
  40.3 0.1 convolution_convert_fusion
  40.4 0.7 reshape.55.base_ref
  41.1 20.5 %taps.15 = f32[1152,128]{1,0:T(8,128)} custom-call(s32[1]{0:T(128)} %bitcast.11.dest_ref, s32[256]{0:T(256)} %reshape.55.base_ref, bf16[256,4736]{1,0:T(8,128)(2,1)} %lon_solve.1.ct_ref, f32[8,5,32,128]{3,2,1,0:T(8,128)} %copy-done, bf16[128,128]{1,0:T(8,128)(2,1)} %constant.89.clone.tri_ref), custom_call_target="tpu_custom_call" | custom-call | flops 2415919104 | bytes 2424832 | tf_op jit(solution)/shard_map/taps/pallas_call | solution.py:246
  61.6 0.2 collective-permute-start.10
  61.8 20.5 %taps.10 = f32[1152,128]{1,0:T(8,128)} custom-call(s32[1]{0:T(128)} %bitcast.6.dest_ref, s32[256]{0:T(256)} %reshape.55.base_ref, bf16[256,4736]{1,0:T(8,128)(2,1)} %lon_solve.1.ct_ref, f32[8,5,32,128]{3,2,1,0:T(8,128)} %copy-done, bf16[128,128]{1,0:T(8,128)(2,1)} %constant.89.clone.tri_ref), custom_call_target="tpu_custom_call" | custom-call | flops 2415919104 | bytes 2424832 | tf_op jit(solution)/shard_map/taps/pallas_call | solution.py:246
  82.3 0.1 collective-permute-start.5
  82.3 20.5 %taps.11 = f32[1152,128]{1,0:T(8,128)} custom-call(s32[1]{0:T(128)} %bitcast.7.dest_ref, s32[256]{0:T(256)} %reshape.55.base_ref, bf16[256,4736]{1,0:T(8,128)(2,1)} %lon_solve.1.ct_ref, f32[8,5,32,128]{3,2,1,0:T(8,128)} %copy-done, bf16[128,128]{1,0:T(8,128)(2,1)} %constant.89.clone.tri_ref), custom_call_target="tpu_custom_call" | custom-call | flops 2415919104 | bytes 2424832 | tf_op jit(solution)/shard_map/taps/pallas_call | solution.py:246
  102.8 0.1 collective-permute-start.6
  102.9 20.5 %taps.12 = f32[1152,128]{1,0:T(8,128)} custom-call(s32[1]{0:T(128)} %bitcast.8.dest_ref, s32[256]{0:T(256)} %reshape.55.base_ref, bf16[256,4736]{1,0:T(8,128)(2,1)} %lon_solve.1.ct_ref, f32[8,5,32,128]{3,2,1,0:T(8,128)} %copy-done, bf16[128,128]{1,0:T(8,128)(2,1)} %constant.89.clone.tri_ref), custom_call_target="tpu_custom_call" | custom-call | flops 2415919104 | bytes 2424832 | tf_op jit(solution)/shard_map/taps/pallas_call | solution.py:246
  123.4 5.7 %collective-permute-start.7 = (f32[1152,128]{1,0:T(8,128)}, f32[1152,128]{1,0:T(8,128)S(1)}, u32[]{:S(2)}, u32[]{:S(2)}) collective-permute-start(f32[1152,128]{1,0:T(8,128)} %taps.12), channel_id=1, source_target_pairs={{0,4},{1,5},{2,6},{3,7},{4,0},{5,1},{6,2},{7,3},{8,12},{9,13},{10,... | collective-permute-start | bytes 1769480 | tf_op jit(solution)/shard_map/ppermute | solution.py:367
  129.1 20.5 %taps.13 = f32[1152,128]{1,0:T(8,128)} custom-call(s32[1]{0:T(128)} %bitcast.9.dest_ref, s32[256]{0:T(256)} %reshape.55.base_ref, bf16[256,4736]{1,0:T(8,128)(2,1)} %lon_solve.1.ct_ref, f32[8,5,32,128]{3,2,1,0:T(8,128)} %copy-done, bf16[128,128]{1,0:T(8,128)(2,1)} %constant.89.clone.tri_ref), custom_call_target="tpu_custom_call" | custom-call | flops 2415919104 | bytes 2424832 | tf_op jit(solution)/shard_map/taps/pallas_call | solution.py:246
  149.6 0.1 collective-permute-start.8
  149.7 20.5 %taps.14 = f32[1152,128]{1,0:T(8,128)} custom-call(s32[1]{0:T(128)} %bitcast.10.dest_ref, s32[256]{0:T(256)} %reshape.55.base_ref, bf16[256,4736]{1,0:T(8,128)(2,1)} %lon_solve.1.ct_ref, f32[8,5,32,128]{3,2,1,0:T(8,128)} %copy-done, bf16[128,128]{1,0:T(8,128)(2,1)} %constant.89.clone.tri_ref), custom_call_target="tpu_custom_call" | custom-call | flops 2415919104 | bytes 2424832 | tf_op jit(solution)/shard_map/taps/pallas_call | solution.py:246
  170.2 0.0 copy-start.10
  170.2 20.5 %taps.9 = f32[1152,128]{1,0:T(8,128)} custom-call(s32[1]{0:T(128)} %bitcast.5.dest_ref, s32[256]{0:T(256)} %reshape.55.base_ref, bf16[256,4736]{1,0:T(8,128)(2,1)} %lon_solve.1.ct_ref, f32[8,5,32,128]{3,2,1,0:T(8,128)} %copy-done, bf16[128,128]{1,0:T(8,128)(2,1)} %constant.89.clone.tri_ref), custom_call_target="tpu_custom_call" | custom-call | flops 2415919104 | bytes 2424832 | tf_op jit(solution)/shard_map/taps/pallas_call | solution.py:246
  190.7 2.4 %collective-permute-start.9 = (f32[1152,128]{1,0:T(8,128)}, f32[1152,128]{1,0:T(8,128)S(1)}, u32[]{:S(2)}, u32[]{:S(2)}) collective-permute-start(f32[1152,128]{1,0:T(8,128)} %taps.14), channel_id=1, source_target_pairs={{0,6},{1,7},{2,0},{3,1},{4,2},{5,3},{6,4},{7,5},{8,14},{9,15},{10,... | collective-permute-start | bytes 1769480 | tf_op jit(solution)/shard_map/ppermute | solution.py:367
  193.1 0.6 collective-permute-start.4
  193.7 0.7 fusion.6
  194.4 0.9 fusion.1
  195.3 0.7 convert_element_type.51
  196.0 1.3 fusion.5.target_ref
  197.3 20.5 %taps.8.refs_0_ = f32[1152,128]{1,0:T(8,128)} custom-call(s32[1]{0:T(128)} %bitcast.2.dest_ref, s32[256]{0:T(256)} %reshape.55.base_ref, bf16[256,4736]{1,0:T(8,128)(2,1)} %lon_solve.1.ct_ref, f32[8,5,32,128]{3,2,1,0:T(8,128)} %copy-done, bf16[128,128]{1,0:T(8,128)(2,1)} %constant.89.clone.tri_ref), custom_call_target="tpu_custom_call" | custom-call | flops 2415919104 | bytes 2424832 | tf_op jit(solution)/shard_map/taps/pallas_call | solution.py:246
  217.9 2.0 collective-permute-done.4.refs_1_
  219.9 8.8 %place.1 = f32[3072,128]{1,0:T(8,128)} custom-call(s32[3072]{0:T(1024)} %fusion.5.target_ref, f32[1152,128]{1,0:T(8,128)} %taps.8.refs_0_, f32[1152,128]{1,0:T(8,128)} %collective-permute-done.4.refs_1_, f32[1152,128]{1,0:T(8,128)} %copy-done.2, f32[1152,128]{1,0:T(8,128)} %copy-done.3, f32[1152,128]{1,0:T(8,128)} %copy-done.4, f32[1152,128]{1,0:T(8,128)} %copy-done.5, ...), custom_call_target="tpu_custom_call" | custom-call | bytes 9437184 | tf_op jit(solution)/shard_map/place/pallas_call | solution.py:295
  (35 shorter events, 0.1 us)
Async XLA Ops:
  2.3 15.6 %copy-start.12 = (s32[1,1,3072,1]{2,3,1,0:T(1,128)S(1)}, s32[1,1,3072,1]{2,3,1,0:T(1,128)}, u32[]{:S(2)}) copy-start(s32[1,1,3072,1]{2,3,1,0:T(1,128)} %param.20) | copy-start | bytes 36868
  3.3 36.9 %all-to-all-start = ((f32[8,5,32,128]{3,2,1,0:T(8,128)}), f32[8,5,32,128]{3,2,1,0:T(8,128)S(1)}, u32[]{:S(2)}, u32[]{:S(2)}) async-start(f32[8,5,32,128]{3,2,1,0:T(8,128)} %broadcast_in_dim.6), calls=%async_computation | async-start | bytes 1310720 | tf_op jit(solution)/shard_map/all_to_all | solution.py:346
  13.0 6.3 %collective-permute-start.1 = (f32[4,96,128]{2,1,0:T(8,128)}, f32[4,96,128]{2,1,0:T(8,128)S(1)}, u32[]{:S(2)}, u32[]{:S(2)}) collective-permute-start(f32[4,96,128]{2,1,0:T(8,128)} %get-tuple-element.13), channel_id=1, source_target_pairs={{8,0},{16,8},{24,16},{9,1},{17,9},{25,17},{10,2},{18,10},{26,18},{... | collective-permute-start | bytes 589832 | tf_op jit(solution)/shard_map/ppermute | solution.py:339
  14.3 5.0 %collective-permute-start = (f32[3,96,128]{2,1,0:T(8,128)}, f32[3,96,128]{2,1,0:T(8,128)S(1)}, u32[]{:S(2)}, u32[]{:S(2)}) collective-permute-start(f32[3,96,128]{2,1,0:T(8,128)} %get-tuple-element.12), channel_id=1, source_target_pairs={{0,8},{8,16},{16,24},{1,9},{9,17},{17,25},{2,10},{10,18},{18,26},{... | collective-permute-start | bytes 442376 | tf_op jit(solution)/shard_map/ppermute | solution.py:338
  19.3 0.7 copy-start.8
  19.3 0.7 copy-start.7
  23.5 11.7 %collective-permute-start.3 = (f32[3,37,128]{2,1,0:T(8,128)}, f32[3,37,128]{2,1,0:T(8,128)S(1)}, u32[]{:S(2)}, u32[]{:S(2)}) collective-permute-start(f32[3,37,128]{2,1,0:T(8,128)} %get-tuple-element.18), channel_id=1, source_target_pairs={{1,0},{2,1},{3,2},{4,3},{5,4},{6,5},{7,6},{0,7},{9,8},{10,9},{11,1... | collective-permute-start | bytes 170504 | tf_op jit(solution)/shard_map/ppermute | solution.py:352
  28.3 7.0 %collective-permute-start.2 = (f32[2,37,128]{2,1,0:T(8,128)}, f32[2,37,128]{2,1,0:T(8,128)S(1)}, u32[]{:S(2)}, u32[]{:S(2)}) collective-permute-start(f32[2,37,128]{2,1,0:T(8,128)} %get-tuple-element.17), channel_id=1, source_target_pairs={{0,1},{1,2},{2,3},{3,4},{4,5},{5,6},{6,7},{7,0},{8,9},{9,10},{10,1... | collective-permute-start | bytes 113672 | tf_op jit(solution)/shard_map/ppermute | solution.py:351
  35.3 0.6 copy-start.13
  35.3 0.6 copy-start.11
  35.9 4.4 %copy-start.9 = (f32[32,32]{1,0:T(8,128)S(1)}, f32[32,32]{1,0:T(8,128)}, u32[]{:S(2)}) copy-start(f32[32,32]{1,0:T(8,128)} %constant.86.clone) | copy-start | bytes 12292
  40.2 0.9 copy-start
  61.6 129.1 %collective-permute-start.10 = (f32[1152,128]{1,0:T(8,128)}, f32[1152,128]{1,0:T(8,128)S(1)}, u32[]{:S(2)}, u32[]{:S(2)}) collective-permute-start(f32[1152,128]{1,0:T(8,128)} %taps.15), channel_id=1, source_target_pairs={{0,7},{1,0},{2,1},{3,2},{4,3},{5,4},{6,5},{7,6},{8,15},{9,8},{10,9... | collective-permute-start | bytes 1769480 | tf_op jit(solution)/shard_map/ppermute | solution.py:367
  82.3 110.8 %collective-permute-start.5 = (f32[1152,128]{1,0:T(8,128)}, f32[1152,128]{1,0:T(8,128)S(1)}, u32[]{:S(2)}, u32[]{:S(2)}) collective-permute-start(f32[1152,128]{1,0:T(8,128)} %taps.10), channel_id=1, source_target_pairs={{0,2},{1,3},{2,4},{3,5},{4,6},{5,7},{6,0},{7,1},{8,10},{9,11},{10,... | collective-permute-start | bytes 1769480 | tf_op jit(solution)/shard_map/ppermute | solution.py:367
  102.8 115.0 %collective-permute-start.6 = (f32[1152,128]{1,0:T(8,128)}, f32[1152,128]{1,0:T(8,128)S(1)}, u32[]{:S(2)}, u32[]{:S(2)}) collective-permute-start(f32[1152,128]{1,0:T(8,128)} %taps.11), channel_id=1, source_target_pairs={{0,3},{1,4},{2,5},{3,6},{4,7},{5,0},{6,1},{7,2},{8,11},{9,12},{10,... | collective-permute-start | bytes 1769480 | tf_op jit(solution)/shard_map/ppermute | solution.py:367
  123.4 94.4 %collective-permute-start.7 = (f32[1152,128]{1,0:T(8,128)}, f32[1152,128]{1,0:T(8,128)S(1)}, u32[]{:S(2)}, u32[]{:S(2)}) collective-permute-start(f32[1152,128]{1,0:T(8,128)} %taps.12), channel_id=1, source_target_pairs={{0,4},{1,5},{2,6},{3,7},{4,0},{5,1},{6,2},{7,3},{8,12},{9,13},{10,... | collective-permute-start | bytes 1769480 | tf_op jit(solution)/shard_map/ppermute | solution.py:367
  149.6 68.3 %collective-permute-start.8 = (f32[1152,128]{1,0:T(8,128)}, f32[1152,128]{1,0:T(8,128)S(1)}, u32[]{:S(2)}, u32[]{:S(2)}) collective-permute-start(f32[1152,128]{1,0:T(8,128)} %taps.13), channel_id=1, source_target_pairs={{0,5},{1,6},{2,7},{3,0},{4,1},{5,2},{6,3},{7,4},{8,13},{9,14},{10,... | collective-permute-start | bytes 1769480 | tf_op jit(solution)/shard_map/ppermute | solution.py:367
  170.2 23.5 %copy-start.10 = (f32[32,32]{1,0:T(8,128)S(1)}, f32[32,32]{1,0:T(8,128)}, u32[]{:S(2)}) copy-start(f32[32,32]{1,0:T(8,128)} %constant.86.clone) | copy-start | bytes 12292
  170.2 23.5 %copy-start.14 = (f32[8,32]{1,0:T(8,128)S(1)}, f32[8,32]{1,0:T(8,128)}, u32[]{:S(2)}) copy-start(f32[8,32]{1,0:T(8,128)} %convert_reduce_fusion.1) | copy-start | bytes 3076
  190.7 27.1 %copy-start.1 = (f32[1152,128]{1,0:T(8,128)}, f32[1152,128]{1,0:T(8,128)S(1)}, u32[]{:S(2)}) copy-start(f32[1152,128]{1,0:T(8,128)S(1)} %collective-permute-done.10.refs_7_) | copy-start | bytes 1769476
  190.7 27.2 %collective-permute-start.9 = (f32[1152,128]{1,0:T(8,128)}, f32[1152,128]{1,0:T(8,128)S(1)}, u32[]{:S(2)}, u32[]{:S(2)}) collective-permute-start(f32[1152,128]{1,0:T(8,128)} %taps.14), channel_id=1, source_target_pairs={{0,6},{1,7},{2,0},{3,1},{4,2},{5,3},{6,4},{7,5},{8,14},{9,15},{10,... | collective-permute-start | bytes 1769480 | tf_op jit(solution)/shard_map/ppermute | solution.py:367
  193.1 24.7 %copy-start.2 = (f32[1152,128]{1,0:T(8,128)}, f32[1152,128]{1,0:T(8,128)S(1)}, u32[]{:S(2)}) copy-start(f32[1152,128]{1,0:T(8,128)S(1)} %collective-permute-done.5.refs_2_) | copy-start | bytes 1769476
  193.1 26.7 %collective-permute-start.4 = (f32[1152,128]{1,0:T(8,128)}, f32[1152,128]{1,0:T(8,128)}, u32[]{:S(2)}, u32[]{:S(2)}) collective-permute-start(f32[1152,128]{1,0:T(8,128)} %taps.9), channel_id=1, source_target_pairs={{0,1},{1,2},{2,3},{3,4},{4,5},{5,6},{6,7},{7,0},{8,9},{9,10},{10,1... | collective-permute-start | bytes 1769480 | tf_op jit(solution)/shard_map/ppermute | solution.py:367
  217.8 2.0 copy-start.3
  217.8 2.0 copy-start.4
  217.8 2.0 copy-start.5
  217.9 2.0 copy-start.6

commit v2 on v1

--- a/solution.py
+++ b/solution.py
@@ -25,6 +25,11 @@
     return high, (x - high.astype(F32)).astype(BF)
 
 
+def thirds(x):
+    high, low = split(x)
+    return jnp.concatenate([high, low, high], axis=1)
+
+
 def dot(a, b):
     return lax.dot_general(a, b, (((1,), (0,)), ((), ())), preferred_element_type=F32)
 
@@ -40,8 +45,19 @@
     ]
 
 
-def edge_kernel(s_ref, down_ref, up_ref, top_ref, bottom_ref):
-    rows = s_ref.shape[0]
+def edge_kernel(
+    s_ref, owner_ref, column_ref, shift_ref, frac_ref, down_ref, up_ref, top_ref, bottom_ref, words_ref
+):
+    rows, cols = s_ref.shape[:2]
+    top_row = lax.axis_index("lat") * rows
+    lat_total = rows * lax.axis_size("lat")
+    arrival = lax.broadcasted_iota(jnp.int32, (rows, cols), 0) + top_row
+    row = jnp.clip(arrival - 1 + shift_ref[...], 1, lat_total - 3).astype(F32)
+    column = (owner_ref[...] * cols + column_ref[...]).astype(F32)
+    for k in range(words_ref.shape[0]):
+        for w, word in enumerate((column, row, frac_ref[0], frac_ref[1])):
+            words_ref[k, w] = jnp.full((rows, LANES), -1.0, F32)
+            words_ref[k, w, :, :cols] = word
     first, last = s_ref[0], s_ref[rows - 1]
     far = 1.0 / (1.0 - POLE)
 
@@ -70,16 +86,17 @@
         top_ref[1 + k] = 2.0 * first - s_ref[UP - k]
 
 
-def edges(s):
+def edges(s, owner, columns, lat_shift, fractions):
     rows, cols, ch = s.shape
     shape = lambda n: jax.ShapeDtypeStruct((n, cols, ch), F32)
+    words = jax.ShapeDtypeStruct((lax.axis_size("lon"), 4, rows, LANES), F32)
     return pl.pallas_call(
         edge_kernel,
-        out_shape=(shape(UP + 1), shape(DOWN + 1), shape(UP + 1), shape(DOWN + 1)),
+        out_shape=(shape(UP + 1), shape(DOWN + 1), shape(UP + 1), shape(DOWN + 1), words),
         cost_estimate=pl.CostEstimate(flops=6 * s.size, bytes_accessed=6 * s.size, transcendentals=0),
         compiler_params=pltpu.CompilerParams(vmem_limit_bytes=VMEM_LIMIT),
         name="edges",
-    )(s)
+    )(s, owner, columns, lat_shift, fractions)
 
 
 def lat_kernel(s_ref, above_ref, below_ref, top_ref, bottom_ref, wr_ref, wl_ref, out_ref, right_ref, left_ref):
@@ -134,7 +151,7 @@
     )(s, above, below, top, bottom, wide(wr), wide(wl))
 
 
-def lon_kernel(x_ref, west_ref, east_ref, gh_ref, gl_ref, out_ref):
+def lon_kernel(x_ref, west_ref, east_ref, green_ref, out_ref):
     total, cols, ch = x_ref.shape
     pad = LANES - cols - (LEFT + RIGHT + 2)
     for e in range(total):
@@ -143,13 +160,8 @@
         parts += [east_ref[k, pl.ds(e, 1)] for k in range(RIGHT + 1)]
         parts += [jnp.zeros((pad, ch), F32)]
         turned = jnp.concatenate(parts, axis=0).T
-        high, low = split(turned)
-        both = jnp.concatenate([high, low], axis=0)
-        main = dot(both, gh_ref[...])
-        value = main[:ch] + main[ch:] + dot(high, gl_ref[...])
-        high, low = split(value)
-        out_ref[:ch, e * LANES : (e + 1) * LANES] = high
-        out_ref[ch:, e * LANES : (e + 1) * LANES] = low
+        value = dot(thirds(turned), green_ref[...])
+        out_ref[e * ch : (e + 1) * ch] = thirds(value)
 
 
 def lon_solve(x, west, east):
@@ -168,107 +180,149 @@
     high, low = split(green)
     return pl.pallas_call(
         lon_kernel,
-        out_shape=jax.ShapeDtypeStruct((2 * ch, total * LANES), BF),
+        out_shape=jax.ShapeDtypeStruct((total * ch, 3 * LANES), BF),
         cost_estimate=pl.CostEstimate(
             flops=6 * total * LANES * LANES * ch, bytes_accessed=8 * x.size, transcendentals=0
         ),
         compiler_params=pltpu.CompilerParams(vmem_limit_bytes=VMEM_LIMIT),
         name="lon_solve",
-    )(x, west, east, high, low)
-
-
-def tap_kernel(dest_ref, base_ref, ct_ref, cells_ref, tri_ref, out_ref, rank, wh, wl, packed, sem, *, cap, span):
-    rows = cells_ref.shape[2]
-    ch = ct_ref.shape[0] // 2
-    me = lax.axis_index("lon").astype(F32)
+    )(x, west, east, jnp.concatenate([high, high, low], axis=0))
+
+
+def tap_kernel(dest_ref, base_ref, ct_ref, *refs, count, cols, cap, span):
+    cells_refs, tri_ref = refs[:count], refs[count]
+    out_refs = refs[count + 1 : 2 * count + 1]
+    rank, place, lon_w, lat_w, near, later, packed, sems = refs[2 * count + 1 :]
+    rows = rank.shape[1]
+    ch = packed.shape[2]
     band = lax.axis_index("lat")
     lat_total = rows * lax.axis_size("lat")
-    wh[...] = jnp.zeros_like(wh)
-    wl[...] = jnp.zeros_like(wl)
-    mine = cells_ref[0, 0] == me
-    before = dot(jnp.where(mine, 1.0, 0.0).astype(BF), tri_ref[...])
-    rank[...] = jnp.where(mine, before, -1000.0)
+    origin = (dest_ref[count] * cols).astype(F32)
+
+    def window_of(i):
+        return i - jnp.where(band * rows + i == lat_total - 1, 1, 0)
+
+    glob = lax.broadcasted_iota(jnp.int32, (rows, LANES), 0) + band * rows
+    first = (glob - jnp.where(glob == lat_total - 1, 1, 0) - 1).astype(F32)
+    for d in range(count):
+        local = cells_refs[d][0, 0] - origin
+        mine = (local >= 0.0) & (local < float(cols))
+        one = jnp.where(mine, 1.0, 0.0)
+        rank[d] = jnp.where(mine, dot(one.astype(BF), tri_ref[...]), -1000.0)
+        place[d] = local
+        turn = cells_refs[d][0, 1] - first
+        a = spline_weights(cells_refs[d][0, 2])
+        for n, w in enumerate(spline_weights(cells_refs[d][0, 3])):
+            lon_w[d, n] = w * one
+        for e in range(TAPS):
+            total = jnp.zeros_like(one)
+            for t in range(3):
+                if 0 <= e - t < 4:
+                    total = jnp.where(turn == float(t), a[e - t], total)
+            lat_w[d, e] = total
+    for buffer in (near, later):
+        for k in range(3):
+            buffer[k * LANES + span : (k + 1) * LANES] = jnp.zeros((LANES - span, count * LANES), BF)
     column = lax.broadcasted_iota(jnp.int32, (span, LANES), 0).astype(F32)
     step = lax.broadcasted_iota(jnp.int32, (8, LANES), 0)
-    first = dest_ref[0] * rows
-
-    @pl.loop(0, rows)
-    def _(i):
+
+    def build(i, buffer):
         here = pl.ds(i, 1)
-        one = jnp.where(cells_ref[0, 0, here] == me, 1.0, 0.0)
-        a = spline_weights(cells_ref[0, 3, here])
-        b = [w * one for w in spline_weights(cells_ref[0, 4, here])]
-        glob = band * rows + i
-        start = i - jnp.where(glob == lat_total - 1, 1, 0)
-        dep = jnp.clip(glob.astype(F32) - 1.0 + cells_ref[0, 2, here], 1.0, lat_total - 3.0)
-        turn = dep - (glob - i + start - 1).astype(F32)
-        far = column - cells_ref[0, 1, here]
-        basis = jnp.where(
-            far == 0.0, b[0], jnp.where(far == 1.0, b[1], jnp.where(far == 2.0, b[2], jnp.where(far == 3.0, b[3], 0.0)))
-        )
-        zero = jnp.zeros_like(one)
-        for e in range(TAPS):
-            lat_w = zero
-            for t in range(3):
-                if 0 <= e - t < 4:
-                    lat_w = jnp.where(turn == float(t), a[e - t], lat_w)
-            high, low = split(basis * lat_w)
-            wh[e * LANES : e * LANES + span] = high
-            wl[e * LANES : e * LANES + span] = low
-        window = pl.ds(pl.multiple_of(start * LANES, LANES), TAPS * LANES)
-        main = dot(ct_ref[:, window], wh[...])
-        value = main[:ch] + main[ch:] + dot(ct_ref[:ch, window], wl[...])
-        high, low = split(value)
-        base = base_ref[first + i]
-        odd = lax.rem(base, 8)
-        spot = rank[here] + odd.astype(F32)
-        pick = jnp.where(column == spot, 1.0, 0.0).astype(BF)
-        got = lax.dot_general(
-            jnp.concatenate([pick, pick], axis=1),
-            jnp.concatenate([high, low], axis=1),
-            (((1,), (1,)), ((), ())),
-            preferred_element_type=F32,
-        )
-        at = pl.multiple_of(base - odd, 8)
-        packed[pl.ds(at, 8)] = jnp.where(step < odd, packed[pl.ds(at, 8)], got[:8])
-        packed[pl.ds(pl.multiple_of(at + 8, 8), span - 8)] = got[8:]
-
-    copy = pltpu.make_async_copy(packed.at[pl.ds(0, cap)], out_ref, sem)
-    copy.start()
-    copy.wait()
-
-
-def taps(dest, base, ct, cells, cap):
-    count, words, rows, lanes = cells.shape
-    ch = ct.shape[0] // 2
-    span = 104
+        for d in range(count):
+            far = column - place[d, here]
+            basis = jnp.where(far == 0.0, lon_w[d, 0, here], 0.0)
+            for n in range(1, 4):
+                basis = jnp.where(far == float(n), lon_w[d, n, here], basis)
+            high, low = split(basis)
+            lanes = pl.ds(d * LANES, LANES)
+            buffer[0:span, lanes] = high
+            buffer[LANES : LANES + span, lanes] = high
+            buffer[2 * LANES : 2 * LANES + span, lanes] = low
+
+    def emit(i, buffer):
+        half = TAPS // 2
+        lines = []
+        for part in range(2):
+            at = pl.multiple_of((window_of(i) + part * half) * ch, ch)
+            lines.append(dot(ct_ref[pl.ds(at, half * ch)], buffer[...]))
+        for d in range(count):
+            terms = []
+            for e in range(TAPS):
+                block = lines[e // half][e % half * ch : (e % half + 1) * ch, d * LANES : (d + 1) * LANES]
+                terms.append(block * lat_w[d, e, pl.ds(i, 1)])
+            value = ((terms[0] + terms[1]) + terms[2]) + ((terms[3] + terms[4]) + terms[5])
+            high, low = split(value)
+            base = base_ref[dest_ref[d] * rows + i]
+            odd = lax.rem(base, 8)
+            spot = rank[d, pl.ds(i, 1)] + odd.astype(F32)
+            pick = jnp.where(column == spot, 1.0, 0.0).astype(BF)
+            got = lax.dot_general(
+                jnp.concatenate([pick, pick], axis=1),
+                jnp.concatenate([high, low], axis=1),
+                (((1,), (1,)), ((), ())),
+                preferred_element_type=F32,
+            )
+            at = pl.multiple_of(base - odd, 8)
+            packed[d, pl.ds(at, 8)] = jnp.where(step < odd, packed[d, pl.ds(at, 8)], got[:8])
+            packed[d, pl.ds(pl.multiple_of(at + 8, 8), span - 8)] = got[8:]
+
+    build(0, near)
+
+    @pl.loop(0, rows // 2)
+    def _(pair):
+        i = 2 * pair
+        emit(i, near)
+        build(i + 1, later)
+        emit(i + 1, later)
+        build(jnp.minimum(i + 2, rows - 1), near)
+
+    copies = [
+        pltpu.make_async_copy(packed.at[d, pl.ds(0, cap)], out_refs[d], sems.at[d]) for d in range(count)
+    ]
+    for copy in copies:
+        copy.start()
+    for copy in copies:
+        copy.wait()
+
+
+def taps(dests, sector, base, ct, cells, cols, cap):
+    _, words, rows, lanes = cells.shape
+    count = len(dests)
+    ch = ct.shape[0] // (rows + UP + DOWN)
+    span = 112
     tri = jnp.asarray(np.triu(np.ones((lanes, lanes)), 1), BF)
+    weights = pltpu.VMEM((3 * LANES, count * lanes), BF)
+    meta = jnp.stack([*dests, sector]).astype(jnp.int32)
     return pl.pallas_call(
-        functools.partial(tap_kernel, cap=cap, span=span),
-        out_shape=jax.ShapeDtypeStruct((cap, ch), F32),
+        functools.partial(tap_kernel, count=count, cols=cols, cap=cap, span=span),
+        out_shape=[jax.ShapeDtypeStruct((cap, ch), F32)] * count,
         grid_spec=pltpu.PrefetchScalarGridSpec(
             num_scalar_prefetch=2,
             grid=(1,),
-            in_specs=[
-                pl.BlockSpec(ct.shape, lambda g, d, b: (0, 0)),
-                pl.BlockSpec((1, words, rows, lanes), lambda g, d, b: (d[0], 0, 0, 0)),
-                pl.BlockSpec(tri.shape, lambda g, d, b: (0, 0)),
-            ],
-            out_specs=pl.BlockSpec(memory_space=pl.ANY),
+            in_specs=[pl.BlockSpec(ct.shape, lambda g, d, b: (0, 0))]
+            + [
+                pl.BlockSpec((1, words, rows, lanes), functools.partial(lambda g, d, b, k: (d[k], 0, 0, 0), k=k))
+                for k in range(count)
+            ]
+            + [pl.BlockSpec(tri.shape, lambda g, d, b: (0, 0))],
+            out_specs=[pl.BlockSpec(memory_space=pl.ANY)] * count,
             scratch_shapes=[
-                pltpu.VMEM((rows, lanes), F32),
-                pltpu.VMEM((TAPS * LANES, lanes), BF),
-                pltpu.VMEM((TAPS * LANES, lanes), BF),
-                pltpu.VMEM((cap + span + 8, ch), F32),
-                pltpu.SemaphoreType.DMA,
+                pltpu.VMEM((count, rows, lanes), F32),
+                pltpu.VMEM((count, rows, lanes), F32),
+                pltpu.VMEM((count, 4, rows, lanes), F32),
+                pltpu.VMEM((count, TAPS, rows, lanes), F32),
+                weights,
+                weights,
+                pltpu.VMEM((count, cap + span + 8, ch), F32),
+                pltpu.SemaphoreType.DMA((count,)),
             ],
         ),
         cost_estimate=pl.CostEstimate(
-            flops=6 * rows * TAPS * LANES * ch * LANES, bytes_accessed=2 * ct.size, transcendentals=0
+            flops=6 * count * rows * TAPS * LANES * ch * LANES, bytes_accessed=2 * ct.size, transcendentals=0
         ),
         compiler_params=pltpu.CompilerParams(vmem_limit_bytes=VMEM_LIMIT),
         name="taps",
-    )(dest, base, ct, cells, tri)
+    )(meta, base, ct, *([cells] * count), tri)
 
 
 def place_kernel(target_ref, *refs, cap):
@@ -334,24 +388,18 @@
     cells = rows * cols
     cap = 3 * cells // sectors
 
-    down, up, top, bottom = edges(tracers)
+    owner = owners.reshape(rows, cols)
+    down, up, top, bottom, words = edges(tracers, owner, columns, lat_shift, fractions)
     above = lax.ppermute(down, "lat", [(i, i + 1) for i in range(bands - 1)])
     below = lax.ppermute(up, "lat", [(i + 1, i) for i in range(bands - 1)])
-
-    owner = owners.reshape(rows, cols)
-    words = jnp.stack(
-        [owner.astype(F32), columns.astype(F32), lat_shift.astype(F32), fractions[0], fractions[1]], axis=0
-    )
-    words = jnp.pad(words, ((0, 0), (0, 0), (0, LANES - cols)), constant_values=-1.0)
-    asked = lax.all_to_all(
-        jnp.broadcast_to(words[None], (sectors,) + words.shape), "lon", split_axis=0, concat_axis=0, tiled=True
-    )
+    asked = lax.all_to_all(words, "lon", split_axis=0, concat_axis=0, tiled=True)
 
     x, right, left = lat_solve(tracers, above, below, top, bottom)
     west = lax.ppermute(right, "lon", [(i, (i + 1) % sectors) for i in range(sectors)])
     east = lax.ppermute(left, "lon", [((i + 1) % sectors, i) for i in range(sectors)])
 
-    base = bases((asked[:, 0] == me.astype(F32)).astype(F32)).astype(jnp.int32).reshape(-1)
+    local = asked[:, 0] - (me * cols).astype(F32)
+    base = bases(((local >= 0.0) & (local < float(cols))).astype(F32)).astype(jnp.int32).reshape(-1)
     every = jnp.arange(sectors, dtype=jnp.int32)
     mask = owner[None] == every[:, None, None]
     before, own_base = earlier(mask)
@@ -360,12 +408,13 @@
 
     ct = lon_solve(x, west, east)
     parts = [None] * sectors
-    for k in sorted(range(sectors), key=lambda k: (k == 0, abs(2 * k - sectors))):
-        dest = ((me + k) % sectors).reshape(1)
-        value = taps(dest, base, ct, asked, cap)
-        if k:
-            value = lax.ppermute(value, "lon", [(i, (i + k) % sectors) for i in range(sectors)])
-        parts[k] = value
+    order = sorted(range(sectors), key=lambda k: (k == 0, abs(2 * k - sectors)))
+    for pair in [order[n : n + 2] for n in range(0, sectors, 2)]:
+        values = taps([(me + k) % sectors for k in pair], me, base, ct, asked, cols, cap)
+        for k, value in zip(pair, values):
+            if k:
+                value = lax.ppermute(value, "lon", [(i, (i + k) % sectors) for i in range(sectors)])
+            parts[k] = value
     return place(target, parts).reshape(rows, cols, ch)
 
 

time: 230 us -> 172 us (0.75)
  the two profiles are of different devices: /device:TPU:0 before, /device:TPU:3 now
where the time goes in v2:
time: 172 us; the launch traced here: 171 us
  Pallas kernels  96.9 us (56%)
  waiting for transfers between devices  41.9 us (24%)
  starting transfers between devices  22.7 us (13%)
  other arithmetic  4.82 us (3%)
  local copies, waits for them, and re-layouts  3.95 us (2%)
    pallas_call x4, Pallas kernels, taps(): pl.pallas_call(functools.partial(tap_kernel, count=count, cols=cols, cap=...  77.2 us
    ppermute x7, waiting for transfers between devices, body(): lax.ppermute(value, 'lon', [(i, (i + k) % sectors) for i in range(sectors)])  37 us
    ppermute x7, starting transfers between devices, body(): lax.ppermute(value, 'lon', [(i, (i + k) % sectors) for i in range(sectors)])  9.28 us
    pallas_call x1, Pallas kernels, place(): pl.pallas_call(functools.partial(place_kernel, cap=cap), out_shape=jax.Sh...  8.81 us
    all_to_all x1, starting transfers between devices, body(): lax.all_to_all(words, 'lon', split_axis=0, concat_axis=0, tiled=True)  5.78 us
    pallas_call x1, Pallas kernels, lon_solve(): pl.pallas_call(lon_kernel, out_shape=jax.ShapeDtypeStruct((total * ch, 3...  4.56 us
    pallas_call x1, Pallas kernels, lat_solve(): pl.pallas_call(lat_kernel, out_shape=(jax.ShapeDtypeStruct((total, cols,...  3.55 us
  transfers between devices with their start and end apart: 12, of which 6 were waited for; matrix products, arithmetic and copies ran while one was open for 2% of the time, Pallas kernels for 39%

profile of v2, /device:TPU:3, one launch (start us, length us, event | category | flops | bytes accessed | tf_op | source)
XLA Modules:
  0.0 171.0 jit_solution(6207966721793336232)
XLA Ops:
  0.0 0.5 broadcast.34
  0.5 2.0 %broadcast_subtract_fusion = (s32[1,1,3072,1]{2,3,1,0:T(1,128)}, s32[3072]{0:T(1024)S(1)}) fusion(s32[1,1,3072,1]{2,3,1,0:T(1,128)} %param.16, s32[]{:T(128)} %axis_index.12, s32[]{:T(128)} %broadcast.34), kind=kLoop, calls=%fused_computation.15 | loop fusion | flops 3072 | bytes 36872 | tf_op jit(solution)/shard_map/sub | solution.py:407
  2.5 0.7 eq.26.owner_ref
  3.1 2.7 %edges.1 = (f32[3,96,128]{2,1,0:T(8,128)}, f32[4,96,128]{2,1,0:T(8,128)}, f32[3,96,128]{2,1,0:T(8,128)}, f32[4,96,128]{2,1,0:T(8,128)}, f32[8,4,32,128]{3,2,1,0:T(8,128)}) custom-call(f32[32,96,128]{2,1,0:T(8,128)} %s_ref.3, s32[32,96]{1,0:T(8,128)} %eq.26.owner_ref, s32[32,96]{1,0:T(8,128)} %column_ref.1, s32[32,96]{1,0:T(8,128)} %shift_ref.1, ...), custom_call_target="tpu_custom_call" | custom-call | flops 2359296 | bytes 2359296 | tf_op jit(solution)/shard_map/edges/pallas_call | solution.py:93
  5.9 5.8 %all-to-all-start = ((f32[8,4,32,128]{3,2,1,0:T(8,128)}), f32[8,4,32,128]{3,2,1,0:T(8,128)S(1)}, u32[]{:S(2)}, u32[]{:S(2)}) async-start(f32[8,4,32,128]{3,2,1,0:T(8,128)} %get-tuple-element.21), calls=%async_computation | async-start | bytes 1048576 | tf_op jit(solution)/shard_map/all_to_all | solution.py:395
  11.6 3.1 %collective-permute-start.1 = (f32[4,96,128]{2,1,0:T(8,128)}, f32[4,96,128]{2,1,0:T(8,128)S(1)}, u32[]{:S(2)}, u32[]{:S(2)}) collective-permute-start(f32[4,96,128]{2,1,0:T(8,128)} %get-tuple-element.23), channel_id=1, source_target_pairs={{8,0},{16,8},{24,16},{9,1},{17,9},{25,17},{10,2},{18,10},{26,18},{... | collective-permute-start | bytes 589832 | tf_op jit(solution)/shard_map/ppermute | solution.py:394
  14.8 3.0 %collective-permute-start = (f32[3,96,128]{2,1,0:T(8,128)}, f32[3,96,128]{2,1,0:T(8,128)S(1)}, u32[]{:S(2)}, u32[]{:S(2)}) collective-permute-start(f32[3,96,128]{2,1,0:T(8,128)} %get-tuple-element.22), channel_id=1, source_target_pairs={{0,8},{8,16},{16,24},{1,9},{9,17},{17,25},{2,10},{10,18},{18,26},{... | collective-permute-start | bytes 442376 | tf_op jit(solution)/shard_map/ppermute | solution.py:393
  17.9 0.7 add_add_fusion
  18.6 1.7 collective-permute-done.above_ref
  20.2 0.0 collective-permute-done.1.below_ref
  20.2 0.6 copy-done.9
  20.9 0.1 copy-done.7
  21.0 3.5 %lat_solve.1 = (f32[37,96,128]{2,1,0:T(8,128)}, f32[2,37,128]{2,1,0:T(8,128)}, f32[3,37,128]{2,1,0:T(8,128)}) custom-call(f32[32,96,128]{2,1,0:T(8,128)} %s_ref.3, f32[3,96,128]{2,1,0:T(8,128)} %copy-done.9, f32[4,96,128]{2,1,0:T(8,128)} %copy-done.7, f32[3,96,128]{2,1,0:T(8,128)} %get-tuple-element.24.top_ref, f32[4,96,128]{2,1,0:T(8,128)} %get-tuple-element.25.bottom_ref, ...), custom_call_target="tpu_custom_call" | custom-call | flops 3932160 | bytes 3932160 | tf_op jit(solution)/shard_map/lat_solve/pallas_call | solution.py:141
  24.5 1.2 collective-permute-start.2
  25.7 0.3 collective-permute-start.3
  26.0 0.7 add_add_fusion.2
  26.7 0.9 collective-permute-done.2.west_ref
  27.6 2.3 %collective-permute-done.3.east_ref = f32[3,37,128]{2,1,0:T(8,128)S(1)} collective-permute-done((f32[3,37,128]{2,1,0:T(8,128)}, f32[3,37,128]{2,1,0:T(8,128)S(1)}, u32[]{:S(2)}, u32[]{:S(2)}) %collective-permute-start.3) | collective-permute-done | bytes 56864 | tf_op jit(solution)/shard_map/ppermute | solution.py:399
  29.9 0.6 copy-done.11
  30.5 4.6 %lon_solve.1.ct_ref = bf16[4736,384]{1,0:T(8,128)(2,1)} custom-call(f32[37,96,128]{2,1,0:T(8,128)} %get-tuple-element.26.x_ref, f32[2,37,128]{2,1,0:T(8,128)} %copy-done.12, f32[3,37,128]{2,1,0:T(8,128)} %copy-done.11, bf16[384,128]{1,0:T(8,128)(2,1)} %constant.98.green_ref), custom_call_target="tpu_custom_call" | custom-call | flops 465567744 | bytes 3637248 | tf_op jit(solution)/shard_map/lon_solve/pallas_call | solution.py:181
  35.1 0.0 all-to-all-done.refs_0_.refs_1_
  35.1 0.1 convert_reduce_fusion
  35.2 0.1 convolution_convert_fusion
  35.3 0.7 reshape.23.base_ref
  36.0 19.3 %taps.7 = (f32[1152,128]{1,0:T(8,128)}, f32[1152,128]{1,0:T(8,128)}) custom-call(s32[3]{0:T(128)} %get-tuple-element.42.dest_ref, s32[256]{0:T(256)} %reshape.23.base_ref, bf16[4736,384]{1,0:T(8,128)(2,1)} %lon_solve.1.ct_ref, f32[8,4,32,128]{3,2,1,0:T(8,128)} %copy-done, f32[8,4,32,128]{3,2,1,0:T(8,128)} %copy-done, bf16[128,128]{1,0:T(8,128)(2,1)} %constant.92.clone.refs_2_), custom_call_target="tpu_custom_call" | custom-call | flops 4831838208 | bytes 3637248 | tf_op jit(solution)/shard_map/taps/pallas_call | solution.py:296
  55.3 1.4 collective-permute-start.6
  56.7 1.2 collective-permute-start.7
  57.9 19.3 %taps.6 = (f32[1152,128]{1,0:T(8,128)}, f32[1152,128]{1,0:T(8,128)}) custom-call(s32[3]{0:T(128)} %get-tuple-element.41.dest_ref, s32[256]{0:T(256)} %reshape.23.base_ref, bf16[4736,384]{1,0:T(8,128)(2,1)} %lon_solve.1.ct_ref, f32[8,4,32,128]{3,2,1,0:T(8,128)} %copy-done, f32[8,4,32,128]{3,2,1,0:T(8,128)} %copy-done, bf16[128,128]{1,0:T(8,128)(2,1)} %constant.92.clone.refs_2_), custom_call_target="tpu_custom_call" | custom-call | flops 4831838208 | bytes 3637248 | tf_op jit(solution)/shard_map/taps/pallas_call | solution.py:296
  77.1 1.5 collective-permute-start.5
  78.6 4.1 %collective-permute-start.8 = (f32[1152,128]{1,0:T(8,128)}, f32[1152,128]{1,0:T(8,128)S(1)}, u32[]{:S(2)}, u32[]{:S(2)}) collective-permute-start(f32[1152,128]{1,0:T(8,128)} %get-tuple-element.34), channel_id=1, source_target_pairs={{0,5},{1,6},{2,7},{3,0},{4,1},{5,2},{6,3},{7,4},{8,13},{9,14},{10,... | collective-permute-start | bytes 1769480 | tf_op jit(solution)/shard_map/ppermute | solution.py:416
  82.7 19.3 %taps.5 = (f32[1152,128]{1,0:T(8,128)}, f32[1152,128]{1,0:T(8,128)}) custom-call(s32[3]{0:T(128)} %get-tuple-element.40.dest_ref, s32[256]{0:T(256)} %reshape.23.base_ref, bf16[4736,384]{1,0:T(8,128)(2,1)} %lon_solve.1.ct_ref, f32[8,4,32,128]{3,2,1,0:T(8,128)} %copy-done, f32[8,4,32,128]{3,2,1,0:T(8,128)} %copy-done, bf16[128,128]{1,0:T(8,128)(2,1)} %constant.92.clone.refs_2_), custom_call_target="tpu_custom_call" | custom-call | flops 4831838208 | bytes 3637248 | tf_op jit(solution)/shard_map/taps/pallas_call | solution.py:296
  102.0 0.1 collective-permute-start.4
  102.1 0.0 copy-start.13
  102.1 19.4 %taps.4 = (f32[1152,128]{1,0:T(8,128)}, f32[1152,128]{1,0:T(8,128)}) custom-call(s32[3]{0:T(128)} %get-tuple-element.39.dest_ref, s32[256]{0:T(256)} %reshape.23.base_ref, bf16[4736,384]{1,0:T(8,128)(2,1)} %lon_solve.1.ct_ref, f32[8,4,32,128]{3,2,1,0:T(8,128)} %copy-done, f32[8,4,32,128]{3,2,1,0:T(8,128)} %copy-done, bf16[128,128]{1,0:T(8,128)(2,1)} %constant.92.clone.refs_2_), custom_call_target="tpu_custom_call" | custom-call | flops 4831838208 | bytes 3637248 | tf_op jit(solution)/shard_map/taps/pallas_call | solution.py:296
  121.5 0.0 collective-permute-done.6.refs_3_
  121.5 1.1 collective-permute-start.9
  122.6 12.5 %collective-permute-done.7.refs_4_ = f32[1152,128]{1,0:T(8,128)S(1)} collective-permute-done((f32[1152,128]{1,0:T(8,128)}, f32[1152,128]{1,0:T(8,128)S(1)}, u32[]{:S(2)}, u32[]{:S(2)}) %collective-permute-start.7) | collective-permute-done | bytes 589856 | tf_op jit(solution)/shard_map/ppermute | solution.py:416
  135.2 0.0 collective-permute-start.10
  135.2 0.1 convert_reduce_fusion.1
  135.3 0.1 fusion.6
  135.4 0.2 fusion.1
  135.6 0.7 convert_element_type.32
  136.3 1.3 fusion.5.target_ref
  137.6 0.0 collective-permute-done.5.refs_2_
  137.7 0.0 collective-permute-done.4.refs_1_
  137.7 19.0 %collective-permute-done.9.refs_6_ = f32[1152,128]{1,0:T(8,128)S(1)} collective-permute-done((f32[1152,128]{1,0:T(8,128)}, f32[1152,128]{1,0:T(8,128)S(1)}, u32[]{:S(2)}, u32[]{:S(2)}) %collective-permute-start.9) | collective-permute-done | bytes 589856 | tf_op jit(solution)/shard_map/ppermute | solution.py:416
  156.7 5.4 %collective-permute-done.10.refs_7_ = f32[1152,128]{1,0:T(8,128)} collective-permute-done((f32[1152,128]{1,0:T(8,128)}, f32[1152,128]{1,0:T(8,128)}, u32[]{:S(2)}, u32[]{:S(2)}) %collective-permute-start.10) | collective-permute-done | bytes 589856 | tf_op jit(solution)/shard_map/ppermute | solution.py:416
  162.2 8.8 %place.1 = f32[3072,128]{1,0:T(8,128)} custom-call(s32[3072]{0:T(1024)} %fusion.5.target_ref, f32[1152,128]{1,0:T(8,128)} %get-tuple-element.29.refs_0_, f32[1152,128]{1,0:T(8,128)} %copy-done.5, f32[1152,128]{1,0:T(8,128)} %copy-done.3, f32[1152,128]{1,0:T(8,128)} %copy-done.1, f32[1152,128]{1,0:T(8,128)} %copy-done.2, f32[1152,128]{1,0:T(8,128)} %copy-done.4, ...), custom_call_target="tpu_custom_call" | custom-call | bytes 9437184 | tf_op jit(solution)/shard_map/place/pallas_call | solution.py:349
  (26 shorter events, 0.1 us)
Async XLA Ops:
  5.9 29.2 %all-to-all-start = ((f32[8,4,32,128]{3,2,1,0:T(8,128)}), f32[8,4,32,128]{3,2,1,0:T(8,128)S(1)}, u32[]{:S(2)}, u32[]{:S(2)}) async-start(f32[8,4,32,128]{3,2,1,0:T(8,128)} %get-tuple-element.21), calls=%async_computation | async-start | bytes 1048576 | tf_op jit(solution)/shard_map/all_to_all | solution.py:395
  11.6 8.6 %collective-permute-start.1 = (f32[4,96,128]{2,1,0:T(8,128)}, f32[4,96,128]{2,1,0:T(8,128)S(1)}, u32[]{:S(2)}, u32[]{:S(2)}) collective-permute-start(f32[4,96,128]{2,1,0:T(8,128)} %get-tuple-element.23), channel_id=1, source_target_pairs={{8,0},{16,8},{24,16},{9,1},{17,9},{25,17},{10,2},{18,10},{26,18},{... | collective-permute-start | bytes 589832 | tf_op jit(solution)/shard_map/ppermute | solution.py:394
  14.8 5.4 %collective-permute-start = (f32[3,96,128]{2,1,0:T(8,128)}, f32[3,96,128]{2,1,0:T(8,128)S(1)}, u32[]{:S(2)}, u32[]{:S(2)}) collective-permute-start(f32[3,96,128]{2,1,0:T(8,128)} %get-tuple-element.22), channel_id=1, source_target_pairs={{0,8},{8,16},{16,24},{1,9},{9,17},{17,25},{2,10},{10,18},{18,26},{... | collective-permute-start | bytes 442376 | tf_op jit(solution)/shard_map/ppermute | solution.py:393
  20.2 0.7 copy-start.9
  20.2 0.7 copy-start.7
  24.5 3.1 %collective-permute-start.2 = (f32[2,37,128]{2,1,0:T(8,128)}, f32[2,37,128]{2,1,0:T(8,128)S(1)}, u32[]{:S(2)}, u32[]{:S(2)}) collective-permute-start(f32[2,37,128]{2,1,0:T(8,128)} %get-tuple-element.27), channel_id=1, source_target_pairs={{0,1},{1,2},{2,3},{3,4},{4,5},{5,6},{6,7},{7,0},{8,9},{9,10},{10,1... | collective-permute-start | bytes 113672 | tf_op jit(solution)/shard_map/ppermute | solution.py:398
  25.7 4.2 %collective-permute-start.3 = (f32[3,37,128]{2,1,0:T(8,128)}, f32[3,37,128]{2,1,0:T(8,128)S(1)}, u32[]{:S(2)}, u32[]{:S(2)}) collective-permute-start(f32[3,37,128]{2,1,0:T(8,128)} %get-tuple-element.28), channel_id=1, source_target_pairs={{1,0},{2,1},{3,2},{4,3},{5,4},{6,5},{7,6},{0,7},{9,8},{10,9},{11,1... | collective-permute-start | bytes 170504 | tf_op jit(solution)/shard_map/ppermute | solution.py:399
  27.6 2.3 %copy-start.12 = (f32[2,37,128]{2,1,0:T(8,128)}, f32[2,37,128]{2,1,0:T(8,128)S(1)}, u32[]{:S(2)}) copy-start(f32[2,37,128]{2,1,0:T(8,128)S(1)} %collective-permute-done.2.west_ref) | copy-start | bytes 113668
  29.9 0.6 copy-start.11
  30.5 4.7 %copy-start.10 = (f32[32,32]{1,0:T(8,128)S(1)}, f32[32,32]{1,0:T(8,128)}, u32[]{:S(2)}) copy-start(f32[32,32]{1,0:T(8,128)} %constant.89.clone) | copy-start | bytes 12292
  35.1 0.9 copy-start
  55.3 66.2 %collective-permute-start.6 = (f32[1152,128]{1,0:T(8,128)}, f32[1152,128]{1,0:T(8,128)S(1)}, u32[]{:S(2)}, u32[]{:S(2)}) collective-permute-start(f32[1152,128]{1,0:T(8,128)} %get-tuple-element.32), channel_id=1, source_target_pairs={{0,3},{1,4},{2,5},{3,6},{4,7},{5,0},{6,1},{7,2},{8,11},{9,12},{10,... | collective-permute-start | bytes 1769480 | tf_op jit(solution)/shard_map/ppermute | solution.py:416
  56.7 78.5 %collective-permute-start.7 = (f32[1152,128]{1,0:T(8,128)}, f32[1152,128]{1,0:T(8,128)S(1)}, u32[]{:S(2)}, u32[]{:S(2)}) collective-permute-start(f32[1152,128]{1,0:T(8,128)} %get-tuple-element.33), channel_id=1, source_target_pairs={{0,4},{1,5},{2,6},{3,7},{4,0},{5,1},{6,2},{7,3},{8,12},{9,13},{10,... | collective-permute-start | bytes 1769480 | tf_op jit(solution)/shard_map/ppermute | solution.py:416
  77.1 60.5 %collective-permute-start.5 = (f32[1152,128]{1,0:T(8,128)}, f32[1152,128]{1,0:T(8,128)S(1)}, u32[]{:S(2)}, u32[]{:S(2)}) collective-permute-start(f32[1152,128]{1,0:T(8,128)} %get-tuple-element.31), channel_id=1, source_target_pairs={{0,2},{1,3},{2,4},{3,5},{4,6},{5,7},{6,0},{7,1},{8,10},{9,11},{10,... | collective-permute-start | bytes 1769480 | tf_op jit(solution)/shard_map/ppermute | solution.py:416
  78.6 59.0 %collective-permute-start.8 = (f32[1152,128]{1,0:T(8,128)}, f32[1152,128]{1,0:T(8,128)S(1)}, u32[]{:S(2)}, u32[]{:S(2)}) collective-permute-start(f32[1152,128]{1,0:T(8,128)} %get-tuple-element.34), channel_id=1, source_target_pairs={{0,5},{1,6},{2,7},{3,0},{4,1},{5,2},{6,3},{7,4},{8,13},{9,14},{10,... | collective-permute-start | bytes 1769480 | tf_op jit(solution)/shard_map/ppermute | solution.py:416
  102.0 35.6 %collective-permute-start.4 = (f32[1152,128]{1,0:T(8,128)}, f32[1152,128]{1,0:T(8,128)S(1)}, u32[]{:S(2)}, u32[]{:S(2)}) collective-permute-start(f32[1152,128]{1,0:T(8,128)} %get-tuple-element.30), channel_id=1, source_target_pairs={{0,1},{1,2},{2,3},{3,4},{4,5},{5,6},{6,7},{7,0},{8,9},{9,10},{10,1... | collective-permute-start | bytes 1769480 | tf_op jit(solution)/shard_map/ppermute | solution.py:416
  102.1 33.1 %copy-start.8 = (s32[32,96]{1,0:T(8,128)S(1)}, s32[32,96]{1,0:T(8,128)}, u32[]{:S(2)}) copy-start(s32[32,96]{1,0:T(8,128)} %eq.26.owner_ref) | copy-start | bytes 36868
  102.1 33.4 %copy-start.13 = (bf16[96,96,1]{1,0,2:T(8,128)(2,1)S(1)}, bf16[96,96,1]{1,0,2:T(8,128)(2,1)}, u32[]{:S(2)}) copy-start(bf16[96,96,1]{1,0,2:T(8,128)(2,1)} %constant.99) | copy-start | bytes 55300
  121.5 40.6 %copy-start.1 = (f32[1152,128]{1,0:T(8,128)}, f32[1152,128]{1,0:T(8,128)S(1)}, u32[]{:S(2)}) copy-start(f32[1152,128]{1,0:T(8,128)S(1)} %collective-permute-done.6.refs_3_) | copy-start | bytes 1769476
  121.5 35.1 %collective-permute-start.9 = (f32[1152,128]{1,0:T(8,128)}, f32[1152,128]{1,0:T(8,128)S(1)}, u32[]{:S(2)}, u32[]{:S(2)}) collective-permute-start(f32[1152,128]{1,0:T(8,128)} %get-tuple-element.35), channel_id=1, source_target_pairs={{0,6},{1,7},{2,0},{3,1},{4,2},{5,3},{6,4},{7,5},{8,14},{9,15},{10,... | collective-permute-start | bytes 1769480 | tf_op jit(solution)/shard_map/ppermute | solution.py:416
  135.2 26.9 %copy-start.2 = (f32[1152,128]{1,0:T(8,128)}, f32[1152,128]{1,0:T(8,128)S(1)}, u32[]{:S(2)}) copy-start(f32[1152,128]{1,0:T(8,128)S(1)} %collective-permute-done.7.refs_4_) | copy-start | bytes 1769476
  135.2 26.9 %collective-permute-start.10 = (f32[1152,128]{1,0:T(8,128)}, f32[1152,128]{1,0:T(8,128)}, u32[]{:S(2)}, u32[]{:S(2)}) collective-permute-start(f32[1152,128]{1,0:T(8,128)} %get-tuple-element.36), channel_id=1, source_target_pairs={{0,7},{1,0},{2,1},{3,2},{4,3},{5,4},{6,5},{7,6},{8,15},{9,8},{10,9... | collective-permute-start | bytes 1769480 | tf_op jit(solution)/shard_map/ppermute | solution.py:416
  137.6 24.5 %copy-start.3 = (f32[1152,128]{1,0:T(8,128)}, f32[1152,128]{1,0:T(8,128)S(1)}, u32[]{:S(2)}) copy-start(f32[1152,128]{1,0:T(8,128)S(1)} %collective-permute-done.5.refs_2_) | copy-start | bytes 1769476
  137.6 24.5 %copy-start.4 = (f32[1152,128]{1,0:T(8,128)}, f32[1152,128]{1,0:T(8,128)S(1)}, u32[]{:S(2)}) copy-start(f32[1152,128]{1,0:T(8,128)S(1)} %collective-permute-done.8.refs_5_) | copy-start | bytes 1769476
  137.7 24.5 %copy-start.5 = (f32[1152,128]{1,0:T(8,128)}, f32[1152,128]{1,0:T(8,128)S(1)}, u32[]{:S(2)}) copy-start(f32[1152,128]{1,0:T(8,128)S(1)} %collective-permute-done.4.refs_1_) | copy-start | bytes 1769476
  156.7 5.5 %copy-start.6 = (f32[1152,128]{1,0:T(8,128)}, f32[1152,128]{1,0:T(8,128)S(1)}, u32[]{:S(2)}) copy-start(f32[1152,128]{1,0:T(8,128)S(1)} %collective-permute-done.9.refs_6_) | copy-start | bytes 1769476

commit v3 on v2

--- a/solution.py
+++ b/solution.py
@@ -8,6 +8,7 @@
 from jax.experimental import pallas as pl
 from jax.experimental.pallas import tpu as pltpu
 from jax.sharding import PartitionSpec as P
+
 
 POLE = math.sqrt(3.0) - 2.0
 GAIN = math.sqrt(3.0)
@@ -189,15 +190,23 @@
     )(x, west, east, jnp.concatenate([high, high, low], axis=0))
 
 
-def tap_kernel(dest_ref, base_ref, ct_ref, *refs, count, cols, cap, span):
+def tap_kernel(meta_ref, base_ref, *refs, tables, count, cols, cap, span, at):
+    meta = lambda k: meta_ref[at + k]
+    table_refs, refs = refs[:tables], refs[tables:]
     cells_refs, tri_ref = refs[:count], refs[count]
     out_refs = refs[count + 1 : 2 * count + 1]
-    rank, place, lon_w, lat_w, near, later, packed, sems = refs[2 * count + 1 :]
+    rank, place, lon_w, lat_w, near, later, packed, ct_ref, sems, table_sem = refs[2 * count + 1 :]
+    for n, table_ref in enumerate(table_refs):
+
+        @pl.when(meta(count + 1) == n)
+        def _(table_ref=table_ref):
+            pltpu.make_async_copy(table_ref, ct_ref, table_sem).start()
+
     rows = rank.shape[1]
     ch = packed.shape[2]
     band = lax.axis_index("lat")
     lat_total = rows * lax.axis_size("lat")
-    origin = (dest_ref[count] * cols).astype(F32)
+    origin = (meta(count) * cols).astype(F32)
 
     def window_of(i):
         return i - jnp.where(band * rows + i == lat_total - 1, 1, 0)
@@ -252,7 +261,7 @@
                 terms.append(block * lat_w[d, e, pl.ds(i, 1)])
             value = ((terms[0] + terms[1]) + terms[2]) + ((terms[3] + terms[4]) + terms[5])
             high, low = split(value)
-            base = base_ref[dest_ref[d] * rows + i]
+            base = base_ref[meta(count + 2 + d) + i]
             odd = lax.rem(base, 8)
             spot = rank[d, pl.ds(i, 1)] + odd.astype(F32)
             pick = jnp.where(column == spot, 1.0, 0.0).astype(BF)
@@ -267,6 +276,7 @@
             packed[d, pl.ds(pl.multiple_of(at + 8, 8), span - 8)] = got[8:]
 
     build(0, near)
+    pltpu.make_async_copy(table_refs[0], ct_ref, table_sem).wait()
 
     @pl.loop(0, rows // 2)
     def _(pair):
@@ -285,26 +295,24 @@
         copy.wait()
 
 
-def taps(dests, sector, base, ct, cells, cols, cap):
+def taps(meta, at, count, base, tables, cells, cols, cap):
     _, words, rows, lanes = cells.shape
-    count = len(dests)
-    ch = ct.shape[0] // (rows + UP + DOWN)
+    ch = tables[0].shape[0] // (rows + UP + DOWN)
     span = 112
     tri = jnp.asarray(np.triu(np.ones((lanes, lanes)), 1), BF)
     weights = pltpu.VMEM((3 * LANES, count * lanes), BF)
-    meta = jnp.stack([*dests, sector]).astype(jnp.int32)
     return pl.pallas_call(
-        functools.partial(tap_kernel, count=count, cols=cols, cap=cap, span=span),
+        functools.partial(tap_kernel, tables=len(tables), count=count, cols=cols, cap=cap, span=span, at=at),
         out_shape=[jax.ShapeDtypeStruct((cap, ch), F32)] * count,
         grid_spec=pltpu.PrefetchScalarGridSpec(
             num_scalar_prefetch=2,
             grid=(1,),
-            in_specs=[pl.BlockSpec(ct.shape, lambda g, d, b: (0, 0))]
+            in_specs=[pl.BlockSpec(memory_space=pl.ANY)] * len(tables)
             + [
-                pl.BlockSpec((1, words, rows, lanes), functools.partial(lambda g, d, b, k: (d[k], 0, 0, 0), k=k))
+                pl.BlockSpec((1, words, rows, lanes), functools.partial(lambda g, m, b, k: (m[k], 0, 0, 0), k=at + k))
                 for k in range(count)
             ]
-            + [pl.BlockSpec(tri.shape, lambda g, d, b: (0, 0))],
+            + [pl.BlockSpec(tri.shape, lambda g, m, b: (0, 0))],
             out_specs=[pl.BlockSpec(memory_space=pl.ANY)] * count,
             scratch_shapes=[
                 pltpu.VMEM((count, rows, lanes), F32),
@@ -314,15 +322,17 @@
                 weights,
                 weights,
                 pltpu.VMEM((count, cap + span + 8, ch), F32),
+                pltpu.VMEM(tables[0].shape, BF),
                 pltpu.SemaphoreType.DMA((count,)),
+                pltpu.SemaphoreType.DMA,
             ],
         ),
         cost_estimate=pl.CostEstimate(
-            flops=6 * count * rows * TAPS * LANES * ch * LANES, bytes_accessed=2 * ct.size, transcendentals=0
+            flops=6 * count * rows * TAPS * LANES * ch * LANES, bytes_accessed=2 * tables[0].size, transcendentals=0
         ),
         compiler_params=pltpu.CompilerParams(vmem_limit_bytes=VMEM_LIMIT),
         name="taps",
-    )(meta, base, ct, *([cells] * count), tri)
+    )(meta, base, *tables, *([cells] * count), tri)
 
 
 def place_kernel(target_ref, *refs, cap):
@@ -363,7 +373,7 @@
 
 
 def earlier(mask):
-    rows, cols = mask.shape[1:]
+    _, cols = mask.shape[1:]
     ones = mask.astype(F32)
     before = lax.dot_general(
         mask.astype(BF),
@@ -380,14 +390,21 @@
     return jnp.dot(totals, jnp.asarray(np.triu(np.ones((rows, rows)), 1), F32), precision=lax.Precision.HIGHEST)
 
 
-def body(tracers, owners, columns, lat_shift, fractions):
+def transport(tracers, owners, columns, lat_shift, fractions):
     rows, cols, ch = tracers.shape
     bands = lax.axis_size("lat")
     sectors = lax.axis_size("lon")
+    band = lax.axis_index("lat")
     me = lax.axis_index("lon")
     cells = rows * cols
     cap = 3 * cells // sectors
-
+    quarter = sectors // 4
+    at = lambda q, o: q * quarter + o
+    mirror = [(at(q, o), at((0, 2, 1, 3)[q], o)) for q in (1, 2) for o in range(quarter)]
+    mine, offset = me // quarter, me % quarter
+    middle = (mine == 1) | (mine == 2)
+
+    mirrored = lax.ppermute(tracers, "lon", mirror)
     owner = owners.reshape(rows, cols)
     down, up, top, bottom, words = edges(tracers, owner, columns, lat_shift, fractions)
     above = lax.ppermute(down, "lat", [(i, i + 1) for i in range(bands - 1)])
@@ -397,24 +414,58 @@
     x, right, left = lat_solve(tracers, above, below, top, bottom)
     west = lax.ppermute(right, "lon", [(i, (i + 1) % sectors) for i in range(sectors)])
     east = lax.ppermute(left, "lon", [((i + 1) % sectors, i) for i in range(sectors)])
-
-    local = asked[:, 0] - (me * cols).astype(F32)
-    base = bases(((local >= 0.0) & (local < float(cols))).astype(F32)).astype(jnp.int32).reshape(-1)
+    above, below, right = lax.optimization_barrier((above, below, right))
+    rim = jnp.concatenate(
+        [jnp.where(band == 0, top, above), jnp.where(band == bands - 1, bottom, below)], axis=0
+    )
+    rim = lax.ppermute(rim, "lon", mirror)
+    sides = lax.ppermute(jnp.concatenate([west, east], axis=0), "lon", mirror)
+
+    origins = np.array([[s * cols, dict(mirror).get(s, s) * cols] for s in range(sectors)], np.float32)
+    local = asked[None, :, 0] - jnp.asarray(origins)[me][:, None, None, None]
+    inside = ((local >= 0.0) & (local < float(cols))).astype(F32).reshape(2 * sectors, rows, -1)
+    base = bases(inside).astype(jnp.int32).reshape(-1)
+
+    own = lon_solve(x, west, east)
+    late_owner, x = lax.optimization_barrier((owner, x))
     every = jnp.arange(sectors, dtype=jnp.int32)
-    mask = owner[None] == every[:, None, None]
+    mask = late_owner[None] == every[:, None, None]
     before, own_base = earlier(mask)
     slot = jnp.sum(jnp.where(mask, before + own_base[:, :, None], 0.0), axis=0).astype(jnp.int32)
-    target = ((me - owner) % sectors * cap + slot).reshape(cells)
-
-    ct = lon_solve(x, west, east)
+    q = late_owner // quarter
+    alike = ((q == 1) | (q == 2)) == middle
+    early = ((q == 1) | (q == 2)) == (q // 2 == mine // 2)
+    part = jnp.where(early, jnp.where(alike, 1, 0), jnp.where(alike, 3, 2)) * quarter
+    target = ((part + (offset - late_owner) % quarter) * cap + slot).reshape(cells)
+
+    goals = ((2, 0, 3, 1), (3, 1, 2, 0), (1, 0, 3, 2), (0, 1, 2, 3))
+    shifts = list(range(quarter))[::-1]
+    calls = [(group, shifts[n : n + 2]) for group in range(4) for n in range(0, quarter, 2)]
+    plan = []
+    for s in range(sectors):
+        k, o = s // quarter, s % quarter
+        row = []
+        for group, pair in calls:
+            which = int(group >= 2 and k in (1, 2))
+            dests = [at(goals[group][k], (o + a) % quarter) for a in pair]
+            row += dests + [dict(mirror).get(s, s) if which else s, which]
+            row += [(which * sectors + dest) * rows for dest in dests]
+        plan.append(row)
+    meta = jnp.asarray(np.array(plan, np.int32))[me]
+
     parts = [None] * sectors
-    order = sorted(range(sectors), key=lambda k: (k == 0, abs(2 * k - sectors)))
-    for pair in [order[n : n + 2] for n in range(0, sectors, 2)]:
-        values = taps([(me + k) % sectors for k in pair], me, base, ct, asked, cols, cap)
-        for k, value in zip(pair, values):
-            if k:
-                value = lax.ppermute(value, "lon", [(i, (i + k) % sectors) for i in range(sectors)])
-            parts[k] = value
+    tables, done = [own], 0
+    for group, pair in calls:
+        if group == 2 and len(tables) == 1:
+            other, _, _ = lat_solve(mirrored, rim[: UP + 1], rim[UP + 1 :], rim[: UP + 1], rim[UP + 1 :])
+            tables = [own, lon_solve(other, sides[: LEFT + 1], sides[LEFT + 1 :])]
+        values = taps(meta, done, len(pair), base, tables, asked, cols, cap)
+        done += 2 * len(pair) + 2
+        for a, value in zip(pair, values):
+            moves = [(at(k, o), at(goals[group][k], (o + a) % quarter)) for k in range(4) for o in range(quarter)]
+            if any(i != j for i, j in moves):
+                value = lax.ppermute(value, "lon", moves)
+            parts[group * quarter + a] = value
     return place(target, parts).reshape(rows, cols, ch)
 
 
@@ -427,4 +478,4 @@
         P(None, "lat", "lon"),
     )
     out_specs = P("lat", "lon", None)
-    return jax.shard_map(body, mesh=mesh, in_specs=in_specs, out_specs=out_specs, check_vma=False)
+    return jax.shard_map(transport, mesh=mesh, in_specs=in_specs, out_specs=out_specs, check_vma=False)

time: 172 us -> 216 us (1.26)
  the two profiles are of different devices: /device:TPU:3 before, /device:TPU:0 now
where the time goes in v3:
time: 216 us; the launch traced here: 214 us
  Pallas kernels  107 us (50%)
  waiting for transfers between devices  47.5 us (22%)
  starting transfers between devices  47.4 us (22%)
  local copies, waits for them, and re-layouts  9 us (4%)
  other arithmetic  2.77 us (1%)
    pallas_call x4, Pallas kernels, taps(): pl.pallas_call(functools.partial(tap_kernel, tables=len(tables), count=co...  79.4 us
    ppermute x7, starting transfers between devices, transport(): value = lax.ppermute(value, 'lon', moves)  27.9 us
    ppermute x7, waiting for transfers between devices, transport(): value = lax.ppermute(value, 'lon', moves)  24 us
    all_to_all x1, waiting for transfers between devices, transport(): lax.all_to_all(words, 'lon', split_axis=0, concat_axis=0, tiled=True)  19.4 us
    pallas_call x2, Pallas kernels, lon_solve(): pl.pallas_call(lon_kernel, out_shape=jax.ShapeDtypeStruct((total * ch, 3...  9.03 us
    pallas_call x1, Pallas kernels, place(): pl.pallas_call(functools.partial(place_kernel, cap=cap), out_shape=jax.Sh...  8.81 us
    all_to_all x1, starting transfers between devices, transport(): lax.all_to_all(words, 'lon', split_axis=0, concat_axis=0, tiled=True)  8.12 us
    pallas_call x2, Pallas kernels, lat_solve(): pl.pallas_call(lat_kernel, out_shape=(jax.ShapeDtypeStruct((total, cols,...  7.12 us
  transfers between devices with their start and end apart: 15, of which 4 were waited for; matrix products, arithmetic and copies ran while one was open for 4% of the time, Pallas kernels for 45%

profile of v3, /device:TPU:0, one launch (start us, length us, event | category | flops | bytes accessed | tf_op | source)
XLA Modules:
  0.0 214.5 jit_solution(16290539354188183211)
XLA Ops:
  0.0 0.5 broadcast.42
  0.5 1.4 reduce.4
  1.9 0.7 reshape.22.owner_ref
  2.6 2.7 %edges.1 = (f32[3,96,128]{2,1,0:T(8,128)}, f32[4,96,128]{2,1,0:T(8,128)}, f32[3,96,128]{2,1,0:T(8,128)}, f32[4,96,128]{2,1,0:T(8,128)}, f32[8,4,32,128]{3,2,1,0:T(8,128)}) custom-call(f32[32,96,128]{2,1,0:T(8,128)} %s_ref.3, s32[32,96]{1,0:T(8,128)} %reshape.22.owner_ref, s32[32,96]{1,0:T(8,128)} %column_ref.1, s32[32,96]{1,0:T(8,128)} %shift_ref.1, ...), custom_call_target="tpu_custom_call" | custom-call | flops 2359296 | bytes 2359296 | tf_op jit(solution)/shard_map/edges/pallas_call | solution.py:94
  5.3 1.4 collective-permute-start.1
  6.7 3.0 %collective-permute-start = (f32[3,96,128]{2,1,0:T(8,128)}, f32[3,96,128]{2,1,0:T(8,128)S(1)}, u32[]{:S(2)}, u32[]{:S(2)}) collective-permute-start(f32[3,96,128]{2,1,0:T(8,128)} %get-tuple-element.25), channel_id=1, source_target_pairs={{0,8},{8,16},{16,24},{1,9},{9,17},{17,25},{2,10},{10,18},{18,26},{... | collective-permute-start | bytes 442376 | tf_op jit(solution)/shard_map/ppermute | solution.py:410
  9.8 0.8 collective-permute-start.8
  10.5 8.1 %all-to-all-start = ((f32[8,4,32,128]{3,2,1,0:T(8,128)}), f32[8,4,32,128]{3,2,1,0:T(8,128)S(1)}, u32[]{:S(2)}, u32[]{:S(2)}) async-start(f32[8,4,32,128]{3,2,1,0:T(8,128)} %get-tuple-element.31), calls=%async_computation | async-start | bytes 1048576 | tf_op jit(solution)/shard_map/all_to_all | solution.py:412
  18.7 0.6 copy-done.5
  19.3 0.1 copy-done.3
  19.4 3.5 %lat_solve.2 = (f32[37,96,128]{2,1,0:T(8,128)}, f32[2,37,128]{2,1,0:T(8,128)}, f32[3,37,128]{2,1,0:T(8,128)}) custom-call(f32[32,96,128]{2,1,0:T(8,128)} %s_ref.3, f32[3,96,128]{2,1,0:T(8,128)} %copy-done.5, f32[4,96,128]{2,1,0:T(8,128)} %copy-done.3, f32[3,96,128]{2,1,0:T(8,128)} %get-tuple-element.27.top_ref, f32[4,96,128]{2,1,0:T(8,128)} %get-tuple-element.28.bottom_ref, ...), custom_call_target="tpu_custom_call" | custom-call | flops 3932160 | bytes 3932160 | tf_op jit(solution)/shard_map/lat_solve/pallas_call | solution.py:142
  22.9 2.0 collective-permute-start.2
  25.0 1.0 broadcast_select_fusion
  26.0 0.7 collective-permute-start.9
  26.7 2.8 %collective-permute-start.3 = (f32[3,37,128]{2,1,0:T(8,128)}, f32[3,37,128]{2,1,0:T(8,128)S(1)}, u32[]{:S(2)}, u32[]{:S(2)}) collective-permute-start(f32[3,37,128]{2,1,0:T(8,128)} %get-tuple-element.33), channel_id=1, source_target_pairs={{1,0},{2,1},{3,2},{4,3},{5,4},{6,5},{7,6},{0,7},{9,8},{10,9},{11,1... | collective-permute-start | bytes 170504 | tf_op jit(solution)/shard_map/ppermute | solution.py:416
  29.4 0.7 dynamic-slice_bitcast_fusion
  30.1 4.1 %collective-permute-done.2.west_ref = f32[2,37,128]{2,1,0:T(8,128)S(1)} collective-permute-done((f32[2,37,128]{2,1,0:T(8,128)}, f32[2,37,128]{2,1,0:T(8,128)S(1)}, u32[]{:S(2)}, u32[]{:S(2)}) %collective-permute-start.2) | collective-permute-done | bytes 37920 | tf_op jit(solution)/shard_map/ppermute | solution.py:415
  34.2 0.7 collective-permute-start.10
  34.9 1.3 dynamic-slice_bitcast_fusion.1.meta_ref
  36.2 4.5 %lon_solve.2.refs_0_ = bf16[4736,384]{1,0:T(8,128)(2,1)} custom-call(f32[37,96,128]{2,1,0:T(8,128)} %get-tuple-element.29.x_ref, f32[2,37,128]{2,1,0:T(8,128)} %copy-done.13, f32[3,37,128]{2,1,0:T(8,128)} %copy-done.12, bf16[384,128]{1,0:T(8,128)(2,1)} %constant.107.green_ref), custom_call_target="tpu_custom_call" | custom-call | flops 465567744 | bytes 3637248 | tf_op jit(solution)/shard_map/lon_solve/pallas_call | solution.py:182
  40.7 0.6 slice.26.east_ref
  41.3 0.6 slice.25.west_ref
  41.9 0.7 slice.24.below_ref.bottom_ref
  42.6 0.7 slice.23.above_ref.top_ref
  43.3 19.4 %all-to-all-done.refs_1_.refs_2_.refs_3_ = f32[8,4,32,128]{3,2,1,0:T(8,128)S(1)} async-done(((f32[8,4,32,128]{3,2,1,0:T(8,128)}), f32[8,4,32,128]{3,2,1,0:T(8,128)S(1)}, u32[]{:S(2)}, u32[]{:S(2)}) %all-to-all-start) | async-done | bytes 524320 | tf_op jit(solution)/shard_map/all_to_all | solution.py:412
  62.7 0.2 convert_reduce_fusion
  62.9 0.1 convolution_convert_fusion
  63.1 0.7 reshape.24.base_ref
  63.8 19.8 %taps.5 = (f32[1152,128]{1,0:T(8,128)}, f32[1152,128]{1,0:T(8,128)}) custom-call(s32[24]{0:T(128)} %dynamic-slice_bitcast_fusion.1.meta_ref, s32[512]{0:T(512)} %reshape.24.base_ref, bf16[4736,384]{1,0:T(8,128)(2,1)} %lon_solve.2.refs_0_, f32[8,4,32,128]{3,2,1,0:T(8,128)} %copy-done.1, f32[8,4,32,128]{3,2,1,0:T(8,128)} %copy-done.1, ...), custom_call_target="tpu_custom_call" | custom-call | flops 4831838208 | bytes 3637248 | tf_op jit(solution)/shard_map/taps/pallas_call | solution.py:304
  83.6 5.7 %collective-permute-start.6 = (f32[1152,128]{1,0:T(8,128)}, f32[1152,128]{1,0:T(8,128)S(1)}, u32[]{:S(2)}, u32[]{:S(2)}) collective-permute-start(f32[1152,128]{1,0:T(8,128)} %get-tuple-element.36), channel_id=1, source_target_pairs={{0,6},{1,7},{2,2},{3,3},{4,4},{5,5},{6,0},{7,1},{8,14},{9,15},{10,... | collective-permute-start | bytes 1769480 | tf_op jit(solution)/shard_map/ppermute | solution.py:467
  89.3 1.9 collective-permute-start.7
  91.2 19.8 %taps.4 = (f32[1152,128]{1,0:T(8,128)}, f32[1152,128]{1,0:T(8,128)}) custom-call(s32[24]{0:T(128)} %dynamic-slice_bitcast_fusion.1.meta_ref, s32[512]{0:T(512)} %reshape.24.base_ref, bf16[4736,384]{1,0:T(8,128)(2,1)} %lon_solve.2.refs_0_, f32[8,4,32,128]{3,2,1,0:T(8,128)} %copy-done.1, f32[8,4,32,128]{3,2,1,0:T(8,128)} %copy-done.1, ...), custom_call_target="tpu_custom_call" | custom-call | flops 4831838208 | bytes 3637248 | tf_op jit(solution)/shard_map/taps/pallas_call | solution.py:304
  111.1 16.6 %collective-permute-start.4 = (f32[1152,128]{1,0:T(8,128)}, f32[1152,128]{1,0:T(8,128)S(1)}, u32[]{:S(2)}, u32[]{:S(2)}) collective-permute-start(f32[1152,128]{1,0:T(8,128)} %get-tuple-element.34), channel_id=1, source_target_pairs={{0,4},{1,5},{2,0},{3,1},{4,6},{5,7},{6,2},{7,3},{8,12},{9,13},{10,... | collective-permute-start | bytes 1769480 | tf_op jit(solution)/shard_map/ppermute | solution.py:467
  127.7 1.1 copy-done
  128.9 3.6 %lat_solve.3 = (f32[37,96,128]{2,1,0:T(8,128)}, f32[2,37,128]{2,1,0:T(8,128)}, f32[3,37,128]{2,1,0:T(8,128)}) custom-call(f32[32,96,128]{2,1,0:T(8,128)} %copy-done, f32[3,96,128]{2,1,0:T(8,128)} %slice.23.above_ref.top_ref, f32[4,96,128]{2,1,0:T(8,128)} %slice.24.below_ref.bottom_ref, f32[3,96,128]{2,1,0:T(8,128)} %slice.23.above_ref.top_ref, ...), custom_call_target="tpu_custom_call" | custom-call | flops 3932160 | bytes 3932160 | tf_op jit(solution)/shard_map/lat_solve/pallas_call | solution.py:142
  132.5 4.5 %lon_solve.3.refs_1_ = bf16[4736,384]{1,0:T(8,128)(2,1)} custom-call(f32[37,96,128]{2,1,0:T(8,128)} %get-tuple-element.40.x_ref, f32[2,37,128]{2,1,0:T(8,128)} %slice.25.west_ref, f32[3,37,128]{2,1,0:T(8,128)} %slice.26.east_ref, bf16[384,128]{1,0:T(8,128)(2,1)} %constant.107.green_ref), custom_call_target="tpu_custom_call" | custom-call | flops 465567744 | bytes 3637248 | tf_op jit(solution)/shard_map/lon_solve/pallas_call | solution.py:182
  137.0 19.9 %taps.7 = (f32[1152,128]{1,0:T(8,128)}, f32[1152,128]{1,0:T(8,128)}) custom-call(s32[24]{0:T(128)} %dynamic-slice_bitcast_fusion.1.meta_ref, s32[512]{0:T(512)} %reshape.24.base_ref, bf16[4736,384]{1,0:T(8,128)(2,1)} %lon_solve.2.refs_0_, bf16[4736,384]{1,0:T(8,128)(2,1)} %lon_solve.3.refs_1_, f32[8,4,32,128]{3,2,1,0:T(8,128)} %copy-done.1, ...), custom_call_target="tpu_custom_call" | custom-call | flops 4831838208 | bytes 3637248 | tf_op jit(solution)/shard_map/taps/pallas_call | solution.py:304
  156.9 0.0 copy-start.15
  156.9 1.6 collective-permute-start.13
  158.5 19.9 %taps.6 = (f32[1152,128]{1,0:T(8,128)}, f32[1152,128]{1,0:T(8,128)}) custom-call(s32[24]{0:T(128)} %dynamic-slice_bitcast_fusion.1.meta_ref, s32[512]{0:T(512)} %reshape.24.base_ref, bf16[4736,384]{1,0:T(8,128)(2,1)} %lon_solve.2.refs_0_, bf16[4736,384]{1,0:T(8,128)(2,1)} %lon_solve.3.refs_1_, f32[8,4,32,128]{3,2,1,0:T(8,128)} %copy-done.1, ...), custom_call_target="tpu_custom_call" | custom-call | flops 4831838208 | bytes 3637248 | tf_op jit(solution)/shard_map/taps/pallas_call | solution.py:304
  178.4 2.1 collective-permute-start.11
  180.5 0.1 convert_reduce_fusion.1
  180.6 0.1 fusion.14
  180.7 0.2 fusion.1
  180.9 0.7 reshape.23.target_ref
  181.6 13.2 %collective-permute-done.11.refs_4_ = f32[1152,128]{1,0:T(8,128)S(1)} collective-permute-done((f32[1152,128]{1,0:T(8,128)}, f32[1152,128]{1,0:T(8,128)S(1)}, u32[]{:S(2)}, u32[]{:S(2)}) %collective-permute-start.11) | collective-permute-done | bytes 589856 | tf_op jit(solution)/shard_map/ppermute | solution.py:467
  194.9 10.8 %collective-permute-done.12.refs_5_ = f32[1152,128]{1,0:T(8,128)} collective-permute-done((f32[1152,128]{1,0:T(8,128)}, f32[1152,128]{1,0:T(8,128)}, u32[]{:S(2)}, u32[]{:S(2)}) %collective-permute-start.12) | collective-permute-done | bytes 589856 | tf_op jit(solution)/shard_map/ppermute | solution.py:467
  205.7 8.8 %place.1 = f32[3072,128]{1,0:T(8,128)} custom-call(s32[3072]{0:T(1024)} %reshape.23.target_ref, f32[1152,128]{1,0:T(8,128)} %copy-done.8, f32[1152,128]{1,0:T(8,128)} %collective-permute-done.5.refs_1_, f32[1152,128]{1,0:T(8,128)} %copy-done.6, f32[1152,128]{1,0:T(8,128)} %copy-done.7, f32[1152,128]{1,0:T(8,128)} %copy-done.10, ...), custom_call_target="tpu_custom_call" | custom-call | bytes 9437184 | tf_op jit(solution)/shard_map/place/pallas_call | solution.py:359
  (46 shorter events, 0.2 us)
Async XLA Ops:
  5.3 19.6 %copy-start.4 = (f32[3,96,128]{2,1,0:T(8,128)S(1)}, f32[3,96,128]{2,1,0:T(8,128)}, u32[]{:S(2)}) copy-start(f32[3,96,128]{2,1,0:T(8,128)} %get-tuple-element.27.top_ref) | copy-start | bytes 442372
  5.3 13.4 %collective-permute-start.1 = (f32[4,96,128]{2,1,0:T(8,128)}, f32[4,96,128]{2,1,0:T(8,128)S(1)}, u32[]{:S(2)}, u32[]{:S(2)}) collective-permute-start(f32[4,96,128]{2,1,0:T(8,128)} %get-tuple-element.26), channel_id=1, source_target_pairs={{8,0},{16,8},{24,16},{9,1},{17,9},{25,17},{10,2},{18,10},{26,18},{... | collective-permute-start | bytes 589832 | tf_op jit(solution)/shard_map/ppermute | solution.py:411
  6.7 12.0 %collective-permute-start = (f32[3,96,128]{2,1,0:T(8,128)}, f32[3,96,128]{2,1,0:T(8,128)S(1)}, u32[]{:S(2)}, u32[]{:S(2)}) collective-permute-start(f32[3,96,128]{2,1,0:T(8,128)} %get-tuple-element.25), channel_id=1, source_target_pairs={{0,8},{8,16},{16,24},{1,9},{9,17},{17,25},{2,10},{10,18},{18,26},{... | collective-permute-start | bytes 442376 | tf_op jit(solution)/shard_map/ppermute | solution.py:410
  9.8 117.9 %collective-permute-start.8 = (f32[32,96,128]{2,1,0:T(8,128)}, f32[32,96,128]{2,1,0:T(8,128)S(1)}, u32[]{:S(2)}, u32[]{:S(2)}) collective-permute-start(f32[32,96,128]{2,1,0:T(8,128)} %s_ref.3), channel_id=1, source_target_pairs={{2,4},{3,5},{4,2},{5,3},{10,12},{11,13},{12,10},{13,11},{18,20},{1... | collective-permute-start | bytes 4718600 | tf_op jit(solution)/shard_map/ppermute | solution.py:407
  10.5 14.4 %copy-start.2 = (f32[4,96,128]{2,1,0:T(8,128)S(1)}, f32[4,96,128]{2,1,0:T(8,128)}, u32[]{:S(2)}) copy-start(f32[4,96,128]{2,1,0:T(8,128)} %get-tuple-element.28.bottom_ref) | copy-start | bytes 589828
  10.5 52.2 %all-to-all-start = ((f32[8,4,32,128]{3,2,1,0:T(8,128)}), f32[8,4,32,128]{3,2,1,0:T(8,128)S(1)}, u32[]{:S(2)}, u32[]{:S(2)}) async-start(f32[8,4,32,128]{3,2,1,0:T(8,128)} %get-tuple-element.31), calls=%async_computation | async-start | bytes 1048576 | tf_op jit(solution)/shard_map/all_to_all | solution.py:412
  18.7 0.7 copy-start.5
  18.7 0.7 copy-start.3
  22.9 11.3 %collective-permute-start.2 = (f32[2,37,128]{2,1,0:T(8,128)}, f32[2,37,128]{2,1,0:T(8,128)S(1)}, u32[]{:S(2)}, u32[]{:S(2)}) collective-permute-start(f32[2,37,128]{2,1,0:T(8,128)} %get-tuple-element.32), channel_id=1, source_target_pairs={{0,1},{1,2},{2,3},{3,4},{4,5},{5,6},{6,7},{7,0},{8,9},{9,10},{10,1... | collective-permute-start | bytes 113672 | tf_op jit(solution)/shard_map/ppermute | solution.py:415
  26.0 15.9 %collective-permute-start.9 = (f32[7,96,128]{2,1,0:T(8,128)S(1)}, f32[7,96,128]{2,1,0:T(8,128)S(1)}, u32[]{:S(2)}, u32[]{:S(2)}) collective-permute-start(f32[7,96,128]{2,1,0:T(8,128)S(1)} %pad_maximum_fusion), channel_id=1, source_target_pairs={{2,4},{3,5},{4,2},{5,3},{10,12},{11,13},{12,10},{13,11},{18,20},{1... | collective-permute-start | bytes 1032200 | tf_op jit(solution)/shard_map/ppermute | solution.py:421
  26.7 7.5 %collective-permute-start.3 = (f32[3,37,128]{2,1,0:T(8,128)}, f32[3,37,128]{2,1,0:T(8,128)S(1)}, u32[]{:S(2)}, u32[]{:S(2)}) collective-permute-start(f32[3,37,128]{2,1,0:T(8,128)} %get-tuple-element.33), channel_id=1, source_target_pairs={{1,0},{2,1},{3,2},{4,3},{5,4},{6,5},{7,6},{0,7},{9,8},{10,9},{11,1... | collective-permute-start | bytes 170504 | tf_op jit(solution)/shard_map/ppermute | solution.py:416
  34.2 2.0 copy-start.13
  34.2 2.0 copy-start.12
  34.2 6.5 %collective-permute-start.10 = (f32[5,37,128]{2,1,0:T(8,128)S(1)}, f32[5,37,128]{2,1,0:T(8,128)S(1)}, u32[]{:S(2)}, u32[]{:S(2)}) collective-permute-start(f32[5,37,128]{2,1,0:T(8,128)S(1)} %pad_maximum_fusion.1), channel_id=1, source_target_pairs={{2,4},{3,5},{4,2},{5,3},{10,12},{11,13},{12,10},{13,11},{18,20},{1... | collective-permute-start | bytes 284168 | tf_op jit(solution)/shard_map/ppermute | solution.py:422
  36.2 26.8 %copy-start.14 = (f32[32,32]{1,0:T(8,128)S(1)}, f32[32,32]{1,0:T(8,128)}, u32[]{:S(2)}) copy-start(f32[32,32]{1,0:T(8,128)} %constant.97.clone) | copy-start | bytes 12292
  62.7 1.1 copy-start.1
  83.6 94.8 %collective-permute-start.6 = (f32[1152,128]{1,0:T(8,128)}, f32[1152,128]{1,0:T(8,128)S(1)}, u32[]{:S(2)}, u32[]{:S(2)}) collective-permute-start(f32[1152,128]{1,0:T(8,128)} %get-tuple-element.36), channel_id=1, source_target_pairs={{0,6},{1,7},{2,2},{3,3},{4,4},{5,5},{6,0},{7,1},{8,14},{9,15},{10,... | collective-permute-start | bytes 1769480 | tf_op jit(solution)/shard_map/ppermute | solution.py:467
  89.3 91.2 %collective-permute-start.7 = (f32[1152,128]{1,0:T(8,128)}, f32[1152,128]{1,0:T(8,128)S(1)}, u32[]{:S(2)}, u32[]{:S(2)}) collective-permute-start(f32[1152,128]{1,0:T(8,128)} %get-tuple-element.37), channel_id=1, source_target_pairs={{0,7},{1,6},{2,3},{3,2},{4,5},{5,4},{6,1},{7,0},{8,15},{9,14},{10,... | collective-permute-start | bytes 1769480 | tf_op jit(solution)/shard_map/ppermute | solution.py:467
  111.1 70.5 %collective-permute-start.4 = (f32[1152,128]{1,0:T(8,128)}, f32[1152,128]{1,0:T(8,128)S(1)}, u32[]{:S(2)}, u32[]{:S(2)}) collective-permute-start(f32[1152,128]{1,0:T(8,128)} %get-tuple-element.34), channel_id=1, source_target_pairs={{0,4},{1,5},{2,0},{3,1},{4,6},{5,7},{6,2},{7,3},{8,12},{9,13},{10,... | collective-permute-start | bytes 1769480 | tf_op jit(solution)/shard_map/ppermute | solution.py:467
  127.7 53.9 %collective-permute-start.5 = (f32[1152,128]{1,0:T(8,128)}, f32[1152,128]{1,0:T(8,128)}, u32[]{:S(2)}, u32[]{:S(2)}) collective-permute-start(f32[1152,128]{1,0:T(8,128)} %get-tuple-element.35), channel_id=1, source_target_pairs={{0,5},{1,4},{2,1},{3,0},{4,7},{5,6},{6,3},{7,2},{8,13},{9,12},{10,... | collective-permute-start | bytes 1769480 | tf_op jit(solution)/shard_map/ppermute | solution.py:467
  127.7 1.1 copy-start
  156.9 23.6 %copy-start.11 = (s32[32,96]{1,0:T(8,128)S(1)}, s32[32,96]{1,0:T(8,128)}, u32[]{:S(2)}) copy-start(s32[32,96]{1,0:T(8,128)} %reshape.22.owner_ref) | copy-start | bytes 36868
  156.9 23.8 %copy-start.15 = (bf16[96,96,1]{1,0,2:T(8,128)(2,1)S(1)}, bf16[96,96,1]{1,0,2:T(8,128)(2,1)}, u32[]{:S(2)}) copy-start(bf16[96,96,1]{1,0,2:T(8,128)(2,1)} %constant.108) | copy-start | bytes 55300
  156.9 24.7 %collective-permute-start.13 = (f32[1152,128]{1,0:T(8,128)}, f32[1152,128]{1,0:T(8,128)S(1)}, u32[]{:S(2)}, u32[]{:S(2)}) collective-permute-start(f32[1152,128]{1,0:T(8,128)} %get-tuple-element.44), channel_id=1, source_target_pairs={{0,1},{1,0},{2,3},{3,2},{4,5},{5,4},{6,7},{7,6},{8,9},{9,8},{10,11... | collective-permute-start | bytes 1769480 | tf_op jit(solution)/shard_map/ppermute | solution.py:467
  178.4 27.3 %copy-start.6 = (f32[1152,128]{1,0:T(8,128)}, f32[1152,128]{1,0:T(8,128)S(1)}, u32[]{:S(2)}) copy-start(f32[1152,128]{1,0:T(8,128)S(1)} %collective-permute-done.6.refs_2_) | copy-start | bytes 1769476
  178.4 16.5 %collective-permute-start.11 = (f32[1152,128]{1,0:T(8,128)}, f32[1152,128]{1,0:T(8,128)S(1)}, u32[]{:S(2)}, u32[]{:S(2)}) collective-permute-start(f32[1152,128]{1,0:T(8,128)} %get-tuple-element.41), channel_id=1, source_target_pairs={{0,2},{1,3},{2,0},{3,1},{4,6},{5,7},{6,4},{7,5},{8,10},{9,11},{10,... | collective-permute-start | bytes 1769480 | tf_op jit(solution)/shard_map/ppermute | solution.py:467
  180.4 25.2 %copy-start.7 = (f32[1152,128]{1,0:T(8,128)}, f32[1152,128]{1,0:T(8,128)S(1)}, u32[]{:S(2)}) copy-start(f32[1152,128]{1,0:T(8,128)S(1)} %collective-permute-done.7.refs_3_) | copy-start | bytes 1769476
  180.5 25.2 %collective-permute-start.12 = (f32[1152,128]{1,0:T(8,128)}, f32[1152,128]{1,0:T(8,128)}, u32[]{:S(2)}, u32[]{:S(2)}) collective-permute-start(f32[1152,128]{1,0:T(8,128)} %get-tuple-element.42), channel_id=1, source_target_pairs={{0,3},{1,2},{2,1},{3,0},{4,7},{5,6},{6,5},{7,4},{8,11},{9,10},{10,... | collective-permute-start | bytes 1769480 | tf_op jit(solution)/shard_map/ppermute | solution.py:467
  181.6 24.0 %copy-start.8 = (f32[1152,128]{1,0:T(8,128)}, f32[1152,128]{1,0:T(8,128)S(1)}, u32[]{:S(2)}) copy-start(f32[1152,128]{1,0:T(8,128)S(1)} %collective-permute-done.4.refs_0_) | copy-start | bytes 1769476
  181.6 24.0 %copy-start.9 = (f32[1152,128]{1,0:T(8,128)}, f32[1152,128]{1,0:T(8,128)S(1)}, u32[]{:S(2)}) copy-start(f32[1152,128]{1,0:T(8,128)S(1)} %collective-permute-done.13.refs_7_) | copy-start | bytes 1769476
  194.9 10.8 %copy-start.10 = (f32[1152,128]{1,0:T(8,128)}, f32[1152,128]{1,0:T(8,128)S(1)}, u32[]{:S(2)}) copy-start(f32[1152,128]{1,0:T(8,128)S(1)} %collective-permute-done.11.refs_4_) | copy-start | bytes 1769476

commit v4 on v3

--- a/solution.py
+++ b/solution.py
@@ -100,8 +100,11 @@
     )(s, owner, columns, lat_shift, fractions)
 
 
-def lat_kernel(s_ref, above_ref, below_ref, top_ref, bottom_ref, wr_ref, wl_ref, out_ref, right_ref, left_ref):
-    rows, cols, _ = s_ref.shape
+def lat_kernel(*refs, pieces):
+    s_refs, refs = refs[:pieces], refs[pieces:]
+    above_ref, below_ref, top_ref, bottom_ref, wr_ref, wl_ref, out_ref, right_ref, left_ref = refs
+    depth, cols, _ = s_refs[0].shape
+    rows = depth * pieces
     band = lax.axis_index("lat")
     at_top = band == 0
     at_bottom = band == lax.axis_size("lat") - 1
@@ -112,7 +115,7 @@
             return jnp.where(at_top, top_ref[1 + e], above_ref[1 + e])
         if e >= UP + rows:
             return jnp.where(at_bottom, bottom_ref[e - UP - rows], below_ref[e - UP - rows])
-        return s_ref[e - UP]
+        return s_refs[(e - UP) // depth][(e - UP) % depth]
 
     acc = jnp.where(at_bottom, bottom_ref[DOWN], below_ref[DOWN])
     for e in range(total - 1, -1, -1):
@@ -132,24 +135,26 @@
         left_ref[RIGHT, pl.ds(e, 1)] = jnp.sum(value * wl_ref[...], axis=0, keepdims=True)
 
 
-def lat_solve(s, above, below, top, bottom):
-    rows, cols, ch = s.shape
+def lat_solve(pieces, above, below, top, bottom):
+    depth, cols, ch = pieces[0].shape
+    rows = depth * len(pieces)
     total = rows + UP + DOWN
     place = np.arange(cols)
     wr = np.where(place < cols - LEFT, POLE ** np.maximum(cols - LEFT - 1 - place, 0), 0.0)
     wl = np.where(place >= RIGHT, POLE ** np.maximum(place - RIGHT, 0), 0.0)
     wide = lambda w: jnp.asarray(np.broadcast_to(w[:, None], (cols, ch)).astype(np.float32))
+    size = rows * cols * ch
     return pl.pallas_call(
-        lat_kernel,
+        functools.partial(lat_kernel, pieces=len(pieces)),
         out_shape=(
             jax.ShapeDtypeStruct((total, cols, ch), F32),
             jax.ShapeDtypeStruct((LEFT + 1, total, ch), F32),
             jax.ShapeDtypeStruct((RIGHT + 1, total, ch), F32),
         ),
-        cost_estimate=pl.CostEstimate(flops=10 * s.size, bytes_accessed=10 * s.size, transcendentals=0),
+        cost_estimate=pl.CostEstimate(flops=10 * size, bytes_accessed=10 * size, transcendentals=0),
         compiler_params=pltpu.CompilerParams(vmem_limit_bytes=VMEM_LIMIT),
         name="lat_solve",
-    )(s, above, below, top, bottom, wide(wr), wide(wl))
+    )(*pieces, above, below, top, bottom, wide(wr), wide(wl))
 
 
 def lon_kernel(x_ref, west_ref, east_ref, green_ref, out_ref):
@@ -404,14 +409,15 @@
     mine, offset = me // quarter, me % quarter
     middle = (mine == 1) | (mine == 2)
 
-    mirrored = lax.ppermute(tracers, "lon", mirror)
+    upper = lax.ppermute(tracers[: rows // 2], "lon", mirror)
+    lower = lax.ppermute(tracers[rows // 2 :], "lon", mirror)
     owner = owners.reshape(rows, cols)
     down, up, top, bottom, words = edges(tracers, owner, columns, lat_shift, fractions)
     above = lax.ppermute(down, "lat", [(i, i + 1) for i in range(bands - 1)])
     below = lax.ppermute(up, "lat", [(i + 1, i) for i in range(bands - 1)])
     asked = lax.all_to_all(words, "lon", split_axis=0, concat_axis=0, tiled=True)
 
-    x, right, left = lat_solve(tracers, above, below, top, bottom)
+    x, right, left = lat_solve([tracers], above, below, top, bottom)
     west = lax.ppermute(right, "lon", [(i, (i + 1) % sectors) for i in range(sectors)])
     east = lax.ppermute(left, "lon", [((i + 1) % sectors, i) for i in range(sectors)])
     above, below, right = lax.optimization_barrier((above, below, right))
@@ -457,7 +463,7 @@
     tables, done = [own], 0
     for group, pair in calls:
         if group == 2 and len(tables) == 1:
-            other, _, _ = lat_solve(mirrored, rim[: UP + 1], rim[UP + 1 :], rim[: UP + 1], rim[UP + 1 :])
+            other, _, _ = lat_solve([upper, lower], rim[: UP + 1], rim[UP + 1 :], rim[: UP + 1], rim[UP + 1 :])
             tables = [own, lon_solve(other, sides[: LEFT + 1], sides[LEFT + 1 :])]
         values = taps(meta, done, len(pair), base, tables, asked, cols, cap)
         done += 2 * len(pair) + 2

time: 216 us -> 226 us (1.046)
  starting transfers between devices: 47.4 us -> 66.7 us
  waiting for transfers between devices: 47.5 us -> 34.7 us
  local copies, waits for them, and re-layouts: 9 us -> 12.3 us
    ppermute x7, starting transfers between devices: 27.9 us -> 42.5 us  [transport(): value = lax.ppermute(value, 'lon', moves)]
    all_to_all x1, waiting for transfers between devices: 19.4 us -> 5.12 us  [transport(): lax.all_to_all(words, 'lon', split_axis=0, concat_axis=0, tiled=True)]
    ppermute x7, waiting for transfers between devices: 24 us -> 27.2 us  [transport(): value = lax.ppermute(value, 'lon', moves)]
    all_to_all x1, starting transfers between devices: 8.12 us -> 10.8 us  [transport(): lax.all_to_all(words, 'lon', split_axis=0, concat_axis=0, tiled=True)]
  transfers between devices with their start and end apart: 15 -> 16, of which waited for: 4 -> 6; matrix products, arithmetic and copies ran while one was open for 4% -> 5% of each run, Pallas kernels for 45% -> 34%
where the time goes in v4:
time: 226 us; the launch traced here: 225 us
  Pallas kernels  107 us (47%)
  starting transfers between devices  66.7 us (30%)
  waiting for transfers between devices  34.7 us (15%)
  local copies, waits for them, and re-layouts  12.3 us (5%)
  other arithmetic  3.5 us (2%)
    pallas_call x4, Pallas kernels, taps(): pl.pallas_call(functools.partial(tap_kernel, tables=len(tables), count=co...  79.5 us
    ppermute x7, starting transfers between devices, transport(): value = lax.ppermute(value, 'lon', moves)  42.5 us
    ppermute x7, waiting for transfers between devices, transport(): value = lax.ppermute(value, 'lon', moves)  27.2 us
    all_to_all x1, starting transfers between devices, transport(): lax.all_to_all(words, 'lon', split_axis=0, concat_axis=0, tiled=True)  10.8 us
    pallas_call x2, Pallas kernels, lon_solve(): pl.pallas_call(lon_kernel, out_shape=jax.ShapeDtypeStruct((total * ch, 3...  9.01 us
    pallas_call x1, Pallas kernels, place(): pl.pallas_call(functools.partial(place_kernel, cap=cap), out_shape=jax.Sh...  8.81 us
    pallas_call x2, Pallas kernels, lat_solve(): pl.pallas_call(functools.partial(lat_kernel, pieces=len(pieces)), out_sha...  7.03 us
    all_to_all x1, waiting for transfers between devices, transport(): lax.all_to_all(words, 'lon', split_axis=0, concat_axis=0, tiled=True)  5.12 us
  transfers between devices with their start and end apart: 16, of which 6 were waited for; matrix products, arithmetic and copies ran while one was open for 5% of the time, Pallas kernels for 34%

profile of v4, /device:TPU:0, one launch (start us, length us, event | category | flops | bytes accessed | tf_op | source)
XLA Modules:
  0.0 224.9 jit_solution(4204346685375283477)
XLA Ops:
  0.0 0.5 broadcast.42
  0.5 1.4 reduce.4
  1.9 0.7 reshape.22.owner_ref
  2.6 2.8 %edges.1 = (f32[3,96,128]{2,1,0:T(8,128)}, f32[4,96,128]{2,1,0:T(8,128)}, f32[3,96,128]{2,1,0:T(8,128)}, f32[4,96,128]{2,1,0:T(8,128)}, f32[8,4,32,128]{3,2,1,0:T(8,128)}) custom-call(f32[32,96,128]{2,1,0:T(8,128)} %refs_0_.1, s32[32,96]{1,0:T(8,128)} %reshape.22.owner_ref, s32[32,96]{1,0:T(8,128)} %column_ref.1, s32[32,96]{1,0:T(8,128)} %shift_ref.1, ...), custom_call_target="tpu_custom_call" | custom-call | flops 2359296 | bytes 2359296 | tf_op jit(solution)/shard_map/edges/pallas_call | solution.py:94
  5.3 1.3 collective-permute-start.1
  6.6 3.7 %collective-permute-start = (f32[3,96,128]{2,1,0:T(8,128)}, f32[3,96,128]{2,1,0:T(8,128)}, u32[]{:S(2)}, u32[]{:S(2)}) collective-permute-start(f32[3,96,128]{2,1,0:T(8,128)} %get-tuple-element.25), channel_id=1, source_target_pairs={{0,8},{8,16},{16,24},{1,9},{9,17},{17,25},{2,10},{10,18},{18,26},{... | collective-permute-start | bytes 442376 | tf_op jit(solution)/shard_map/ppermute | solution.py:416
  10.3 1.0 fusion.14
  11.3 0.8 collective-permute-start.8
  12.1 0.7 collective-permute-start.9
  12.9 10.8 %all-to-all-start = ((f32[8,4,32,128]{3,2,1,0:T(8,128)}), f32[8,4,32,128]{3,2,1,0:T(8,128)S(1)}, u32[]{:S(2)}, u32[]{:S(2)}) async-start(f32[8,4,32,128]{3,2,1,0:T(8,128)} %get-tuple-element.31), calls=%async_computation | async-start | bytes 1048576 | tf_op jit(solution)/shard_map/all_to_all | solution.py:418
  23.7 0.7 copy-done.3
  24.4 3.5 %lat_solve.2 = (f32[37,96,128]{2,1,0:T(8,128)}, f32[2,37,128]{2,1,0:T(8,128)}, f32[3,37,128]{2,1,0:T(8,128)}) custom-call(f32[32,96,128]{2,1,0:T(8,128)} %refs_0_.1, f32[3,96,128]{2,1,0:T(8,128)} %collective-permute-done.refs_1_, f32[4,96,128]{2,1,0:T(8,128)} %copy-done.3, f32[3,96,128]{2,1,0:T(8,128)} %get-tuple-element.27.refs_3_, ...), custom_call_target="tpu_custom_call" | custom-call | flops 3932160 | bytes 3932160 | tf_op jit(solution)/shard_map/lat_solve/pallas_call | solution.py:147
  27.9 2.0 collective-permute-start.2
  30.0 1.0 broadcast_select_fusion
  30.9 0.8 pad_maximum_fusion
  31.7 1.4 collective-permute-start.10
  33.1 2.7 %collective-permute-start.3 = (f32[3,37,128]{2,1,0:T(8,128)}, f32[3,37,128]{2,1,0:T(8,128)S(1)}, u32[]{:S(2)}, u32[]{:S(2)}) collective-permute-start(f32[3,37,128]{2,1,0:T(8,128)} %get-tuple-element.33), channel_id=1, source_target_pairs={{1,0},{2,1},{3,2},{4,3},{5,4},{6,5},{7,6},{0,7},{9,8},{10,9},{11,1... | collective-permute-start | bytes 170504 | tf_op jit(solution)/shard_map/ppermute | solution.py:422
  35.8 0.7 dynamic-slice_bitcast_fusion
  36.5 1.8 collective-permute-done.2.west_ref
  38.3 0.4 collective-permute-done.3.east_ref
  38.8 0.7 collective-permute-start.11
  39.5 1.2 dynamic-slice_bitcast_fusion.1.meta_ref
  40.7 4.5 %lon_solve.2.refs_0_ = bf16[4736,384]{1,0:T(8,128)(2,1)} custom-call(f32[37,96,128]{2,1,0:T(8,128)} %get-tuple-element.29.x_ref, f32[2,37,128]{2,1,0:T(8,128)} %copy-done.15, f32[3,37,128]{2,1,0:T(8,128)} %copy-done.14, bf16[384,128]{1,0:T(8,128)(2,1)} %constant.107.green_ref), custom_call_target="tpu_custom_call" | custom-call | flops 465567744 | bytes 3637248 | tf_op jit(solution)/shard_map/lon_solve/pallas_call | solution.py:187
  45.2 0.6 slice.34.east_ref
  45.8 0.6 slice.33.west_ref
  46.4 1.6 slice.32.refs_3_.refs_5_
  48.0 1.6 slice.31.refs_2_.refs_4_
  49.6 0.9 copy-done.4
  50.5 0.9 copy-done.5
  51.3 3.5 %lat_solve.3 = (f32[37,96,128]{2,1,0:T(8,128)}, f32[2,37,128]{2,1,0:T(8,128)}, f32[3,37,128]{2,1,0:T(8,128)}) custom-call(f32[16,96,128]{2,1,0:T(8,128)} %copy-done.4, f32[16,96,128]{2,1,0:T(8,128)} %copy-done.5, f32[3,96,128]{2,1,0:T(8,128)} %slice.31.refs_2_.refs_4_, f32[4,96,128]{2,1,0:T(8,128)} %slice.32.refs_3_.refs_5_, ...), custom_call_target="tpu_custom_call" | custom-call | flops 3932160 | bytes 3932160 | tf_op jit(solution)/shard_map/lat_solve/pallas_call | solution.py:147
  54.8 4.5 %lon_solve.3.refs_1_ = bf16[4736,384]{1,0:T(8,128)(2,1)} custom-call(f32[37,96,128]{2,1,0:T(8,128)} %get-tuple-element.40.x_ref, f32[2,37,128]{2,1,0:T(8,128)} %slice.33.west_ref, f32[3,37,128]{2,1,0:T(8,128)} %slice.34.east_ref, bf16[384,128]{1,0:T(8,128)(2,1)} %constant.107.green_ref), custom_call_target="tpu_custom_call" | custom-call | flops 465567744 | bytes 3637248 | tf_op jit(solution)/shard_map/lon_solve/pallas_call | solution.py:187
  59.4 5.1 %all-to-all-done.refs_1_.refs_2_.refs_3_ = f32[8,4,32,128]{3,2,1,0:T(8,128)S(1)} async-done(((f32[8,4,32,128]{3,2,1,0:T(8,128)}), f32[8,4,32,128]{3,2,1,0:T(8,128)S(1)}, u32[]{:S(2)}, u32[]{:S(2)}) %all-to-all-start) | async-done | bytes 524320 | tf_op jit(solution)/shard_map/all_to_all | solution.py:418
  64.5 0.2 convert_reduce_fusion
  64.9 0.6 reshape.24.base_ref
  65.5 19.9 %taps.7 = (f32[1152,128]{1,0:T(8,128)}, f32[1152,128]{1,0:T(8,128)}) custom-call(s32[24]{0:T(128)} %dynamic-slice_bitcast_fusion.1.meta_ref, s32[512]{0:T(512)} %reshape.24.base_ref, bf16[4736,384]{1,0:T(8,128)(2,1)} %lon_solve.2.refs_0_, bf16[4736,384]{1,0:T(8,128)(2,1)} %lon_solve.3.refs_1_, f32[8,4,32,128]{3,2,1,0:T(8,128)} %copy-done.1, ...), custom_call_target="tpu_custom_call" | custom-call | flops 4831838208 | bytes 3637248 | tf_op jit(solution)/shard_map/taps/pallas_call | solution.py:309
  85.4 2.4 %collective-permute-start.14 = (f32[1152,128]{1,0:T(8,128)}, f32[1152,128]{1,0:T(8,128)S(1)}, u32[]{:S(2)}, u32[]{:S(2)}) collective-permute-start(f32[1152,128]{1,0:T(8,128)} %get-tuple-element.44), channel_id=1, source_target_pairs={{0,1},{1,0},{2,3},{3,2},{4,5},{5,4},{6,7},{7,6},{8,9},{9,8},{10,11... | collective-permute-start | bytes 1769480 | tf_op jit(solution)/shard_map/ppermute | solution.py:473
  87.8 19.9 %taps.6 = (f32[1152,128]{1,0:T(8,128)}, f32[1152,128]{1,0:T(8,128)}) custom-call(s32[24]{0:T(128)} %dynamic-slice_bitcast_fusion.1.meta_ref, s32[512]{0:T(512)} %reshape.24.base_ref, bf16[4736,384]{1,0:T(8,128)(2,1)} %lon_solve.2.refs_0_, bf16[4736,384]{1,0:T(8,128)(2,1)} %lon_solve.3.refs_1_, f32[8,4,32,128]{3,2,1,0:T(8,128)} %copy-done.1, ...), custom_call_target="tpu_custom_call" | custom-call | flops 4831838208 | bytes 3637248 | tf_op jit(solution)/shard_map/taps/pallas_call | solution.py:309
  107.8 29.8 %collective-permute-start.12 = (f32[1152,128]{1,0:T(8,128)}, f32[1152,128]{1,0:T(8,128)S(1)}, u32[]{:S(2)}, u32[]{:S(2)}) collective-permute-start(f32[1152,128]{1,0:T(8,128)} %get-tuple-element.41), channel_id=1, source_target_pairs={{0,2},{1,3},{2,0},{3,1},{4,6},{5,7},{6,4},{7,5},{8,10},{9,11},{10,... | collective-permute-start | bytes 1769480 | tf_op jit(solution)/shard_map/ppermute | solution.py:473
  137.6 19.9 %taps.5 = (f32[1152,128]{1,0:T(8,128)}, f32[1152,128]{1,0:T(8,128)}) custom-call(s32[24]{0:T(128)} %dynamic-slice_bitcast_fusion.1.meta_ref, s32[512]{0:T(512)} %reshape.24.base_ref, bf16[4736,384]{1,0:T(8,128)(2,1)} %lon_solve.2.refs_0_, f32[8,4,32,128]{3,2,1,0:T(8,128)} %copy-done.1, f32[8,4,32,128]{3,2,1,0:T(8,128)} %copy-done.1, ...), custom_call_target="tpu_custom_call" | custom-call | flops 4831838208 | bytes 3637248 | tf_op jit(solution)/shard_map/taps/pallas_call | solution.py:309
  157.5 4.8 %collective-permute-start.6 = (f32[1152,128]{1,0:T(8,128)}, f32[1152,128]{1,0:T(8,128)S(1)}, u32[]{:S(2)}, u32[]{:S(2)}) collective-permute-start(f32[1152,128]{1,0:T(8,128)} %get-tuple-element.36), channel_id=1, source_target_pairs={{0,6},{1,7},{2,2},{3,3},{4,4},{5,5},{6,0},{7,1},{8,14},{9,15},{10,... | collective-permute-start | bytes 1769480 | tf_op jit(solution)/shard_map/ppermute | solution.py:473
  162.3 2.0 collective-permute-start.7
  164.3 19.8 %taps.4 = (f32[1152,128]{1,0:T(8,128)}, f32[1152,128]{1,0:T(8,128)}) custom-call(s32[24]{0:T(128)} %dynamic-slice_bitcast_fusion.1.meta_ref, s32[512]{0:T(512)} %reshape.24.base_ref, bf16[4736,384]{1,0:T(8,128)(2,1)} %lon_solve.2.refs_0_, f32[8,4,32,128]{3,2,1,0:T(8,128)} %copy-done.1, f32[8,4,32,128]{3,2,1,0:T(8,128)} %copy-done.1, ...), custom_call_target="tpu_custom_call" | custom-call | flops 4831838208 | bytes 3637248 | tf_op jit(solution)/shard_map/taps/pallas_call | solution.py:309
  184.2 3.4 %collective-permute-start.5 = (f32[1152,128]{1,0:T(8,128)}, f32[1152,128]{1,0:T(8,128)}, u32[]{:S(2)}, u32[]{:S(2)}) collective-permute-start(f32[1152,128]{1,0:T(8,128)} %get-tuple-element.35), channel_id=1, source_target_pairs={{0,5},{1,4},{2,1},{3,0},{4,7},{5,6},{6,3},{7,2},{8,13},{9,12},{10,... | collective-permute-start | bytes 1769480 | tf_op jit(solution)/shard_map/ppermute | solution.py:473
  188.1 0.7 reshape.23.target_ref
  188.8 3.2 %collective-permute-done.7.refs_3_ = f32[1152,128]{1,0:T(8,128)S(1)} collective-permute-done((f32[1152,128]{1,0:T(8,128)}, f32[1152,128]{1,0:T(8,128)S(1)}, u32[]{:S(2)}, u32[]{:S(2)}) %collective-permute-start.7) | collective-permute-done | bytes 589856 | tf_op jit(solution)/shard_map/ppermute | solution.py:473
  192.0 11.6 %collective-permute-done.4.refs_0_ = f32[1152,128]{1,0:T(8,128)S(1)} collective-permute-done((f32[1152,128]{1,0:T(8,128)}, f32[1152,128]{1,0:T(8,128)S(1)}, u32[]{:S(2)}, u32[]{:S(2)}) %collective-permute-start.4) | collective-permute-done | bytes 589856 | tf_op jit(solution)/shard_map/ppermute | solution.py:473
  203.6 12.4 %collective-permute-done.5.refs_1_ = f32[1152,128]{1,0:T(8,128)} collective-permute-done((f32[1152,128]{1,0:T(8,128)}, f32[1152,128]{1,0:T(8,128)}, u32[]{:S(2)}, u32[]{:S(2)}) %collective-permute-start.5) | collective-permute-done | bytes 589856 | tf_op jit(solution)/shard_map/ppermute | solution.py:473
  216.1 8.8 %place.1 = f32[3072,128]{1,0:T(8,128)} custom-call(s32[3072]{0:T(1024)} %reshape.23.target_ref, f32[1152,128]{1,0:T(8,128)} %copy-done.12, f32[1152,128]{1,0:T(8,128)} %collective-permute-done.5.refs_1_, f32[1152,128]{1,0:T(8,128)} %copy-done.10, f32[1152,128]{1,0:T(8,128)} %copy-done.11, f32[1152,128]{1,0:T(8,128)} %copy-done.8, f32[1152,128]{1,0:T(8,128)} %copy-done.9, ...), custom_call_target="tpu_custom_call" | custom-call | bytes 9437184 | tf_op jit(solution)/shard_map/place/pallas_call | solution.py:364
  (53 shorter events, 0.8 us)
Async XLA Ops:
  0.0 10.3 %copy-start = (f32[32,96,128]{2,1,0:T(8,128)S(1)}, f32[32,96,128]{2,1,0:T(8,128)}, u32[]{:S(2)}) copy-start(f32[32,96,128]{2,1,0:T(8,128)} %refs_0_.1) | copy-start | bytes 4718596
  5.3 18.4 %collective-permute-start.1 = (f32[4,96,128]{2,1,0:T(8,128)}, f32[4,96,128]{2,1,0:T(8,128)S(1)}, u32[]{:S(2)}, u32[]{:S(2)}) collective-permute-start(f32[4,96,128]{2,1,0:T(8,128)} %get-tuple-element.26), channel_id=1, source_target_pairs={{8,0},{16,8},{24,16},{9,1},{17,9},{25,17},{10,2},{18,10},{26,18},{... | collective-permute-start | bytes 589832 | tf_op jit(solution)/shard_map/ppermute | solution.py:417
  6.6 17.1 %collective-permute-start = (f32[3,96,128]{2,1,0:T(8,128)}, f32[3,96,128]{2,1,0:T(8,128)}, u32[]{:S(2)}, u32[]{:S(2)}) collective-permute-start(f32[3,96,128]{2,1,0:T(8,128)} %get-tuple-element.25), channel_id=1, source_target_pairs={{0,8},{8,16},{16,24},{1,9},{9,17},{17,25},{2,10},{10,18},{18,26},{... | collective-permute-start | bytes 442376 | tf_op jit(solution)/shard_map/ppermute | solution.py:416
  11.3 18.6 %copy-start.6 = (f32[3,96,128]{2,1,0:T(8,128)S(1)}, f32[3,96,128]{2,1,0:T(8,128)}, u32[]{:S(2)}) copy-start(f32[3,96,128]{2,1,0:T(8,128)} %get-tuple-element.27.refs_3_) | copy-start | bytes 442372
  11.3 38.3 %collective-permute-start.8 = (f32[16,96,128]{2,1,0:T(8,128)}, f32[16,96,128]{2,1,0:T(8,128)S(1)}, u32[]{:S(2)}, u32[]{:S(2)}) collective-permute-start(f32[16,96,128]{2,1,0:T(8,128)} %get-tuple-element.46), channel_id=1, source_target_pairs={{2,4},{3,5},{4,2},{5,3},{10,12},{11,13},{12,10},{13,11},{18,20},{1... | collective-permute-start | bytes 2359304 | tf_op jit(solution)/shard_map/ppermute | solution.py:412
  12.1 37.5 %collective-permute-start.9 = (f32[16,96,128]{2,1,0:T(8,128)S(1)}, f32[16,96,128]{2,1,0:T(8,128)S(1)}, u32[]{:S(2)}, u32[]{:S(2)}) collective-permute-start(f32[16,96,128]{2,1,0:T(8,128)S(1)} %get-tuple-element.45), channel_id=1, source_target_pairs={{2,4},{3,5},{4,2},{5,3},{10,12},{11,13},{12,10},{13,11},{18,20},{1... | collective-permute-start | bytes 2359304 | tf_op jit(solution)/shard_map/ppermute | solution.py:413
  12.8 17.1 %copy-start.2 = (f32[4,96,128]{2,1,0:T(8,128)S(1)}, f32[4,96,128]{2,1,0:T(8,128)}, u32[]{:S(2)}) copy-start(f32[4,96,128]{2,1,0:T(8,128)} %get-tuple-element.28.refs_4_) | copy-start | bytes 589828
  12.9 51.6 %all-to-all-start = ((f32[8,4,32,128]{3,2,1,0:T(8,128)}), f32[8,4,32,128]{3,2,1,0:T(8,128)S(1)}, u32[]{:S(2)}, u32[]{:S(2)}) async-start(f32[8,4,32,128]{3,2,1,0:T(8,128)} %get-tuple-element.31), calls=%async_computation | async-start | bytes 1048576 | tf_op jit(solution)/shard_map/all_to_all | solution.py:418
  23.7 0.7 copy-start.3
  27.9 10.4 %collective-permute-start.2 = (f32[2,37,128]{2,1,0:T(8,128)}, f32[2,37,128]{2,1,0:T(8,128)S(1)}, u32[]{:S(2)}, u32[]{:S(2)}) collective-permute-start(f32[2,37,128]{2,1,0:T(8,128)} %get-tuple-element.32), channel_id=1, source_target_pairs={{0,1},{1,2},{2,3},{3,4},{4,5},{5,6},{6,7},{7,0},{8,9},{9,10},{10,1... | collective-permute-start | bytes 113672 | tf_op jit(solution)/shard_map/ppermute | solution.py:421
  31.7 14.7 %collective-permute-start.10 = (f32[7,96,128]{2,1,0:T(8,128)}, f32[7,96,128]{2,1,0:T(8,128)}, u32[]{:S(2)}, u32[]{:S(2)}) collective-permute-start(f32[7,96,128]{2,1,0:T(8,128)} %pad_maximum_fusion), channel_id=1, source_target_pairs={{2,4},{3,5},{4,2},{5,3},{10,12},{11,13},{12,10},{13,11},{18,20},{1... | collective-permute-start | bytes 1032200 | tf_op jit(solution)/shard_map/ppermute | solution.py:427
  33.1 5.7 %collective-permute-start.3 = (f32[3,37,128]{2,1,0:T(8,128)}, f32[3,37,128]{2,1,0:T(8,128)S(1)}, u32[]{:S(2)}, u32[]{:S(2)}) collective-permute-start(f32[3,37,128]{2,1,0:T(8,128)} %get-tuple-element.33), channel_id=1, source_target_pairs={{1,0},{2,1},{3,2},{4,3},{5,4},{6,5},{7,6},{0,7},{9,8},{10,9},{11,1... | collective-permute-start | bytes 170504 | tf_op jit(solution)/shard_map/ppermute | solution.py:422
  38.3 2.3 %copy-start.15 = (f32[2,37,128]{2,1,0:T(8,128)}, f32[2,37,128]{2,1,0:T(8,128)S(1)}, u32[]{:S(2)}) copy-start(f32[2,37,128]{2,1,0:T(8,128)S(1)} %collective-permute-done.2.west_ref) | copy-start | bytes 113668
  38.8 1.9 copy-start.14
  38.8 6.4 %collective-permute-start.11 = (f32[5,37,128]{2,1,0:T(8,128)S(1)}, f32[5,37,128]{2,1,0:T(8,128)S(1)}, u32[]{:S(2)}, u32[]{:S(2)}) collective-permute-start(f32[5,37,128]{2,1,0:T(8,128)S(1)} %pad_maximum_fusion.1), channel_id=1, source_target_pairs={{2,4},{3,5},{4,2},{5,3},{10,12},{11,13},{12,10},{13,11},{18,20},{1... | collective-permute-start | bytes 284168 | tf_op jit(solution)/shard_map/ppermute | solution.py:428
  49.6 0.9 copy-start.4
  50.5 0.9 copy-start.5
  54.8 9.9 %copy-start.16 = (f32[32,32]{1,0:T(8,128)S(1)}, f32[32,32]{1,0:T(8,128)}, u32[]{:S(2)}) copy-start(f32[32,32]{1,0:T(8,128)} %constant.97.clone) | copy-start | bytes 12292
  64.5 1.0 copy-start.1
  85.4 98.7 %collective-permute-start.14 = (f32[1152,128]{1,0:T(8,128)}, f32[1152,128]{1,0:T(8,128)S(1)}, u32[]{:S(2)}, u32[]{:S(2)}) collective-permute-start(f32[1152,128]{1,0:T(8,128)} %get-tuple-element.44), channel_id=1, source_target_pairs={{0,1},{1,0},{2,3},{3,2},{4,5},{5,4},{6,7},{7,6},{8,9},{9,8},{10,11... | collective-permute-start | bytes 1769480 | tf_op jit(solution)/shard_map/ppermute | solution.py:473
  107.8 76.4 %collective-permute-start.12 = (f32[1152,128]{1,0:T(8,128)}, f32[1152,128]{1,0:T(8,128)S(1)}, u32[]{:S(2)}, u32[]{:S(2)}) collective-permute-start(f32[1152,128]{1,0:T(8,128)} %get-tuple-element.41), channel_id=1, source_target_pairs={{0,2},{1,3},{2,0},{3,1},{4,6},{5,7},{6,4},{7,5},{8,10},{9,11},{10,... | collective-permute-start | bytes 1769480 | tf_op jit(solution)/shard_map/ppermute | solution.py:473
  137.6 51.2 %collective-permute-start.13 = (f32[1152,128]{1,0:T(8,128)}, f32[1152,128]{1,0:T(8,128)S(1)}, u32[]{:S(2)}, u32[]{:S(2)}) collective-permute-start(f32[1152,128]{1,0:T(8,128)} %get-tuple-element.42), channel_id=1, source_target_pairs={{0,3},{1,2},{2,1},{3,0},{4,7},{5,6},{6,5},{7,4},{8,11},{9,10},{10,... | collective-permute-start | bytes 1769480 | tf_op jit(solution)/shard_map/ppermute | solution.py:473
  157.5 31.3 %collective-permute-start.6 = (f32[1152,128]{1,0:T(8,128)}, f32[1152,128]{1,0:T(8,128)S(1)}, u32[]{:S(2)}, u32[]{:S(2)}) collective-permute-start(f32[1152,128]{1,0:T(8,128)} %get-tuple-element.36), channel_id=1, source_target_pairs={{0,6},{1,7},{2,2},{3,3},{4,4},{5,5},{6,0},{7,1},{8,14},{9,15},{10,... | collective-permute-start | bytes 1769480 | tf_op jit(solution)/shard_map/ppermute | solution.py:473
  162.3 25.3 %copy-start.13 = (s32[32,96]{1,0:T(8,128)S(1)}, s32[32,96]{1,0:T(8,128)}, u32[]{:S(2)}) copy-start(s32[32,96]{1,0:T(8,128)} %reshape.22.owner_ref) | copy-start | bytes 36868
  162.3 25.6 %copy-start.17 = (bf16[96,96,1]{1,0,2:T(8,128)(2,1)S(1)}, bf16[96,96,1]{1,0,2:T(8,128)(2,1)}, u32[]{:S(2)}) copy-start(bf16[96,96,1]{1,0,2:T(8,128)(2,1)} %constant.108) | copy-start | bytes 55300
  162.3 29.7 %collective-permute-start.7 = (f32[1152,128]{1,0:T(8,128)}, f32[1152,128]{1,0:T(8,128)S(1)}, u32[]{:S(2)}, u32[]{:S(2)}) collective-permute-start(f32[1152,128]{1,0:T(8,128)} %get-tuple-element.37), channel_id=1, source_target_pairs={{0,7},{1,6},{2,3},{3,2},{4,5},{5,4},{6,1},{7,0},{8,15},{9,14},{10,... | collective-permute-start | bytes 1769480 | tf_op jit(solution)/shard_map/ppermute | solution.py:473
  184.1 31.9 %copy-start.7 = (f32[1152,128]{1,0:T(8,128)}, f32[1152,128]{1,0:T(8,128)S(1)}, u32[]{:S(2)}) copy-start(f32[1152,128]{1,0:T(8,128)S(1)} %collective-permute-done.14.refs_7_) | copy-start | bytes 1769476
  184.1 19.5 %collective-permute-start.4 = (f32[1152,128]{1,0:T(8,128)}, f32[1152,128]{1,0:T(8,128)S(1)}, u32[]{:S(2)}, u32[]{:S(2)}) collective-permute-start(f32[1152,128]{1,0:T(8,128)} %get-tuple-element.34), channel_id=1, source_target_pairs={{0,4},{1,5},{2,0},{3,1},{4,6},{5,7},{6,2},{7,3},{8,12},{9,13},{10,... | collective-permute-start | bytes 1769480 | tf_op jit(solution)/shard_map/ppermute | solution.py:473
  184.2 31.8 %copy-start.8 = (f32[1152,128]{1,0:T(8,128)}, f32[1152,128]{1,0:T(8,128)S(1)}, u32[]{:S(2)}) copy-start(f32[1152,128]{1,0:T(8,128)S(1)} %collective-permute-done.12.refs_4_) | copy-start | bytes 1769476
  184.2 31.8 %collective-permute-start.5 = (f32[1152,128]{1,0:T(8,128)}, f32[1152,128]{1,0:T(8,128)}, u32[]{:S(2)}, u32[]{:S(2)}) collective-permute-start(f32[1152,128]{1,0:T(8,128)} %get-tuple-element.35), channel_id=1, source_target_pairs={{0,5},{1,4},{2,1},{3,0},{4,7},{5,6},{6,3},{7,2},{8,13},{9,12},{10,... | collective-permute-start | bytes 1769480 | tf_op jit(solution)/shard_map/ppermute | solution.py:473
  188.8 27.3 %copy-start.9 = (f32[1152,128]{1,0:T(8,128)}, f32[1152,128]{1,0:T(8,128)S(1)}, u32[]{:S(2)}) copy-start(f32[1152,128]{1,0:T(8,128)S(1)} %collective-permute-done.13.refs_5_) | copy-start | bytes 1769476
  188.8 27.3 %copy-start.10 = (f32[1152,128]{1,0:T(8,128)}, f32[1152,128]{1,0:T(8,128)S(1)}, u32[]{:S(2)}) copy-start(f32[1152,128]{1,0:T(8,128)S(1)} %collective-permute-done.6.refs_2_) | copy-start | bytes 1769476
  192.0 24.0 %copy-start.11 = (f32[1152,128]{1,0:T(8,128)}, f32[1152,128]{1,0:T(8,128)S(1)}, u32[]{:S(2)}) copy-start(f32[1152,128]{1,0:T(8,128)S(1)} %collective-permute-done.7.refs_3_) | copy-start | bytes 1769476
  203.6 12.4 %copy-start.12 = (f32[1152,128]{1,0:T(8,128)}, f32[1152,128]{1,0:T(8,128)S(1)}, u32[]{:S(2)}) copy-start(f32[1152,128]{1,0:T(8,128)S(1)} %collective-permute-done.4.refs_0_) | copy-start | bytes 1769476

commit v5 on v4

--- a/solution.py
+++ b/solution.py
@@ -100,29 +100,53 @@
     )(s, owner, columns, lat_shift, fractions)
 
 
-def lat_kernel(*refs, pieces):
+def lat_kernel(*refs, pieces, head):
     s_refs, refs = refs[:pieces], refs[pieces:]
-    above_ref, below_ref, top_ref, bottom_ref, wr_ref, wl_ref, out_ref, right_ref, left_ref = refs
-    depth, cols, _ = s_refs[0].shape
-    rows = depth * pieces
+    if pieces == 1:
+        above_ref, below_ref, top_ref, bottom_ref, wr_ref, wl_ref, out_ref, right_ref, left_ref, rest_ref = refs
+        rows, cols, _ = s_refs[0].shape
+    else:
+        wr_ref, wl_ref, out_ref, right_ref, left_ref = refs
+        cols = s_refs[0].shape[1]
+        rows = out_ref.shape[0] - UP - DOWN
     band = lax.axis_index("lat")
     at_top = band == 0
     at_bottom = band == lax.axis_size("lat") - 1
     total = rows + UP + DOWN
 
+    def over(k):
+        if pieces == 1:
+            return jnp.where(at_top, top_ref[k], above_ref[k])
+        return s_refs[1][rows - head + k]
+
+    def under(k):
+        if pieces == 1:
+            return jnp.where(at_bottom, bottom_ref[k], below_ref[k])
+        return s_refs[1][rows - head + UP + 1 + k]
+
     def row(e):
         if e < UP:
-            return jnp.where(at_top, top_ref[1 + e], above_ref[1 + e])
+            return over(1 + e)
         if e >= UP + rows:
-            return jnp.where(at_bottom, bottom_ref[e - UP - rows], below_ref[e - UP - rows])
-        return s_refs[(e - UP) // depth][(e - UP) % depth]
-
-    acc = jnp.where(at_bottom, bottom_ref[DOWN], below_ref[DOWN])
+            return under(e - UP - rows)
+        if pieces == 1 or e - UP < head:
+            return s_refs[0][e - UP]
+        return s_refs[1][e - UP - head]
+
+    if pieces == 1:
+        for r in range(head, rows):
+            rest_ref[r - head] = s_refs[0][r]
+        for k in range(UP + 1):
+            rest_ref[rows - head + k] = over(k)
+        for k in range(DOWN + 1):
+            rest_ref[rows - head + UP + 1 + k] = under(k)
+
+    acc = under(DOWN)
     for e in range(total - 1, -1, -1):
         acc = POLE * acc
         out_ref[e] = acc
         acc = acc + row(e)
-    acc = jnp.where(at_top, top_ref[0], above_ref[0])
+    acc = over(0)
     for e in range(total):
         acc = row(e) + POLE * acc
         value = GAIN * (out_ref[e] + acc)
@@ -135,42 +159,53 @@
         left_ref[RIGHT, pl.ds(e, 1)] = jnp.sum(value * wl_ref[...], axis=0, keepdims=True)
 
 
-def lat_solve(pieces, above, below, top, bottom):
-    depth, cols, ch = pieces[0].shape
-    rows = depth * len(pieces)
+def lat_solve(rows, head, pieces, halos=()):
+    _, cols, ch = pieces[0].shape
     total = rows + UP + DOWN
     place = np.arange(cols)
     wr = np.where(place < cols - LEFT, POLE ** np.maximum(cols - LEFT - 1 - place, 0), 0.0)
     wl = np.where(place >= RIGHT, POLE ** np.maximum(place - RIGHT, 0), 0.0)
     wide = lambda w: jnp.asarray(np.broadcast_to(w[:, None], (cols, ch)).astype(np.float32))
     size = rows * cols * ch
+    shapes = [
+        jax.ShapeDtypeStruct((total, cols, ch), F32),
+        jax.ShapeDtypeStruct((LEFT + 1, total, ch), F32),
+        jax.ShapeDtypeStruct((RIGHT + 1, total, ch), F32),
+    ]
+    if halos:
+        shapes.append(jax.ShapeDtypeStruct((rows - head + UP + DOWN + 2, cols, ch), F32))
     return pl.pallas_call(
-        functools.partial(lat_kernel, pieces=len(pieces)),
-        out_shape=(
-            jax.ShapeDtypeStruct((total, cols, ch), F32),
-            jax.ShapeDtypeStruct((LEFT + 1, total, ch), F32),
-            jax.ShapeDtypeStruct((RIGHT + 1, total, ch), F32),
-        ),
+        functools.partial(lat_kernel, pieces=len(pieces), head=head),
+        out_shape=shapes,
         cost_estimate=pl.CostEstimate(flops=10 * size, bytes_accessed=10 * size, transcendentals=0),
         compiler_params=pltpu.CompilerParams(vmem_limit_bytes=VMEM_LIMIT),
         name="lat_solve",
-    )(*pieces, above, below, top, bottom, wide(wr), wide(wl))
-
-
-def lon_kernel(x_ref, west_ref, east_ref, green_ref, out_ref):
+    )(*pieces, *halos, wide(wr), wide(wl))
+
+
+def lon_kernel(x_ref, *refs, packed):
+    if packed:
+        sides_ref, green_ref, out_ref = refs
+    else:
+        west_ref, east_ref, green_ref, out_ref, sides_ref = refs
+        sides_ref[: LEFT + 1] = west_ref[...]
+        sides_ref[LEFT + 1 :] = east_ref[...]
     total, cols, ch = x_ref.shape
     pad = LANES - cols - (LEFT + RIGHT + 2)
     for e in range(total):
         parts = [x_ref[e]]
-        parts += [west_ref[k, pl.ds(e, 1)] for k in range(LEFT + 1)]
-        parts += [east_ref[k, pl.ds(e, 1)] for k in range(RIGHT + 1)]
+        if packed:
+            parts += [sides_ref[k, pl.ds(e, 1)] for k in range(LEFT + RIGHT + 2)]
+        else:
+            parts += [west_ref[k, pl.ds(e, 1)] for k in range(LEFT + 1)]
+            parts += [east_ref[k, pl.ds(e, 1)] for k in range(RIGHT + 1)]
         parts += [jnp.zeros((pad, ch), F32)]
         turned = jnp.concatenate(parts, axis=0).T
         value = dot(thirds(turned), green_ref[...])
         out_ref[e * ch : (e + 1) * ch] = thirds(value)
 
 
-def lon_solve(x, west, east):
+def lon_solve(x, *sides):
     total, cols, ch = x.shape
     width = cols + LEFT + RIGHT
     j = np.arange(width) - LEFT
@@ -184,20 +219,24 @@
     green[cols + LEFT + 1 + RIGHT, :width] = POLE ** (cols + RIGHT - j)
     green = jnp.asarray((GAIN * green).astype(np.float32))
     high, low = split(green)
+    packed = len(sides) == 1
+    shapes = [jax.ShapeDtypeStruct((total * ch, 3 * LANES), BF)]
+    if not packed:
+        shapes.append(jax.ShapeDtypeStruct((LEFT + RIGHT + 2, total, ch), F32))
     return pl.pallas_call(
-        lon_kernel,
-        out_shape=jax.ShapeDtypeStruct((total * ch, 3 * LANES), BF),
+        functools.partial(lon_kernel, packed=packed),
+        out_shape=shapes,
         cost_estimate=pl.CostEstimate(
             flops=6 * total * LANES * LANES * ch, bytes_accessed=8 * x.size, transcendentals=0
         ),
         compiler_params=pltpu.CompilerParams(vmem_limit_bytes=VMEM_LIMIT),
         name="lon_solve",
-    )(x, west, east, jnp.concatenate([high, high, low], axis=0))
+    )(x, *sides, jnp.concatenate([high, high, low], axis=0))
 
 
 def tap_kernel(meta_ref, base_ref, *refs, tables, count, cols, cap, span, at):
     meta = lambda k: meta_ref[at + k]
-    table_refs, refs = refs[:tables], refs[tables:]
+    table_refs, refs = refs[:tables], refs[tables + 1 :]
     cells_refs, tri_ref = refs[:count], refs[count]
     out_refs = refs[count + 1 : 2 * count + 1]
     rank, place, lon_w, lat_w, near, later, packed, ct_ref, sems, table_sem = refs[2 * count + 1 :]
@@ -300,7 +339,7 @@
         copy.wait()
 
 
-def taps(meta, at, count, base, tables, cells, cols, cap):
+def taps(meta, at, count, base, tables, cells, cols, cap, after):
     _, words, rows, lanes = cells.shape
     ch = tables[0].shape[0] // (rows + UP + DOWN)
     span = 112
@@ -312,7 +351,7 @@
         grid_spec=pltpu.PrefetchScalarGridSpec(
             num_scalar_prefetch=2,
             grid=(1,),
-            in_specs=[pl.BlockSpec(memory_space=pl.ANY)] * len(tables)
+            in_specs=[pl.BlockSpec(memory_space=pl.ANY)] * (len(tables) + 1)
             + [
                 pl.BlockSpec((1, words, rows, lanes), functools.partial(lambda g, m, b, k: (m[k], 0, 0, 0), k=at + k))
                 for k in range(count)
@@ -337,7 +376,7 @@
         ),
         compiler_params=pltpu.CompilerParams(vmem_limit_bytes=VMEM_LIMIT),
         name="taps",
-    )(meta, base, *tables, *([cells] * count), tri)
+    )(meta, base, *tables, after, *([cells] * count), tri)
 
 
 def place_kernel(target_ref, *refs, cap):
@@ -399,7 +438,6 @@
     rows, cols, ch = tracers.shape
     bands = lax.axis_size("lat")
     sectors = lax.axis_size("lon")
-    band = lax.axis_index("lat")
     me = lax.axis_index("lon")
     cells = rows * cols
     cap = 3 * cells // sectors
@@ -409,30 +447,25 @@
     mine, offset = me // quarter, me % quarter
     middle = (mine == 1) | (mine == 2)
 
-    upper = lax.ppermute(tracers[: rows // 2], "lon", mirror)
-    lower = lax.ppermute(tracers[rows // 2 :], "lon", mirror)
+    head = rows // 4
+    first = lax.ppermute(tracers[:head], "lon", mirror)
     owner = owners.reshape(rows, cols)
     down, up, top, bottom, words = edges(tracers, owner, columns, lat_shift, fractions)
     above = lax.ppermute(down, "lat", [(i, i + 1) for i in range(bands - 1)])
     below = lax.ppermute(up, "lat", [(i + 1, i) for i in range(bands - 1)])
     asked = lax.all_to_all(words, "lon", split_axis=0, concat_axis=0, tiled=True)
 
-    x, right, left = lat_solve([tracers], above, below, top, bottom)
+    x, right, left, rest = lat_solve(rows, head, [tracers], (above, below, top, bottom))
     west = lax.ppermute(right, "lon", [(i, (i + 1) % sectors) for i in range(sectors)])
     east = lax.ppermute(left, "lon", [((i + 1) % sectors, i) for i in range(sectors)])
-    above, below, right = lax.optimization_barrier((above, below, right))
-    rim = jnp.concatenate(
-        [jnp.where(band == 0, top, above), jnp.where(band == bands - 1, bottom, below)], axis=0
-    )
-    rim = lax.ppermute(rim, "lon", mirror)
-    sides = lax.ppermute(jnp.concatenate([west, east], axis=0), "lon", mirror)
-
     origins = np.array([[s * cols, dict(mirror).get(s, s) * cols] for s in range(sectors)], np.float32)
     local = asked[None, :, 0] - jnp.asarray(origins)[me][:, None, None, None]
     inside = ((local >= 0.0) & (local < float(cols))).astype(F32).reshape(2 * sectors, rows, -1)
     base = bases(inside).astype(jnp.int32).reshape(-1)
 
-    own = lon_solve(x, west, east)
+    own, sides = lon_solve(x, west, east)
+    rest = lax.ppermute(rest, "lon", mirror)
+    sides = lax.ppermute(sides, "lon", mirror)
     late_owner, x = lax.optimization_barrier((owner, x))
     every = jnp.arange(sectors, dtype=jnp.int32)
     mask = late_owner[None] == every[:, None, None]
@@ -460,12 +493,12 @@
     meta = jnp.asarray(np.array(plan, np.int32))[me]
 
     parts = [None] * sectors
-    tables, done = [own], 0
+    tables, done, values = [own], 0, [own]
     for group, pair in calls:
         if group == 2 and len(tables) == 1:
-            other, _, _ = lat_solve([upper, lower], rim[: UP + 1], rim[UP + 1 :], rim[: UP + 1], rim[UP + 1 :])
-            tables = [own, lon_solve(other, sides[: LEFT + 1], sides[LEFT + 1 :])]
-        values = taps(meta, done, len(pair), base, tables, asked, cols, cap)
+            other = lat_solve(rows, head, [first, rest])[0]
+            tables = [own, lon_solve(other, sides)[0]]
+        values = taps(meta, done, len(pair), base, tables, asked, cols, cap, values[0])
         done += 2 * len(pair) + 2
         for a, value in zip(pair, values):
             moves = [(at(k, o), at(goals[group][k], (o + a) % quarter)) for k in range(4) for o in range(quarter)]

time: 226 us -> 196 us (0.87)
  waiting for transfers between devices: 34.7 us -> 14.7 us
  starting transfers between devices: 66.7 us -> 62 us
  local copies, waits for them, and re-layouts: 12.3 us -> 8.49 us
    ppermute x7, waiting for transfers between devices: 27.2 us -> 11.8 us  [transport(): value = lax.ppermute(value, 'lon', moves)]
    all_to_all x1, waiting for transfers between devices: 5.12 us -> 0.01 us  [transport(): lax.all_to_all(words, 'lon', split_axis=0, concat_axis=0, tiled=True)]
    slice x5 -> x1, local copies, waits for them, and re-layouts: 5.41 us -> 1.02 us  [transport(): first = lax.ppermute(tracers[:head], 'lon', mirror)]
    all_to_all x1, starting transfers between devices: 10.8 us -> 7.28 us  [transport(): lax.all_to_all(words, 'lon', split_axis=0, concat_axis=0, tiled=True)]
  transfers between devices with their start and end apart: 16 -> 15, of which waited for: 6 -> 4; matrix products, arithmetic and copies ran while one was open for 5% -> 3% of each run, Pallas kernels for 34% -> 49%
where the time goes in v5:
time: 196 us; the launch traced here: 195 us
  Pallas kernels  107 us (55%)
  starting transfers between devices  62 us (32%)
  waiting for transfers between devices  14.7 us (8%)
  local copies, waits for them, and re-layouts  8.49 us (4%)
    pallas_call x4, Pallas kernels, taps(): pl.pallas_call(functools.partial(tap_kernel, tables=len(tables), count=co...  79.4 us
    ppermute x7, starting transfers between devices, transport(): value = lax.ppermute(value, 'lon', moves)  42.9 us
    ppermute x7, waiting for transfers between devices, transport(): value = lax.ppermute(value, 'lon', moves)  11.8 us
    pallas_call x2, Pallas kernels, lon_solve(): pl.pallas_call(functools.partial(lon_kernel, packed=packed), out_shape=sh...  9.06 us
    pallas_call x1, Pallas kernels, place(): pl.pallas_call(functools.partial(place_kernel, cap=cap), out_shape=jax.Sh...  8.81 us
    pallas_call x2, Pallas kernels, lat_solve(): pl.pallas_call(functools.partial(lat_kernel, pieces=len(pieces), head=hea...  7.42 us
    all_to_all x1, starting transfers between devices, transport(): lax.all_to_all(words, 'lon', split_axis=0, concat_axis=0, tiled=True)  7.28 us
  transfers between devices with their start and end apart: 15, of which 4 were waited for; matrix products, arithmetic and copies ran while one was open for 3% of the time, Pallas kernels for 49%

profile of v5, /device:TPU:0, one launch (start us, length us, event | category | flops | bytes accessed | tf_op | source)
XLA Modules:
  0.0 195.0 jit_solution(10619066708532651607)
XLA Ops:
  0.0 0.5 broadcast.42
  0.5 1.4 reduce.4
  1.9 0.7 reshape.22.owner_ref
  2.6 2.7 %edges.1 = (f32[3,96,128]{2,1,0:T(8,128)}, f32[4,96,128]{2,1,0:T(8,128)}, f32[3,96,128]{2,1,0:T(8,128)}, f32[4,96,128]{2,1,0:T(8,128)}, f32[8,4,32,128]{3,2,1,0:T(8,128)}) custom-call(f32[32,96,128]{2,1,0:T(8,128)} %refs_0_.1, s32[32,96]{1,0:T(8,128)} %reshape.22.owner_ref, s32[32,96]{1,0:T(8,128)} %column_ref.1, s32[32,96]{1,0:T(8,128)} %shift_ref.1, ...), custom_call_target="tpu_custom_call" | custom-call | flops 2359296 | bytes 2359296 | tf_op jit(solution)/shard_map/edges/pallas_call | solution.py:94
  5.3 7.3 %all-to-all-start = ((f32[8,4,32,128]{3,2,1,0:T(8,128)}), f32[8,4,32,128]{3,2,1,0:T(8,128)S(1)}, u32[]{:S(2)}, u32[]{:S(2)}) async-start(f32[8,4,32,128]{3,2,1,0:T(8,128)} %get-tuple-element.32), calls=%async_computation | async-start | bytes 1048576 | tf_op jit(solution)/shard_map/all_to_all | solution.py:456
  12.6 1.3 collective-permute-start.1
  13.9 3.0 %collective-permute-start = (f32[3,96,128]{2,1,0:T(8,128)}, f32[3,96,128]{2,1,0:T(8,128)S(1)}, u32[]{:S(2)}, u32[]{:S(2)}) collective-permute-start(f32[3,96,128]{2,1,0:T(8,128)} %get-tuple-element.26), channel_id=1, source_target_pairs={{0,8},{8,16},{16,24},{1,9},{9,17},{17,25},{2,10},{10,18},{18,26},{... | collective-permute-start | bytes 442376 | tf_op jit(solution)/shard_map/ppermute | solution.py:454
  16.9 1.0 slice.7
  17.9 0.7 collective-permute-start.8
  18.6 1.3 dynamic-slice_bitcast_fusion.1.meta_ref
  19.9 0.6 copy-done.10
  20.6 0.1 copy-done.9
  20.7 4.0 %lat_solve.2 = (f32[37,96,128]{2,1,0:T(8,128)}, f32[2,37,128]{2,1,0:T(8,128)}, f32[3,37,128]{2,1,0:T(8,128)}, f32[31,96,128]{2,1,0:T(8,128)}) custom-call(f32[32,96,128]{2,1,0:T(8,128)} %refs_0_.1, f32[3,96,128]{2,1,0:T(8,128)} %copy-done.10, f32[4,96,128]{2,1,0:T(8,128)} %copy-done.9, f32[3,96,128]{2,1,0:T(8,128)} %get-tuple-element.28.refs_3_, ...), custom_call_target="tpu_custom_call" | custom-call | flops 3932160 | bytes 3932160 | tf_op jit(solution)/shard_map/lat_solve/pallas_call | solution.py:177
  24.7 2.0 %collective-permute-start.2 = (f32[2,37,128]{2,1,0:T(8,128)}, f32[2,37,128]{2,1,0:T(8,128)S(1)}, u32[]{:S(2)}, u32[]{:S(2)}) collective-permute-start(f32[2,37,128]{2,1,0:T(8,128)} %get-tuple-element.33), channel_id=1, source_target_pairs={{0,1},{1,2},{2,3},{3,4},{4,5},{5,6},{6,7},{7,0},{8,9},{9,10},{10,1... | collective-permute-start | bytes 113672 | tf_op jit(solution)/shard_map/ppermute | solution.py:459
  26.7 2.8 %collective-permute-start.3 = (f32[3,37,128]{2,1,0:T(8,128)}, f32[3,37,128]{2,1,0:T(8,128)S(1)}, u32[]{:S(2)}, u32[]{:S(2)}) collective-permute-start(f32[3,37,128]{2,1,0:T(8,128)} %get-tuple-element.34), channel_id=1, source_target_pairs={{1,0},{2,1},{3,2},{4,3},{5,4},{6,5},{7,6},{0,7},{9,8},{10,9},{11,1... | collective-permute-start | bytes 170504 | tf_op jit(solution)/shard_map/ppermute | solution.py:460
  29.5 0.7 dynamic-slice_bitcast_fusion
  30.2 0.7 collective-permute-start.9
  30.9 0.8 collective-permute-done.2.refs_0_
  31.7 2.1 %collective-permute-done.3.refs_1_ = f32[3,37,128]{2,1,0:T(8,128)S(1)} collective-permute-done((f32[3,37,128]{2,1,0:T(8,128)}, f32[3,37,128]{2,1,0:T(8,128)S(1)}, u32[]{:S(2)}, u32[]{:S(2)}) %collective-permute-start.3) | collective-permute-done | bytes 56864 | tf_op jit(solution)/shard_map/ppermute | solution.py:460
  33.8 0.6 copy-done.12
  34.4 4.5 %lon_solve.2 = (bf16[4736,384]{1,0:T(8,128)(2,1)}, f32[5,37,128]{2,1,0:T(8,128)}) custom-call(f32[37,96,128]{2,1,0:T(8,128)} %get-tuple-element.30.x_ref, f32[2,37,128]{2,1,0:T(8,128)} %copy-done.13, f32[3,37,128]{2,1,0:T(8,128)} %copy-done.12, bf16[384,128]{1,0:T(8,128)(2,1)} %constant.103.refs_2_.refs_1_), custom_call_target="tpu_custom_call" | custom-call | flops 465567744 | bytes 3637248 | tf_op jit(solution)/shard_map/lon_solve/pallas_call | solution.py:226
  38.9 1.3 collective-permute-start.10
  40.2 0.2 convert_reduce_fusion
  40.5 0.1 convolution_convert_fusion
  40.6 0.7 reshape.24.base_ref
  41.3 19.8 %taps.4 = (f32[1152,128]{1,0:T(8,128)}, f32[1152,128]{1,0:T(8,128)}) custom-call(s32[24]{0:T(128)} %dynamic-slice_bitcast_fusion.1.meta_ref, s32[512]{0:T(512)} %reshape.24.base_ref, bf16[4736,384]{1,0:T(8,128)(2,1)} %get-tuple-element.35.refs_0_.refs_1_, bf16[4736,384]{1,0:T(8,128)(2,1)} %get-tuple-element.35.refs_0_.refs_1_, f32[8,4,32,128]{3,2,1,0:T(8,128)} %copy-done.1, ...), custom_call_target="tpu_custom_call" | custom-call | flops 4831838208 | bytes 3637248 | tf_op jit(solution)/shard_map/taps/pallas_call | solution.py:348
  61.1 5.3 %collective-permute-start.4 = (f32[1152,128]{1,0:T(8,128)}, f32[1152,128]{1,0:T(8,128)S(1)}, u32[]{:S(2)}, u32[]{:S(2)}) collective-permute-start(f32[1152,128]{1,0:T(8,128)} %get-tuple-element.36), channel_id=1, source_target_pairs={{0,4},{1,5},{2,0},{3,1},{4,6},{5,7},{6,2},{7,3},{8,12},{9,13},{10,... | collective-permute-start | bytes 1769480 | tf_op jit(solution)/shard_map/ppermute | solution.py:506
  66.4 1.4 collective-permute-start.5
  67.8 19.8 %taps.5 = (f32[1152,128]{1,0:T(8,128)}, f32[1152,128]{1,0:T(8,128)}) custom-call(s32[24]{0:T(128)} %dynamic-slice_bitcast_fusion.1.meta_ref, s32[512]{0:T(512)} %reshape.24.base_ref, bf16[4736,384]{1,0:T(8,128)(2,1)} %get-tuple-element.35.refs_0_.refs_1_, f32[1152,128]{1,0:T(8,128)} %get-tuple-element.37.refs_1_, f32[8,4,32,128]{3,2,1,0:T(8,128)} %copy-done.1, ...), custom_call_target="tpu_custom_call" | custom-call | flops 4831838208 | bytes 3637248 | tf_op jit(solution)/shard_map/taps/pallas_call | solution.py:348
  87.7 0.7 copy-done.7
  88.4 3.4 %collective-permute-start.6 = (f32[1152,128]{1,0:T(8,128)}, f32[1152,128]{1,0:T(8,128)S(1)}, u32[]{:S(2)}, u32[]{:S(2)}) collective-permute-start(f32[1152,128]{1,0:T(8,128)} %get-tuple-element.38), channel_id=1, source_target_pairs={{0,6},{1,7},{2,2},{3,3},{4,4},{5,5},{6,0},{7,1},{8,14},{9,15},{10,... | collective-permute-start | bytes 1769480 | tf_op jit(solution)/shard_map/ppermute | solution.py:506
  91.9 2.3 %collective-permute-start.7 = (f32[1152,128]{1,0:T(8,128)}, f32[1152,128]{1,0:T(8,128)}, u32[]{:S(2)}, u32[]{:S(2)}) collective-permute-start(f32[1152,128]{1,0:T(8,128)} %get-tuple-element.39.refs_2_), channel_id=1, source_target_pairs={{0,7},{1,6},{2,3},{3,2},{4,5},{5,4},{6,1},{7,0},{8,15},{9,14},{10,... | collective-permute-start | bytes 1769480 | tf_op jit(solution)/shard_map/ppermute | solution.py:506
  94.1 3.4 %lat_solve.3 = (f32[37,96,128]{2,1,0:T(8,128)}, f32[2,37,128]{2,1,0:T(8,128)}, f32[3,37,128]{2,1,0:T(8,128)}) custom-call(f32[8,96,128]{2,1,0:T(8,128)} %copy-done.7, f32[31,96,128]{2,1,0:T(8,128)} %copy-done, f32[96,128]{1,0:T(8,128)} %constant.90.clone.refs_5_.refs_2_, f32[96,128]{1,0:T(8,128)} %constant.91.clone.refs_6_.refs_3_), custom_call_target="tpu_custom_call" | custom-call | flops 3932160 | bytes 3932160 | tf_op jit(solution)/shard_map/lat_solve/pallas_call | solution.py:177
  97.5 4.6 %lon_solve.3.refs_1_ = bf16[4736,384]{1,0:T(8,128)(2,1)} custom-call(f32[37,96,128]{2,1,0:T(8,128)} %get-tuple-element.41.x_ref, f32[5,37,128]{2,1,0:T(8,128)} %collective-permute-done.10.refs_0_, bf16[384,128]{1,0:T(8,128)(2,1)} %constant.103.refs_2_.refs_1_), custom_call_target="tpu_custom_call" | custom-call | flops 465567744 | bytes 3637248 | tf_op jit(solution)/shard_map/lon_solve/pallas_call | solution.py:226
  102.1 19.9 %taps.6 = (f32[1152,128]{1,0:T(8,128)}, f32[1152,128]{1,0:T(8,128)}) custom-call(s32[24]{0:T(128)} %dynamic-slice_bitcast_fusion.1.meta_ref, s32[512]{0:T(512)} %reshape.24.base_ref, bf16[4736,384]{1,0:T(8,128)(2,1)} %get-tuple-element.35.refs_0_.refs_1_, bf16[4736,384]{1,0:T(8,128)(2,1)} %lon_solve.3.refs_1_, f32[1152,128]{1,0:T(8,128)} %get-tuple-element.39.refs_2_, ...), custom_call_target="tpu_custom_call" | custom-call | flops 4831838208 | bytes 3637248 | tf_op jit(solution)/shard_map/taps/pallas_call | solution.py:348
  122.0 0.0 copy-start.14
  122.0 29.3 %collective-permute-start.12 = (f32[1152,128]{1,0:T(8,128)}, f32[1152,128]{1,0:T(8,128)S(1)}, u32[]{:S(2)}, u32[]{:S(2)}) collective-permute-start(f32[1152,128]{1,0:T(8,128)} %get-tuple-element.44.refs_2_), channel_id=1, source_target_pairs={{0,3},{1,2},{2,1},{3,0},{4,7},{5,6},{6,5},{7,4},{8,11},{9,10},{10,... | collective-permute-start | bytes 1769480 | tf_op jit(solution)/shard_map/ppermute | solution.py:506
  151.3 19.9 %taps.7 = (f32[1152,128]{1,0:T(8,128)}, f32[1152,128]{1,0:T(8,128)}) custom-call(s32[24]{0:T(128)} %dynamic-slice_bitcast_fusion.1.meta_ref, s32[512]{0:T(512)} %reshape.24.base_ref, bf16[4736,384]{1,0:T(8,128)(2,1)} %get-tuple-element.35.refs_0_.refs_1_, bf16[4736,384]{1,0:T(8,128)(2,1)} %lon_solve.3.refs_1_, f32[1152,128]{1,0:T(8,128)} %get-tuple-element.44.refs_2_, ...), custom_call_target="tpu_custom_call" | custom-call | flops 4831838208 | bytes 3637248 | tf_op jit(solution)/shard_map/taps/pallas_call | solution.py:348
  171.2 1.2 collective-permute-start.13
  172.4 0.1 convert_reduce_fusion.1
  172.5 0.1 fusion.14
  172.6 0.2 fusion.1
  172.9 0.7 reshape.23.target_ref
  173.5 11.3 %collective-permute-done.13.refs_7_ = f32[1152,128]{1,0:T(8,128)S(1)} collective-permute-done((f32[1152,128]{1,0:T(8,128)}, f32[1152,128]{1,0:T(8,128)S(1)}, u32[]{:S(2)}, u32[]{:S(2)}) %collective-permute-start.13) | collective-permute-done | bytes 589856 | tf_op jit(solution)/shard_map/ppermute | solution.py:506
  184.9 0.4 collective-permute-done.11.refs_4_
  185.3 0.4 copy-done.6
  185.7 0.4 copy-done.5
  186.2 8.8 %place.1 = f32[3072,128]{1,0:T(8,128)} custom-call(s32[3072]{0:T(1024)} %reshape.23.target_ref, f32[1152,128]{1,0:T(8,128)} %copy-done.2, f32[1152,128]{1,0:T(8,128)} %copy-done.3, f32[1152,128]{1,0:T(8,128)} %copy-done.4, f32[1152,128]{1,0:T(8,128)} %collective-permute-done.7.refs_3_, f32[1152,128]{1,0:T(8,128)} %collective-permute-done.11.refs_4_, ...), custom_call_target="tpu_custom_call" | custom-call | bytes 9437184 | tf_op jit(solution)/shard_map/place/pallas_call | solution.py:403
  (37 shorter events, 0.1 us)
Async XLA Ops:
  5.3 34.9 %all-to-all-start = ((f32[8,4,32,128]{3,2,1,0:T(8,128)}), f32[8,4,32,128]{3,2,1,0:T(8,128)S(1)}, u32[]{:S(2)}, u32[]{:S(2)}) async-start(f32[8,4,32,128]{3,2,1,0:T(8,128)} %get-tuple-element.32), calls=%async_computation | async-start | bytes 1048576 | tf_op jit(solution)/shard_map/all_to_all | solution.py:456
  12.6 7.4 %collective-permute-start.1 = (f32[4,96,128]{2,1,0:T(8,128)}, f32[4,96,128]{2,1,0:T(8,128)S(1)}, u32[]{:S(2)}, u32[]{:S(2)}) collective-permute-start(f32[4,96,128]{2,1,0:T(8,128)} %get-tuple-element.27), channel_id=1, source_target_pairs={{8,0},{16,8},{24,16},{9,1},{17,9},{25,17},{10,2},{18,10},{26,18},{... | collective-permute-start | bytes 589832 | tf_op jit(solution)/shard_map/ppermute | solution.py:455
  13.9 6.1 %collective-permute-start = (f32[3,96,128]{2,1,0:T(8,128)}, f32[3,96,128]{2,1,0:T(8,128)S(1)}, u32[]{:S(2)}, u32[]{:S(2)}) collective-permute-start(f32[3,96,128]{2,1,0:T(8,128)} %get-tuple-element.26), channel_id=1, source_target_pairs={{0,8},{8,16},{16,24},{1,9},{9,17},{17,25},{2,10},{10,18},{18,26},{... | collective-permute-start | bytes 442376 | tf_op jit(solution)/shard_map/ppermute | solution.py:454
  17.9 69.7 %collective-permute-start.8 = (f32[8,96,128]{2,1,0:T(8,128)S(1)}, f32[8,96,128]{2,1,0:T(8,128)S(1)}, u32[]{:S(2)}, u32[]{:S(2)}) collective-permute-start(f32[8,96,128]{2,1,0:T(8,128)S(1)} %slice.7), channel_id=1, source_target_pairs={{2,4},{3,5},{4,2},{5,3},{10,12},{11,13},{12,10},{13,11},{18,20},{1... | collective-permute-start | bytes 1179656 | tf_op jit(solution)/shard_map/ppermute | solution.py:451
  19.9 0.7 copy-start.10
  19.9 0.7 copy-start.9
  24.7 15.8 %copy-start.11 = (f32[32,32]{1,0:T(8,128)S(1)}, f32[32,32]{1,0:T(8,128)}, u32[]{:S(2)}) copy-start(f32[32,32]{1,0:T(8,128)} %constant.93.clone) | copy-start | bytes 12292
  24.7 7.0 %collective-permute-start.2 = (f32[2,37,128]{2,1,0:T(8,128)}, f32[2,37,128]{2,1,0:T(8,128)S(1)}, u32[]{:S(2)}, u32[]{:S(2)}) collective-permute-start(f32[2,37,128]{2,1,0:T(8,128)} %get-tuple-element.33), channel_id=1, source_target_pairs={{0,1},{1,2},{2,3},{3,4},{4,5},{5,6},{6,7},{7,0},{8,9},{9,10},{10,1... | collective-permute-start | bytes 113672 | tf_op jit(solution)/shard_map/ppermute | solution.py:459
  26.7 7.1 %collective-permute-start.3 = (f32[3,37,128]{2,1,0:T(8,128)}, f32[3,37,128]{2,1,0:T(8,128)S(1)}, u32[]{:S(2)}, u32[]{:S(2)}) collective-permute-start(f32[3,37,128]{2,1,0:T(8,128)} %get-tuple-element.34), channel_id=1, source_target_pairs={{1,0},{2,1},{3,2},{4,3},{5,4},{6,5},{7,6},{0,7},{9,8},{10,9},{11,1... | collective-permute-start | bytes 170504 | tf_op jit(solution)/shard_map/ppermute | solution.py:460
  30.2 61.7 %collective-permute-start.9 = (f32[31,96,128]{2,1,0:T(8,128)}, f32[31,96,128]{2,1,0:T(8,128)S(1)}, u32[]{:S(2)}, u32[]{:S(2)}) collective-permute-start(f32[31,96,128]{2,1,0:T(8,128)} %get-tuple-element.40), channel_id=1, source_target_pairs={{2,4},{3,5},{4,2},{5,3},{10,12},{11,13},{12,10},{13,11},{18,20},{1... | collective-permute-start | bytes 4571144 | tf_op jit(solution)/shard_map/ppermute | solution.py:467
  31.7 2.1 %copy-start.13 = (f32[2,37,128]{2,1,0:T(8,128)}, f32[2,37,128]{2,1,0:T(8,128)S(1)}, u32[]{:S(2)}) copy-start(f32[2,37,128]{2,1,0:T(8,128)S(1)} %collective-permute-done.2.refs_0_) | copy-start | bytes 113668
  33.8 0.6 copy-start.12
  38.9 58.6 %collective-permute-start.10 = (f32[5,37,128]{2,1,0:T(8,128)}, f32[5,37,128]{2,1,0:T(8,128)}, u32[]{:S(2)}, u32[]{:S(2)}) collective-permute-start(f32[5,37,128]{2,1,0:T(8,128)} %get-tuple-element.42), channel_id=1, source_target_pairs={{2,4},{3,5},{4,2},{5,3},{10,12},{11,13},{12,10},{13,11},{18,20},{1... | collective-permute-start | bytes 284168 | tf_op jit(solution)/shard_map/ppermute | solution.py:468
  40.2 1.1 copy-start.1
  61.1 110.0 %collective-permute-start.4 = (f32[1152,128]{1,0:T(8,128)}, f32[1152,128]{1,0:T(8,128)S(1)}, u32[]{:S(2)}, u32[]{:S(2)}) collective-permute-start(f32[1152,128]{1,0:T(8,128)} %get-tuple-element.36), channel_id=1, source_target_pairs={{0,4},{1,5},{2,0},{3,1},{4,6},{5,7},{6,2},{7,3},{8,12},{9,13},{10,... | collective-permute-start | bytes 1769480 | tf_op jit(solution)/shard_map/ppermute | solution.py:506
  66.4 105.9 %collective-permute-start.5 = (f32[1152,128]{1,0:T(8,128)}, f32[1152,128]{1,0:T(8,128)S(1)}, u32[]{:S(2)}, u32[]{:S(2)}) collective-permute-start(f32[1152,128]{1,0:T(8,128)} %get-tuple-element.37.refs_1_), channel_id=1, source_target_pairs={{0,5},{1,4},{2,1},{3,0},{4,7},{5,6},{6,3},{7,2},{8,13},{9,12},{10,... | collective-permute-start | bytes 1769480 | tf_op jit(solution)/shard_map/ppermute | solution.py:506
  87.7 0.7 copy-start.7
  88.4 85.1 %collective-permute-start.6 = (f32[1152,128]{1,0:T(8,128)}, f32[1152,128]{1,0:T(8,128)S(1)}, u32[]{:S(2)}, u32[]{:S(2)}) collective-permute-start(f32[1152,128]{1,0:T(8,128)} %get-tuple-element.38), channel_id=1, source_target_pairs={{0,6},{1,7},{2,2},{3,3},{4,4},{5,5},{6,0},{7,1},{8,14},{9,15},{10,... | collective-permute-start | bytes 1769480 | tf_op jit(solution)/shard_map/ppermute | solution.py:506
  91.9 2.3 %copy-start = (f32[31,96,128]{2,1,0:T(8,128)}, f32[31,96,128]{2,1,0:T(8,128)S(1)}, u32[]{:S(2)}) copy-start(f32[31,96,128]{2,1,0:T(8,128)S(1)} %collective-permute-done.9.refs_1_) | copy-start | bytes 4571140
  91.9 81.7 %collective-permute-start.7 = (f32[1152,128]{1,0:T(8,128)}, f32[1152,128]{1,0:T(8,128)}, u32[]{:S(2)}, u32[]{:S(2)}) collective-permute-start(f32[1152,128]{1,0:T(8,128)} %get-tuple-element.39.refs_2_), channel_id=1, source_target_pairs={{0,7},{1,6},{2,3},{3,2},{4,5},{5,4},{6,1},{7,0},{8,15},{9,14},{10,... | collective-permute-start | bytes 1769480 | tf_op jit(solution)/shard_map/ppermute | solution.py:506
  122.0 50.4 %copy-start.8 = (s32[32,96]{1,0:T(8,128)S(1)}, s32[32,96]{1,0:T(8,128)}, u32[]{:S(2)}) copy-start(s32[32,96]{1,0:T(8,128)} %reshape.22.owner_ref) | copy-start | bytes 36868
  122.0 50.6 %copy-start.14 = (bf16[96,96,1]{1,0,2:T(8,128)(2,1)S(1)}, bf16[96,96,1]{1,0,2:T(8,128)(2,1)}, u32[]{:S(2)}) copy-start(bf16[96,96,1]{1,0,2:T(8,128)(2,1)} %constant.104) | copy-start | bytes 55300
  122.0 63.3 %collective-permute-start.12 = (f32[1152,128]{1,0:T(8,128)}, f32[1152,128]{1,0:T(8,128)S(1)}, u32[]{:S(2)}, u32[]{:S(2)}) collective-permute-start(f32[1152,128]{1,0:T(8,128)} %get-tuple-element.44.refs_2_), channel_id=1, source_target_pairs={{0,3},{1,2},{2,1},{3,0},{4,7},{5,6},{6,5},{7,4},{8,11},{9,10},{10,... | collective-permute-start | bytes 1769480 | tf_op jit(solution)/shard_map/ppermute | solution.py:506
  171.2 14.1 %copy-start.2 = (f32[1152,128]{1,0:T(8,128)}, f32[1152,128]{1,0:T(8,128)S(1)}, u32[]{:S(2)}) copy-start(f32[1152,128]{1,0:T(8,128)S(1)} %collective-permute-done.4.refs_0_) | copy-start | bytes 1769476
  171.2 13.7 %collective-permute-start.13 = (f32[1152,128]{1,0:T(8,128)}, f32[1152,128]{1,0:T(8,128)S(1)}, u32[]{:S(2)}, u32[]{:S(2)}) collective-permute-start(f32[1152,128]{1,0:T(8,128)} %get-tuple-element.46), channel_id=1, source_target_pairs={{0,1},{1,0},{2,3},{3,2},{4,5},{5,4},{6,7},{7,6},{8,9},{9,8},{10,11... | collective-permute-start | bytes 1769480 | tf_op jit(solution)/shard_map/ppermute | solution.py:506
  172.4 12.9 %copy-start.3 = (f32[1152,128]{1,0:T(8,128)}, f32[1152,128]{1,0:T(8,128)S(1)}, u32[]{:S(2)}) copy-start(f32[1152,128]{1,0:T(8,128)S(1)} %collective-permute-done.5.refs_1_) | copy-start | bytes 1769476
  172.4 12.9 %collective-permute-start.11 = (f32[1152,128]{1,0:T(8,128)}, f32[1152,128]{1,0:T(8,128)}, u32[]{:S(2)}, u32[]{:S(2)}) collective-permute-start(f32[1152,128]{1,0:T(8,128)} %get-tuple-element.43), channel_id=1, source_target_pairs={{0,2},{1,3},{2,0},{3,1},{4,6},{5,7},{6,4},{7,5},{8,10},{9,11},{10,... | collective-permute-start | bytes 1769480 | tf_op jit(solution)/shard_map/ppermute | solution.py:506
  173.5 11.8 %copy-start.4 = (f32[1152,128]{1,0:T(8,128)}, f32[1152,128]{1,0:T(8,128)S(1)}, u32[]{:S(2)}) copy-start(f32[1152,128]{1,0:T(8,128)S(1)} %collective-permute-done.6.refs_2_) | copy-start | bytes 1769476
  184.9 0.9 copy-start.6
  185.3 0.9 copy-start.5

commit v6 on v5

--- a/solution.py
+++ b/solution.py
@@ -389,11 +389,11 @@
     for copy in copies:
         copy.wait()
 
-    @pl.loop(0, out_ref.shape[0] // 8)
+    @pl.loop(0, out_ref.shape[0] // 32)
     def _(group):
-        at = pl.multiple_of(group * 8, 8)
-        lines = [gathered[pl.ds(target_ref[at + k], 1)] for k in range(8)]
-        out_ref[pl.ds(at, 8)] = jnp.concatenate(lines, axis=0)
+        at = pl.multiple_of(group * 32, 32)
+        for k in range(32):
+            out_ref[pl.ds(at + k, 1)] = gathered[pl.ds(target_ref[at + k], 1)]
 
 
 def place(target, parts):
@@ -411,7 +411,7 @@
             scratch_shapes=[pltpu.VMEM((count * cap, ch), F32), pltpu.SemaphoreType.DMA((count,))],
         ),
         cost_estimate=pl.CostEstimate(flops=0, bytes_accessed=8 * count * cap * ch, transcendentals=0),
-        compiler_params=pltpu.CompilerParams(vmem_limit_bytes=VMEM_LIMIT),
+        compiler_params=pltpu.CompilerParams(vmem_limit_bytes=16 * 1024 * 1024),
         name="place",
     )(target, *parts)
 
@@ -447,7 +447,7 @@
     mine, offset = me // quarter, me % quarter
     middle = (mine == 1) | (mine == 2)
 
-    head = rows // 4
+    head = rows // 2
     first = lax.ppermute(tracers[:head], "lon", mirror)
     owner = owners.reshape(rows, cols)
     down, up, top, bottom, words = edges(tracers, owner, columns, lat_shift, fractions)

time: 196 us -> 174 us (0.89)
  starting transfers between devices: 62 us -> 45.5 us
  waiting for transfers between devices: 14.7 us -> 11.4 us
  Pallas kernels: 107 us -> 105 us
    ppermute x7, starting transfers between devices: 42.9 us -> 25.6 us  [transport(): value = lax.ppermute(value, 'lon', moves)]
    ppermute x7, waiting for transfers between devices: 11.8 us -> 8.85 us  [transport(): value = lax.ppermute(value, 'lon', moves)]
    pallas_call x1, Pallas kernels: 8.81 us -> 6.36 us  [place(): pl.pallas_call(functools.partial(place_kernel, cap=cap), out_shape=jax.Sh...]
  transfers between devices with their start and end apart: 15 -> 15, of which waited for: 4 -> 4; matrix products, arithmetic and copies ran while one was open for 3% -> 3% of each run, Pallas kernels for 49% -> 55%
where the time goes in v6:
time: 174 us; the launch traced here: 173 us
  Pallas kernels  105 us (60%)
  starting transfers between devices  45.5 us (26%)
  waiting for transfers between devices  11.4 us (7%)
  local copies, waits for them, and re-layouts  8.02 us (5%)
  other arithmetic  2.34 us (1%)
    pallas_call x4, Pallas kernels, taps(): pl.pallas_call(functools.partial(tap_kernel, tables=len(tables), count=co...  79.4 us
    ppermute x7, starting transfers between devices, transport(): value = lax.ppermute(value, 'lon', moves)  25.6 us
    pallas_call x2, Pallas kernels, lon_solve(): pl.pallas_call(functools.partial(lon_kernel, packed=packed), out_shape=sh...  9.06 us
    ppermute x7, waiting for transfers between devices, transport(): value = lax.ppermute(value, 'lon', moves)  8.85 us
    pallas_call x2, Pallas kernels, lat_solve(): pl.pallas_call(functools.partial(lat_kernel, pieces=len(pieces), head=hea...  7.31 us
    all_to_all x1, starting transfers between devices, transport(): lax.all_to_all(words, 'lon', split_axis=0, concat_axis=0, tiled=True)  7.28 us
    pallas_call x1, Pallas kernels, place(): pl.pallas_call(functools.partial(place_kernel, cap=cap), out_shape=jax.Sh...  6.36 us
  transfers between devices with their start and end apart: 15, of which 4 were waited for; matrix products, arithmetic and copies ran while one was open for 3% of the time, Pallas kernels for 55%

profile of v6, /device:TPU:0, one launch (start us, length us, event | category | flops | bytes accessed | tf_op | source)
XLA Modules:
  0.0 172.8 jit_solution(6484226971903880404)
XLA Ops:
  0.0 0.5 broadcast.42
  0.5 1.4 reduce.4
  1.9 0.7 reshape.22.owner_ref
  2.6 2.7 %edges.1 = (f32[3,96,128]{2,1,0:T(8,128)}, f32[4,96,128]{2,1,0:T(8,128)}, f32[3,96,128]{2,1,0:T(8,128)}, f32[4,96,128]{2,1,0:T(8,128)}, f32[8,4,32,128]{3,2,1,0:T(8,128)}) custom-call(f32[32,96,128]{2,1,0:T(8,128)} %refs_0_.1, s32[32,96]{1,0:T(8,128)} %reshape.22.owner_ref, s32[32,96]{1,0:T(8,128)} %column_ref.1, s32[32,96]{1,0:T(8,128)} %shift_ref.1, ...), custom_call_target="tpu_custom_call" | custom-call | flops 2359296 | bytes 2359296 | tf_op jit(solution)/shard_map/edges/pallas_call | solution.py:94
  5.3 7.3 %all-to-all-start = ((f32[8,4,32,128]{3,2,1,0:T(8,128)}), f32[8,4,32,128]{3,2,1,0:T(8,128)S(1)}, u32[]{:S(2)}, u32[]{:S(2)}) async-start(f32[8,4,32,128]{3,2,1,0:T(8,128)} %get-tuple-element.32), calls=%async_computation | async-start | bytes 1048576 | tf_op jit(solution)/shard_map/all_to_all | solution.py:456
  12.6 1.3 collective-permute-start.1
  13.9 3.0 %collective-permute-start = (f32[3,96,128]{2,1,0:T(8,128)}, f32[3,96,128]{2,1,0:T(8,128)S(1)}, u32[]{:S(2)}, u32[]{:S(2)}) collective-permute-start(f32[3,96,128]{2,1,0:T(8,128)} %get-tuple-element.26), channel_id=1, source_target_pairs={{0,8},{8,16},{16,24},{1,9},{9,17},{17,25},{2,10},{10,18},{18,26},{... | collective-permute-start | bytes 442376 | tf_op jit(solution)/shard_map/ppermute | solution.py:454
  16.9 1.0 slice.7
  17.9 1.6 collective-permute-start.8
  19.5 1.3 dynamic-slice_bitcast_fusion.1.meta_ref
  20.8 0.6 copy-done.6
  21.4 0.1 copy-done.5
  21.5 3.9 %lat_solve.2 = (f32[37,96,128]{2,1,0:T(8,128)}, f32[2,37,128]{2,1,0:T(8,128)}, f32[3,37,128]{2,1,0:T(8,128)}, f32[23,96,128]{2,1,0:T(8,128)}) custom-call(f32[32,96,128]{2,1,0:T(8,128)} %refs_0_.1, f32[3,96,128]{2,1,0:T(8,128)} %copy-done.6, f32[4,96,128]{2,1,0:T(8,128)} %copy-done.5, f32[3,96,128]{2,1,0:T(8,128)} %get-tuple-element.28.refs_3_, ...), custom_call_target="tpu_custom_call" | custom-call | flops 3932160 | bytes 3932160 | tf_op jit(solution)/shard_map/lat_solve/pallas_call | solution.py:177
  25.4 2.0 %collective-permute-start.2 = (f32[2,37,128]{2,1,0:T(8,128)}, f32[2,37,128]{2,1,0:T(8,128)S(1)}, u32[]{:S(2)}, u32[]{:S(2)}) collective-permute-start(f32[2,37,128]{2,1,0:T(8,128)} %get-tuple-element.33), channel_id=1, source_target_pairs={{0,1},{1,2},{2,3},{3,4},{4,5},{5,6},{6,7},{7,0},{8,9},{9,10},{10,1... | collective-permute-start | bytes 113672 | tf_op jit(solution)/shard_map/ppermute | solution.py:459
  27.4 2.8 %collective-permute-start.3 = (f32[3,37,128]{2,1,0:T(8,128)}, f32[3,37,128]{2,1,0:T(8,128)S(1)}, u32[]{:S(2)}, u32[]{:S(2)}) collective-permute-start(f32[3,37,128]{2,1,0:T(8,128)} %get-tuple-element.34), channel_id=1, source_target_pairs={{1,0},{2,1},{3,2},{4,3},{5,4},{6,5},{7,6},{0,7},{9,8},{10,9},{11,1... | collective-permute-start | bytes 170504 | tf_op jit(solution)/shard_map/ppermute | solution.py:460
  30.2 0.7 dynamic-slice_bitcast_fusion
  30.9 0.7 collective-permute-start.9
  31.6 0.8 collective-permute-done.2.refs_0_
  32.4 1.7 %collective-permute-done.3.refs_1_ = f32[3,37,128]{2,1,0:T(8,128)S(1)} collective-permute-done((f32[3,37,128]{2,1,0:T(8,128)}, f32[3,37,128]{2,1,0:T(8,128)S(1)}, u32[]{:S(2)}, u32[]{:S(2)}) %collective-permute-start.3) | collective-permute-done | bytes 56864 | tf_op jit(solution)/shard_map/ppermute | solution.py:460
  34.2 0.6 copy-done.8
  34.8 4.5 %lon_solve.2 = (bf16[4736,384]{1,0:T(8,128)(2,1)}, f32[5,37,128]{2,1,0:T(8,128)}) custom-call(f32[37,96,128]{2,1,0:T(8,128)} %get-tuple-element.30.x_ref, f32[2,37,128]{2,1,0:T(8,128)} %copy-done.9, f32[3,37,128]{2,1,0:T(8,128)} %copy-done.8, bf16[384,128]{1,0:T(8,128)(2,1)} %constant.103.refs_2_.refs_1_), custom_call_target="tpu_custom_call" | custom-call | flops 465567744 | bytes 3637248 | tf_op jit(solution)/shard_map/lon_solve/pallas_call | solution.py:226
  39.3 1.3 collective-permute-start.10
  40.6 0.2 convert_reduce_fusion
  40.8 0.1 convolution_convert_fusion
  40.9 0.7 reshape.24.base_ref
  41.6 19.9 %taps.4 = (f32[1152,128]{1,0:T(8,128)}, f32[1152,128]{1,0:T(8,128)}) custom-call(s32[24]{0:T(128)} %dynamic-slice_bitcast_fusion.1.meta_ref, s32[512]{0:T(512)} %reshape.24.base_ref, bf16[4736,384]{1,0:T(8,128)(2,1)} %get-tuple-element.35.refs_0_.refs_1_, bf16[4736,384]{1,0:T(8,128)(2,1)} %get-tuple-element.35.refs_0_.refs_1_, f32[8,4,32,128]{3,2,1,0:T(8,128)} %copy-done.3, ...), custom_call_target="tpu_custom_call" | custom-call | flops 4831838208 | bytes 3637248 | tf_op jit(solution)/shard_map/taps/pallas_call | solution.py:348
  61.5 13.5 %collective-permute-start.4 = (f32[1152,128]{1,0:T(8,128)}, f32[1152,128]{1,0:T(8,128)S(1)}, u32[]{:S(2)}, u32[]{:S(2)}) collective-permute-start(f32[1152,128]{1,0:T(8,128)} %get-tuple-element.36), channel_id=1, source_target_pairs={{0,4},{1,5},{2,0},{3,1},{4,6},{5,7},{6,2},{7,3},{8,12},{9,13},{10,... | collective-permute-start | bytes 1769480 | tf_op jit(solution)/shard_map/ppermute | solution.py:506
  75.0 2.7 %collective-permute-start.5 = (f32[1152,128]{1,0:T(8,128)}, f32[1152,128]{1,0:T(8,128)S(1)}, u32[]{:S(2)}, u32[]{:S(2)}) collective-permute-start(f32[1152,128]{1,0:T(8,128)} %get-tuple-element.37.refs_1_), channel_id=1, source_target_pairs={{0,5},{1,4},{2,1},{3,0},{4,7},{5,6},{6,3},{7,2},{8,13},{9,12},{10,... | collective-permute-start | bytes 1769480 | tf_op jit(solution)/shard_map/ppermute | solution.py:506
  77.7 19.8 %taps.5 = (f32[1152,128]{1,0:T(8,128)}, f32[1152,128]{1,0:T(8,128)}) custom-call(s32[24]{0:T(128)} %dynamic-slice_bitcast_fusion.1.meta_ref, s32[512]{0:T(512)} %reshape.24.base_ref, bf16[4736,384]{1,0:T(8,128)(2,1)} %get-tuple-element.35.refs_0_.refs_1_, f32[1152,128]{1,0:T(8,128)} %get-tuple-element.37.refs_1_, f32[8,4,32,128]{3,2,1,0:T(8,128)} %copy-done.3, ...), custom_call_target="tpu_custom_call" | custom-call | flops 4831838208 | bytes 3637248 | tf_op jit(solution)/shard_map/taps/pallas_call | solution.py:348
  97.5 2.8 %collective-permute-start.6 = (f32[1152,128]{1,0:T(8,128)}, f32[1152,128]{1,0:T(8,128)S(1)}, u32[]{:S(2)}, u32[]{:S(2)}) collective-permute-start(f32[1152,128]{1,0:T(8,128)} %get-tuple-element.38), channel_id=1, source_target_pairs={{0,6},{1,7},{2,2},{3,3},{4,4},{5,5},{6,0},{7,1},{8,14},{9,15},{10,... | collective-permute-start | bytes 1769480 | tf_op jit(solution)/shard_map/ppermute | solution.py:506
  100.4 2.9 %collective-permute-start.7 = (f32[1152,128]{1,0:T(8,128)}, f32[1152,128]{1,0:T(8,128)S(1)}, u32[]{:S(2)}, u32[]{:S(2)}) collective-permute-start(f32[1152,128]{1,0:T(8,128)} %get-tuple-element.39.refs_2_), channel_id=1, source_target_pairs={{0,7},{1,6},{2,3},{3,2},{4,5},{5,4},{6,1},{7,0},{8,15},{9,14},{10,... | collective-permute-start | bytes 1769480 | tf_op jit(solution)/shard_map/ppermute | solution.py:506
  103.3 3.4 %lat_solve.3 = (f32[37,96,128]{2,1,0:T(8,128)}, f32[2,37,128]{2,1,0:T(8,128)}, f32[3,37,128]{2,1,0:T(8,128)}) custom-call(f32[16,96,128]{2,1,0:T(8,128)} %collective-permute-done.8.refs_0_, f32[23,96,128]{2,1,0:T(8,128)} %copy-done.2, f32[96,128]{1,0:T(8,128)} %constant.90.clone.refs_5_.refs_2_, f32[96,128]{1,0:T(8,128)} %constant.91.clone.refs_6_.refs_3_), custom_call_target="tpu_custom_call" | custom-call | flops 3932160 | bytes 3932160 | tf_op jit(solution)/shard_map/lat_solve/pallas_call | solution.py:177
  106.7 4.6 %lon_solve.3.refs_1_ = bf16[4736,384]{1,0:T(8,128)(2,1)} custom-call(f32[37,96,128]{2,1,0:T(8,128)} %get-tuple-element.41.x_ref, f32[5,37,128]{2,1,0:T(8,128)} %collective-permute-done.10.refs_0_, bf16[384,128]{1,0:T(8,128)(2,1)} %constant.103.refs_2_.refs_1_), custom_call_target="tpu_custom_call" | custom-call | flops 465567744 | bytes 3637248 | tf_op jit(solution)/shard_map/lon_solve/pallas_call | solution.py:226
  111.3 19.8 %taps.6 = (f32[1152,128]{1,0:T(8,128)}, f32[1152,128]{1,0:T(8,128)}) custom-call(s32[24]{0:T(128)} %dynamic-slice_bitcast_fusion.1.meta_ref, s32[512]{0:T(512)} %reshape.24.base_ref, bf16[4736,384]{1,0:T(8,128)(2,1)} %get-tuple-element.35.refs_0_.refs_1_, bf16[4736,384]{1,0:T(8,128)(2,1)} %lon_solve.3.refs_1_, f32[1152,128]{1,0:T(8,128)} %get-tuple-element.39.refs_2_, ...), custom_call_target="tpu_custom_call" | custom-call | flops 4831838208 | bytes 3637248 | tf_op jit(solution)/shard_map/taps/pallas_call | solution.py:348
  131.1 0.0 copy-start.10
  131.1 0.1 collective-permute-start.12
  131.2 19.9 %taps.7 = (f32[1152,128]{1,0:T(8,128)}, f32[1152,128]{1,0:T(8,128)}) custom-call(s32[24]{0:T(128)} %dynamic-slice_bitcast_fusion.1.meta_ref, s32[512]{0:T(512)} %reshape.24.base_ref, bf16[4736,384]{1,0:T(8,128)(2,1)} %get-tuple-element.35.refs_0_.refs_1_, bf16[4736,384]{1,0:T(8,128)(2,1)} %lon_solve.3.refs_1_, f32[1152,128]{1,0:T(8,128)} %get-tuple-element.44.refs_2_, ...), custom_call_target="tpu_custom_call" | custom-call | flops 4831838208 | bytes 3637248 | tf_op jit(solution)/shard_map/taps/pallas_call | solution.py:348
  151.1 1.6 collective-permute-start.13
  152.8 1.9 %collective-permute-start.11 = (f32[1152,128]{1,0:T(8,128)}, f32[1152,128]{1,0:T(8,128)}, u32[]{:S(2)}, u32[]{:S(2)}) collective-permute-start(f32[1152,128]{1,0:T(8,128)} %get-tuple-element.43), channel_id=1, source_target_pairs={{0,2},{1,3},{2,0},{3,1},{4,6},{5,7},{6,4},{7,5},{8,10},{9,11},{10,... | collective-permute-start | bytes 1769480 | tf_op jit(solution)/shard_map/ppermute | solution.py:506
  154.7 0.1 convert_reduce_fusion.1
  154.8 0.1 fusion.14
  154.9 0.2 fusion.1
  155.1 0.6 fusion.10
  155.8 0.8 reshape.23.target_ref
  156.6 7.6 %collective-permute-done.13.refs_7_ = f32[1152,128]{1,0:T(8,128)S(1)} collective-permute-done((f32[1152,128]{1,0:T(8,128)}, f32[1152,128]{1,0:T(8,128)S(1)}, u32[]{:S(2)}, u32[]{:S(2)}) %collective-permute-start.13) | collective-permute-done | bytes 589856 | tf_op jit(solution)/shard_map/ppermute | solution.py:506
  164.1 1.3 collective-permute-done.11.refs_4_
  165.4 1.1 copy-done
  166.5 6.4 %place.1 = f32[3072,128]{1,0:T(8,128)} custom-call(s32[3072]{0:T(1024)S(1)} %reshape.23.target_ref, f32[1152,128]{1,0:T(8,128)S(1)} %collective-permute-done.4.refs_0_, f32[1152,128]{1,0:T(8,128)S(1)} %collective-permute-done.5.refs_1_, f32[1152,128]{1,0:T(8,128)S(1)} %collective-permute-done.6.refs_2_, f32[1152,128]{1,0:T(8,128)S(1)} %collective-permute-done.7.refs_3_, ...), custom_call_target="tpu_custom_call" | custom-call | bytes 9437184 | tf_op jit(solution)/shard_map/place/pallas_call | solution.py:403
  (29 shorter events, 0.1 us)
Async XLA Ops:
  0.0 16.9 %copy-start.1 = (f32[32,96,128]{2,1,0:T(8,128)S(1)}, f32[32,96,128]{2,1,0:T(8,128)}, u32[]{:S(2)}) copy-start(f32[32,96,128]{2,1,0:T(8,128)} %refs_0_.1) | copy-start | bytes 4718596
  5.3 35.3 %all-to-all-start = ((f32[8,4,32,128]{3,2,1,0:T(8,128)}), f32[8,4,32,128]{3,2,1,0:T(8,128)S(1)}, u32[]{:S(2)}, u32[]{:S(2)}) async-start(f32[8,4,32,128]{3,2,1,0:T(8,128)} %get-tuple-element.32), calls=%async_computation | async-start | bytes 1048576 | tf_op jit(solution)/shard_map/all_to_all | solution.py:456
  12.6 8.2 %collective-permute-start.1 = (f32[4,96,128]{2,1,0:T(8,128)}, f32[4,96,128]{2,1,0:T(8,128)S(1)}, u32[]{:S(2)}, u32[]{:S(2)}) collective-permute-start(f32[4,96,128]{2,1,0:T(8,128)} %get-tuple-element.27), channel_id=1, source_target_pairs={{8,0},{16,8},{24,16},{9,1},{17,9},{25,17},{10,2},{18,10},{26,18},{... | collective-permute-start | bytes 589832 | tf_op jit(solution)/shard_map/ppermute | solution.py:455
  13.9 6.9 %collective-permute-start = (f32[3,96,128]{2,1,0:T(8,128)}, f32[3,96,128]{2,1,0:T(8,128)S(1)}, u32[]{:S(2)}, u32[]{:S(2)}) collective-permute-start(f32[3,96,128]{2,1,0:T(8,128)} %get-tuple-element.26), channel_id=1, source_target_pairs={{0,8},{8,16},{16,24},{1,9},{9,17},{17,25},{2,10},{10,18},{18,26},{... | collective-permute-start | bytes 442376 | tf_op jit(solution)/shard_map/ppermute | solution.py:454
  17.9 79.6 %collective-permute-start.8 = (f32[16,96,128]{2,1,0:T(8,128)}, f32[16,96,128]{2,1,0:T(8,128)}, u32[]{:S(2)}, u32[]{:S(2)}) collective-permute-start(f32[16,96,128]{2,1,0:T(8,128)} %slice.7), channel_id=1, source_target_pairs={{2,4},{3,5},{4,2},{5,3},{10,12},{11,13},{12,10},{13,11},{18,20},{1... | collective-permute-start | bytes 2359304 | tf_op jit(solution)/shard_map/ppermute | solution.py:451
  20.7 0.7 copy-start.6
  20.7 0.7 copy-start.5
  25.4 15.4 %copy-start.7 = (f32[32,32]{1,0:T(8,128)S(1)}, f32[32,32]{1,0:T(8,128)}, u32[]{:S(2)}) copy-start(f32[32,32]{1,0:T(8,128)} %constant.93.clone) | copy-start | bytes 12292
  25.4 7.0 %collective-permute-start.2 = (f32[2,37,128]{2,1,0:T(8,128)}, f32[2,37,128]{2,1,0:T(8,128)S(1)}, u32[]{:S(2)}, u32[]{:S(2)}) collective-permute-start(f32[2,37,128]{2,1,0:T(8,128)} %get-tuple-element.33), channel_id=1, source_target_pairs={{0,1},{1,2},{2,3},{3,4},{4,5},{5,6},{6,7},{7,0},{8,9},{9,10},{10,1... | collective-permute-start | bytes 113672 | tf_op jit(solution)/shard_map/ppermute | solution.py:459
  27.4 6.7 %collective-permute-start.3 = (f32[3,37,128]{2,1,0:T(8,128)}, f32[3,37,128]{2,1,0:T(8,128)S(1)}, u32[]{:S(2)}, u32[]{:S(2)}) collective-permute-start(f32[3,37,128]{2,1,0:T(8,128)} %get-tuple-element.34), channel_id=1, source_target_pairs={{1,0},{2,1},{3,2},{4,3},{5,4},{6,5},{7,6},{0,7},{9,8},{10,9},{11,1... | collective-permute-start | bytes 170504 | tf_op jit(solution)/shard_map/ppermute | solution.py:460
  30.9 69.5 %collective-permute-start.9 = (f32[23,96,128]{2,1,0:T(8,128)}, f32[23,96,128]{2,1,0:T(8,128)S(1)}, u32[]{:S(2)}, u32[]{:S(2)}) collective-permute-start(f32[23,96,128]{2,1,0:T(8,128)} %get-tuple-element.40), channel_id=1, source_target_pairs={{2,4},{3,5},{4,2},{5,3},{10,12},{11,13},{12,10},{13,11},{18,20},{1... | collective-permute-start | bytes 3391496 | tf_op jit(solution)/shard_map/ppermute | solution.py:467
  32.4 1.8 %copy-start.9 = (f32[2,37,128]{2,1,0:T(8,128)}, f32[2,37,128]{2,1,0:T(8,128)S(1)}, u32[]{:S(2)}) copy-start(f32[2,37,128]{2,1,0:T(8,128)S(1)} %collective-permute-done.2.refs_0_) | copy-start | bytes 113668
  34.1 0.6 copy-start.8
  39.3 67.4 %collective-permute-start.10 = (f32[5,37,128]{2,1,0:T(8,128)}, f32[5,37,128]{2,1,0:T(8,128)}, u32[]{:S(2)}, u32[]{:S(2)}) collective-permute-start(f32[5,37,128]{2,1,0:T(8,128)} %get-tuple-element.42), channel_id=1, source_target_pairs={{2,4},{3,5},{4,2},{5,3},{10,12},{11,13},{12,10},{13,11},{18,20},{1... | collective-permute-start | bytes 284168 | tf_op jit(solution)/shard_map/ppermute | solution.py:468
  40.6 1.1 copy-start.3
  61.5 89.6 %collective-permute-start.4 = (f32[1152,128]{1,0:T(8,128)}, f32[1152,128]{1,0:T(8,128)S(1)}, u32[]{:S(2)}, u32[]{:S(2)}) collective-permute-start(f32[1152,128]{1,0:T(8,128)} %get-tuple-element.36), channel_id=1, source_target_pairs={{0,4},{1,5},{2,0},{3,1},{4,6},{5,7},{6,2},{7,3},{8,12},{9,13},{10,... | collective-permute-start | bytes 1769480 | tf_op jit(solution)/shard_map/ppermute | solution.py:506
  75.0 77.7 %collective-permute-start.5 = (f32[1152,128]{1,0:T(8,128)}, f32[1152,128]{1,0:T(8,128)S(1)}, u32[]{:S(2)}, u32[]{:S(2)}) collective-permute-start(f32[1152,128]{1,0:T(8,128)} %get-tuple-element.37.refs_1_), channel_id=1, source_target_pairs={{0,5},{1,4},{2,1},{3,0},{4,7},{5,6},{6,3},{7,2},{8,13},{9,12},{10,... | collective-permute-start | bytes 1769480 | tf_op jit(solution)/shard_map/ppermute | solution.py:506
  97.5 59.0 %collective-permute-start.6 = (f32[1152,128]{1,0:T(8,128)}, f32[1152,128]{1,0:T(8,128)S(1)}, u32[]{:S(2)}, u32[]{:S(2)}) collective-permute-start(f32[1152,128]{1,0:T(8,128)} %get-tuple-element.38), channel_id=1, source_target_pairs={{0,6},{1,7},{2,2},{3,3},{4,4},{5,5},{6,0},{7,1},{8,14},{9,15},{10,... | collective-permute-start | bytes 1769480 | tf_op jit(solution)/shard_map/ppermute | solution.py:506
  100.4 2.9 %copy-start.2 = (f32[23,96,128]{2,1,0:T(8,128)}, f32[23,96,128]{2,1,0:T(8,128)S(1)}, u32[]{:S(2)}) copy-start(f32[23,96,128]{2,1,0:T(8,128)S(1)} %collective-permute-done.9.refs_1_) | copy-start | bytes 3391492
  100.4 56.2 %collective-permute-start.7 = (f32[1152,128]{1,0:T(8,128)}, f32[1152,128]{1,0:T(8,128)S(1)}, u32[]{:S(2)}, u32[]{:S(2)}) collective-permute-start(f32[1152,128]{1,0:T(8,128)} %get-tuple-element.39.refs_2_), channel_id=1, source_target_pairs={{0,7},{1,6},{2,3},{3,2},{4,5},{5,4},{6,1},{7,0},{8,15},{9,14},{10,... | collective-permute-start | bytes 1769480 | tf_op jit(solution)/shard_map/ppermute | solution.py:506
  131.1 23.6 %copy-start.4 = (s32[32,96]{1,0:T(8,128)S(1)}, s32[32,96]{1,0:T(8,128)}, u32[]{:S(2)}) copy-start(s32[32,96]{1,0:T(8,128)} %reshape.22.owner_ref) | copy-start | bytes 36868
  131.1 23.8 %copy-start.10 = (bf16[96,96,1]{1,0,2:T(8,128)(2,1)S(1)}, bf16[96,96,1]{1,0,2:T(8,128)(2,1)}, u32[]{:S(2)}) copy-start(bf16[96,96,1]{1,0,2:T(8,128)(2,1)} %constant.104) | copy-start | bytes 55300
  131.1 34.3 %collective-permute-start.12 = (f32[1152,128]{1,0:T(8,128)}, f32[1152,128]{1,0:T(8,128)S(1)}, u32[]{:S(2)}, u32[]{:S(2)}) collective-permute-start(f32[1152,128]{1,0:T(8,128)} %get-tuple-element.44.refs_2_), channel_id=1, source_target_pairs={{0,3},{1,2},{2,1},{3,0},{4,7},{5,6},{6,5},{7,4},{8,11},{9,10},{10,... | collective-permute-start | bytes 1769480 | tf_op jit(solution)/shard_map/ppermute | solution.py:506
  151.1 13.0 %collective-permute-start.13 = (f32[1152,128]{1,0:T(8,128)}, f32[1152,128]{1,0:T(8,128)S(1)}, u32[]{:S(2)}, u32[]{:S(2)}) collective-permute-start(f32[1152,128]{1,0:T(8,128)} %get-tuple-element.46), channel_id=1, source_target_pairs={{0,1},{1,0},{2,3},{3,2},{4,5},{5,4},{6,7},{7,6},{8,9},{9,8},{10,11... | collective-permute-start | bytes 1769480 | tf_op jit(solution)/shard_map/ppermute | solution.py:506
  152.8 12.6 %collective-permute-start.11 = (f32[1152,128]{1,0:T(8,128)}, f32[1152,128]{1,0:T(8,128)}, u32[]{:S(2)}, u32[]{:S(2)}) collective-permute-start(f32[1152,128]{1,0:T(8,128)} %get-tuple-element.43), channel_id=1, source_target_pairs={{0,2},{1,3},{2,0},{3,1},{4,6},{5,7},{6,4},{7,5},{8,10},{9,11},{10,... | collective-permute-start | bytes 1769480 | tf_op jit(solution)/shard_map/ppermute | solution.py:506
  165.4 1.1 copy-start

commit v7 on v6

--- a/solution.py
+++ b/solution.py
@@ -239,7 +239,7 @@
     table_refs, refs = refs[:tables], refs[tables + 1 :]
     cells_refs, tri_ref = refs[:count], refs[count]
     out_refs = refs[count + 1 : 2 * count + 1]
-    rank, place, lon_w, lat_w, near, later, packed, ct_ref, sems, table_sem = refs[2 * count + 1 :]
+    rank, words, got, tab, near, later, packed, ct_ref, sems, table_sem = refs[2 * count + 1 :]
     for n, table_ref in enumerate(table_refs):
 
         @pl.when(meta(count + 1) == n)
@@ -247,88 +247,143 @@
             pltpu.make_async_copy(table_ref, ct_ref, table_sem).start()
 
     rows = rank.shape[1]
+    pairs = rows // 2
     ch = packed.shape[2]
+    window = TAPS + 1
     band = lax.axis_index("lat")
-    lat_total = rows * lax.axis_size("lat")
     origin = (meta(count) * cols).astype(F32)
-
-    def window_of(i):
-        return i - jnp.where(band * rows + i == lat_total - 1, 1, 0)
-
-    glob = lax.broadcasted_iota(jnp.int32, (rows, LANES), 0) + band * rows
-    first = (glob - jnp.where(glob == lat_total - 1, 1, 0) - 1).astype(F32)
     for d in range(count):
         local = cells_refs[d][0, 0] - origin
         mine = (local >= 0.0) & (local < float(cols))
         one = jnp.where(mine, 1.0, 0.0)
         rank[d] = jnp.where(mine, dot(one.astype(BF), tri_ref[...]), -1000.0)
-        place[d] = local
-        turn = cells_refs[d][0, 1] - first
-        a = spline_weights(cells_refs[d][0, 2])
-        for n, w in enumerate(spline_weights(cells_refs[d][0, 3])):
-            lon_w[d, n] = w * one
-        for e in range(TAPS):
-            total = jnp.zeros_like(one)
-            for t in range(3):
-                if 0 <= e - t < 4:
-                    total = jnp.where(turn == float(t), a[e - t], total)
-            lat_w[d, e] = total
+        parts = [local, cells_refs[d][0, 1] - (band * rows - UP).astype(F32)]
+        for w in (2, 3):
+            left = cells_refs[d][0, w]
+            for _ in range(3):
+                part = left.astype(BF).astype(F32)
+                parts.append(part)
+                left = left - part
+        for w, part in enumerate(parts):
+            words[d, :, w, :] = part
     for buffer in (near, later):
         for k in range(3):
             buffer[k * LANES + span : (k + 1) * LANES] = jnp.zeros((LANES - span, count * LANES), BF)
-    column = lax.broadcasted_iota(jnp.int32, (span, LANES), 0).astype(F32)
-    step = lax.broadcasted_iota(jnp.int32, (8, LANES), 0)
-
-    def build(i, buffer):
-        here = pl.ds(i, 1)
+    column = lax.broadcasted_iota(jnp.int32, (span, count * LANES), 0).astype(F32)
+    slot = lax.broadcasted_iota(jnp.int32, (LANES, LANES), 0)
+    place = slot.astype(F32)
+
+    def spot(j, d):
+        start = meta(count + 2 + d) + 2 * j
+        base = base_ref[start]
+        return base, lax.rem(base, 8), base_ref[start + 1] - base, base_ref[start + 2] - base
+
+    def gather(j, lap):
+        i = 2 * j
+        found = []
         for d in range(count):
-            far = column - place[d, here]
-            basis = jnp.where(far == 0.0, lon_w[d, 0, here], 0.0)
-            for n in range(1, 4):
-                basis = jnp.where(far == float(n), lon_w[d, n, here], basis)
-            high, low = split(basis)
-            lanes = pl.ds(d * LANES, LANES)
-            buffer[0:span, lanes] = high
-            buffer[LANES : LANES + span, lanes] = high
-            buffer[2 * LANES : 2 * LANES + span, lanes] = low
-
-    def emit(i, buffer):
-        half = TAPS // 2
+            _, odd, count_first, _ = spot(j, d)
+            skip = odd - lap * LANES
+            picks = [
+                jnp.where(place == rank[d, pl.ds(i, 1)] + skip.astype(F32), 1.0, 0.0),
+                jnp.where(place == rank[d, pl.ds(i + 1, 1)] + (skip + count_first).astype(F32), 1.0, 0.0),
+            ]
+            found.append(
+                lax.dot_general(
+                    jnp.concatenate([words[d, i], words[d, i + 1]], axis=1).astype(BF),
+                    jnp.concatenate(picks, axis=1).astype(BF),
+                    (((1,), (1,)), ((), ())),
+                    preferred_element_type=F32,
+                )
+            )
+        return found
+
+    def keep(j, found):
+        for d in range(count):
+            got[j, :, d * LANES : (d + 1) * LANES] = found[d]
+
+    def weigh(read, write, first):
+        a = spline_weights(read(2) + read(3) + read(4))
+        b = spline_weights(read(5) + read(6) + read(7))
+        turn = read(1) - 1.0 - first
+        write(0, read(0))
+        for n in range(4):
+            write(1 + n, b[n])
+        for e in range(window):
+            total = jnp.zeros_like(turn)
+            for t in range(4):
+                if 0 <= e - t < 4:
+                    total = jnp.where(turn == float(t), a[e - t], total)
+            write(5 + e, total)
+
+    def write_all(n, value):
+        tab[:, n, :] = value
+
+    def build(j, buffer):
+        far = column - tab[j, 0:1]
+        basis = jnp.where(far == 0.0, tab[j, 1:2], 0.0)
+        for n in range(1, 4):
+            basis = jnp.where(far == float(n), tab[j, 1 + n : 2 + n], basis)
+        high, low = split(basis)
+        buffer[0:span] = high
+        buffer[LANES : LANES + span] = high
+        buffer[2 * LANES : 2 * LANES + span] = low
+
+    def emit(j, buffer, lap):
+        half = window * ch // 2
         lines = []
         for part in range(2):
-            at = pl.multiple_of((window_of(i) + part * half) * ch, ch)
-            lines.append(dot(ct_ref[pl.ds(at, half * ch)], buffer[...]))
+            first = pl.multiple_of(2 * j * ch + part * half, half)
+            lines.append(dot(ct_ref[pl.ds(first, half)], buffer[...]))
+        lines = jnp.concatenate(lines, axis=0)
+        terms = [lines[e * ch : (e + 1) * ch] * tab[j, 5 + e : 6 + e] for e in range(window)]
+        value = ((terms[0] + terms[1]) + (terms[2] + terms[3])) + ((terms[4] + terms[5]) + terms[6])
         for d in range(count):
-            terms = []
-            for e in range(TAPS):
-                block = lines[e // half][e % half * ch : (e % half + 1) * ch, d * LANES : (d + 1) * LANES]
-                terms.append(block * lat_w[d, e, pl.ds(i, 1)])
-            value = ((terms[0] + terms[1]) + terms[2]) + ((terms[3] + terms[4]) + terms[5])
-            high, low = split(value)
-            base = base_ref[meta(count + 2 + d) + i]
-            odd = lax.rem(base, 8)
-            spot = rank[d, pl.ds(i, 1)] + odd.astype(F32)
-            pick = jnp.where(column == spot, 1.0, 0.0).astype(BF)
-            got = lax.dot_general(
-                jnp.concatenate([pick, pick], axis=1),
-                jnp.concatenate([high, low], axis=1),
-                (((1,), (1,)), ((), ())),
-                preferred_element_type=F32,
-            )
-            at = pl.multiple_of(base - odd, 8)
-            packed[d, pl.ds(at, 8)] = jnp.where(step < odd, packed[d, pl.ds(at, 8)], got[:8])
-            packed[d, pl.ds(pl.multiple_of(at + 8, 8), span - 8)] = got[8:]
-
+            turned = value[:, d * LANES : (d + 1) * LANES].T
+            base, odd, _, total = spot(j, d)
+            to = pl.multiple_of(base - odd + lap * LANES, 8)
+            if lap:
+                whole = pl.ds(to, LANES)
+                packed[d, whole] = jnp.where(slot < odd + total - lap * LANES, turned, packed[d, whole])
+            else:
+                packed[d, pl.ds(to, 8)] = jnp.where(slot[:8] < odd, packed[d, pl.ds(to, 8)], turned[:8])
+                packed[d, pl.ds(pl.multiple_of(to + 8, 8), LANES - 8)] = turned[8:]
+
+    @pl.loop(0, pairs // 2)
+    def _(k):
+        found = [gather(2 * k, 0), gather(2 * k + 1, 0)]
+        keep(2 * k, found[0])
+        keep(2 * k + 1, found[1])
+
+    even = 2 * lax.broadcasted_iota(jnp.int32, (pairs, count * LANES), 0)
+    weigh(lambda w: got[:, w, :], write_all, even.astype(F32))
     build(0, near)
     pltpu.make_async_copy(table_refs[0], ct_ref, table_sem).wait()
 
-    @pl.loop(0, rows // 2)
-    def _(pair):
-        i = 2 * pair
-        emit(i, near)
-        build(i + 1, later)
-        emit(i + 1, later)
-        build(jnp.minimum(i + 2, rows - 1), near)
+    @pl.loop(0, pairs // 2)
+    def _(k):
+        emit(2 * k, near, 0)
+        build(2 * k + 1, later)
+        emit(2 * k + 1, later, 0)
+        build(jnp.minimum(2 * k + 2, pairs - 1), near)
+
+    @pl.loop(0, pairs)
+    def _(j):
+        over = False
+        for d in range(count):
+            _, odd, _, total = spot(j, d)
+            over = over | (odd + total > LANES)
+
+        @pl.when(over)
+        def _():
+            keep(j, gather(j, 1))
+
+            def write_one(n, value):
+                tab[j, n : n + 1] = value
+
+            weigh(lambda w: got[j, w : w + 1], write_one, (2 * j).astype(F32))
+            build(j, near)
+            emit(j, near, 1)
 
     copies = [
         pltpu.make_async_copy(packed.at[d, pl.ds(0, cap)], out_refs[d], sems.at[d]) for d in range(count)
@@ -360,12 +415,12 @@
             out_specs=[pl.BlockSpec(memory_space=pl.ANY)] * count,
             scratch_shapes=[
                 pltpu.VMEM((count, rows, lanes), F32),
-                pltpu.VMEM((count, rows, lanes), F32),
-                pltpu.VMEM((count, 4, rows, lanes), F32),
-                pltpu.VMEM((count, TAPS, rows, lanes), F32),
+                pltpu.VMEM((count, rows, 8, lanes), F32),
+                pltpu.VMEM((rows // 2, 8, count * lanes), F32),
+                pltpu.VMEM((rows // 2, 16, count * lanes), F32),
                 weights,
                 weights,
-                pltpu.VMEM((count, cap + span + 8, ch), F32),
+                pltpu.VMEM((count, cap + 2 * lanes + 8, ch), F32),
                 pltpu.VMEM(tables[0].shape, BF),
                 pltpu.SemaphoreType.DMA((count,)),
                 pltpu.SemaphoreType.DMA,
@@ -431,7 +486,7 @@
 def bases(ones):
     rows = ones.shape[1]
     totals = jnp.sum(ones, axis=2)
-    return jnp.dot(totals, jnp.asarray(np.triu(np.ones((rows, rows)), 1), F32), precision=lax.Precision.HIGHEST)
+    return jnp.dot(totals, jnp.asarray(np.triu(np.ones((rows, rows + 1)), 1), F32), precision=lax.Precision.HIGHEST)
 
 
 def transport(tracers, owners, columns, lat_shift, fractions):
@@ -470,7 +525,7 @@
     every = jnp.arange(sectors, dtype=jnp.int32)
     mask = late_owner[None] == every[:, None, None]
     before, own_base = earlier(mask)
-    slot = jnp.sum(jnp.where(mask, before + own_base[:, :, None], 0.0), axis=0).astype(jnp.int32)
+    slot = jnp.sum(jnp.where(mask, before + own_base[:, :-1, None], 0.0), axis=0).astype(jnp.int32)
     q = late_owner // quarter
     alike = ((q == 1) | (q == 2)) == middle
     early = ((q == 1) | (q == 2)) == (q // 2 == mine // 2)
@@ -488,7 +543,7 @@
             which = int(group >= 2 and k in (1, 2))
             dests = [at(goals[group][k], (o + a) % quarter) for a in pair]
             row += dests + [dict(mirror).get(s, s) if which else s, which]
-            row += [(which * sectors + dest) * rows for dest in dests]
+            row += [(which * sectors + dest) * (rows + 1) for dest in dests]
         plan.append(row)
     meta = jnp.asarray(np.array(plan, np.int32))[me]
 

time: 174 us -> 176 us (1.011)
  Pallas kernels: 105 us -> 70.4 us
  starting transfers between devices: 45.5 us -> 80.1 us
  waiting for transfers between devices: 11.4 us -> 13.5 us
    ppermute x7, starting transfers between devices: 25.6 us -> 60.2 us  [transport(): value = lax.ppermute(value, 'lon', moves)]
    pallas_call x4, Pallas kernels: 79.4 us -> 44.9 us  [taps(): pl.pallas_call(functools.partial(tap_kernel, tables=len(tables), count=co...]
    ppermute x7, waiting for transfers between devices: 8.85 us -> 10.9 us  [transport(): value = lax.ppermute(value, 'lon', moves)]
  transfers between devices with their start and end apart: 15 -> 15, of which waited for: 4 -> 4; matrix products, arithmetic and copies ran while one was open for 3% -> 3% of each run, Pallas kernels for 55% -> 35%
where the time goes in v7:
time: 176 us; the launch traced here: 175 us
  starting transfers between devices  80.1 us (46%)
  Pallas kernels  70.4 us (40%)
  waiting for transfers between devices  13.5 us (8%)
  local copies, waits for them, and re-layouts  8.03 us (5%)
  other arithmetic  2.34 us (1%)
    ppermute x7, starting transfers between devices, transport(): value = lax.ppermute(value, 'lon', moves)  60.2 us
    pallas_call x4, Pallas kernels, taps(): pl.pallas_call(functools.partial(tap_kernel, tables=len(tables), count=co...  44.9 us
    ppermute x7, waiting for transfers between devices, transport(): value = lax.ppermute(value, 'lon', moves)  10.9 us
    pallas_call x2, Pallas kernels, lon_solve(): pl.pallas_call(functools.partial(lon_kernel, packed=packed), out_shape=sh...  9.06 us
    pallas_call x2, Pallas kernels, lat_solve(): pl.pallas_call(functools.partial(lat_kernel, pieces=len(pieces), head=hea...  7.31 us
    all_to_all x1, starting transfers between devices, transport(): lax.all_to_all(words, 'lon', split_axis=0, concat_axis=0, tiled=True)  7.28 us
    pallas_call x1, Pallas kernels, place(): pl.pallas_call(functools.partial(place_kernel, cap=cap), out_shape=jax.Sh...  6.36 us
  transfers between devices with their start and end apart: 15, of which 4 were waited for; matrix products, arithmetic and copies ran while one was open for 3% of the time, Pallas kernels for 35%

profile of v7, /device:TPU:0, one launch (start us, length us, event | category | flops | bytes accessed | tf_op | source)
XLA Modules:
  0.0 175.1 jit_solution(7644083131673918053)
XLA Ops:
  0.0 0.5 broadcast.42
  0.5 1.4 reduce.4
  1.9 0.7 reshape.22.owner_ref
  2.6 2.7 %edges.1 = (f32[3,96,128]{2,1,0:T(8,128)}, f32[4,96,128]{2,1,0:T(8,128)}, f32[3,96,128]{2,1,0:T(8,128)}, f32[4,96,128]{2,1,0:T(8,128)}, f32[8,4,32,128]{3,2,1,0:T(8,128)}) custom-call(f32[32,96,128]{2,1,0:T(8,128)} %refs_0_.1, s32[32,96]{1,0:T(8,128)} %reshape.22.owner_ref, s32[32,96]{1,0:T(8,128)} %column_ref.1, s32[32,96]{1,0:T(8,128)} %shift_ref.1, ...), custom_call_target="tpu_custom_call" | custom-call | flops 2359296 | bytes 2359296 | tf_op jit(solution)/shard_map/edges/pallas_call | solution.py:94
  5.3 7.3 %all-to-all-start = ((f32[8,4,32,128]{3,2,1,0:T(8,128)}), f32[8,4,32,128]{3,2,1,0:T(8,128)S(1)}, u32[]{:S(2)}, u32[]{:S(2)}) async-start(f32[8,4,32,128]{3,2,1,0:T(8,128)} %get-tuple-element.32), calls=%async_computation | async-start | bytes 1048576 | tf_op jit(solution)/shard_map/all_to_all | solution.py:511
  12.6 1.3 collective-permute-start.1
  13.9 3.0 %collective-permute-start = (f32[3,96,128]{2,1,0:T(8,128)}, f32[3,96,128]{2,1,0:T(8,128)S(1)}, u32[]{:S(2)}, u32[]{:S(2)}) collective-permute-start(f32[3,96,128]{2,1,0:T(8,128)} %get-tuple-element.26), channel_id=1, source_target_pairs={{0,8},{8,16},{16,24},{1,9},{9,17},{17,25},{2,10},{10,18},{18,26},{... | collective-permute-start | bytes 442376 | tf_op jit(solution)/shard_map/ppermute | solution.py:509
  16.9 1.0 slice.11
  17.9 1.6 collective-permute-start.8
  19.5 1.3 dynamic-slice_bitcast_fusion.1.meta_ref
  20.8 0.6 copy-done.6
  21.4 0.1 copy-done.5
  21.5 3.9 %lat_solve.2 = (f32[37,96,128]{2,1,0:T(8,128)}, f32[2,37,128]{2,1,0:T(8,128)}, f32[3,37,128]{2,1,0:T(8,128)}, f32[23,96,128]{2,1,0:T(8,128)}) custom-call(f32[32,96,128]{2,1,0:T(8,128)} %refs_0_.1, f32[3,96,128]{2,1,0:T(8,128)} %copy-done.6, f32[4,96,128]{2,1,0:T(8,128)} %copy-done.5, f32[3,96,128]{2,1,0:T(8,128)} %get-tuple-element.28.refs_3_, ...), custom_call_target="tpu_custom_call" | custom-call | flops 3932160 | bytes 3932160 | tf_op jit(solution)/shard_map/lat_solve/pallas_call | solution.py:177
  25.4 2.0 %collective-permute-start.2 = (f32[2,37,128]{2,1,0:T(8,128)}, f32[2,37,128]{2,1,0:T(8,128)S(1)}, u32[]{:S(2)}, u32[]{:S(2)}) collective-permute-start(f32[2,37,128]{2,1,0:T(8,128)} %get-tuple-element.33), channel_id=1, source_target_pairs={{0,1},{1,2},{2,3},{3,4},{4,5},{5,6},{6,7},{7,0},{8,9},{9,10},{10,1... | collective-permute-start | bytes 113672 | tf_op jit(solution)/shard_map/ppermute | solution.py:514
  27.4 2.8 %collective-permute-start.3 = (f32[3,37,128]{2,1,0:T(8,128)}, f32[3,37,128]{2,1,0:T(8,128)S(1)}, u32[]{:S(2)}, u32[]{:S(2)}) collective-permute-start(f32[3,37,128]{2,1,0:T(8,128)} %get-tuple-element.34), channel_id=1, source_target_pairs={{1,0},{2,1},{3,2},{4,3},{5,4},{6,5},{7,6},{0,7},{9,8},{10,9},{11,1... | collective-permute-start | bytes 170504 | tf_op jit(solution)/shard_map/ppermute | solution.py:515
  30.2 0.7 dynamic-slice_bitcast_fusion
  30.9 0.7 collective-permute-start.9
  31.6 0.8 collective-permute-done.2.refs_0_
  32.4 1.7 collective-permute-done.3.refs_1_
  34.2 0.6 copy-done.8
  34.8 4.5 %lon_solve.2 = (bf16[4736,384]{1,0:T(8,128)(2,1)}, f32[5,37,128]{2,1,0:T(8,128)}) custom-call(f32[37,96,128]{2,1,0:T(8,128)} %get-tuple-element.30.x_ref, f32[2,37,128]{2,1,0:T(8,128)} %copy-done.9, f32[3,37,128]{2,1,0:T(8,128)} %copy-done.8, bf16[384,128]{1,0:T(8,128)(2,1)} %constant.103.refs_2_.refs_1_), custom_call_target="tpu_custom_call" | custom-call | flops 465567744 | bytes 3637248 | tf_op jit(solution)/shard_map/lon_solve/pallas_call | solution.py:226
  39.3 1.3 collective-permute-start.10
  40.6 0.2 convert_reduce_fusion
  40.8 0.1 convolution_convert_fusion
  40.9 0.7 reshape.24.base_ref
  41.6 11.2 %taps.4 = (f32[1152,128]{1,0:T(8,128)}, f32[1152,128]{1,0:T(8,128)}) custom-call(s32[24]{0:T(128)} %dynamic-slice_bitcast_fusion.1.meta_ref, s32[528]{0:T(1024)} %reshape.24.base_ref, bf16[4736,384]{1,0:T(8,128)(2,1)} %get-tuple-element.35.refs_0_.refs_1_, bf16[4736,384]{1,0:T(8,128)(2,1)} %get-tuple-element.35.refs_0_.refs_1_, f32[8,4,32,128]{3,2,1,0:T(8,128)} %copy-done.3, ...), custom_call_target="tpu_custom_call" | custom-call | flops 4831838208 | bytes 3637248 | tf_op jit(solution)/shard_map/taps/pallas_call | solution.py:403
  52.9 13.5 %collective-permute-start.4 = (f32[1152,128]{1,0:T(8,128)}, f32[1152,128]{1,0:T(8,128)S(1)}, u32[]{:S(2)}, u32[]{:S(2)}) collective-permute-start(f32[1152,128]{1,0:T(8,128)} %get-tuple-element.36), channel_id=1, source_target_pairs={{0,4},{1,5},{2,0},{3,1},{4,6},{5,7},{6,2},{7,3},{8,12},{9,13},{10,... | collective-permute-start | bytes 1769480 | tf_op jit(solution)/shard_map/ppermute | solution.py:561
  66.4 2.7 %collective-permute-start.5 = (f32[1152,128]{1,0:T(8,128)}, f32[1152,128]{1,0:T(8,128)S(1)}, u32[]{:S(2)}, u32[]{:S(2)}) collective-permute-start(f32[1152,128]{1,0:T(8,128)} %get-tuple-element.37.refs_1_), channel_id=1, source_target_pairs={{0,5},{1,4},{2,1},{3,0},{4,7},{5,6},{6,3},{7,2},{8,13},{9,12},{10,... | collective-permute-start | bytes 1769480 | tf_op jit(solution)/shard_map/ppermute | solution.py:561
  69.0 11.2 %taps.5 = (f32[1152,128]{1,0:T(8,128)}, f32[1152,128]{1,0:T(8,128)}) custom-call(s32[24]{0:T(128)} %dynamic-slice_bitcast_fusion.1.meta_ref, s32[528]{0:T(1024)} %reshape.24.base_ref, bf16[4736,384]{1,0:T(8,128)(2,1)} %get-tuple-element.35.refs_0_.refs_1_, f32[1152,128]{1,0:T(8,128)} %get-tuple-element.37.refs_1_, f32[8,4,32,128]{3,2,1,0:T(8,128)} %copy-done.3, ...), custom_call_target="tpu_custom_call" | custom-call | flops 4831838208 | bytes 3637248 | tf_op jit(solution)/shard_map/taps/pallas_call | solution.py:403
  80.2 3.0 %collective-permute-start.6 = (f32[1152,128]{1,0:T(8,128)}, f32[1152,128]{1,0:T(8,128)S(1)}, u32[]{:S(2)}, u32[]{:S(2)}) collective-permute-start(f32[1152,128]{1,0:T(8,128)} %get-tuple-element.38), channel_id=1, source_target_pairs={{0,6},{1,7},{2,2},{3,3},{4,4},{5,5},{6,0},{7,1},{8,14},{9,15},{10,... | collective-permute-start | bytes 1769480 | tf_op jit(solution)/shard_map/ppermute | solution.py:561
  83.3 0.0 copy-start.2
  83.3 2.9 %collective-permute-start.7 = (f32[1152,128]{1,0:T(8,128)}, f32[1152,128]{1,0:T(8,128)S(1)}, u32[]{:S(2)}, u32[]{:S(2)}) collective-permute-start(f32[1152,128]{1,0:T(8,128)} %get-tuple-element.39.refs_2_), channel_id=1, source_target_pairs={{0,7},{1,6},{2,3},{3,2},{4,5},{5,4},{6,1},{7,0},{8,15},{9,14},{10,... | collective-permute-start | bytes 1769480 | tf_op jit(solution)/shard_map/ppermute | solution.py:561
  86.2 3.4 %lat_solve.3 = (f32[37,96,128]{2,1,0:T(8,128)}, f32[2,37,128]{2,1,0:T(8,128)}, f32[3,37,128]{2,1,0:T(8,128)}) custom-call(f32[16,96,128]{2,1,0:T(8,128)} %collective-permute-done.8.refs_0_, f32[23,96,128]{2,1,0:T(8,128)} %copy-done.2, f32[96,128]{1,0:T(8,128)} %constant.90.clone.refs_5_.refs_2_, f32[96,128]{1,0:T(8,128)} %constant.91.clone.refs_6_.refs_3_), custom_call_target="tpu_custom_call" | custom-call | flops 3932160 | bytes 3932160 | tf_op jit(solution)/shard_map/lat_solve/pallas_call | solution.py:177
  89.6 4.6 %lon_solve.3.refs_1_ = bf16[4736,384]{1,0:T(8,128)(2,1)} custom-call(f32[37,96,128]{2,1,0:T(8,128)} %get-tuple-element.41.x_ref, f32[5,37,128]{2,1,0:T(8,128)} %collective-permute-done.10.refs_0_, bf16[384,128]{1,0:T(8,128)(2,1)} %constant.103.refs_2_.refs_1_), custom_call_target="tpu_custom_call" | custom-call | flops 465567744 | bytes 3637248 | tf_op jit(solution)/shard_map/lon_solve/pallas_call | solution.py:226
  94.2 11.2 %taps.6 = (f32[1152,128]{1,0:T(8,128)}, f32[1152,128]{1,0:T(8,128)}) custom-call(s32[24]{0:T(128)} %dynamic-slice_bitcast_fusion.1.meta_ref, s32[528]{0:T(1024)} %reshape.24.base_ref, bf16[4736,384]{1,0:T(8,128)(2,1)} %get-tuple-element.35.refs_0_.refs_1_, bf16[4736,384]{1,0:T(8,128)(2,1)} %lon_solve.3.refs_1_, f32[1152,128]{1,0:T(8,128)} %get-tuple-element.39.refs_2_, ...), custom_call_target="tpu_custom_call" | custom-call | flops 4831838208 | bytes 3637248 | tf_op jit(solution)/shard_map/taps/pallas_call | solution.py:403
  105.4 0.0 copy-start.10
  105.4 37.0 %collective-permute-start.12 = (f32[1152,128]{1,0:T(8,128)}, f32[1152,128]{1,0:T(8,128)S(1)}, u32[]{:S(2)}, u32[]{:S(2)}) collective-permute-start(f32[1152,128]{1,0:T(8,128)} %get-tuple-element.44.refs_2_), channel_id=1, source_target_pairs={{0,3},{1,2},{2,1},{3,0},{4,7},{5,6},{6,5},{7,4},{8,11},{9,10},{10,... | collective-permute-start | bytes 1769480 | tf_op jit(solution)/shard_map/ppermute | solution.py:561
  142.4 11.3 %taps.7 = (f32[1152,128]{1,0:T(8,128)}, f32[1152,128]{1,0:T(8,128)}) custom-call(s32[24]{0:T(128)} %dynamic-slice_bitcast_fusion.1.meta_ref, s32[528]{0:T(1024)} %reshape.24.base_ref, bf16[4736,384]{1,0:T(8,128)(2,1)} %get-tuple-element.35.refs_0_.refs_1_, bf16[4736,384]{1,0:T(8,128)(2,1)} %lon_solve.3.refs_1_, f32[1152,128]{1,0:T(8,128)} %get-tuple-element.44.refs_2_, ...), custom_call_target="tpu_custom_call" | custom-call | flops 4831838208 | bytes 3637248 | tf_op jit(solution)/shard_map/taps/pallas_call | solution.py:403
  153.7 1.1 collective-permute-start.13
  154.8 0.1 convert_reduce_fusion.1
  154.9 0.1 fusion.11
  155.0 0.2 fusion.1
  155.2 0.6 fusion.10
  155.8 0.8 reshape.23.target_ref
  156.6 10.3 %collective-permute-done.13.refs_7_ = f32[1152,128]{1,0:T(8,128)S(1)} collective-permute-done((f32[1152,128]{1,0:T(8,128)}, f32[1152,128]{1,0:T(8,128)S(1)}, u32[]{:S(2)}, u32[]{:S(2)}) %collective-permute-start.13) | collective-permute-done | bytes 589856 | tf_op jit(solution)/shard_map/ppermute | solution.py:561
  167.0 0.6 collective-permute-done.11.refs_4_
  167.5 1.1 copy-done
  168.6 6.4 %place.1 = f32[3072,128]{1,0:T(8,128)} custom-call(s32[3072]{0:T(1024)S(1)} %reshape.23.target_ref, f32[1152,128]{1,0:T(8,128)S(1)} %collective-permute-done.4.refs_0_, f32[1152,128]{1,0:T(8,128)S(1)} %collective-permute-done.5.refs_1_, f32[1152,128]{1,0:T(8,128)S(1)} %collective-permute-done.6.refs_2_, f32[1152,128]{1,0:T(8,128)S(1)} %collective-permute-done.7.refs_3_, ...), custom_call_target="tpu_custom_call" | custom-call | bytes 9437184 | tf_op jit(solution)/shard_map/place/pallas_call | solution.py:458
  (29 shorter events, 0.1 us)
Async XLA Ops:
  0.0 16.9 %copy-start.1 = (f32[32,96,128]{2,1,0:T(8,128)S(1)}, f32[32,96,128]{2,1,0:T(8,128)}, u32[]{:S(2)}) copy-start(f32[32,96,128]{2,1,0:T(8,128)} %refs_0_.1) | copy-start | bytes 4718596
  5.3 35.3 %all-to-all-start = ((f32[8,4,32,128]{3,2,1,0:T(8,128)}), f32[8,4,32,128]{3,2,1,0:T(8,128)S(1)}, u32[]{:S(2)}, u32[]{:S(2)}) async-start(f32[8,4,32,128]{3,2,1,0:T(8,128)} %get-tuple-element.32), calls=%async_computation | async-start | bytes 1048576 | tf_op jit(solution)/shard_map/all_to_all | solution.py:511
  12.6 8.2 %collective-permute-start.1 = (f32[4,96,128]{2,1,0:T(8,128)}, f32[4,96,128]{2,1,0:T(8,128)S(1)}, u32[]{:S(2)}, u32[]{:S(2)}) collective-permute-start(f32[4,96,128]{2,1,0:T(8,128)} %get-tuple-element.27), channel_id=1, source_target_pairs={{8,0},{16,8},{24,16},{9,1},{17,9},{25,17},{10,2},{18,10},{26,18},{... | collective-permute-start | bytes 589832 | tf_op jit(solution)/shard_map/ppermute | solution.py:510
  13.9 6.9 %collective-permute-start = (f32[3,96,128]{2,1,0:T(8,128)}, f32[3,96,128]{2,1,0:T(8,128)S(1)}, u32[]{:S(2)}, u32[]{:S(2)}) collective-permute-start(f32[3,96,128]{2,1,0:T(8,128)} %get-tuple-element.26), channel_id=1, source_target_pairs={{0,8},{8,16},{16,24},{1,9},{9,17},{17,25},{2,10},{10,18},{18,26},{... | collective-permute-start | bytes 442376 | tf_op jit(solution)/shard_map/ppermute | solution.py:509
  17.9 62.3 %collective-permute-start.8 = (f32[16,96,128]{2,1,0:T(8,128)}, f32[16,96,128]{2,1,0:T(8,128)}, u32[]{:S(2)}, u32[]{:S(2)}) collective-permute-start(f32[16,96,128]{2,1,0:T(8,128)} %slice.11), channel_id=1, source_target_pairs={{2,4},{3,5},{4,2},{5,3},{10,12},{11,13},{12,10},{13,11},{18,20},{1... | collective-permute-start | bytes 2359304 | tf_op jit(solution)/shard_map/ppermute | solution.py:506
  20.7 0.7 copy-start.6
  20.7 0.7 copy-start.5
  25.4 15.4 %copy-start.7 = (f32[32,33]{1,0:T(8,128)S(1)}, f32[32,33]{1,0:T(8,128)}, u32[]{:S(2)}) copy-start(f32[32,33]{1,0:T(8,128)} %constant.93.clone) | copy-start | bytes 12676
  25.4 7.0 %collective-permute-start.2 = (f32[2,37,128]{2,1,0:T(8,128)}, f32[2,37,128]{2,1,0:T(8,128)S(1)}, u32[]{:S(2)}, u32[]{:S(2)}) collective-permute-start(f32[2,37,128]{2,1,0:T(8,128)} %get-tuple-element.33), channel_id=1, source_target_pairs={{0,1},{1,2},{2,3},{3,4},{4,5},{5,6},{6,7},{7,0},{8,9},{9,10},{10,1... | collective-permute-start | bytes 113672 | tf_op jit(solution)/shard_map/ppermute | solution.py:514
  27.4 6.7 %collective-permute-start.3 = (f32[3,37,128]{2,1,0:T(8,128)}, f32[3,37,128]{2,1,0:T(8,128)S(1)}, u32[]{:S(2)}, u32[]{:S(2)}) collective-permute-start(f32[3,37,128]{2,1,0:T(8,128)} %get-tuple-element.34), channel_id=1, source_target_pairs={{1,0},{2,1},{3,2},{4,3},{5,4},{6,5},{7,6},{0,7},{9,8},{10,9},{11,1... | collective-permute-start | bytes 170504 | tf_op jit(solution)/shard_map/ppermute | solution.py:515
  30.9 52.4 %collective-permute-start.9 = (f32[23,96,128]{2,1,0:T(8,128)}, f32[23,96,128]{2,1,0:T(8,128)S(1)}, u32[]{:S(2)}, u32[]{:S(2)}) collective-permute-start(f32[23,96,128]{2,1,0:T(8,128)} %get-tuple-element.40), channel_id=1, source_target_pairs={{2,4},{3,5},{4,2},{5,3},{10,12},{11,13},{12,10},{13,11},{18,20},{1... | collective-permute-start | bytes 3391496 | tf_op jit(solution)/shard_map/ppermute | solution.py:522
  32.4 1.8 %copy-start.9 = (f32[2,37,128]{2,1,0:T(8,128)}, f32[2,37,128]{2,1,0:T(8,128)S(1)}, u32[]{:S(2)}) copy-start(f32[2,37,128]{2,1,0:T(8,128)S(1)} %collective-permute-done.2.refs_0_) | copy-start | bytes 113668
  34.1 0.6 copy-start.8
  39.3 50.3 %collective-permute-start.10 = (f32[5,37,128]{2,1,0:T(8,128)}, f32[5,37,128]{2,1,0:T(8,128)}, u32[]{:S(2)}, u32[]{:S(2)}) collective-permute-start(f32[5,37,128]{2,1,0:T(8,128)} %get-tuple-element.42), channel_id=1, source_target_pairs={{2,4},{3,5},{4,2},{5,3},{10,12},{11,13},{12,10},{13,11},{18,20},{1... | collective-permute-start | bytes 284168 | tf_op jit(solution)/shard_map/ppermute | solution.py:523
  40.6 1.1 copy-start.3
  52.9 100.8 %collective-permute-start.4 = (f32[1152,128]{1,0:T(8,128)}, f32[1152,128]{1,0:T(8,128)S(1)}, u32[]{:S(2)}, u32[]{:S(2)}) collective-permute-start(f32[1152,128]{1,0:T(8,128)} %get-tuple-element.36), channel_id=1, source_target_pairs={{0,4},{1,5},{2,0},{3,1},{4,6},{5,7},{6,2},{7,3},{8,12},{9,13},{10,... | collective-permute-start | bytes 1769480 | tf_op jit(solution)/shard_map/ppermute | solution.py:561
  66.4 88.4 %collective-permute-start.5 = (f32[1152,128]{1,0:T(8,128)}, f32[1152,128]{1,0:T(8,128)S(1)}, u32[]{:S(2)}, u32[]{:S(2)}) collective-permute-start(f32[1152,128]{1,0:T(8,128)} %get-tuple-element.37.refs_1_), channel_id=1, source_target_pairs={{0,5},{1,4},{2,1},{3,0},{4,7},{5,6},{6,3},{7,2},{8,13},{9,12},{10,... | collective-permute-start | bytes 1769480 | tf_op jit(solution)/shard_map/ppermute | solution.py:561
  80.2 76.4 %collective-permute-start.6 = (f32[1152,128]{1,0:T(8,128)}, f32[1152,128]{1,0:T(8,128)S(1)}, u32[]{:S(2)}, u32[]{:S(2)}) collective-permute-start(f32[1152,128]{1,0:T(8,128)} %get-tuple-element.38), channel_id=1, source_target_pairs={{0,6},{1,7},{2,2},{3,3},{4,4},{5,5},{6,0},{7,1},{8,14},{9,15},{10,... | collective-permute-start | bytes 1769480 | tf_op jit(solution)/shard_map/ppermute | solution.py:561
  83.3 2.9 %copy-start.2 = (f32[23,96,128]{2,1,0:T(8,128)}, f32[23,96,128]{2,1,0:T(8,128)S(1)}, u32[]{:S(2)}) copy-start(f32[23,96,128]{2,1,0:T(8,128)S(1)} %collective-permute-done.9.refs_1_) | copy-start | bytes 3391492
  83.3 73.4 %collective-permute-start.7 = (f32[1152,128]{1,0:T(8,128)}, f32[1152,128]{1,0:T(8,128)S(1)}, u32[]{:S(2)}, u32[]{:S(2)}) collective-permute-start(f32[1152,128]{1,0:T(8,128)} %get-tuple-element.39.refs_2_), channel_id=1, source_target_pairs={{0,7},{1,6},{2,3},{3,2},{4,5},{5,4},{6,1},{7,0},{8,15},{9,14},{10,... | collective-permute-start | bytes 1769480 | tf_op jit(solution)/shard_map/ppermute | solution.py:561
  105.4 49.4 %copy-start.4 = (s32[32,96]{1,0:T(8,128)S(1)}, s32[32,96]{1,0:T(8,128)}, u32[]{:S(2)}) copy-start(s32[32,96]{1,0:T(8,128)} %reshape.22.owner_ref) | copy-start | bytes 36868
  105.4 49.7 %copy-start.10 = (bf16[96,96,1]{1,0,2:T(8,128)(2,1)S(1)}, bf16[96,96,1]{1,0,2:T(8,128)(2,1)}, u32[]{:S(2)}) copy-start(bf16[96,96,1]{1,0,2:T(8,128)(2,1)} %constant.104) | copy-start | bytes 55300
  105.4 62.1 %collective-permute-start.12 = (f32[1152,128]{1,0:T(8,128)}, f32[1152,128]{1,0:T(8,128)S(1)}, u32[]{:S(2)}, u32[]{:S(2)}) collective-permute-start(f32[1152,128]{1,0:T(8,128)} %get-tuple-element.44.refs_2_), channel_id=1, source_target_pairs={{0,3},{1,2},{2,1},{3,0},{4,7},{5,6},{6,5},{7,4},{8,11},{9,10},{10,... | collective-permute-start | bytes 1769480 | tf_op jit(solution)/shard_map/ppermute | solution.py:561
  153.7 13.2 %collective-permute-start.13 = (f32[1152,128]{1,0:T(8,128)}, f32[1152,128]{1,0:T(8,128)S(1)}, u32[]{:S(2)}, u32[]{:S(2)}) collective-permute-start(f32[1152,128]{1,0:T(8,128)} %get-tuple-element.46), channel_id=1, source_target_pairs={{0,1},{1,0},{2,3},{3,2},{4,5},{5,4},{6,7},{7,6},{8,9},{9,8},{10,11... | collective-permute-start | bytes 1769480 | tf_op jit(solution)/shard_map/ppermute | solution.py:561
  154.8 12.8 %collective-permute-start.11 = (f32[1152,128]{1,0:T(8,128)}, f32[1152,128]{1,0:T(8,128)}, u32[]{:S(2)}, u32[]{:S(2)}) collective-permute-start(f32[1152,128]{1,0:T(8,128)} %get-tuple-element.43), channel_id=1, source_target_pairs={{0,2},{1,3},{2,0},{3,1},{4,6},{5,7},{6,4},{7,5},{8,10},{9,11},{10,... | collective-permute-start | bytes 1769480 | tf_op jit(solution)/shard_map/ppermute | solution.py:561
  167.5 1.1 copy-start

commit v8 on v7

--- a/solution.py
+++ b/solution.py
@@ -234,8 +234,9 @@
     )(x, *sides, jnp.concatenate([high, high, low], axis=0))
 
 
-def tap_kernel(meta_ref, base_ref, *refs, tables, count, cols, cap, span, at):
-    meta = lambda k: meta_ref[at + k]
+def tap_kernel(meta_ref, base_ref, *refs, tables, count, cols, cap, span, width, at):
+    mine_at = lax.axis_index("lon") * width + at
+    meta = lambda k: meta_ref[mine_at + k]
     table_refs, refs = refs[:tables], refs[tables + 1 :]
     cells_refs, tri_ref = refs[:count], refs[count]
     out_refs = refs[count + 1 : 2 * count + 1]
@@ -394,21 +395,23 @@
         copy.wait()
 
 
-def taps(meta, at, count, base, tables, cells, cols, cap, after):
+def taps(meta, width, at, count, base, tables, cells, cols, cap, after):
     _, words, rows, lanes = cells.shape
     ch = tables[0].shape[0] // (rows + UP + DOWN)
     span = 112
     tri = jnp.asarray(np.triu(np.ones((lanes, lanes)), 1), BF)
     weights = pltpu.VMEM((3 * LANES, count * lanes), BF)
     return pl.pallas_call(
-        functools.partial(tap_kernel, tables=len(tables), count=count, cols=cols, cap=cap, span=span, at=at),
+        functools.partial(
+            tap_kernel, tables=len(tables), count=count, cols=cols, cap=cap, span=span, width=width, at=at
+        ),
         out_shape=[jax.ShapeDtypeStruct((cap, ch), F32)] * count,
         grid_spec=pltpu.PrefetchScalarGridSpec(
             num_scalar_prefetch=2,
             grid=(1,),
             in_specs=[pl.BlockSpec(memory_space=pl.ANY)] * (len(tables) + 1)
             + [
-                pl.BlockSpec((1, words, rows, lanes), functools.partial(lambda g, m, b, k: (m[k], 0, 0, 0), k=at + k))
+                pl.BlockSpec((1, words, rows, lanes), functools.partial(lambda g, m, b, k: (m[lax.axis_index("lon") * width + k], 0, 0, 0), k=at + k))
                 for k in range(count)
             ]
             + [pl.BlockSpec(tri.shape, lambda g, m, b: (0, 0))],
@@ -502,7 +505,7 @@
     mine, offset = me // quarter, me % quarter
     middle = (mine == 1) | (mine == 2)
 
-    head = rows // 2
+    head = 5 * rows // 8
     first = lax.ppermute(tracers[:head], "lon", mirror)
     owner = owners.reshape(rows, cols)
     down, up, top, bottom, words = edges(tracers, owner, columns, lat_shift, fractions)
@@ -545,7 +548,7 @@
             row += dests + [dict(mirror).get(s, s) if which else s, which]
             row += [(which * sectors + dest) * (rows + 1) for dest in dests]
         plan.append(row)
-    meta = jnp.asarray(np.array(plan, np.int32))[me]
+    meta, width = jnp.asarray(np.array(plan, np.int32).reshape(-1)), len(plan[0])
 
     parts = [None] * sectors
     tables, done, values = [own], 0, [own]
@@ -553,7 +556,7 @@
         if group == 2 and len(tables) == 1:
             other = lat_solve(rows, head, [first, rest])[0]
             tables = [own, lon_solve(other, sides)[0]]
-        values = taps(meta, done, len(pair), base, tables, asked, cols, cap, values[0])
+        values = taps(meta, width, done, len(pair), base, tables, asked, cols, cap, values[0])
         done += 2 * len(pair) + 2
         for a, value in zip(pair, values):
             moves = [(at(k, o), at(goals[group][k], (o + a) % quarter)) for k in range(4) for o in range(quarter)]

time: 176 us -> 166 us (0.943)
  starting transfers between devices: 80.1 us -> 73.9 us
  waiting for transfers between devices: 13.5 us -> 10.2 us
    ppermute x7, starting transfers between devices: 60.2 us -> 54.6 us  [transport(): value = lax.ppermute(value, 'lon', moves)]
    ppermute x7, waiting for transfers between devices: 10.9 us -> 7.86 us  [transport(): value = lax.ppermute(value, 'lon', moves)]
    unnamed x23 -> x25, local copies, waits for them, and re-layouts: 2.95 us -> 3.58 us
  transfers between devices with their start and end apart: 15 -> 15, of which waited for: 4 -> 3; matrix products, arithmetic and copies ran while one was open for 3% -> 3% of each run, Pallas kernels for 35% -> 37%
where the time goes in v8:
time: 166 us; the launch traced here: 165 us
  starting transfers between devices  73.9 us (45%)
  Pallas kernels  70.5 us (42%)
  waiting for transfers between devices  10.2 us (6%)
  local copies, waits for them, and re-layouts  7.43 us (4%)
  other arithmetic  2.35 us (1%)
    ppermute x7, starting transfers between devices, transport(): value = lax.ppermute(value, 'lon', moves)  54.6 us
    pallas_call x4, Pallas kernels, taps(): pl.pallas_call(functools.partial(tap_kernel, tables=len(tables), count=co...  45 us
    pallas_call x2, Pallas kernels, lon_solve(): pl.pallas_call(functools.partial(lon_kernel, packed=packed), out_shape=sh...  9.07 us
    ppermute x7, waiting for transfers between devices, transport(): value = lax.ppermute(value, 'lon', moves)  7.86 us
    all_to_all x1, starting transfers between devices, transport(): lax.all_to_all(words, 'lon', split_axis=0, concat_axis=0, tiled=True)  7.28 us
    pallas_call x2, Pallas kernels, lat_solve(): pl.pallas_call(functools.partial(lat_kernel, pieces=len(pieces), head=hea...  7.27 us
    pallas_call x1, Pallas kernels, place(): pl.pallas_call(functools.partial(place_kernel, cap=cap), out_shape=jax.Sh...  6.36 us
    unnamed x25, local copies, waits for them, and re-layouts  3.58 us
  transfers between devices with their start and end apart: 15, of which 3 were waited for; matrix products, arithmetic and copies ran while one was open for 3% of the time, Pallas kernels for 37%

profile of v8, /device:TPU:0, one launch (start us, length us, event | category | flops | bytes accessed | tf_op | source)
XLA Modules:
  0.0 165.3 jit_solution(4095523537295499668)
XLA Ops:
  0.0 0.5 broadcast.42
  0.5 1.4 reduce.4
  1.9 0.7 reshape.22.owner_ref
  2.6 2.8 %edges.1 = (f32[3,96,128]{2,1,0:T(8,128)}, f32[4,96,128]{2,1,0:T(8,128)}, f32[3,96,128]{2,1,0:T(8,128)}, f32[4,96,128]{2,1,0:T(8,128)}, f32[8,4,32,128]{3,2,1,0:T(8,128)}) custom-call(f32[32,96,128]{2,1,0:T(8,128)} %refs_0_.1, s32[32,96]{1,0:T(8,128)} %reshape.22.owner_ref, s32[32,96]{1,0:T(8,128)} %column_ref.1, s32[32,96]{1,0:T(8,128)} %shift_ref.1, ...), custom_call_target="tpu_custom_call" | custom-call | flops 2359296 | bytes 2359296 | tf_op jit(solution)/shard_map/edges/pallas_call | solution.py:94
  5.4 7.3 %all-to-all-start = ((f32[8,4,32,128]{3,2,1,0:T(8,128)}), f32[8,4,32,128]{3,2,1,0:T(8,128)S(1)}, u32[]{:S(2)}, u32[]{:S(2)}) async-start(f32[8,4,32,128]{3,2,1,0:T(8,128)} %get-tuple-element.32), calls=%async_computation | async-start | bytes 1048576 | tf_op jit(solution)/shard_map/all_to_all | solution.py:514
  12.6 1.3 collective-permute-start.1
  13.9 3.0 %collective-permute-start = (f32[3,96,128]{2,1,0:T(8,128)}, f32[3,96,128]{2,1,0:T(8,128)S(1)}, u32[]{:S(2)}, u32[]{:S(2)}) collective-permute-start(f32[3,96,128]{2,1,0:T(8,128)} %get-tuple-element.26), channel_id=1, source_target_pairs={{0,8},{8,16},{16,24},{1,9},{9,17},{17,25},{2,10},{10,18},{18,26},{... | collective-permute-start | bytes 442376 | tf_op jit(solution)/shard_map/ppermute | solution.py:512
  17.0 1.0 slice.11
  18.0 0.7 collective-permute-start.8
  18.8 0.6 copy-done.6
  19.4 0.1 copy-done.5
  19.5 3.9 %lat_solve.2 = (f32[37,96,128]{2,1,0:T(8,128)}, f32[2,37,128]{2,1,0:T(8,128)}, f32[3,37,128]{2,1,0:T(8,128)}, f32[19,96,128]{2,1,0:T(8,128)}) custom-call(f32[32,96,128]{2,1,0:T(8,128)} %refs_0_.1, f32[3,96,128]{2,1,0:T(8,128)} %copy-done.6, f32[4,96,128]{2,1,0:T(8,128)} %copy-done.5, f32[3,96,128]{2,1,0:T(8,128)} %get-tuple-element.28.refs_3_, ...), custom_call_target="tpu_custom_call" | custom-call | flops 3932160 | bytes 3932160 | tf_op jit(solution)/shard_map/lat_solve/pallas_call | solution.py:177
  23.3 2.0 %collective-permute-start.2 = (f32[2,37,128]{2,1,0:T(8,128)}, f32[2,37,128]{2,1,0:T(8,128)S(1)}, u32[]{:S(2)}, u32[]{:S(2)}) collective-permute-start(f32[2,37,128]{2,1,0:T(8,128)} %get-tuple-element.33), channel_id=1, source_target_pairs={{0,1},{1,2},{2,3},{3,4},{4,5},{5,6},{6,7},{7,0},{8,9},{9,10},{10,1... | collective-permute-start | bytes 113672 | tf_op jit(solution)/shard_map/ppermute | solution.py:517
  25.4 2.8 %collective-permute-start.3 = (f32[3,37,128]{2,1,0:T(8,128)}, f32[3,37,128]{2,1,0:T(8,128)S(1)}, u32[]{:S(2)}, u32[]{:S(2)}) collective-permute-start(f32[3,37,128]{2,1,0:T(8,128)} %get-tuple-element.34), channel_id=1, source_target_pairs={{1,0},{2,1},{3,2},{4,3},{5,4},{6,5},{7,6},{0,7},{9,8},{10,9},{11,1... | collective-permute-start | bytes 170504 | tf_op jit(solution)/shard_map/ppermute | solution.py:518
  28.1 0.7 dynamic-slice_bitcast_fusion
  28.8 1.6 collective-permute-start.9
  30.4 2.3 %collective-permute-done.3.refs_1_ = f32[3,37,128]{2,1,0:T(8,128)S(1)} collective-permute-done((f32[3,37,128]{2,1,0:T(8,128)}, f32[3,37,128]{2,1,0:T(8,128)S(1)}, u32[]{:S(2)}, u32[]{:S(2)}) %collective-permute-start.3) | collective-permute-done | bytes 56864 | tf_op jit(solution)/shard_map/ppermute | solution.py:518
  32.8 0.6 copy-done.9
  33.4 4.5 %lon_solve.2 = (bf16[4736,384]{1,0:T(8,128)(2,1)}, f32[5,37,128]{2,1,0:T(8,128)}) custom-call(f32[37,96,128]{2,1,0:T(8,128)} %get-tuple-element.30.x_ref, f32[2,37,128]{2,1,0:T(8,128)} %copy-done.10, f32[3,37,128]{2,1,0:T(8,128)} %copy-done.9, bf16[384,128]{1,0:T(8,128)(2,1)} %constant.103.refs_2_.refs_1_), custom_call_target="tpu_custom_call" | custom-call | flops 465567744 | bytes 3637248 | tf_op jit(solution)/shard_map/lon_solve/pallas_call | solution.py:226
  37.9 0.7 collective-permute-start.10
  38.6 0.2 convert_reduce_fusion
  38.8 0.1 convolution_convert_fusion
  38.9 0.7 reshape.24.base_ref
  39.6 11.2 %taps.4 = (f32[1152,128]{1,0:T(8,128)}, f32[1152,128]{1,0:T(8,128)}) custom-call(s32[192]{0:T(256)} %constant.96.clone.meta_ref, s32[528]{0:T(1024)} %reshape.24.base_ref, bf16[4736,384]{1,0:T(8,128)(2,1)} %get-tuple-element.35.refs_0_.refs_1_, bf16[4736,384]{1,0:T(8,128)(2,1)} %get-tuple-element.35.refs_0_.refs_1_, f32[8,4,32,128]{3,2,1,0:T(8,128)} %copy-done.3, ...), custom_call_target="tpu_custom_call" | custom-call | flops 4831838208 | bytes 3637248 | tf_op jit(solution)/shard_map/taps/pallas_call | solution.py:404
  50.9 19.8 %collective-permute-start.4 = (f32[1152,128]{1,0:T(8,128)}, f32[1152,128]{1,0:T(8,128)S(1)}, u32[]{:S(2)}, u32[]{:S(2)}) collective-permute-start(f32[1152,128]{1,0:T(8,128)} %get-tuple-element.36), channel_id=1, source_target_pairs={{0,4},{1,5},{2,0},{3,1},{4,6},{5,7},{6,2},{7,3},{8,12},{9,13},{10,... | collective-permute-start | bytes 1769480 | tf_op jit(solution)/shard_map/ppermute | solution.py:564
  70.7 2.7 %collective-permute-start.5 = (f32[1152,128]{1,0:T(8,128)}, f32[1152,128]{1,0:T(8,128)S(1)}, u32[]{:S(2)}, u32[]{:S(2)}) collective-permute-start(f32[1152,128]{1,0:T(8,128)} %get-tuple-element.37.refs_1_), channel_id=1, source_target_pairs={{0,5},{1,4},{2,1},{3,0},{4,7},{5,6},{6,3},{7,2},{8,13},{9,12},{10,... | collective-permute-start | bytes 1769480 | tf_op jit(solution)/shard_map/ppermute | solution.py:564
  73.3 11.2 %taps.5 = (f32[1152,128]{1,0:T(8,128)}, f32[1152,128]{1,0:T(8,128)}) custom-call(s32[192]{0:T(256)} %constant.96.clone.meta_ref, s32[528]{0:T(1024)} %reshape.24.base_ref, bf16[4736,384]{1,0:T(8,128)(2,1)} %get-tuple-element.35.refs_0_.refs_1_, f32[1152,128]{1,0:T(8,128)} %get-tuple-element.37.refs_1_, f32[8,4,32,128]{3,2,1,0:T(8,128)} %copy-done.3, ...), custom_call_target="tpu_custom_call" | custom-call | flops 4831838208 | bytes 3637248 | tf_op jit(solution)/shard_map/taps/pallas_call | solution.py:404
  84.6 0.0 copy-start.2
  84.6 3.0 %collective-permute-start.6 = (f32[1152,128]{1,0:T(8,128)}, f32[1152,128]{1,0:T(8,128)S(1)}, u32[]{:S(2)}, u32[]{:S(2)}) collective-permute-start(f32[1152,128]{1,0:T(8,128)} %get-tuple-element.38), channel_id=1, source_target_pairs={{0,6},{1,7},{2,2},{3,3},{4,4},{5,5},{6,0},{7,1},{8,14},{9,15},{10,... | collective-permute-start | bytes 1769480 | tf_op jit(solution)/shard_map/ppermute | solution.py:564
  87.6 2.9 %collective-permute-start.7 = (f32[1152,128]{1,0:T(8,128)}, f32[1152,128]{1,0:T(8,128)S(1)}, u32[]{:S(2)}, u32[]{:S(2)}) collective-permute-start(f32[1152,128]{1,0:T(8,128)} %get-tuple-element.39.refs_2_), channel_id=1, source_target_pairs={{0,7},{1,6},{2,3},{3,2},{4,5},{5,4},{6,1},{7,0},{8,15},{9,14},{10,... | collective-permute-start | bytes 1769480 | tf_op jit(solution)/shard_map/ppermute | solution.py:564
  90.5 3.4 %lat_solve.3 = (f32[37,96,128]{2,1,0:T(8,128)}, f32[2,37,128]{2,1,0:T(8,128)}, f32[3,37,128]{2,1,0:T(8,128)}) custom-call(f32[20,96,128]{2,1,0:T(8,128)} %copy-done.2, f32[19,96,128]{2,1,0:T(8,128)} %collective-permute-done.9.refs_1_, f32[96,128]{1,0:T(8,128)} %constant.90.clone.refs_5_.refs_2_, f32[96,128]{1,0:T(8,128)} %constant.91.clone.refs_6_.refs_3_), custom_call_target="tpu_custom_call" | custom-call | flops 3932160 | bytes 3932160 | tf_op jit(solution)/shard_map/lat_solve/pallas_call | solution.py:177
  93.9 0.6 copy-done.7
  94.6 4.6 %lon_solve.3.refs_1_ = bf16[4736,384]{1,0:T(8,128)(2,1)} custom-call(f32[37,96,128]{2,1,0:T(8,128)} %get-tuple-element.41.x_ref, f32[5,37,128]{2,1,0:T(8,128)} %copy-done.7, bf16[384,128]{1,0:T(8,128)(2,1)} %constant.103.refs_2_.refs_1_), custom_call_target="tpu_custom_call" | custom-call | flops 465567744 | bytes 3637248 | tf_op jit(solution)/shard_map/lon_solve/pallas_call | solution.py:226
  99.2 11.2 %taps.6 = (f32[1152,128]{1,0:T(8,128)}, f32[1152,128]{1,0:T(8,128)}) custom-call(s32[192]{0:T(256)} %constant.96.clone.meta_ref, s32[528]{0:T(1024)} %reshape.24.base_ref, bf16[4736,384]{1,0:T(8,128)(2,1)} %get-tuple-element.35.refs_0_.refs_1_, bf16[4736,384]{1,0:T(8,128)(2,1)} %lon_solve.3.refs_1_, f32[1152,128]{1,0:T(8,128)} %get-tuple-element.39.refs_2_, ...), custom_call_target="tpu_custom_call" | custom-call | flops 4831838208 | bytes 3637248 | tf_op jit(solution)/shard_map/taps/pallas_call | solution.py:404
  110.4 0.0 copy-start.11
  110.4 25.6 %collective-permute-start.12 = (f32[1152,128]{1,0:T(8,128)}, f32[1152,128]{1,0:T(8,128)S(1)}, u32[]{:S(2)}, u32[]{:S(2)}) collective-permute-start(f32[1152,128]{1,0:T(8,128)} %get-tuple-element.44.refs_2_), channel_id=1, source_target_pairs={{0,3},{1,2},{2,1},{3,0},{4,7},{5,6},{6,5},{7,4},{8,11},{9,10},{10,... | collective-permute-start | bytes 1769480 | tf_op jit(solution)/shard_map/ppermute | solution.py:564
  136.0 11.3 %taps.7 = (f32[1152,128]{1,0:T(8,128)}, f32[1152,128]{1,0:T(8,128)}) custom-call(s32[192]{0:T(256)} %constant.96.clone.meta_ref, s32[528]{0:T(1024)} %reshape.24.base_ref, bf16[4736,384]{1,0:T(8,128)(2,1)} %get-tuple-element.35.refs_0_.refs_1_, bf16[4736,384]{1,0:T(8,128)(2,1)} %lon_solve.3.refs_1_, f32[1152,128]{1,0:T(8,128)} %get-tuple-element.44.refs_2_, ...), custom_call_target="tpu_custom_call" | custom-call | flops 4831838208 | bytes 3637248 | tf_op jit(solution)/shard_map/taps/pallas_call | solution.py:404
  147.3 0.1 collective-permute-start.13
  147.4 0.6 collective-permute-start.11
  148.0 0.1 convert_reduce_fusion.1
  148.1 0.1 fusion.11
  148.2 0.2 fusion.1
  148.4 0.6 fusion.10
  149.0 0.8 reshape.23.target_ref
  149.8 7.7 %collective-permute-done.13.refs_7_ = f32[1152,128]{1,0:T(8,128)S(1)} collective-permute-done((f32[1152,128]{1,0:T(8,128)}, f32[1152,128]{1,0:T(8,128)S(1)}, u32[]{:S(2)}, u32[]{:S(2)}) %collective-permute-start.13) | collective-permute-done | bytes 589856 | tf_op jit(solution)/shard_map/ppermute | solution.py:564
  157.5 0.2 collective-permute-done.11.refs_4_
  157.7 1.1 copy-done
  158.7 6.4 %place.1 = f32[3072,128]{1,0:T(8,128)} custom-call(s32[3072]{0:T(1024)S(1)} %reshape.23.target_ref, f32[1152,128]{1,0:T(8,128)S(1)} %collective-permute-done.4.refs_0_, f32[1152,128]{1,0:T(8,128)S(1)} %collective-permute-done.5.refs_1_, f32[1152,128]{1,0:T(8,128)S(1)} %collective-permute-done.6.refs_2_, f32[1152,128]{1,0:T(8,128)S(1)} %collective-permute-done.7.refs_3_, ...), custom_call_target="tpu_custom_call" | custom-call | bytes 9437184 | tf_op jit(solution)/shard_map/place/pallas_call | solution.py:461
  (30 shorter events, 0.1 us)
Async XLA Ops:
  0.0 17.0 %copy-start.1 = (f32[32,96,128]{2,1,0:T(8,128)S(1)}, f32[32,96,128]{2,1,0:T(8,128)}, u32[]{:S(2)}) copy-start(f32[32,96,128]{2,1,0:T(8,128)} %refs_0_.1) | copy-start | bytes 4718596
  5.4 33.2 %all-to-all-start = ((f32[8,4,32,128]{3,2,1,0:T(8,128)}), f32[8,4,32,128]{3,2,1,0:T(8,128)S(1)}, u32[]{:S(2)}, u32[]{:S(2)}) async-start(f32[8,4,32,128]{3,2,1,0:T(8,128)} %get-tuple-element.32), calls=%async_computation | async-start | bytes 1048576 | tf_op jit(solution)/shard_map/all_to_all | solution.py:514
  12.6 6.1 %collective-permute-start.1 = (f32[4,96,128]{2,1,0:T(8,128)}, f32[4,96,128]{2,1,0:T(8,128)S(1)}, u32[]{:S(2)}, u32[]{:S(2)}) collective-permute-start(f32[4,96,128]{2,1,0:T(8,128)} %get-tuple-element.27), channel_id=1, source_target_pairs={{8,0},{16,8},{24,16},{9,1},{17,9},{25,17},{10,2},{18,10},{26,18},{... | collective-permute-start | bytes 589832 | tf_op jit(solution)/shard_map/ppermute | solution.py:513
  13.9 4.8 %collective-permute-start = (f32[3,96,128]{2,1,0:T(8,128)}, f32[3,96,128]{2,1,0:T(8,128)S(1)}, u32[]{:S(2)}, u32[]{:S(2)}) collective-permute-start(f32[3,96,128]{2,1,0:T(8,128)} %get-tuple-element.26), channel_id=1, source_target_pairs={{0,8},{8,16},{16,24},{1,9},{9,17},{17,25},{2,10},{10,18},{18,26},{... | collective-permute-start | bytes 442376 | tf_op jit(solution)/shard_map/ppermute | solution.py:512
  18.0 66.6 %collective-permute-start.8 = (f32[20,96,128]{2,1,0:T(8,128)}, f32[20,96,128]{2,1,0:T(8,128)S(1)}, u32[]{:S(2)}, u32[]{:S(2)}) collective-permute-start(f32[20,96,128]{2,1,0:T(8,128)} %slice.11), channel_id=1, source_target_pairs={{2,4},{3,5},{4,2},{5,3},{10,12},{11,13},{12,10},{13,11},{18,20},{1... | collective-permute-start | bytes 2949128 | tf_op jit(solution)/shard_map/ppermute | solution.py:509
  18.7 0.7 copy-start.6
  18.8 0.7 copy-start.5
  23.3 15.5 %copy-start.8 = (f32[32,33]{1,0:T(8,128)S(1)}, f32[32,33]{1,0:T(8,128)}, u32[]{:S(2)}) copy-start(f32[32,33]{1,0:T(8,128)} %constant.93.clone) | copy-start | bytes 12676
  23.3 7.1 %collective-permute-start.2 = (f32[2,37,128]{2,1,0:T(8,128)}, f32[2,37,128]{2,1,0:T(8,128)S(1)}, u32[]{:S(2)}, u32[]{:S(2)}) collective-permute-start(f32[2,37,128]{2,1,0:T(8,128)} %get-tuple-element.33), channel_id=1, source_target_pairs={{0,1},{1,2},{2,3},{3,4},{4,5},{5,6},{6,7},{7,0},{8,9},{9,10},{10,1... | collective-permute-start | bytes 113672 | tf_op jit(solution)/shard_map/ppermute | solution.py:517
  25.4 7.4 %collective-permute-start.3 = (f32[3,37,128]{2,1,0:T(8,128)}, f32[3,37,128]{2,1,0:T(8,128)S(1)}, u32[]{:S(2)}, u32[]{:S(2)}) collective-permute-start(f32[3,37,128]{2,1,0:T(8,128)} %get-tuple-element.34), channel_id=1, source_target_pairs={{1,0},{2,1},{3,2},{4,3},{5,4},{6,5},{7,6},{0,7},{9,8},{10,9},{11,1... | collective-permute-start | bytes 170504 | tf_op jit(solution)/shard_map/ppermute | solution.py:518
  28.8 58.8 %collective-permute-start.9 = (f32[19,96,128]{2,1,0:T(8,128)}, f32[19,96,128]{2,1,0:T(8,128)}, u32[]{:S(2)}, u32[]{:S(2)}) collective-permute-start(f32[19,96,128]{2,1,0:T(8,128)} %get-tuple-element.40), channel_id=1, source_target_pairs={{2,4},{3,5},{4,2},{5,3},{10,12},{11,13},{12,10},{13,11},{18,20},{1... | collective-permute-start | bytes 2801672 | tf_op jit(solution)/shard_map/ppermute | solution.py:525
  30.4 2.4 %copy-start.10 = (f32[2,37,128]{2,1,0:T(8,128)}, f32[2,37,128]{2,1,0:T(8,128)S(1)}, u32[]{:S(2)}) copy-start(f32[2,37,128]{2,1,0:T(8,128)S(1)} %collective-permute-done.2.refs_0_) | copy-start | bytes 113668
  32.8 0.6 copy-start.9
  37.9 56.1 %collective-permute-start.10 = (f32[5,37,128]{2,1,0:T(8,128)}, f32[5,37,128]{2,1,0:T(8,128)S(1)}, u32[]{:S(2)}, u32[]{:S(2)}) collective-permute-start(f32[5,37,128]{2,1,0:T(8,128)} %get-tuple-element.42), channel_id=1, source_target_pairs={{2,4},{3,5},{4,2},{5,3},{10,12},{11,13},{12,10},{13,11},{18,20},{1... | collective-permute-start | bytes 284168 | tf_op jit(solution)/shard_map/ppermute | solution.py:526
  38.5 1.1 copy-start.3
  50.9 96.4 %collective-permute-start.4 = (f32[1152,128]{1,0:T(8,128)}, f32[1152,128]{1,0:T(8,128)S(1)}, u32[]{:S(2)}, u32[]{:S(2)}) collective-permute-start(f32[1152,128]{1,0:T(8,128)} %get-tuple-element.36), channel_id=1, source_target_pairs={{0,4},{1,5},{2,0},{3,1},{4,6},{5,7},{6,2},{7,3},{8,12},{9,13},{10,... | collective-permute-start | bytes 1769480 | tf_op jit(solution)/shard_map/ppermute | solution.py:564
  70.7 76.7 %collective-permute-start.5 = (f32[1152,128]{1,0:T(8,128)}, f32[1152,128]{1,0:T(8,128)S(1)}, u32[]{:S(2)}, u32[]{:S(2)}) collective-permute-start(f32[1152,128]{1,0:T(8,128)} %get-tuple-element.37.refs_1_), channel_id=1, source_target_pairs={{0,5},{1,4},{2,1},{3,0},{4,7},{5,6},{6,3},{7,2},{8,13},{9,12},{10,... | collective-permute-start | bytes 1769480 | tf_op jit(solution)/shard_map/ppermute | solution.py:564
  84.6 5.9 %copy-start.2 = (f32[20,96,128]{2,1,0:T(8,128)}, f32[20,96,128]{2,1,0:T(8,128)S(1)}, u32[]{:S(2)}) copy-start(f32[20,96,128]{2,1,0:T(8,128)S(1)} %collective-permute-done.8.refs_0_) | copy-start | bytes 2949124
  84.6 65.2 %collective-permute-start.6 = (f32[1152,128]{1,0:T(8,128)}, f32[1152,128]{1,0:T(8,128)S(1)}, u32[]{:S(2)}, u32[]{:S(2)}) collective-permute-start(f32[1152,128]{1,0:T(8,128)} %get-tuple-element.38), channel_id=1, source_target_pairs={{0,6},{1,7},{2,2},{3,3},{4,4},{5,5},{6,0},{7,1},{8,14},{9,15},{10,... | collective-permute-start | bytes 1769480 | tf_op jit(solution)/shard_map/ppermute | solution.py:564
  87.6 62.2 %collective-permute-start.7 = (f32[1152,128]{1,0:T(8,128)}, f32[1152,128]{1,0:T(8,128)S(1)}, u32[]{:S(2)}, u32[]{:S(2)}) collective-permute-start(f32[1152,128]{1,0:T(8,128)} %get-tuple-element.39.refs_2_), channel_id=1, source_target_pairs={{0,7},{1,6},{2,3},{3,2},{4,5},{5,4},{6,1},{7,0},{8,15},{9,14},{10,... | collective-permute-start | bytes 1769480 | tf_op jit(solution)/shard_map/ppermute | solution.py:564
  93.9 0.6 copy-start.7
  110.4 37.6 %copy-start.4 = (s32[32,96]{1,0:T(8,128)S(1)}, s32[32,96]{1,0:T(8,128)}, u32[]{:S(2)}) copy-start(s32[32,96]{1,0:T(8,128)} %reshape.22.owner_ref) | copy-start | bytes 36868
  110.4 37.8 %copy-start.11 = (bf16[96,96,1]{1,0,2:T(8,128)(2,1)S(1)}, bf16[96,96,1]{1,0,2:T(8,128)(2,1)}, u32[]{:S(2)}) copy-start(bf16[96,96,1]{1,0,2:T(8,128)(2,1)} %constant.104) | copy-start | bytes 55300
  110.4 47.3 %collective-permute-start.12 = (f32[1152,128]{1,0:T(8,128)}, f32[1152,128]{1,0:T(8,128)S(1)}, u32[]{:S(2)}, u32[]{:S(2)}) collective-permute-start(f32[1152,128]{1,0:T(8,128)} %get-tuple-element.44.refs_2_), channel_id=1, source_target_pairs={{0,3},{1,2},{2,1},{3,0},{4,7},{5,6},{6,5},{7,4},{8,11},{9,10},{10,... | collective-permute-start | bytes 1769480 | tf_op jit(solution)/shard_map/ppermute | solution.py:564
  147.3 10.2 %collective-permute-start.13 = (f32[1152,128]{1,0:T(8,128)}, f32[1152,128]{1,0:T(8,128)S(1)}, u32[]{:S(2)}, u32[]{:S(2)}) collective-permute-start(f32[1152,128]{1,0:T(8,128)} %get-tuple-element.46), channel_id=1, source_target_pairs={{0,1},{1,0},{2,3},{3,2},{4,5},{5,4},{6,7},{7,6},{8,9},{9,8},{10,11... | collective-permute-start | bytes 1769480 | tf_op jit(solution)/shard_map/ppermute | solution.py:564
  147.4 10.3 %collective-permute-start.11 = (f32[1152,128]{1,0:T(8,128)}, f32[1152,128]{1,0:T(8,128)}, u32[]{:S(2)}, u32[]{:S(2)}) collective-permute-start(f32[1152,128]{1,0:T(8,128)} %get-tuple-element.43), channel_id=1, source_target_pairs={{0,2},{1,3},{2,0},{3,1},{4,6},{5,7},{6,4},{7,5},{8,10},{9,11},{10,... | collective-permute-start | bytes 1769480 | tf_op jit(solution)/shard_map/ppermute | solution.py:564
  157.7 1.1 copy-start

commit v9 on v8

--- a/solution.py
+++ b/solution.py
@@ -464,7 +464,7 @@
         grid_spec=pltpu.PrefetchScalarGridSpec(
             num_scalar_prefetch=1,
             grid=(1,),
-            in_specs=[pl.BlockSpec(memory_space=pl.ANY)] * count,
+            in_specs=[pl.BlockSpec(memory_space=pltpu.HBM)] * count,
             out_specs=pl.BlockSpec((cells, ch), lambda g, t: (0, 0)),
             scratch_shapes=[pltpu.VMEM((count * cap, ch), F32), pltpu.SemaphoreType.DMA((count,))],
         ),
@@ -531,11 +531,11 @@
     slot = jnp.sum(jnp.where(mask, before + own_base[:, :-1, None], 0.0), axis=0).astype(jnp.int32)
     q = late_owner // quarter
     alike = ((q == 1) | (q == 2)) == middle
-    early = ((q == 1) | (q == 2)) == (q // 2 == mine // 2)
-    part = jnp.where(early, jnp.where(alike, 1, 0), jnp.where(alike, 3, 2)) * quarter
+    near = q // 2 == mine // 2
+    part = jnp.where(near, jnp.where(q == mine, 3, 0), jnp.where(alike, 2, 1)) * quarter
     target = ((part + (offset - late_owner) % quarter) * cap + slot).reshape(cells)
 
-    goals = ((2, 0, 3, 1), (3, 1, 2, 0), (1, 0, 3, 2), (0, 1, 2, 3))
+    goals = ((1, 0, 3, 2), (2, 0, 3, 1), (3, 1, 2, 0), (0, 1, 2, 3))
     shifts = list(range(quarter))[::-1]
     calls = [(group, shifts[n : n + 2]) for group in range(4) for n in range(0, quarter, 2)]
     plan = []
@@ -543,7 +543,7 @@
         k, o = s // quarter, s % quarter
         row = []
         for group, pair in calls:
-            which = int(group >= 2 and k in (1, 2))
+            which = int(group in (1, 2) and k in (1, 2))
             dests = [at(goals[group][k], (o + a) % quarter) for a in pair]
             row += dests + [dict(mirror).get(s, s) if which else s, which]
             row += [(which * sectors + dest) * (rows + 1) for dest in dests]
@@ -553,7 +553,7 @@
     parts = [None] * sectors
     tables, done, values = [own], 0, [own]
     for group, pair in calls:
-        if group == 2 and len(tables) == 1:
+        if group == 1 and len(tables) == 1:
             other = lat_solve(rows, head, [first, rest])[0]
             tables = [own, lon_solve(other, sides)[0]]
         values = taps(meta, width, done, len(pair), base, tables, asked, cols, cap, values[0])

time: 166 us -> 159 us (0.958)
  starting transfers between devices: 73.9 us -> 51.9 us
  waiting for transfers between devices: 10.2 us -> 23.3 us
    ppermute x7, starting transfers between devices: 54.6 us -> 32.6 us  [transport(): value = lax.ppermute(value, 'lon', moves)]
    ppermute x7, waiting for transfers between devices: 7.86 us -> 20.8 us  [transport(): value = lax.ppermute(value, 'lon', moves)]
    unnamed x25 -> x23, local copies, waits for them, and re-layouts: 3.58 us -> 4.52 us
  transfers between devices with their start and end apart: 15 -> 15, of which waited for: 3 -> 4; matrix products, arithmetic and copies ran while one was open for 3% -> 3% of each run, Pallas kernels for 37% -> 39%
where the time goes in v9:
time: 159 us; the launch traced here: 157 us
  Pallas kernels  70.6 us (44%)
  starting transfers between devices  51.9 us (33%)
  waiting for transfers between devices  23.3 us (15%)
  local copies, waits for them, and re-layouts  8.33 us (5%)
  other arithmetic  2.34 us (1%)
    pallas_call x4, Pallas kernels, taps(): pl.pallas_call(functools.partial(tap_kernel, tables=len(tables), count=co...  45.1 us
    ppermute x7, starting transfers between devices, transport(): value = lax.ppermute(value, 'lon', moves)  32.6 us
    ppermute x7, waiting for transfers between devices, transport(): value = lax.ppermute(value, 'lon', moves)  20.8 us
    pallas_call x2, Pallas kernels, lon_solve(): pl.pallas_call(functools.partial(lon_kernel, packed=packed), out_shape=sh...  9.07 us
    pallas_call x2, Pallas kernels, lat_solve(): pl.pallas_call(functools.partial(lat_kernel, pieces=len(pieces), head=hea...  7.32 us
    all_to_all x1, starting transfers between devices, transport(): lax.all_to_all(words, 'lon', split_axis=0, concat_axis=0, tiled=True)  7.28 us
    pallas_call x1, Pallas kernels, place(): pl.pallas_call(functools.partial(place_kernel, cap=cap), out_shape=jax.Sh...  6.36 us
    unnamed x23, local copies, waits for them, and re-layouts  4.52 us
  transfers between devices with their start and end apart: 15, of which 4 were waited for; matrix products, arithmetic and copies ran while one was open for 3% of the time, Pallas kernels for 39%

profile of v9, /device:TPU:0, one launch (start us, length us, event | category | flops | bytes accessed | tf_op | source)
XLA Modules:
  0.0 157.2 jit_solution(2425132770464777665)
XLA Ops:
  0.0 0.5 broadcast.41
  0.5 1.4 reduce.4
  1.9 0.7 reshape.22.owner_ref
  2.6 2.7 %edges.1 = (f32[3,96,128]{2,1,0:T(8,128)}, f32[4,96,128]{2,1,0:T(8,128)}, f32[3,96,128]{2,1,0:T(8,128)}, f32[4,96,128]{2,1,0:T(8,128)}, f32[8,4,32,128]{3,2,1,0:T(8,128)}) custom-call(f32[32,96,128]{2,1,0:T(8,128)} %refs_0_.1, s32[32,96]{1,0:T(8,128)} %reshape.22.owner_ref, s32[32,96]{1,0:T(8,128)} %column_ref.1, s32[32,96]{1,0:T(8,128)} %shift_ref.1, ...), custom_call_target="tpu_custom_call" | custom-call | flops 2359296 | bytes 2359296 | tf_op jit(solution)/shard_map/edges/pallas_call | solution.py:94
  5.3 7.3 %all-to-all-start = ((f32[8,4,32,128]{3,2,1,0:T(8,128)}), f32[8,4,32,128]{3,2,1,0:T(8,128)}, u32[]{:S(2)}, u32[]{:S(2)}) async-start(f32[8,4,32,128]{3,2,1,0:T(8,128)} %get-tuple-element.32), calls=%async_computation | async-start | bytes 1048576 | tf_op jit(solution)/shard_map/all_to_all | solution.py:514
  12.6 1.3 collective-permute-start.1
  13.9 3.0 %collective-permute-start = (f32[3,96,128]{2,1,0:T(8,128)}, f32[3,96,128]{2,1,0:T(8,128)S(1)}, u32[]{:S(2)}, u32[]{:S(2)}) collective-permute-start(f32[3,96,128]{2,1,0:T(8,128)} %get-tuple-element.26), channel_id=1, source_target_pairs={{0,8},{8,16},{16,24},{1,9},{9,17},{17,25},{2,10},{10,18},{18,26},{... | collective-permute-start | bytes 442376 | tf_op jit(solution)/shard_map/ppermute | solution.py:512
  16.9 0.1 slice.11
  17.0 0.7 collective-permute-start.6
  17.7 0.4 collective-permute-done.refs_1_
  18.1 0.6 copy-done.5
  18.8 0.1 copy-done.4
  18.8 3.9 %lat_solve.2 = (f32[37,96,128]{2,1,0:T(8,128)}, f32[2,37,128]{2,1,0:T(8,128)}, f32[3,37,128]{2,1,0:T(8,128)}, f32[19,96,128]{2,1,0:T(8,128)}) custom-call(f32[32,96,128]{2,1,0:T(8,128)} %refs_0_.1, f32[3,96,128]{2,1,0:T(8,128)} %copy-done.5, f32[4,96,128]{2,1,0:T(8,128)} %copy-done.4, f32[3,96,128]{2,1,0:T(8,128)} %get-tuple-element.28.refs_3_, ...), custom_call_target="tpu_custom_call" | custom-call | flops 3932160 | bytes 3932160 | tf_op jit(solution)/shard_map/lat_solve/pallas_call | solution.py:177
  22.8 2.0 %collective-permute-start.2 = (f32[2,37,128]{2,1,0:T(8,128)}, f32[2,37,128]{2,1,0:T(8,128)S(1)}, u32[]{:S(2)}, u32[]{:S(2)}) collective-permute-start(f32[2,37,128]{2,1,0:T(8,128)} %get-tuple-element.33), channel_id=1, source_target_pairs={{0,1},{1,2},{2,3},{3,4},{4,5},{5,6},{6,7},{7,0},{8,9},{9,10},{10,1... | collective-permute-start | bytes 113672 | tf_op jit(solution)/shard_map/ppermute | solution.py:517
  24.8 2.8 %collective-permute-start.3 = (f32[3,37,128]{2,1,0:T(8,128)}, f32[3,37,128]{2,1,0:T(8,128)S(1)}, u32[]{:S(2)}, u32[]{:S(2)}) collective-permute-start(f32[3,37,128]{2,1,0:T(8,128)} %get-tuple-element.34), channel_id=1, source_target_pairs={{1,0},{2,1},{3,2},{4,3},{5,4},{6,5},{7,6},{0,7},{9,8},{10,9},{11,1... | collective-permute-start | bytes 170504 | tf_op jit(solution)/shard_map/ppermute | solution.py:518
  27.5 0.7 dynamic-slice_bitcast_fusion
  28.2 1.6 %collective-permute-start.7 = (f32[19,96,128]{2,1,0:T(8,128)}, f32[19,96,128]{2,1,0:T(8,128)}, u32[]{:S(2)}, u32[]{:S(2)}) collective-permute-start(f32[19,96,128]{2,1,0:T(8,128)} %get-tuple-element.38), channel_id=1, source_target_pairs={{2,4},{3,5},{4,2},{5,3},{10,12},{11,13},{12,10},{13,11},{18,20},{1... | collective-permute-start | bytes 2801672 | tf_op jit(solution)/shard_map/ppermute | solution.py:525
  29.8 2.1 %collective-permute-done.3.refs_1_ = f32[3,37,128]{2,1,0:T(8,128)S(1)} collective-permute-done((f32[3,37,128]{2,1,0:T(8,128)}, f32[3,37,128]{2,1,0:T(8,128)S(1)}, u32[]{:S(2)}, u32[]{:S(2)}) %collective-permute-start.3) | collective-permute-done | bytes 56864 | tf_op jit(solution)/shard_map/ppermute | solution.py:518
  31.9 0.6 copy-done.8
  32.5 4.5 %lon_solve.2 = (bf16[4736,384]{1,0:T(8,128)(2,1)}, f32[5,37,128]{2,1,0:T(8,128)}) custom-call(f32[37,96,128]{2,1,0:T(8,128)} %get-tuple-element.30.x_ref, f32[2,37,128]{2,1,0:T(8,128)} %copy-done.9, f32[3,37,128]{2,1,0:T(8,128)} %copy-done.8, bf16[384,128]{1,0:T(8,128)(2,1)} %constant.103.refs_2_.refs_1_), custom_call_target="tpu_custom_call" | custom-call | flops 465567744 | bytes 3637248 | tf_op jit(solution)/shard_map/lon_solve/pallas_call | solution.py:226
  37.0 0.7 collective-permute-start.8
  37.7 0.9 slice_bitcast_fusion
  38.6 0.2 convert_reduce_fusion
  38.8 0.1 convolution_convert_fusion
  39.0 0.7 reshape.24.base_ref
  39.7 11.2 %taps.4 = (f32[1152,128]{1,0:T(8,128)}, f32[1152,128]{1,0:T(8,128)}) custom-call(s32[192]{0:T(256)} %constant.96.clone.meta_ref, s32[528]{0:T(1024)} %reshape.24.base_ref, bf16[4736,384]{1,0:T(8,128)(2,1)} %get-tuple-element.35.refs_0_.refs_1_, bf16[4736,384]{1,0:T(8,128)(2,1)} %get-tuple-element.35.refs_0_.refs_1_, ...), custom_call_target="tpu_custom_call" | custom-call | flops 4831838208 | bytes 3637248 | tf_op jit(solution)/shard_map/taps/pallas_call | solution.py:404
  50.9 21.1 %collective-permute-start.4 = (f32[1152,128]{1,0:T(8,128)}, f32[1152,128]{1,0:T(8,128)S(1)}, u32[]{:S(2)}, u32[]{:S(2)}) collective-permute-start(f32[1152,128]{1,0:T(8,128)} %get-tuple-element.36), channel_id=1, source_target_pairs={{0,2},{1,3},{2,0},{3,1},{4,6},{5,7},{6,4},{7,5},{8,10},{9,11},{10,... | collective-permute-start | bytes 1769480 | tf_op jit(solution)/shard_map/ppermute | solution.py:564
  72.0 0.7 collective-permute-start.5
  72.7 0.9 copy-done.2
  73.7 3.4 %lat_solve.3 = (f32[37,96,128]{2,1,0:T(8,128)}, f32[2,37,128]{2,1,0:T(8,128)}, f32[3,37,128]{2,1,0:T(8,128)}) custom-call(f32[20,96,128]{2,1,0:T(8,128)} %copy-done.2, f32[19,96,128]{2,1,0:T(8,128)} %collective-permute-done.7.refs_1_, f32[96,128]{1,0:T(8,128)} %constant.90.clone.refs_5_.refs_2_, f32[96,128]{1,0:T(8,128)} %constant.91.clone.refs_6_.refs_3_), custom_call_target="tpu_custom_call" | custom-call | flops 3932160 | bytes 3932160 | tf_op jit(solution)/shard_map/lat_solve/pallas_call | solution.py:177
  77.1 0.6 copy-done.6
  77.7 4.6 %lon_solve.3.refs_1_ = bf16[4736,384]{1,0:T(8,128)(2,1)} custom-call(f32[37,96,128]{2,1,0:T(8,128)} %get-tuple-element.39.x_ref, f32[5,37,128]{2,1,0:T(8,128)} %copy-done.6, bf16[384,128]{1,0:T(8,128)(2,1)} %constant.103.refs_2_.refs_1_), custom_call_target="tpu_custom_call" | custom-call | flops 465567744 | bytes 3637248 | tf_op jit(solution)/shard_map/lon_solve/pallas_call | solution.py:226
  82.3 11.3 %taps.5 = (f32[1152,128]{1,0:T(8,128)}, f32[1152,128]{1,0:T(8,128)}) custom-call(s32[192]{0:T(256)} %constant.96.clone.meta_ref, s32[528]{0:T(1024)} %reshape.24.base_ref, bf16[4736,384]{1,0:T(8,128)(2,1)} %get-tuple-element.35.refs_0_.refs_1_, bf16[4736,384]{1,0:T(8,128)(2,1)} %lon_solve.3.refs_1_, f32[1152,128]{1,0:T(8,128)} %get-tuple-element.37.refs_2_, ...), custom_call_target="tpu_custom_call" | custom-call | flops 4831838208 | bytes 3637248 | tf_op jit(solution)/shard_map/taps/pallas_call | solution.py:404
  93.6 3.4 %collective-permute-start.9 = (f32[1152,128]{1,0:T(8,128)}, f32[1152,128]{1,0:T(8,128)S(1)}, u32[]{:S(2)}, u32[]{:S(2)}) collective-permute-start(f32[1152,128]{1,0:T(8,128)} %get-tuple-element.41), channel_id=1, source_target_pairs={{0,4},{1,5},{2,0},{3,1},{4,6},{5,7},{6,2},{7,3},{8,12},{9,13},{10,... | collective-permute-start | bytes 1769480 | tf_op jit(solution)/shard_map/ppermute | solution.py:564
  97.1 11.3 %taps.6 = (f32[1152,128]{1,0:T(8,128)}, f32[1152,128]{1,0:T(8,128)}) custom-call(s32[192]{0:T(256)} %constant.96.clone.meta_ref, s32[528]{0:T(1024)} %reshape.24.base_ref, bf16[4736,384]{1,0:T(8,128)(2,1)} %get-tuple-element.35.refs_0_.refs_1_, bf16[4736,384]{1,0:T(8,128)(2,1)} %lon_solve.3.refs_1_, f32[1152,128]{1,0:T(8,128)} %get-tuple-element.42.refs_2_, ...), custom_call_target="tpu_custom_call" | custom-call | flops 4831838208 | bytes 3637248 | tf_op jit(solution)/shard_map/taps/pallas_call | solution.py:404
  108.4 2.1 %collective-permute-start.12 = (f32[1152,128]{1,0:T(8,128)}, f32[1152,128]{1,0:T(8,128)S(1)}, u32[]{:S(2)}, u32[]{:S(2)}) collective-permute-start(f32[1152,128]{1,0:T(8,128)} %get-tuple-element.44.refs_2_), channel_id=1, source_target_pairs={{0,7},{1,6},{2,3},{3,2},{4,5},{5,4},{6,1},{7,0},{8,15},{9,14},{10,... | collective-permute-start | bytes 1769480 | tf_op jit(solution)/shard_map/ppermute | solution.py:564
  110.6 11.2 %taps.7 = (f32[1152,128]{1,0:T(8,128)}, f32[1152,128]{1,0:T(8,128)}) custom-call(s32[192]{0:T(256)} %constant.96.clone.meta_ref, s32[528]{0:T(1024)} %reshape.24.base_ref, bf16[4736,384]{1,0:T(8,128)(2,1)} %get-tuple-element.35.refs_0_.refs_1_, bf16[4736,384]{1,0:T(8,128)(2,1)} %lon_solve.3.refs_1_, f32[1152,128]{1,0:T(8,128)} %get-tuple-element.44.refs_2_, ...), custom_call_target="tpu_custom_call" | custom-call | flops 4831838208 | bytes 3637248 | tf_op jit(solution)/shard_map/taps/pallas_call | solution.py:404
  121.8 0.9 collective-permute-start.13
  122.7 4.3 %collective-permute-start.11 = (f32[1152,128]{1,0:T(8,128)}, f32[1152,128]{1,0:T(8,128)}, u32[]{:S(2)}, u32[]{:S(2)}) collective-permute-start(f32[1152,128]{1,0:T(8,128)} %get-tuple-element.43), channel_id=1, source_target_pairs={{0,6},{1,7},{2,2},{3,3},{4,4},{5,5},{6,0},{7,1},{8,14},{9,15},{10,... | collective-permute-start | bytes 1769480 | tf_op jit(solution)/shard_map/ppermute | solution.py:564
  127.0 0.1 convert_reduce_fusion.1
  127.1 0.1 fusion.11
  127.3 0.2 fusion.1
  127.4 0.6 fusion.10
  128.1 0.8 reshape.23.target_ref
  128.9 18.8 %collective-permute-done.13.refs_7_ = f32[1152,128]{1,0:T(8,128)S(1)} collective-permute-done((f32[1152,128]{1,0:T(8,128)}, f32[1152,128]{1,0:T(8,128)S(1)}, u32[]{:S(2)}, u32[]{:S(2)}) %collective-permute-start.13) | collective-permute-done | bytes 589856 | tf_op jit(solution)/shard_map/ppermute | solution.py:564
  147.7 2.0 %collective-permute-done.11.refs_4_ = f32[1152,128]{1,0:T(8,128)} collective-permute-done((f32[1152,128]{1,0:T(8,128)}, f32[1152,128]{1,0:T(8,128)}, u32[]{:S(2)}, u32[]{:S(2)}) %collective-permute-start.11) | collective-permute-done | bytes 589856 | tf_op jit(solution)/shard_map/ppermute | solution.py:564
  149.6 1.1 copy-done
  150.7 6.4 %place.1 = f32[3072,128]{1,0:T(8,128)} custom-call(s32[3072]{0:T(1024)S(1)} %reshape.23.target_ref, f32[1152,128]{1,0:T(8,128)S(1)} %collective-permute-done.4.refs_0_, f32[1152,128]{1,0:T(8,128)S(1)} %collective-permute-done.5.refs_1_, f32[1152,128]{1,0:T(8,128)S(1)} %collective-permute-done.9.refs_2_, f32[1152,128]{1,0:T(8,128)S(1)} %collective-permute-done.10.refs_3_, ...), custom_call_target="tpu_custom_call" | custom-call | bytes 9437184 | tf_op jit(solution)/shard_map/place/pallas_call | solution.py:461
  (28 shorter events, 0.1 us)
Async XLA Ops:
  0.0 16.9 %copy-start.1 = (f32[32,96,128]{2,1,0:T(8,128)S(1)}, f32[32,96,128]{2,1,0:T(8,128)}, u32[]{:S(2)}) copy-start(f32[32,96,128]{2,1,0:T(8,128)} %refs_0_.1) | copy-start | bytes 4718596
  5.3 32.4 %all-to-all-start = ((f32[8,4,32,128]{3,2,1,0:T(8,128)}), f32[8,4,32,128]{3,2,1,0:T(8,128)}, u32[]{:S(2)}, u32[]{:S(2)}) async-start(f32[8,4,32,128]{3,2,1,0:T(8,128)} %get-tuple-element.32), calls=%async_computation | async-start | bytes 1048576 | tf_op jit(solution)/shard_map/all_to_all | solution.py:514
  12.6 5.5 %collective-permute-start.1 = (f32[4,96,128]{2,1,0:T(8,128)}, f32[4,96,128]{2,1,0:T(8,128)S(1)}, u32[]{:S(2)}, u32[]{:S(2)}) collective-permute-start(f32[4,96,128]{2,1,0:T(8,128)} %get-tuple-element.27), channel_id=1, source_target_pairs={{8,0},{16,8},{24,16},{9,1},{17,9},{25,17},{10,2},{18,10},{26,18},{... | collective-permute-start | bytes 589832 | tf_op jit(solution)/shard_map/ppermute | solution.py:513
  13.9 4.2 %collective-permute-start = (f32[3,96,128]{2,1,0:T(8,128)}, f32[3,96,128]{2,1,0:T(8,128)S(1)}, u32[]{:S(2)}, u32[]{:S(2)}) collective-permute-start(f32[3,96,128]{2,1,0:T(8,128)} %get-tuple-element.26), channel_id=1, source_target_pairs={{0,8},{8,16},{16,24},{1,9},{9,17},{17,25},{2,10},{10,18},{18,26},{... | collective-permute-start | bytes 442376 | tf_op jit(solution)/shard_map/ppermute | solution.py:512
  17.0 55.7 %collective-permute-start.6 = (f32[20,96,128]{2,1,0:T(8,128)S(1)}, f32[20,96,128]{2,1,0:T(8,128)S(1)}, u32[]{:S(2)}, u32[]{:S(2)}) collective-permute-start(f32[20,96,128]{2,1,0:T(8,128)S(1)} %slice.11), channel_id=1, source_target_pairs={{2,4},{3,5},{4,2},{5,3},{10,12},{11,13},{12,10},{13,11},{18,20},{1... | collective-permute-start | bytes 2949128 | tf_op jit(solution)/shard_map/ppermute | solution.py:509
  18.1 0.7 copy-start.5
  18.1 0.7 copy-start.4
  22.8 16.1 %copy-start.7 = (f32[32,33]{1,0:T(8,128)S(1)}, f32[32,33]{1,0:T(8,128)}, u32[]{:S(2)}) copy-start(f32[32,33]{1,0:T(8,128)} %constant.93.clone) | copy-start | bytes 12676
  22.8 7.1 %collective-permute-start.2 = (f32[2,37,128]{2,1,0:T(8,128)}, f32[2,37,128]{2,1,0:T(8,128)S(1)}, u32[]{:S(2)}, u32[]{:S(2)}) collective-permute-start(f32[2,37,128]{2,1,0:T(8,128)} %get-tuple-element.33), channel_id=1, source_target_pairs={{0,1},{1,2},{2,3},{3,4},{4,5},{5,6},{6,7},{7,0},{8,9},{9,10},{10,1... | collective-permute-start | bytes 113672 | tf_op jit(solution)/shard_map/ppermute | solution.py:517
  24.8 7.1 %collective-permute-start.3 = (f32[3,37,128]{2,1,0:T(8,128)}, f32[3,37,128]{2,1,0:T(8,128)S(1)}, u32[]{:S(2)}, u32[]{:S(2)}) collective-permute-start(f32[3,37,128]{2,1,0:T(8,128)} %get-tuple-element.34), channel_id=1, source_target_pairs={{1,0},{2,1},{3,2},{4,3},{5,4},{6,5},{7,6},{0,7},{9,8},{10,9},{11,1... | collective-permute-start | bytes 170504 | tf_op jit(solution)/shard_map/ppermute | solution.py:518
  28.2 44.5 %collective-permute-start.7 = (f32[19,96,128]{2,1,0:T(8,128)}, f32[19,96,128]{2,1,0:T(8,128)}, u32[]{:S(2)}, u32[]{:S(2)}) collective-permute-start(f32[19,96,128]{2,1,0:T(8,128)} %get-tuple-element.38), channel_id=1, source_target_pairs={{2,4},{3,5},{4,2},{5,3},{10,12},{11,13},{12,10},{13,11},{18,20},{1... | collective-permute-start | bytes 2801672 | tf_op jit(solution)/shard_map/ppermute | solution.py:525
  29.8 2.1 %copy-start.9 = (f32[2,37,128]{2,1,0:T(8,128)}, f32[2,37,128]{2,1,0:T(8,128)S(1)}, u32[]{:S(2)}) copy-start(f32[2,37,128]{2,1,0:T(8,128)S(1)} %collective-permute-done.2.refs_0_) | copy-start | bytes 113668
  31.9 0.6 copy-start.8
  37.0 40.1 %collective-permute-start.8 = (f32[5,37,128]{2,1,0:T(8,128)}, f32[5,37,128]{2,1,0:T(8,128)S(1)}, u32[]{:S(2)}, u32[]{:S(2)}) collective-permute-start(f32[5,37,128]{2,1,0:T(8,128)} %get-tuple-element.40), channel_id=1, source_target_pairs={{2,4},{3,5},{4,2},{5,3},{10,12},{11,13},{12,10},{13,11},{18,20},{1... | collective-permute-start | bytes 284168 | tf_op jit(solution)/shard_map/ppermute | solution.py:526
  50.9 70.9 %collective-permute-start.4 = (f32[1152,128]{1,0:T(8,128)}, f32[1152,128]{1,0:T(8,128)S(1)}, u32[]{:S(2)}, u32[]{:S(2)}) collective-permute-start(f32[1152,128]{1,0:T(8,128)} %get-tuple-element.36), channel_id=1, source_target_pairs={{0,2},{1,3},{2,0},{3,1},{4,6},{5,7},{6,4},{7,5},{8,10},{9,11},{10,... | collective-permute-start | bytes 1769480 | tf_op jit(solution)/shard_map/ppermute | solution.py:564
  72.0 50.7 %collective-permute-start.5 = (f32[1152,128]{1,0:T(8,128)}, f32[1152,128]{1,0:T(8,128)S(1)}, u32[]{:S(2)}, u32[]{:S(2)}) collective-permute-start(f32[1152,128]{1,0:T(8,128)} %get-tuple-element.37.refs_2_), channel_id=1, source_target_pairs={{0,3},{1,2},{2,1},{3,0},{4,7},{5,6},{6,5},{7,4},{8,11},{9,10},{10,... | collective-permute-start | bytes 1769480 | tf_op jit(solution)/shard_map/ppermute | solution.py:564
  72.7 0.9 copy-start.2
  77.1 0.6 copy-start.6
  93.6 35.2 %collective-permute-start.9 = (f32[1152,128]{1,0:T(8,128)}, f32[1152,128]{1,0:T(8,128)S(1)}, u32[]{:S(2)}, u32[]{:S(2)}) collective-permute-start(f32[1152,128]{1,0:T(8,128)} %get-tuple-element.41), channel_id=1, source_target_pairs={{0,4},{1,5},{2,0},{3,1},{4,6},{5,7},{6,2},{7,3},{8,12},{9,13},{10,... | collective-permute-start | bytes 1769480 | tf_op jit(solution)/shard_map/ppermute | solution.py:564
  97.1 31.8 %collective-permute-start.10 = (f32[1152,128]{1,0:T(8,128)}, f32[1152,128]{1,0:T(8,128)S(1)}, u32[]{:S(2)}, u32[]{:S(2)}) collective-permute-start(f32[1152,128]{1,0:T(8,128)} %get-tuple-element.42.refs_2_), channel_id=1, source_target_pairs={{0,5},{1,4},{2,1},{3,0},{4,7},{5,6},{6,3},{7,2},{8,13},{9,12},{10,... | collective-permute-start | bytes 1769480 | tf_op jit(solution)/shard_map/ppermute | solution.py:564
  108.4 18.6 %copy-start.3 = (s32[32,96]{1,0:T(8,128)S(1)}, s32[32,96]{1,0:T(8,128)}, u32[]{:S(2)}) copy-start(s32[32,96]{1,0:T(8,128)} %reshape.22.owner_ref) | copy-start | bytes 36868
  108.4 18.8 %copy-start.10 = (bf16[96,96,1]{1,0,2:T(8,128)(2,1)S(1)}, bf16[96,96,1]{1,0,2:T(8,128)(2,1)}, u32[]{:S(2)}) copy-start(bf16[96,96,1]{1,0,2:T(8,128)(2,1)} %constant.104) | copy-start | bytes 55300
  108.4 41.2 %collective-permute-start.12 = (f32[1152,128]{1,0:T(8,128)}, f32[1152,128]{1,0:T(8,128)S(1)}, u32[]{:S(2)}, u32[]{:S(2)}) collective-permute-start(f32[1152,128]{1,0:T(8,128)} %get-tuple-element.44.refs_2_), channel_id=1, source_target_pairs={{0,7},{1,6},{2,3},{3,2},{4,5},{5,4},{6,1},{7,0},{8,15},{9,14},{10,... | collective-permute-start | bytes 1769480 | tf_op jit(solution)/shard_map/ppermute | solution.py:564
  121.8 25.9 %collective-permute-start.13 = (f32[1152,128]{1,0:T(8,128)}, f32[1152,128]{1,0:T(8,128)S(1)}, u32[]{:S(2)}, u32[]{:S(2)}) collective-permute-start(f32[1152,128]{1,0:T(8,128)} %get-tuple-element.46), channel_id=1, source_target_pairs={{0,1},{1,0},{2,3},{3,2},{4,5},{5,4},{6,7},{7,6},{8,9},{9,8},{10,11... | collective-permute-start | bytes 1769480 | tf_op jit(solution)/shard_map/ppermute | solution.py:564
  122.7 26.9 %collective-permute-start.11 = (f32[1152,128]{1,0:T(8,128)}, f32[1152,128]{1,0:T(8,128)}, u32[]{:S(2)}, u32[]{:S(2)}) collective-permute-start(f32[1152,128]{1,0:T(8,128)} %get-tuple-element.43), channel_id=1, source_target_pairs={{0,6},{1,7},{2,2},{3,3},{4,4},{5,5},{6,0},{7,1},{8,14},{9,15},{10,... | collective-permute-start | bytes 1769480 | tf_op jit(solution)/shard_map/ppermute | solution.py:564
  149.6 1.1 copy-start

commit v10 on v9

--- a/solution.py
+++ b/solution.py
@@ -55,10 +55,9 @@
     arrival = lax.broadcasted_iota(jnp.int32, (rows, cols), 0) + top_row
     row = jnp.clip(arrival - 1 + shift_ref[...], 1, lat_total - 3).astype(F32)
     column = (owner_ref[...] * cols + column_ref[...]).astype(F32)
-    for k in range(words_ref.shape[0]):
-        for w, word in enumerate((column, row, frac_ref[0], frac_ref[1])):
-            words_ref[k, w] = jnp.full((rows, LANES), -1.0, F32)
-            words_ref[k, w, :, :cols] = word
+    for w, word in enumerate((column, row, frac_ref[0], frac_ref[1])):
+        words_ref[w] = jnp.full((rows, LANES), -1.0, F32)
+        words_ref[w, :, :cols] = word
     first, last = s_ref[0], s_ref[rows - 1]
     far = 1.0 / (1.0 - POLE)
 
@@ -90,7 +89,7 @@
 def edges(s, owner, columns, lat_shift, fractions):
     rows, cols, ch = s.shape
     shape = lambda n: jax.ShapeDtypeStruct((n, cols, ch), F32)
-    words = jax.ShapeDtypeStruct((lax.axis_size("lon"), 4, rows, LANES), F32)
+    words = jax.ShapeDtypeStruct((4, rows, LANES), F32)
     return pl.pallas_call(
         edge_kernel,
         out_shape=(shape(UP + 1), shape(DOWN + 1), shape(UP + 1), shape(DOWN + 1), words),
@@ -254,13 +253,13 @@
     band = lax.axis_index("lat")
     origin = (meta(count) * cols).astype(F32)
     for d in range(count):
-        local = cells_refs[d][0, 0] - origin
+        local = cells_refs[d][0] - origin
         mine = (local >= 0.0) & (local < float(cols))
         one = jnp.where(mine, 1.0, 0.0)
         rank[d] = jnp.where(mine, dot(one.astype(BF), tri_ref[...]), -1000.0)
-        parts = [local, cells_refs[d][0, 1] - (band * rows - UP).astype(F32)]
+        parts = [local, cells_refs[d][1] - (band * rows - UP).astype(F32)]
         for w in (2, 3):
-            left = cells_refs[d][0, w]
+            left = cells_refs[d][w]
             for _ in range(3):
                 part = left.astype(BF).astype(F32)
                 parts.append(part)
@@ -396,7 +395,7 @@
 
 
 def taps(meta, width, at, count, base, tables, cells, cols, cap, after):
-    _, words, rows, lanes = cells.shape
+    words, rows, lanes = cells[0].shape
     ch = tables[0].shape[0] // (rows + UP + DOWN)
     span = 112
     tri = jnp.asarray(np.triu(np.ones((lanes, lanes)), 1), BF)
@@ -410,10 +409,7 @@
             num_scalar_prefetch=2,
             grid=(1,),
             in_specs=[pl.BlockSpec(memory_space=pl.ANY)] * (len(tables) + 1)
-            + [
-                pl.BlockSpec((1, words, rows, lanes), functools.partial(lambda g, m, b, k: (m[lax.axis_index("lon") * width + k], 0, 0, 0), k=at + k))
-                for k in range(count)
-            ]
+            + [pl.BlockSpec((words, rows, lanes), lambda g, m, b: (0, 0, 0))] * count
             + [pl.BlockSpec(tri.shape, lambda g, m, b: (0, 0))],
             out_specs=[pl.BlockSpec(memory_space=pl.ANY)] * count,
             scratch_shapes=[
@@ -434,7 +430,7 @@
         ),
         compiler_params=pltpu.CompilerParams(vmem_limit_bytes=VMEM_LIMIT),
         name="taps",
-    )(meta, base, *tables, after, *([cells] * count), tri)
+    )(meta, base, *tables, after, *cells, tri)
 
 
 def place_kernel(target_ref, *refs, cap):
@@ -511,16 +507,37 @@
     down, up, top, bottom, words = edges(tracers, owner, columns, lat_shift, fractions)
     above = lax.ppermute(down, "lat", [(i, i + 1) for i in range(bands - 1)])
     below = lax.ppermute(up, "lat", [(i + 1, i) for i in range(bands - 1)])
-    asked = lax.all_to_all(words, "lon", split_axis=0, concat_axis=0, tiled=True)
+    goals = ((1, 0, 3, 2), (2, 0, 3, 1), (3, 1, 2, 0), (0, 1, 2, 3))
+    shifts = list(range(quarter))[::-1]
+    calls = [(group, shifts[n : n + 2]) for group in range(4) for n in range(0, quarter, 2)]
+    plan = []
+    for s in range(sectors):
+        k, o = s // quarter, s % quarter
+        row = []
+        for group, pair in calls:
+            which = int(group in (1, 2) and k in (1, 2))
+            dests = [at(goals[group][k], (o + a) % quarter) for a in pair]
+            row += dests + [dict(mirror).get(s, s) if which else s, which]
+            row += [d * (rows + 1) for d in range(len(pair))]
+        plan.append(row)
+    meta, width = jnp.asarray(np.array(plan, np.int32).reshape(-1)), len(plan[0])
+
+    def moves_of(group, a):
+        return [(at(k, o), at(goals[group][k], (o + a) % quarter)) for k in range(4) for o in range(quarter)]
+
+    asked = {}
+    for group, pair in calls:
+        for a in pair:
+            back = [(j, i) for i, j in moves_of(group, a)]
+            asked[group, a] = words
+            if any(i != j for i, j in back):
+                asked[group, a] = lax.ppermute(words, "lon", back)
+    served = [[row[sum(2 * len(p) + 2 for _, p in calls[:n]) + len(pair)] for n, (_, pair) in enumerate(calls)] for row in plan]
+    origins = jnp.asarray(np.array(served, np.float32) * cols)[me]
 
     x, right, left, rest = lat_solve(rows, head, [tracers], (above, below, top, bottom))
     west = lax.ppermute(right, "lon", [(i, (i + 1) % sectors) for i in range(sectors)])
     east = lax.ppermute(left, "lon", [((i + 1) % sectors, i) for i in range(sectors)])
-    origins = np.array([[s * cols, dict(mirror).get(s, s) * cols] for s in range(sectors)], np.float32)
-    local = asked[None, :, 0] - jnp.asarray(origins)[me][:, None, None, None]
-    inside = ((local >= 0.0) & (local < float(cols))).astype(F32).reshape(2 * sectors, rows, -1)
-    base = bases(inside).astype(jnp.int32).reshape(-1)
-
     own, sides = lon_solve(x, west, east)
     rest = lax.ppermute(rest, "lon", mirror)
     sides = lax.ppermute(sides, "lon", mirror)
@@ -535,31 +552,19 @@
     part = jnp.where(near, jnp.where(q == mine, 3, 0), jnp.where(alike, 2, 1)) * quarter
     target = ((part + (offset - late_owner) % quarter) * cap + slot).reshape(cells)
 
-    goals = ((1, 0, 3, 2), (2, 0, 3, 1), (3, 1, 2, 0), (0, 1, 2, 3))
-    shifts = list(range(quarter))[::-1]
-    calls = [(group, shifts[n : n + 2]) for group in range(4) for n in range(0, quarter, 2)]
-    plan = []
-    for s in range(sectors):
-        k, o = s // quarter, s % quarter
-        row = []
-        for group, pair in calls:
-            which = int(group in (1, 2) and k in (1, 2))
-            dests = [at(goals[group][k], (o + a) % quarter) for a in pair]
-            row += dests + [dict(mirror).get(s, s) if which else s, which]
-            row += [(which * sectors + dest) * (rows + 1) for dest in dests]
-        plan.append(row)
-    meta, width = jnp.asarray(np.array(plan, np.int32).reshape(-1)), len(plan[0])
-
     parts = [None] * sectors
     tables, done, values = [own], 0, [own]
     for group, pair in calls:
         if group == 1 and len(tables) == 1:
             other = lat_solve(rows, head, [first, rest])[0]
             tables = [own, lon_solve(other, sides)[0]]
-        values = taps(meta, width, done, len(pair), base, tables, asked, cols, cap, values[0])
+        cells_of = [asked[group, a] for a in pair]
+        local = jnp.stack([cells[0] for cells in cells_of]) - origins[calls.index((group, pair))]
+        base = bases(((local >= 0.0) & (local < float(cols))).astype(F32)).astype(jnp.int32).reshape(-1)
+        values = taps(meta, width, done, len(pair), base, tables, cells_of, cols, cap, values[0])
         done += 2 * len(pair) + 2
         for a, value in zip(pair, values):
-            moves = [(at(k, o), at(goals[group][k], (o + a) % quarter)) for k in range(4) for o in range(quarter)]
+            moves = moves_of(group, a)
             if any(i != j for i, j in moves):
                 value = lax.ppermute(value, "lon", moves)
             parts[group * quarter + a] = value

time: 159 us -> 181 us (1.14)
  starting transfers between devices: 51.9 us -> 66.9 us
  local copies, waits for them, and re-layouts: 8.33 us -> 12.8 us
  other arithmetic: 2.34 us -> 5.01 us
    ppermute x0 -> x7, starting transfers between devices: none -> 15.3 us  [transport(): asked[group, a] = lax.ppermute(words, 'lon', back)]
    ppermute x7, starting transfers between devices: 32.6 us -> 41.3 us  [transport(): value = lax.ppermute(value, 'lon', moves)]
    all_to_all x1 -> x0, starting transfers between devices: 7.28 us -> none  [transport(): lax.all_to_all(words, 'lon', split_axis=0, concat_axis=0, tiled=True)]
    slice x0 -> x9, local copies, waits for them, and re-layouts: none -> 2.88 us  [the longest x8 2.21 us: transport(): cells[0]]
    reduce_sum x2 -> x5, other arithmetic: 0.32 us -> 2.98 us  [bases(): totals = jnp.sum(ones, axis=2)]
    reshape x1 -> x4, local copies, waits for them, and re-layouts: 0.68 us -> 2.55 us  [transport(): bases(((local >= 0.0) & (local < float(cols))).astype(F32))]
    unnamed x23 -> x33, local copies, waits for them, and re-layouts: 4.52 us -> 5.17 us
  transfers between devices with their start and end apart: 15 -> 21, of which waited for: 4 -> 3; matrix products, arithmetic and copies ran while one was open for 3% -> 6% of each run, Pallas kernels for 39% -> 34%
where the time goes in v10:
time: 181 us; the launch traced here: 179 us
  Pallas kernels  70.1 us (39%)
  starting transfers between devices  66.9 us (37%)
  waiting for transfers between devices  22.3 us (12%)
  local copies, waits for them, and re-layouts  12.8 us (7%)
  other arithmetic  5.01 us (3%)
    pallas_call x4, Pallas kernels, taps(): pl.pallas_call(functools.partial(tap_kernel, tables=len(tables), count=co...  44.8 us
    ppermute x7, starting transfers between devices, transport(): value = lax.ppermute(value, 'lon', moves)  41.3 us
    ppermute x7, waiting for transfers between devices, transport(): value = lax.ppermute(value, 'lon', moves)  21.7 us
    ppermute x7, starting transfers between devices, transport(): asked[group, a] = lax.ppermute(words, 'lon', back)  15.3 us
    pallas_call x2, Pallas kernels, lon_solve(): pl.pallas_call(functools.partial(lon_kernel, packed=packed), out_shape=sh...  9.08 us
    pallas_call x2, Pallas kernels, lat_solve(): pl.pallas_call(functools.partial(lat_kernel, pieces=len(pieces), head=hea...  7.28 us
    pallas_call x1, Pallas kernels, place(): pl.pallas_call(functools.partial(place_kernel, cap=cap), out_shape=jax.Sh...  6.36 us
    unnamed x33, local copies, waits for them, and re-layouts  5.17 us
  transfers between devices with their start and end apart: 21, of which 3 were waited for; matrix products, arithmetic and copies ran while one was open for 6% of the time, Pallas kernels for 34%

profile of v10, /device:TPU:0, one launch (start us, length us, event | category | flops | bytes accessed | tf_op | source)
XLA Modules:
  0.0 178.5 jit_solution(15553969332041655094)
XLA Ops:
  0.5 1.4 reduce.3
  1.9 0.7 reshape.31.owner_ref
  2.6 2.5 %edges.1 = (f32[3,96,128]{2,1,0:T(8,128)}, f32[4,96,128]{2,1,0:T(8,128)}, f32[3,96,128]{2,1,0:T(8,128)}, f32[4,96,128]{2,1,0:T(8,128)}, f32[4,32,128]{2,1,0:T(8,128)}) custom-call(f32[32,96,128]{2,1,0:T(8,128)} %refs_0_.1, s32[32,96]{1,0:T(8,128)} %reshape.31.owner_ref, s32[32,96]{1,0:T(8,128)} %column_ref.1, s32[32,96]{1,0:T(8,128)} %shift_ref.1, ...), custom_call_target="tpu_custom_call" | custom-call | flops 2359296 | bytes 2359296 | tf_op jit(solution)/shard_map/edges/pallas_call | solution.py:93
  5.1 3.0 %collective-permute-start.19 = (f32[4,32,128]{2,1,0:T(8,128)}, f32[4,32,128]{2,1,0:T(8,128)S(1)}, u32[]{:S(2)}, u32[]{:S(2)}) collective-permute-start(f32[4,32,128]{2,1,0:T(8,128)} %get-tuple-element.32.refs_4_), channel_id=1, source_target_pairs={{1,0},{0,1},{3,2},{2,3},{5,4},{4,5},{7,6},{6,7},{9,8},{8,9},{11,10... | collective-permute-start | bytes 196616 | tf_op jit(solution)/shard_map/ppermute | solution.py:534
  8.1 5.5 %collective-permute-start.16 = (f32[4,32,128]{2,1,0:T(8,128)}, f32[4,32,128]{2,1,0:T(8,128)S(1)}, u32[]{:S(2)}, u32[]{:S(2)}) collective-permute-start(f32[4,32,128]{2,1,0:T(8,128)} %get-tuple-element.32.refs_4_), channel_id=1, source_target_pairs={{6,0},{7,1},{2,2},{3,3},{4,4},{5,5},{0,6},{1,7},{14,8},{15,9},{10,... | collective-permute-start | bytes 196616 | tf_op jit(solution)/shard_map/ppermute | solution.py:534
  13.7 5.2 %collective-permute-start.8 = (f32[4,32,128]{2,1,0:T(8,128)}, f32[4,32,128]{2,1,0:T(8,128)}, u32[]{:S(2)}, u32[]{:S(2)}) collective-permute-start(f32[4,32,128]{2,1,0:T(8,128)} %get-tuple-element.32.refs_4_), channel_id=1, source_target_pairs={{5,0},{4,1},{1,2},{0,3},{7,4},{6,5},{3,6},{2,7},{13,8},{12,9},{9,1... | collective-permute-start | bytes 196616 | tf_op jit(solution)/shard_map/ppermute | solution.py:534
  18.9 0.8 slice.58
  19.8 0.7 constant_dynamic-slice_fusion
  20.5 0.7 fusion.14
  21.8 0.7 convert_reduce_fusion.1
  22.6 1.5 collective-permute-start.2
  24.1 1.3 collective-permute-start
  25.4 0.7 convert_reduce_fusion.2
  26.1 1.3 collective-permute-start.1
  27.5 0.7 collective-permute-start.10
  28.3 0.7 slice.65
  29.1 0.7 slice.64
  29.8 0.8 convert_reduce_fusion.3
  30.6 0.7 convert_reduce_fusion.4
  32.1 3.9 %lat_solve.2 = (f32[37,96,128]{2,1,0:T(8,128)}, f32[2,37,128]{2,1,0:T(8,128)}, f32[3,37,128]{2,1,0:T(8,128)}, f32[19,96,128]{2,1,0:T(8,128)}) custom-call(f32[32,96,128]{2,1,0:T(8,128)} %refs_0_.1, f32[3,96,128]{2,1,0:T(8,128)} %copy-done.6, f32[4,96,128]{2,1,0:T(8,128)} %copy-done.5, f32[3,96,128]{2,1,0:T(8,128)} %get-tuple-element.28.refs_3_, ...), custom_call_target="tpu_custom_call" | custom-call | flops 3932160 | bytes 3932160 | tf_op jit(solution)/shard_map/lat_solve/pallas_call | solution.py:176
  36.0 1.6 collective-permute-start.11
  37.7 1.5 collective-permute-start.4
  39.2 3.2 %collective-permute-start.5 = (f32[3,37,128]{2,1,0:T(8,128)}, f32[3,37,128]{2,1,0:T(8,128)S(1)}, u32[]{:S(2)}, u32[]{:S(2)}) collective-permute-start(f32[3,37,128]{2,1,0:T(8,128)} %get-tuple-element.34), channel_id=1, source_target_pairs={{1,0},{2,1},{3,2},{4,3},{5,4},{6,5},{7,6},{0,7},{9,8},{10,9},{11,1... | collective-permute-start | bytes 170504 | tf_op jit(solution)/shard_map/ppermute | solution.py:540
  42.6 0.6 reshape.36.base_ref
  43.2 0.6 reshape.35.base_ref
  43.8 0.7 reshape.34.base_ref
  44.5 0.7 reshape.33.base_ref
  45.8 0.6 copy-done.8
  46.4 4.5 %lon_solve.2 = (bf16[4736,384]{1,0:T(8,128)(2,1)}, f32[5,37,128]{2,1,0:T(8,128)}) custom-call(f32[37,96,128]{2,1,0:T(8,128)} %get-tuple-element.30.x_ref, f32[2,37,128]{2,1,0:T(8,128)} %copy-done.9, f32[3,37,128]{2,1,0:T(8,128)} %copy-done.8, bf16[384,128]{1,0:T(8,128)(2,1)} %constant.103.refs_2_.refs_1_), custom_call_target="tpu_custom_call" | custom-call | flops 465567744 | bytes 3637248 | tf_op jit(solution)/shard_map/lon_solve/pallas_call | solution.py:225
  50.9 0.7 collective-permute-start.12
  51.6 11.2 %taps.4 = (f32[1152,128]{1,0:T(8,128)}, f32[1152,128]{1,0:T(8,128)}) custom-call(s32[192]{0:T(256)} %constant.90.clone.meta_ref, s32[66]{0:T(128)} %reshape.33.base_ref, bf16[4736,384]{1,0:T(8,128)(2,1)} %get-tuple-element.35.refs_0_.refs_1_, bf16[4736,384]{1,0:T(8,128)(2,1)} %get-tuple-element.35.refs_0_.refs_1_, f32[4,32,128]{2,1,0:T(8,128)} %copy-done.14, ...), custom_call_target="tpu_custom_call" | custom-call | flops 4831838208 | bytes 3637248 | tf_op jit(solution)/shard_map/taps/pallas_call | solution.py:403
  62.8 30.4 %collective-permute-start.6 = (f32[1152,128]{1,0:T(8,128)}, f32[1152,128]{1,0:T(8,128)S(1)}, u32[]{:S(2)}, u32[]{:S(2)}) collective-permute-start(f32[1152,128]{1,0:T(8,128)} %get-tuple-element.36), channel_id=1, source_target_pairs={{0,2},{1,3},{2,0},{3,1},{4,6},{5,7},{6,4},{7,5},{8,10},{9,11},{10,... | collective-permute-start | bytes 1769480 | tf_op jit(solution)/shard_map/ppermute | solution.py:569
  93.3 0.9 copy-done.2
  94.2 3.4 %lat_solve.3 = (f32[37,96,128]{2,1,0:T(8,128)}, f32[2,37,128]{2,1,0:T(8,128)}, f32[3,37,128]{2,1,0:T(8,128)}) custom-call(f32[20,96,128]{2,1,0:T(8,128)} %copy-done.2, f32[19,96,128]{2,1,0:T(8,128)} %collective-permute-done.11.refs_1_, f32[96,128]{1,0:T(8,128)} %constant.92.clone.refs_5_.refs_2_, f32[96,128]{1,0:T(8,128)} %constant.93.clone.refs_6_.refs_3_), custom_call_target="tpu_custom_call" | custom-call | flops 3932160 | bytes 3932160 | tf_op jit(solution)/shard_map/lat_solve/pallas_call | solution.py:176
  97.6 0.6 copy-done.7
  98.3 4.6 %lon_solve.3.refs_1_ = bf16[4736,384]{1,0:T(8,128)(2,1)} custom-call(f32[37,96,128]{2,1,0:T(8,128)} %get-tuple-element.39.x_ref, f32[5,37,128]{2,1,0:T(8,128)} %copy-done.7, bf16[384,128]{1,0:T(8,128)(2,1)} %constant.103.refs_2_.refs_1_), custom_call_target="tpu_custom_call" | custom-call | flops 465567744 | bytes 3637248 | tf_op jit(solution)/shard_map/lon_solve/pallas_call | solution.py:225
  102.9 11.2 %taps.5 = (f32[1152,128]{1,0:T(8,128)}, f32[1152,128]{1,0:T(8,128)}) custom-call(s32[192]{0:T(256)} %constant.90.clone.meta_ref, s32[66]{0:T(128)} %reshape.34.base_ref, bf16[4736,384]{1,0:T(8,128)(2,1)} %get-tuple-element.35.refs_0_.refs_1_, bf16[4736,384]{1,0:T(8,128)(2,1)} %lon_solve.3.refs_1_, f32[1152,128]{1,0:T(8,128)} %get-tuple-element.37.refs_2_, ...), custom_call_target="tpu_custom_call" | custom-call | flops 4831838208 | bytes 3637248 | tf_op jit(solution)/shard_map/taps/pallas_call | solution.py:403
  114.0 3.5 %collective-permute-start.13 = (f32[1152,128]{1,0:T(8,128)}, f32[1152,128]{1,0:T(8,128)S(1)}, u32[]{:S(2)}, u32[]{:S(2)}) collective-permute-start(f32[1152,128]{1,0:T(8,128)} %get-tuple-element.41), channel_id=1, source_target_pairs={{0,4},{1,5},{2,0},{3,1},{4,6},{5,7},{6,2},{7,3},{8,12},{9,13},{10,... | collective-permute-start | bytes 1769480 | tf_op jit(solution)/shard_map/ppermute | solution.py:569
  117.5 11.3 %taps.6 = (f32[1152,128]{1,0:T(8,128)}, f32[1152,128]{1,0:T(8,128)}) custom-call(s32[192]{0:T(256)} %constant.90.clone.meta_ref, s32[66]{0:T(128)} %reshape.35.base_ref, bf16[4736,384]{1,0:T(8,128)(2,1)} %get-tuple-element.35.refs_0_.refs_1_, bf16[4736,384]{1,0:T(8,128)(2,1)} %lon_solve.3.refs_1_, f32[1152,128]{1,0:T(8,128)} %get-tuple-element.42.refs_2_, ...), custom_call_target="tpu_custom_call" | custom-call | flops 4831838208 | bytes 3637248 | tf_op jit(solution)/shard_map/taps/pallas_call | solution.py:403
  128.8 2.1 %collective-permute-start.18 = (f32[1152,128]{1,0:T(8,128)}, f32[1152,128]{1,0:T(8,128)S(1)}, u32[]{:S(2)}, u32[]{:S(2)}) collective-permute-start(f32[1152,128]{1,0:T(8,128)} %get-tuple-element.44.refs_2_), channel_id=1, source_target_pairs={{0,7},{1,6},{2,3},{3,2},{4,5},{5,4},{6,1},{7,0},{8,15},{9,14},{10,... | collective-permute-start | bytes 1769480 | tf_op jit(solution)/shard_map/ppermute | solution.py:569
  130.9 11.2 %taps.7 = (f32[1152,128]{1,0:T(8,128)}, f32[1152,128]{1,0:T(8,128)}) custom-call(s32[192]{0:T(256)} %constant.90.clone.meta_ref, s32[66]{0:T(128)} %reshape.36.base_ref, bf16[4736,384]{1,0:T(8,128)(2,1)} %get-tuple-element.35.refs_0_.refs_1_, bf16[4736,384]{1,0:T(8,128)(2,1)} %lon_solve.3.refs_1_, f32[1152,128]{1,0:T(8,128)} %get-tuple-element.44.refs_2_, ...), custom_call_target="tpu_custom_call" | custom-call | flops 4831838208 | bytes 3637248 | tf_op jit(solution)/shard_map/taps/pallas_call | solution.py:403
  142.1 1.5 collective-permute-start.20
  143.6 3.7 %collective-permute-start.17 = (f32[1152,128]{1,0:T(8,128)}, f32[1152,128]{1,0:T(8,128)}, u32[]{:S(2)}, u32[]{:S(2)}) collective-permute-start(f32[1152,128]{1,0:T(8,128)} %get-tuple-element.43), channel_id=1, source_target_pairs={{0,6},{1,7},{2,2},{3,3},{4,4},{5,5},{6,0},{7,1},{8,14},{9,15},{10,... | collective-permute-start | bytes 1769480 | tf_op jit(solution)/shard_map/ppermute | solution.py:569
  147.8 0.6 fusion.9
  148.4 0.8 reshape.32.target_ref
  149.2 21.7 %collective-permute-done.20.refs_7_ = f32[1152,128]{1,0:T(8,128)S(1)} collective-permute-done((f32[1152,128]{1,0:T(8,128)}, f32[1152,128]{1,0:T(8,128)S(1)}, u32[]{:S(2)}, u32[]{:S(2)}) %collective-permute-start.20) | collective-permute-done | bytes 589856 | tf_op jit(solution)/shard_map/ppermute | solution.py:569
  170.9 1.1 copy-done
  172.0 6.4 %place.1 = f32[3072,128]{1,0:T(8,128)} custom-call(s32[3072]{0:T(1024)S(1)} %reshape.32.target_ref, f32[1152,128]{1,0:T(8,128)S(1)} %collective-permute-done.6.refs_0_, f32[1152,128]{1,0:T(8,128)S(1)} %collective-permute-done.7.refs_1_, f32[1152,128]{1,0:T(8,128)S(1)} %collective-permute-done.13.refs_2_, f32[1152,128]{1,0:T(8,128)S(1)} %collective-permute-done.14.refs_3_, ...), custom_call_target="tpu_custom_call" | custom-call | bytes 9437184 | tf_op jit(solution)/shard_map/place/pallas_call | solution.py:457
  (67 shorter events, 3.9 us)
Async XLA Ops:
  0.0 19.7 %copy-start.1 = (f32[32,96,128]{2,1,0:T(8,128)S(1)}, f32[32,96,128]{2,1,0:T(8,128)}, u32[]{:S(2)}) copy-start(f32[32,96,128]{2,1,0:T(8,128)} %refs_0_.1) | copy-start | bytes 4718596
  2.6 19.9 %copy-start.3 = (f32[32,33]{1,0:T(8,128)S(1)}, f32[32,33]{1,0:T(8,128)}, u32[]{:S(2)}) copy-start(f32[32,33]{1,0:T(8,128)} %constant.96.clone) | copy-start | bytes 12676
  5.1 16.1 %collective-permute-start.19 = (f32[4,32,128]{2,1,0:T(8,128)}, f32[4,32,128]{2,1,0:T(8,128)S(1)}, u32[]{:S(2)}, u32[]{:S(2)}) collective-permute-start(f32[4,32,128]{2,1,0:T(8,128)} %get-tuple-element.32.refs_4_), channel_id=1, source_target_pairs={{1,0},{0,1},{3,2},{2,3},{5,4},{4,5},{7,6},{6,7},{9,8},{8,9},{11,10... | collective-permute-start | bytes 196616 | tf_op jit(solution)/shard_map/ppermute | solution.py:534
  8.1 14.5 %collective-permute-start.16 = (f32[4,32,128]{2,1,0:T(8,128)}, f32[4,32,128]{2,1,0:T(8,128)S(1)}, u32[]{:S(2)}, u32[]{:S(2)}) collective-permute-start(f32[4,32,128]{2,1,0:T(8,128)} %get-tuple-element.32.refs_4_), channel_id=1, source_target_pairs={{6,0},{7,1},{2,2},{3,3},{4,4},{5,5},{0,6},{1,7},{14,8},{15,9},{10,... | collective-permute-start | bytes 196616 | tf_op jit(solution)/shard_map/ppermute | solution.py:534
  13.6 10.5 %collective-permute-start.15 = (f32[4,32,128]{2,1,0:T(8,128)}, f32[4,32,128]{2,1,0:T(8,128)S(1)}, u32[]{:S(2)}, u32[]{:S(2)}) collective-permute-start(f32[4,32,128]{2,1,0:T(8,128)} %get-tuple-element.32.refs_4_), channel_id=1, source_target_pairs={{7,0},{6,1},{3,2},{2,3},{5,4},{4,5},{1,6},{0,7},{15,8},{14,9},{11,... | collective-permute-start | bytes 196616 | tf_op jit(solution)/shard_map/ppermute | solution.py:534
  13.7 12.5 %collective-permute-start.9 = (f32[4,32,128]{2,1,0:T(8,128)}, f32[4,32,128]{2,1,0:T(8,128)}, u32[]{:S(2)}, u32[]{:S(2)}) collective-permute-start(f32[4,32,128]{2,1,0:T(8,128)} %get-tuple-element.32.refs_4_), channel_id=1, source_target_pairs={{4,0},{5,1},{0,2},{1,3},{6,4},{7,5},{2,6},{3,7},{12,8},{13,9},{8,1... | collective-permute-start | bytes 196616 | tf_op jit(solution)/shard_map/ppermute | solution.py:534
  13.7 13.7 %collective-permute-start.8 = (f32[4,32,128]{2,1,0:T(8,128)}, f32[4,32,128]{2,1,0:T(8,128)}, u32[]{:S(2)}, u32[]{:S(2)}) collective-permute-start(f32[4,32,128]{2,1,0:T(8,128)} %get-tuple-element.32.refs_4_), channel_id=1, source_target_pairs={{5,0},{4,1},{1,2},{0,3},{7,4},{6,5},{3,6},{2,7},{13,8},{12,9},{9,1... | collective-permute-start | bytes 196616 | tf_op jit(solution)/shard_map/ppermute | solution.py:534
  21.2 0.6 copy-start.10
  21.2 8.6 %collective-permute-start.3 = (f32[4,32,128]{2,1,0:T(8,128)}, f32[4,32,128]{2,1,0:T(8,128)S(1)}, u32[]{:S(2)}, u32[]{:S(2)}) collective-permute-start(f32[4,32,128]{2,1,0:T(8,128)} %get-tuple-element.32.refs_4_), channel_id=1, source_target_pairs={{2,0},{3,1},{0,2},{1,3},{6,4},{7,5},{4,6},{5,7},{10,8},{11,9},{8,1... | collective-permute-start | bytes 196616 | tf_op jit(solution)/shard_map/ppermute | solution.py:534
  22.6 4.9 %copy-start.11 = (f32[4,32,128]{2,1,0:T(8,128)}, f32[4,32,128]{2,1,0:T(8,128)S(1)}, u32[]{:S(2)}) copy-start(f32[4,32,128]{2,1,0:T(8,128)S(1)} %collective-permute-done.16.refs_4_) | copy-start | bytes 196612
  22.6 7.2 %collective-permute-start.2 = (f32[4,32,128]{2,1,0:T(8,128)}, f32[4,32,128]{2,1,0:T(8,128)S(1)}, u32[]{:S(2)}, u32[]{:S(2)}) collective-permute-start(f32[4,32,128]{2,1,0:T(8,128)} %get-tuple-element.32.refs_4_), channel_id=1, source_target_pairs={{3,0},{2,1},{1,2},{0,3},{7,4},{6,5},{5,6},{4,7},{11,8},{10,9},{9,1... | collective-permute-start | bytes 196616 | tf_op jit(solution)/shard_map/ppermute | solution.py:534
  24.1 3.4 %copy-start.12 = (f32[4,32,128]{2,1,0:T(8,128)}, f32[4,32,128]{2,1,0:T(8,128)S(1)}, u32[]{:S(2)}) copy-start(f32[4,32,128]{2,1,0:T(8,128)S(1)} %collective-permute-done.15.refs_3_) | copy-start | bytes 196612
  24.1 7.2 %collective-permute-start = (f32[3,96,128]{2,1,0:T(8,128)}, f32[3,96,128]{2,1,0:T(8,128)S(1)}, u32[]{:S(2)}, u32[]{:S(2)}) collective-permute-start(f32[3,96,128]{2,1,0:T(8,128)} %get-tuple-element.26), channel_id=1, source_target_pairs={{0,8},{8,16},{16,24},{1,9},{9,17},{17,25},{2,10},{10,18},{18,26},{... | collective-permute-start | bytes 442376 | tf_op jit(solution)/shard_map/ppermute | solution.py:508
  26.1 5.3 %collective-permute-start.1 = (f32[4,96,128]{2,1,0:T(8,128)}, f32[4,96,128]{2,1,0:T(8,128)S(1)}, u32[]{:S(2)}, u32[]{:S(2)}) collective-permute-start(f32[4,96,128]{2,1,0:T(8,128)} %get-tuple-element.27), channel_id=1, source_target_pairs={{8,0},{16,8},{24,16},{9,1},{17,9},{25,17},{10,2},{18,10},{26,18},{... | collective-permute-start | bytes 589832 | tf_op jit(solution)/shard_map/ppermute | solution.py:509
  27.5 65.8 %collective-permute-start.10 = (f32[20,96,128]{2,1,0:T(8,128)S(1)}, f32[20,96,128]{2,1,0:T(8,128)S(1)}, u32[]{:S(2)}, u32[]{:S(2)}) collective-permute-start(f32[20,96,128]{2,1,0:T(8,128)S(1)} %slice.53), channel_id=1, source_target_pairs={{2,4},{3,5},{4,2},{5,3},{10,12},{11,13},{12,10},{13,11},{18,20},{1... | collective-permute-start | bytes 2949128 | tf_op jit(solution)/shard_map/ppermute | solution.py:505
  29.8 21.1 %copy-start.13 = (f32[4,32,128]{2,1,0:T(8,128)}, f32[4,32,128]{2,1,0:T(8,128)S(1)}, u32[]{:S(2)}) copy-start(f32[4,32,128]{2,1,0:T(8,128)S(1)} %collective-permute-done.3.refs_3_) | copy-start | bytes 196612
  29.8 21.1 %copy-start.14 = (f32[4,32,128]{2,1,0:T(8,128)}, f32[4,32,128]{2,1,0:T(8,128)S(1)}, u32[]{:S(2)}) copy-start(f32[4,32,128]{2,1,0:T(8,128)S(1)} %collective-permute-done.2.refs_2_) | copy-start | bytes 196612
  31.3 0.7 copy-start.6
  31.4 0.7 copy-start.5
  36.0 57.3 %collective-permute-start.11 = (f32[19,96,128]{2,1,0:T(8,128)}, f32[19,96,128]{2,1,0:T(8,128)}, u32[]{:S(2)}, u32[]{:S(2)}) collective-permute-start(f32[19,96,128]{2,1,0:T(8,128)} %get-tuple-element.38), channel_id=1, source_target_pairs={{2,4},{3,5},{4,2},{5,3},{10,12},{11,13},{12,10},{13,11},{18,20},{1... | collective-permute-start | bytes 2801672 | tf_op jit(solution)/shard_map/ppermute | solution.py:542
  37.7 7.4 %collective-permute-start.4 = (f32[2,37,128]{2,1,0:T(8,128)}, f32[2,37,128]{2,1,0:T(8,128)S(1)}, u32[]{:S(2)}, u32[]{:S(2)}) collective-permute-start(f32[2,37,128]{2,1,0:T(8,128)} %get-tuple-element.33), channel_id=1, source_target_pairs={{0,1},{1,2},{2,3},{3,4},{4,5},{5,6},{6,7},{7,0},{8,9},{9,10},{10,1... | collective-permute-start | bytes 113672 | tf_op jit(solution)/shard_map/ppermute | solution.py:539
  39.2 6.4 %collective-permute-start.5 = (f32[3,37,128]{2,1,0:T(8,128)}, f32[3,37,128]{2,1,0:T(8,128)S(1)}, u32[]{:S(2)}, u32[]{:S(2)}) collective-permute-start(f32[3,37,128]{2,1,0:T(8,128)} %get-tuple-element.34), channel_id=1, source_target_pairs={{1,0},{2,1},{3,2},{4,3},{5,4},{6,5},{7,6},{0,7},{9,8},{10,9},{11,1... | collective-permute-start | bytes 170504 | tf_op jit(solution)/shard_map/ppermute | solution.py:540
  45.1 0.6 copy-start.9
  45.8 0.6 copy-start.8
  50.9 46.7 %collective-permute-start.12 = (f32[5,37,128]{2,1,0:T(8,128)}, f32[5,37,128]{2,1,0:T(8,128)S(1)}, u32[]{:S(2)}, u32[]{:S(2)}) collective-permute-start(f32[5,37,128]{2,1,0:T(8,128)} %get-tuple-element.40), channel_id=1, source_target_pairs={{2,4},{3,5},{4,2},{5,3},{10,12},{11,13},{12,10},{13,11},{18,20},{1... | collective-permute-start | bytes 284168 | tf_op jit(solution)/shard_map/ppermute | solution.py:543
  62.8 79.4 %collective-permute-start.6 = (f32[1152,128]{1,0:T(8,128)}, f32[1152,128]{1,0:T(8,128)S(1)}, u32[]{:S(2)}, u32[]{:S(2)}) collective-permute-start(f32[1152,128]{1,0:T(8,128)} %get-tuple-element.36), channel_id=1, source_target_pairs={{0,2},{1,3},{2,0},{3,1},{4,6},{5,7},{6,4},{7,5},{8,10},{9,11},{10,... | collective-permute-start | bytes 1769480 | tf_op jit(solution)/shard_map/ppermute | solution.py:569
  93.2 50.5 %collective-permute-start.7 = (f32[1152,128]{1,0:T(8,128)}, f32[1152,128]{1,0:T(8,128)S(1)}, u32[]{:S(2)}, u32[]{:S(2)}) collective-permute-start(f32[1152,128]{1,0:T(8,128)} %get-tuple-element.37.refs_2_), channel_id=1, source_target_pairs={{0,3},{1,2},{2,1},{3,0},{4,7},{5,6},{6,5},{7,4},{8,11},{9,10},{10,... | collective-permute-start | bytes 1769480 | tf_op jit(solution)/shard_map/ppermute | solution.py:569
  93.3 0.9 copy-start.2
  97.6 0.6 copy-start.7
  114.0 35.2 %collective-permute-start.13 = (f32[1152,128]{1,0:T(8,128)}, f32[1152,128]{1,0:T(8,128)S(1)}, u32[]{:S(2)}, u32[]{:S(2)}) collective-permute-start(f32[1152,128]{1,0:T(8,128)} %get-tuple-element.41), channel_id=1, source_target_pairs={{0,4},{1,5},{2,0},{3,1},{4,6},{5,7},{6,2},{7,3},{8,12},{9,13},{10,... | collective-permute-start | bytes 1769480 | tf_op jit(solution)/shard_map/ppermute | solution.py:569
  117.5 31.7 %collective-permute-start.14 = (f32[1152,128]{1,0:T(8,128)}, f32[1152,128]{1,0:T(8,128)S(1)}, u32[]{:S(2)}, u32[]{:S(2)}) collective-permute-start(f32[1152,128]{1,0:T(8,128)} %get-tuple-element.42.refs_2_), channel_id=1, source_target_pairs={{0,5},{1,4},{2,1},{3,0},{4,7},{5,6},{6,3},{7,2},{8,13},{9,12},{10,... | collective-permute-start | bytes 1769480 | tf_op jit(solution)/shard_map/ppermute | solution.py:569
  128.8 18.6 %copy-start.4 = (s32[32,96]{1,0:T(8,128)S(1)}, s32[32,96]{1,0:T(8,128)}, u32[]{:S(2)}) copy-start(s32[32,96]{1,0:T(8,128)} %reshape.31.owner_ref) | copy-start | bytes 36868
  128.8 18.8 %copy-start.15 = (bf16[96,96,1]{1,0,2:T(8,128)(2,1)S(1)}, bf16[96,96,1]{1,0,2:T(8,128)(2,1)}, u32[]{:S(2)}) copy-start(bf16[96,96,1]{1,0,2:T(8,128)(2,1)} %constant.104) | copy-start | bytes 55300
  128.8 42.1 %collective-permute-start.18 = (f32[1152,128]{1,0:T(8,128)}, f32[1152,128]{1,0:T(8,128)S(1)}, u32[]{:S(2)}, u32[]{:S(2)}) collective-permute-start(f32[1152,128]{1,0:T(8,128)} %get-tuple-element.44.refs_2_), channel_id=1, source_target_pairs={{0,7},{1,6},{2,3},{3,2},{4,5},{5,4},{6,1},{7,0},{8,15},{9,14},{10,... | collective-permute-start | bytes 1769480 | tf_op jit(solution)/shard_map/ppermute | solution.py:569
  142.1 28.8 %collective-permute-start.20 = (f32[1152,128]{1,0:T(8,128)}, f32[1152,128]{1,0:T(8,128)S(1)}, u32[]{:S(2)}, u32[]{:S(2)}) collective-permute-start(f32[1152,128]{1,0:T(8,128)} %get-tuple-element.46), channel_id=1, source_target_pairs={{0,1},{1,0},{2,3},{3,2},{4,5},{5,4},{6,7},{7,6},{8,9},{9,8},{10,11... | collective-permute-start | bytes 1769480 | tf_op jit(solution)/shard_map/ppermute | solution.py:569
  143.6 27.3 %collective-permute-start.17 = (f32[1152,128]{1,0:T(8,128)}, f32[1152,128]{1,0:T(8,128)}, u32[]{:S(2)}, u32[]{:S(2)}) collective-permute-start(f32[1152,128]{1,0:T(8,128)} %get-tuple-element.43), channel_id=1, source_target_pairs={{0,6},{1,7},{2,2},{3,3},{4,4},{5,5},{6,0},{7,1},{8,14},{9,15},{10,... | collective-permute-start | bytes 1769480 | tf_op jit(solution)/shard_map/ppermute | solution.py:569
  170.9 1.1 copy-start
